TPU v7x, 256 devices: a whole 4x4x8 slice. The times are simulated.
256 devices in a mesh: freq: 64 (over x, y_hi, z), space: 4 (over y_lo, core).
Axes of the slice: x: 4, y: 4 (y_hi: 2, y_lo: 2; y = y_hi * 2 + y_lo), z: 8, core: 2. Of those that a mesh axis runs over, the one named last changes fastest.
Arguments:
- modes: bfloat16 [8, 64, 2, 3, 24, 512], P(None, 'freq', None, None, None, 'space'), may hold values from -3 to 3
- point_weights: float32 [512], P('space'), may hold values from 0.25 to 4
- triads: int32 [8, 64, 16], P(None, 'freq'), may hold values from 0 to 511, as said below
- counts: int32 [8, 64], P(None, 'freq'), may hold values from 1 to 16, as said below
Outputs:
- grams: float32 [8, 64, 16, 1152], P(None, 'freq')
Inputs may be any that keep to these rules, and one draw needn't show every extreme that they name: `triads`: for each column c, its 128 entries (those beyond a bin's count included) hold, for every residue e modulo 64, exactly 2 values l with l mod 64 = e. `counts`: in every draw all reader bins of some column c have 16 live triads.
All inputs are finite; a program needn't handle non-finite values.
Results may differ from a plain program's by a relative error of at most 0.0029.
Values may be sent and summed in bfloat16 or wider, within the bound.
No kernel may reach another device: no remote copies, remote signals or barrier semaphores. Data moves between devices by JAX's collectives and lax.ppermute only.
A program may use at most 64 MiB of HBM per device.

v0:
```python
import jax
import jax.numpy as jnp
from jax import lax
from jax.sharding import PartitionSpec as P


def shifted(shard, axis, by):
    size = lax.axis_size(axis)
    return lax.ppermute(shard, axis, [(i, (i + by) % size) for i in range(size)])


def deposit(gathered, blocks, owner, req_table):
    wanted = lax.dynamic_index_in_dim(req_table, owner, 0, keepdims=False)
    picked = blocks[wanted]
    return lax.dynamic_update_slice_in_dim(gathered, picked[None], owner, 0)


def body(modes, point_weights, triads, counts):
    stride = lax.axis_size("freq")
    position = lax.axis_index("freq")
    own_modes = modes[:, 0]
    entry_lists = triads[:, 0]
    live_counts = counts[:, 0]
    bin_rows = own_modes.shape[0]
    list_width = entry_lists.shape[1]
    entries = bin_rows * list_width
    all_bins = bin_rows * stride
    capacity = entries // stride
    slot_span = 2 * capacity
    flat_lists = entry_lists.reshape(entries)
    reader = jnp.repeat(jnp.arange(bin_rows, dtype=jnp.int32), list_width)
    k_bins = reader * stride + position
    l_owner = flat_lists % stride
    l_row = flat_lists // stride
    m_bins = (k_bins + flat_lists) % all_bins
    m_owner = m_bins % stride
    m_row = m_bins // stride
    owner_table = (l_owner[:, None] == jnp.arange(stride, dtype=jnp.int32)[None, :]).astype(
        jnp.int32
    )
    slot_rank = jnp.sum((jnp.cumsum(owner_table, axis=0) - owner_table) * owner_table, axis=1)
    slot_l = l_owner * slot_span + slot_rank
    slot_m = m_owner * slot_span + capacity + slot_rank
    slot_ids = jnp.arange(stride * slot_span, dtype=jnp.int32)[None, :]
    req_flat = jnp.sum(
        jnp.where(slot_l[:, None] == slot_ids, l_row[:, None], 0)
        + jnp.where(slot_m[:, None] == slot_ids, m_row[:, None], 0),
        axis=0,
    )
    req_table = req_flat.reshape(stride, slot_span)
    empty = jnp.zeros((stride, slot_span) + own_modes.shape[1:], own_modes.dtype)

    def advance_one(step_index, carried):
        moving, gathered = carried
        moving = shifted(moving, "freq", 1)
        gathered = deposit(gathered, moving, (position - step_index) % stride, req_table)
        return (moving, gathered)

    start = deposit(empty, own_modes, position, req_table)
    _, pulled = lax.fori_loop(1, stride, advance_one, (own_modes, start))
    flat_pull = pulled.reshape((stride * slot_span,) + own_modes.shape[1:])
    block_shape = own_modes.shape[1:]
    seconds = flat_pull[slot_l].reshape((bin_rows, list_width) + block_shape).astype(jnp.float32)
    thirds = flat_pull[slot_m].reshape((bin_rows, list_width) + block_shape)
    firsts = own_modes[:, None].astype(jnp.float32)
    real_part = firsts[:, :, 0] * seconds[:, :, 0] - firsts[:, :, 1] * seconds[:, :, 1]
    imag_part = -(firsts[:, :, 0] * seconds[:, :, 1] + firsts[:, :, 1] * seconds[:, :, 0])
    weighted = (jnp.stack([real_part, imag_part], axis=2) * point_weights).astype(jnp.bfloat16)
    products = jnp.einsum(
        "rtacjp,rtbckp->rtabjk", weighted, thirds, preferred_element_type=jnp.float32
    )
    gram_real = products[:, :, 0, 0] - products[:, :, 1, 1]
    gram_imag = products[:, :, 0, 1] + products[:, :, 1, 0]
    blocks_count = own_modes.shape[3]
    partial_grams = jnp.stack([gram_real, gram_imag], axis=2).reshape(
        bin_rows, list_width, 2 * blocks_count * blocks_count
    )
    summed = lax.psum(partial_grams, "space")
    live_mask = (jnp.arange(list_width, dtype=jnp.int32)[None, :] < live_counts[:, None]).astype(
        jnp.float32
    )
    result = summed / blocks_count * live_mask[:, :, None]
    return result[:, None]


def solution(mesh):
    return jax.shard_map(
        body,
        mesh=mesh,
        in_specs=(
            P(None, "freq", None, None, None, "space"),
            P("space"),
            P(None, "freq", None),
            P(None, "freq"),
        ),
        out_specs=P(None, "freq", None, None),
        check_vma=False,
    )
```

profile of v0, /device:TPU:1, one launch (start us, length us, event | category | flops | bytes accessed | tf_op | source)
XLA Modules:
  0.0 1020.7 jit_solution(12079986639660047375)
XLA Ops:
  17.8 854.5 %while.17 = (s32[]{:T(128)}, bf16[8,2,3,24,128]{4,3,2,1,0:T(8,128)(2,1)S(1)}, bf16[64,4,2,3,24,128]{5,4,3,2,1,0:T(8,128)(2,1)}, s32[]{:T(128)}, s32[64,4]{1,0:T(...) while((s32[]{:T(128)}, bf16[8,2,3,24,128]{4,3,2,1,0:T(8,128)(2,1)S(1)}, ...), condition=%wide.region_4.5_spmd, body=%wide.region_3.4_spmd.sunk | while | flops 1053 | bytes 2363752 | solution.py:60
  20.3 15.5 %collective-permute-done = bf16[8,2,3,24,128]{4,3,2,1,0:T(8,128)(2,1)S(1)} collective-permute-done((bf16[8,2,3,24,128]{4,3,2,1,0:T(8,128)(2,1)S(1)}, bf16[8,2,3,24,128]{4,3,2,1,0:T(8,128)(2,1)S(1)}, u32[]{:S(2)}, u32[]{:S(2)}) %collective-permute-start) | collective-permute-done | bytes 294944 | tf_op jit(solution)/shard_map/while/body/eval_jaxpr/ppermute | solution.py:9
  37.2 12.9 %collective-permute-done = bf16[8,2,3,24,128]{4,3,2,1,0:T(8,128)(2,1)S(1)} collective-permute-done((bf16[8,2,3,24,128]{4,3,2,1,0:T(8,128)(2,1)S(1)}, bf16[8,2,3,24,128]{4,3,2,1,0:T(8,128)(2,1)S(1)}, u32[]{:S(2)}, u32[]{:S(2)}) %collective-permute-start) | collective-permute-done | bytes 294944 | tf_op jit(solution)/shard_map/while/body/eval_jaxpr/ppermute | solution.py:9
  51.6 12.0 %collective-permute-done = bf16[8,2,3,24,128]{4,3,2,1,0:T(8,128)(2,1)S(1)} collective-permute-done((bf16[8,2,3,24,128]{4,3,2,1,0:T(8,128)(2,1)S(1)}, bf16[8,2,3,24,128]{4,3,2,1,0:T(8,128)(2,1)S(1)}, u32[]{:S(2)}, u32[]{:S(2)}) %collective-permute-start) | collective-permute-done | bytes 294944 | tf_op jit(solution)/shard_map/while/body/eval_jaxpr/ppermute | solution.py:9
  90.4 11.2 %collective-permute-done = bf16[8,2,3,24,128]{4,3,2,1,0:T(8,128)(2,1)S(1)} collective-permute-done((bf16[8,2,3,24,128]{4,3,2,1,0:T(8,128)(2,1)S(1)}, bf16[8,2,3,24,128]{4,3,2,1,0:T(8,128)(2,1)S(1)}, u32[]{:S(2)}, u32[]{:S(2)}) %collective-permute-start) | collective-permute-done | bytes 294944 | tf_op jit(solution)/shard_map/while/body/eval_jaxpr/ppermute | solution.py:9
  153.9 12.1 %collective-permute-done = bf16[8,2,3,24,128]{4,3,2,1,0:T(8,128)(2,1)S(1)} collective-permute-done((bf16[8,2,3,24,128]{4,3,2,1,0:T(8,128)(2,1)S(1)}, bf16[8,2,3,24,128]{4,3,2,1,0:T(8,128)(2,1)S(1)}, u32[]{:S(2)}, u32[]{:S(2)}) %collective-permute-start) | collective-permute-done | bytes 294944 | tf_op jit(solution)/shard_map/while/body/eval_jaxpr/ppermute | solution.py:9
  167.4 13.2 %collective-permute-done = bf16[8,2,3,24,128]{4,3,2,1,0:T(8,128)(2,1)S(1)} collective-permute-done((bf16[8,2,3,24,128]{4,3,2,1,0:T(8,128)(2,1)S(1)}, bf16[8,2,3,24,128]{4,3,2,1,0:T(8,128)(2,1)S(1)}, u32[]{:S(2)}, u32[]{:S(2)}) %collective-permute-start) | collective-permute-done | bytes 294944 | tf_op jit(solution)/shard_map/while/body/eval_jaxpr/ppermute | solution.py:9
  182.1 14.6 %collective-permute-done = bf16[8,2,3,24,128]{4,3,2,1,0:T(8,128)(2,1)S(1)} collective-permute-done((bf16[8,2,3,24,128]{4,3,2,1,0:T(8,128)(2,1)S(1)}, bf16[8,2,3,24,128]{4,3,2,1,0:T(8,128)(2,1)S(1)}, u32[]{:S(2)}, u32[]{:S(2)}) %collective-permute-start) | collective-permute-done | bytes 294944 | tf_op jit(solution)/shard_map/while/body/eval_jaxpr/ppermute | solution.py:9
  198.2 13.9 %collective-permute-done = bf16[8,2,3,24,128]{4,3,2,1,0:T(8,128)(2,1)S(1)} collective-permute-done((bf16[8,2,3,24,128]{4,3,2,1,0:T(8,128)(2,1)S(1)}, bf16[8,2,3,24,128]{4,3,2,1,0:T(8,128)(2,1)S(1)}, u32[]{:S(2)}, u32[]{:S(2)}) %collective-permute-start) | collective-permute-done | bytes 294944 | tf_op jit(solution)/shard_map/while/body/eval_jaxpr/ppermute | solution.py:9
  213.5 12.9 %collective-permute-done = bf16[8,2,3,24,128]{4,3,2,1,0:T(8,128)(2,1)S(1)} collective-permute-done((bf16[8,2,3,24,128]{4,3,2,1,0:T(8,128)(2,1)S(1)}, bf16[8,2,3,24,128]{4,3,2,1,0:T(8,128)(2,1)S(1)}, u32[]{:S(2)}, u32[]{:S(2)}) %collective-permute-start) | collective-permute-done | bytes 294944 | tf_op jit(solution)/shard_map/while/body/eval_jaxpr/ppermute | solution.py:9
  227.9 12.0 %collective-permute-done = bf16[8,2,3,24,128]{4,3,2,1,0:T(8,128)(2,1)S(1)} collective-permute-done((bf16[8,2,3,24,128]{4,3,2,1,0:T(8,128)(2,1)S(1)}, bf16[8,2,3,24,128]{4,3,2,1,0:T(8,128)(2,1)S(1)}, u32[]{:S(2)}, u32[]{:S(2)}) %collective-permute-start) | collective-permute-done | bytes 294944 | tf_op jit(solution)/shard_map/while/body/eval_jaxpr/ppermute | solution.py:9
  330.1 12.1 %collective-permute-done = bf16[8,2,3,24,128]{4,3,2,1,0:T(8,128)(2,1)S(1)} collective-permute-done((bf16[8,2,3,24,128]{4,3,2,1,0:T(8,128)(2,1)S(1)}, bf16[8,2,3,24,128]{4,3,2,1,0:T(8,128)(2,1)S(1)}, u32[]{:S(2)}, u32[]{:S(2)}) %collective-permute-start) | collective-permute-done | bytes 294944 | tf_op jit(solution)/shard_map/while/body/eval_jaxpr/ppermute | solution.py:9
  343.7 13.2 %collective-permute-done = bf16[8,2,3,24,128]{4,3,2,1,0:T(8,128)(2,1)S(1)} collective-permute-done((bf16[8,2,3,24,128]{4,3,2,1,0:T(8,128)(2,1)S(1)}, bf16[8,2,3,24,128]{4,3,2,1,0:T(8,128)(2,1)S(1)}, u32[]{:S(2)}, u32[]{:S(2)}) %collective-permute-start) | collective-permute-done | bytes 294944 | tf_op jit(solution)/shard_map/while/body/eval_jaxpr/ppermute | solution.py:9
  358.4 14.5 %collective-permute-done = bf16[8,2,3,24,128]{4,3,2,1,0:T(8,128)(2,1)S(1)} collective-permute-done((bf16[8,2,3,24,128]{4,3,2,1,0:T(8,128)(2,1)S(1)}, bf16[8,2,3,24,128]{4,3,2,1,0:T(8,128)(2,1)S(1)}, u32[]{:S(2)}, u32[]{:S(2)}) %collective-permute-start) | collective-permute-done | bytes 294944 | tf_op jit(solution)/shard_map/while/body/eval_jaxpr/ppermute | solution.py:9
  374.3 13.8 %collective-permute-done = bf16[8,2,3,24,128]{4,3,2,1,0:T(8,128)(2,1)S(1)} collective-permute-done((bf16[8,2,3,24,128]{4,3,2,1,0:T(8,128)(2,1)S(1)}, bf16[8,2,3,24,128]{4,3,2,1,0:T(8,128)(2,1)S(1)}, u32[]{:S(2)}, u32[]{:S(2)}) %collective-permute-start) | collective-permute-done | bytes 294944 | tf_op jit(solution)/shard_map/while/body/eval_jaxpr/ppermute | solution.py:9
  389.7 12.9 %collective-permute-done = bf16[8,2,3,24,128]{4,3,2,1,0:T(8,128)(2,1)S(1)} collective-permute-done((bf16[8,2,3,24,128]{4,3,2,1,0:T(8,128)(2,1)S(1)}, bf16[8,2,3,24,128]{4,3,2,1,0:T(8,128)(2,1)S(1)}, u32[]{:S(2)}, u32[]{:S(2)}) %collective-permute-start) | collective-permute-done | bytes 294944 | tf_op jit(solution)/shard_map/while/body/eval_jaxpr/ppermute | solution.py:9
  404.1 12.0 %collective-permute-done = bf16[8,2,3,24,128]{4,3,2,1,0:T(8,128)(2,1)S(1)} collective-permute-done((bf16[8,2,3,24,128]{4,3,2,1,0:T(8,128)(2,1)S(1)}, bf16[8,2,3,24,128]{4,3,2,1,0:T(8,128)(2,1)S(1)}, u32[]{:S(2)}, u32[]{:S(2)}) %collective-permute-start) | collective-permute-done | bytes 294944 | tf_op jit(solution)/shard_map/while/body/eval_jaxpr/ppermute | solution.py:9
  506.3 12.2 %collective-permute-done = bf16[8,2,3,24,128]{4,3,2,1,0:T(8,128)(2,1)S(1)} collective-permute-done((bf16[8,2,3,24,128]{4,3,2,1,0:T(8,128)(2,1)S(1)}, bf16[8,2,3,24,128]{4,3,2,1,0:T(8,128)(2,1)S(1)}, u32[]{:S(2)}, u32[]{:S(2)}) %collective-permute-start) | collective-permute-done | bytes 294944 | tf_op jit(solution)/shard_map/while/body/eval_jaxpr/ppermute | solution.py:9
  519.9 13.3 %collective-permute-done = bf16[8,2,3,24,128]{4,3,2,1,0:T(8,128)(2,1)S(1)} collective-permute-done((bf16[8,2,3,24,128]{4,3,2,1,0:T(8,128)(2,1)S(1)}, bf16[8,2,3,24,128]{4,3,2,1,0:T(8,128)(2,1)S(1)}, u32[]{:S(2)}, u32[]{:S(2)}) %collective-permute-start) | collective-permute-done | bytes 294944 | tf_op jit(solution)/shard_map/while/body/eval_jaxpr/ppermute | solution.py:9
  534.6 14.7 %collective-permute-done = bf16[8,2,3,24,128]{4,3,2,1,0:T(8,128)(2,1)S(1)} collective-permute-done((bf16[8,2,3,24,128]{4,3,2,1,0:T(8,128)(2,1)S(1)}, bf16[8,2,3,24,128]{4,3,2,1,0:T(8,128)(2,1)S(1)}, u32[]{:S(2)}, u32[]{:S(2)}) %collective-permute-start) | collective-permute-done | bytes 294944 | tf_op jit(solution)/shard_map/while/body/eval_jaxpr/ppermute | solution.py:9
  550.8 13.9 %collective-permute-done = bf16[8,2,3,24,128]{4,3,2,1,0:T(8,128)(2,1)S(1)} collective-permute-done((bf16[8,2,3,24,128]{4,3,2,1,0:T(8,128)(2,1)S(1)}, bf16[8,2,3,24,128]{4,3,2,1,0:T(8,128)(2,1)S(1)}, u32[]{:S(2)}, u32[]{:S(2)}) %collective-permute-start) | collective-permute-done | bytes 294944 | tf_op jit(solution)/shard_map/while/body/eval_jaxpr/ppermute | solution.py:9
  566.1 12.9 %collective-permute-done = bf16[8,2,3,24,128]{4,3,2,1,0:T(8,128)(2,1)S(1)} collective-permute-done((bf16[8,2,3,24,128]{4,3,2,1,0:T(8,128)(2,1)S(1)}, bf16[8,2,3,24,128]{4,3,2,1,0:T(8,128)(2,1)S(1)}, u32[]{:S(2)}, u32[]{:S(2)}) %collective-permute-start) | collective-permute-done | bytes 294944 | tf_op jit(solution)/shard_map/while/body/eval_jaxpr/ppermute | solution.py:9
  580.5 12.0 %collective-permute-done = bf16[8,2,3,24,128]{4,3,2,1,0:T(8,128)(2,1)S(1)} collective-permute-done((bf16[8,2,3,24,128]{4,3,2,1,0:T(8,128)(2,1)S(1)}, bf16[8,2,3,24,128]{4,3,2,1,0:T(8,128)(2,1)S(1)}, u32[]{:S(2)}, u32[]{:S(2)}) %collective-permute-start) | collective-permute-done | bytes 294944 | tf_op jit(solution)/shard_map/while/body/eval_jaxpr/ppermute | solution.py:9
  593.9 11.2 %collective-permute-done = bf16[8,2,3,24,128]{4,3,2,1,0:T(8,128)(2,1)S(1)} collective-permute-done((bf16[8,2,3,24,128]{4,3,2,1,0:T(8,128)(2,1)S(1)}, bf16[8,2,3,24,128]{4,3,2,1,0:T(8,128)(2,1)S(1)}, u32[]{:S(2)}, u32[]{:S(2)}) %collective-permute-start) | collective-permute-done | bytes 294944 | tf_op jit(solution)/shard_map/while/body/eval_jaxpr/ppermute | solution.py:9
  682.7 12.2 %collective-permute-done = bf16[8,2,3,24,128]{4,3,2,1,0:T(8,128)(2,1)S(1)} collective-permute-done((bf16[8,2,3,24,128]{4,3,2,1,0:T(8,128)(2,1)S(1)}, bf16[8,2,3,24,128]{4,3,2,1,0:T(8,128)(2,1)S(1)}, u32[]{:S(2)}, u32[]{:S(2)}) %collective-permute-start) | collective-permute-done | bytes 294944 | tf_op jit(solution)/shard_map/while/body/eval_jaxpr/ppermute | solution.py:9
  696.3 13.2 %collective-permute-done = bf16[8,2,3,24,128]{4,3,2,1,0:T(8,128)(2,1)S(1)} collective-permute-done((bf16[8,2,3,24,128]{4,3,2,1,0:T(8,128)(2,1)S(1)}, bf16[8,2,3,24,128]{4,3,2,1,0:T(8,128)(2,1)S(1)}, u32[]{:S(2)}, u32[]{:S(2)}) %collective-permute-start) | collective-permute-done | bytes 294944 | tf_op jit(solution)/shard_map/while/body/eval_jaxpr/ppermute | solution.py:9
  711.0 14.6 %collective-permute-done = bf16[8,2,3,24,128]{4,3,2,1,0:T(8,128)(2,1)S(1)} collective-permute-done((bf16[8,2,3,24,128]{4,3,2,1,0:T(8,128)(2,1)S(1)}, bf16[8,2,3,24,128]{4,3,2,1,0:T(8,128)(2,1)S(1)}, u32[]{:S(2)}, u32[]{:S(2)}) %collective-permute-start) | collective-permute-done | bytes 294944 | tf_op jit(solution)/shard_map/while/body/eval_jaxpr/ppermute | solution.py:9
  727.0 13.8 %collective-permute-done = bf16[8,2,3,24,128]{4,3,2,1,0:T(8,128)(2,1)S(1)} collective-permute-done((bf16[8,2,3,24,128]{4,3,2,1,0:T(8,128)(2,1)S(1)}, bf16[8,2,3,24,128]{4,3,2,1,0:T(8,128)(2,1)S(1)}, u32[]{:S(2)}, u32[]{:S(2)}) %collective-permute-start) | collective-permute-done | bytes 294944 | tf_op jit(solution)/shard_map/while/body/eval_jaxpr/ppermute | solution.py:9
  742.3 12.9 %collective-permute-done = bf16[8,2,3,24,128]{4,3,2,1,0:T(8,128)(2,1)S(1)} collective-permute-done((bf16[8,2,3,24,128]{4,3,2,1,0:T(8,128)(2,1)S(1)}, bf16[8,2,3,24,128]{4,3,2,1,0:T(8,128)(2,1)S(1)}, u32[]{:S(2)}, u32[]{:S(2)}) %collective-permute-start) | collective-permute-done | bytes 294944 | tf_op jit(solution)/shard_map/while/body/eval_jaxpr/ppermute | solution.py:9
  756.7 12.0 %collective-permute-done = bf16[8,2,3,24,128]{4,3,2,1,0:T(8,128)(2,1)S(1)} collective-permute-done((bf16[8,2,3,24,128]{4,3,2,1,0:T(8,128)(2,1)S(1)}, bf16[8,2,3,24,128]{4,3,2,1,0:T(8,128)(2,1)S(1)}, u32[]{:S(2)}, u32[]{:S(2)}) %collective-permute-start) | collective-permute-done | bytes 294944 | tf_op jit(solution)/shard_map/while/body/eval_jaxpr/ppermute | solution.py:9
  858.9 12.1 %collective-permute-done = bf16[8,2,3,24,128]{4,3,2,1,0:T(8,128)(2,1)S(1)} collective-permute-done((bf16[8,2,3,24,128]{4,3,2,1,0:T(8,128)(2,1)S(1)}, bf16[8,2,3,24,128]{4,3,2,1,0:T(8,128)(2,1)S(1)}, u32[]{:S(2)}, u32[]{:S(2)}) %collective-permute-start) | collective-permute-done | bytes 294944 | tf_op jit(solution)/shard_map/while/body/eval_jaxpr/ppermute | solution.py:9
  910.0 101.9 %all-reduce.2.cloned.1.call-done = f32[8,16,1152]{2,1,0:T(8,128)} async-done(((f32[8,16,1152]{2,1,0:T(8,128)}), f32[8,16,1152]{2,1,0:T(8,128)}) %all-reduce.2.cloned.1.call-update) | async-done | bytes 589840 | tf_op jit(solution)/shard_map/psum | solution.py:78
  (461 shorter events, 511.0 us)
Async XLA Ops:
  6.5 1005.4 %all-reduce.2.cloned.1.call-start = ((), (), s32[]{:S(2)}) async-start(), calls=%async_computation | async-start | bytes 1179648 | tf_op jit(solution)/shard_map/psum | solution.py:78
  17.8 18.0 %collective-permute-start = (bf16[8,2,3,24,128]{4,3,2,1,0:T(8,128)(2,1)S(1)}, bf16[8,2,3,24,128]{4,3,2,1,0:T(8,128)(2,1)S(1)}, u32[]{:S(2)}, u32[]{:S(2)}) collective-permute-start(bf16[8,2,3,24,128]{4,3,2,1,0:T(8,128)(2,1)S(1)} %get-tuple-element.202), channel_id=1, source_target_pairs={{0,4},{4,8},{8,12},{12,16},{16,20},{20,24},{24,28},{28,32},{32,36}... | collective-permute-start | bytes 884744 | tf_op jit(solution)/shard_map/while/body/eval_jaxpr/ppermute | solution.py:9
  37.1 13.1 %collective-permute-start = (bf16[8,2,3,24,128]{4,3,2,1,0:T(8,128)(2,1)S(1)}, bf16[8,2,3,24,128]{4,3,2,1,0:T(8,128)(2,1)S(1)}, u32[]{:S(2)}, u32[]{:S(2)}) collective-permute-start(bf16[8,2,3,24,128]{4,3,2,1,0:T(8,128)(2,1)S(1)} %get-tuple-element.202), channel_id=1, source_target_pairs={{0,4},{4,8},{8,12},{12,16},{16,20},{20,24},{24,28},{28,32},{32,36}... | collective-permute-start | bytes 884744 | tf_op jit(solution)/shard_map/while/body/eval_jaxpr/ppermute | solution.py:9
  51.5 12.2 %collective-permute-start = (bf16[8,2,3,24,128]{4,3,2,1,0:T(8,128)(2,1)S(1)}, bf16[8,2,3,24,128]{4,3,2,1,0:T(8,128)(2,1)S(1)}, u32[]{:S(2)}, u32[]{:S(2)}) collective-permute-start(bf16[8,2,3,24,128]{4,3,2,1,0:T(8,128)(2,1)S(1)} %get-tuple-element.202), channel_id=1, source_target_pairs={{0,4},{4,8},{8,12},{12,16},{16,20},{20,24},{24,28},{28,32},{32,36}... | collective-permute-start | bytes 884744 | tf_op jit(solution)/shard_map/while/body/eval_jaxpr/ppermute | solution.py:9
  64.9 11.4 %collective-permute-start = (bf16[8,2,3,24,128]{4,3,2,1,0:T(8,128)(2,1)S(1)}, bf16[8,2,3,24,128]{4,3,2,1,0:T(8,128)(2,1)S(1)}, u32[]{:S(2)}, u32[]{:S(2)}) collective-permute-start(bf16[8,2,3,24,128]{4,3,2,1,0:T(8,128)(2,1)S(1)} %get-tuple-element.202), channel_id=1, source_target_pairs={{0,4},{4,8},{8,12},{12,16},{16,20},{20,24},{24,28},{28,32},{32,36}... | collective-permute-start | bytes 884744 | tf_op jit(solution)/shard_map/while/body/eval_jaxpr/ppermute | solution.py:9
  77.6 11.4 %collective-permute-start = (bf16[8,2,3,24,128]{4,3,2,1,0:T(8,128)(2,1)S(1)}, bf16[8,2,3,24,128]{4,3,2,1,0:T(8,128)(2,1)S(1)}, u32[]{:S(2)}, u32[]{:S(2)}) collective-permute-start(bf16[8,2,3,24,128]{4,3,2,1,0:T(8,128)(2,1)S(1)} %get-tuple-element.202), channel_id=1, source_target_pairs={{0,4},{4,8},{8,12},{12,16},{16,20},{20,24},{24,28},{28,32},{32,36}... | collective-permute-start | bytes 884744 | tf_op jit(solution)/shard_map/while/body/eval_jaxpr/ppermute | solution.py:9
  90.3 11.4 %collective-permute-start = (bf16[8,2,3,24,128]{4,3,2,1,0:T(8,128)(2,1)S(1)}, bf16[8,2,3,24,128]{4,3,2,1,0:T(8,128)(2,1)S(1)}, u32[]{:S(2)}, u32[]{:S(2)}) collective-permute-start(bf16[8,2,3,24,128]{4,3,2,1,0:T(8,128)(2,1)S(1)} %get-tuple-element.202), channel_id=1, source_target_pairs={{0,4},{4,8},{8,12},{12,16},{16,20},{20,24},{24,28},{28,32},{32,36}... | collective-permute-start | bytes 884744 | tf_op jit(solution)/shard_map/while/body/eval_jaxpr/ppermute | solution.py:9
  153.7 12.3 %collective-permute-start = (bf16[8,2,3,24,128]{4,3,2,1,0:T(8,128)(2,1)S(1)}, bf16[8,2,3,24,128]{4,3,2,1,0:T(8,128)(2,1)S(1)}, u32[]{:S(2)}, u32[]{:S(2)}) collective-permute-start(bf16[8,2,3,24,128]{4,3,2,1,0:T(8,128)(2,1)S(1)} %get-tuple-element.202), channel_id=1, source_target_pairs={{0,4},{4,8},{8,12},{12,16},{16,20},{20,24},{24,28},{28,32},{32,36}... | collective-permute-start | bytes 884744 | tf_op jit(solution)/shard_map/while/body/eval_jaxpr/ppermute | solution.py:9
  167.3 13.4 %collective-permute-start = (bf16[8,2,3,24,128]{4,3,2,1,0:T(8,128)(2,1)S(1)}, bf16[8,2,3,24,128]{4,3,2,1,0:T(8,128)(2,1)S(1)}, u32[]{:S(2)}, u32[]{:S(2)}) collective-permute-start(bf16[8,2,3,24,128]{4,3,2,1,0:T(8,128)(2,1)S(1)} %get-tuple-element.202), channel_id=1, source_target_pairs={{0,4},{4,8},{8,12},{12,16},{16,20},{20,24},{24,28},{28,32},{32,36}... | collective-permute-start | bytes 884744 | tf_op jit(solution)/shard_map/while/body/eval_jaxpr/ppermute | solution.py:9
  182.0 14.8 %collective-permute-start = (bf16[8,2,3,24,128]{4,3,2,1,0:T(8,128)(2,1)S(1)}, bf16[8,2,3,24,128]{4,3,2,1,0:T(8,128)(2,1)S(1)}, u32[]{:S(2)}, u32[]{:S(2)}) collective-permute-start(bf16[8,2,3,24,128]{4,3,2,1,0:T(8,128)(2,1)S(1)} %get-tuple-element.202), channel_id=1, source_target_pairs={{0,4},{4,8},{8,12},{12,16},{16,20},{20,24},{24,28},{28,32},{32,36}... | collective-permute-start | bytes 884744 | tf_op jit(solution)/shard_map/while/body/eval_jaxpr/ppermute | solution.py:9
  198.0 14.0 %collective-permute-start = (bf16[8,2,3,24,128]{4,3,2,1,0:T(8,128)(2,1)S(1)}, bf16[8,2,3,24,128]{4,3,2,1,0:T(8,128)(2,1)S(1)}, u32[]{:S(2)}, u32[]{:S(2)}) collective-permute-start(bf16[8,2,3,24,128]{4,3,2,1,0:T(8,128)(2,1)S(1)} %get-tuple-element.202), channel_id=1, source_target_pairs={{0,4},{4,8},{8,12},{12,16},{16,20},{20,24},{24,28},{28,32},{32,36}... | collective-permute-start | bytes 884744 | tf_op jit(solution)/shard_map/while/body/eval_jaxpr/ppermute | solution.py:9
  213.3 13.1 %collective-permute-start = (bf16[8,2,3,24,128]{4,3,2,1,0:T(8,128)(2,1)S(1)}, bf16[8,2,3,24,128]{4,3,2,1,0:T(8,128)(2,1)S(1)}, u32[]{:S(2)}, u32[]{:S(2)}) collective-permute-start(bf16[8,2,3,24,128]{4,3,2,1,0:T(8,128)(2,1)S(1)} %get-tuple-element.202), channel_id=1, source_target_pairs={{0,4},{4,8},{8,12},{12,16},{16,20},{20,24},{24,28},{28,32},{32,36}... | collective-permute-start | bytes 884744 | tf_op jit(solution)/shard_map/while/body/eval_jaxpr/ppermute | solution.py:9
  227.7 12.2 %collective-permute-start = (bf16[8,2,3,24,128]{4,3,2,1,0:T(8,128)(2,1)S(1)}, bf16[8,2,3,24,128]{4,3,2,1,0:T(8,128)(2,1)S(1)}, u32[]{:S(2)}, u32[]{:S(2)}) collective-permute-start(bf16[8,2,3,24,128]{4,3,2,1,0:T(8,128)(2,1)S(1)} %get-tuple-element.202), channel_id=1, source_target_pairs={{0,4},{4,8},{8,12},{12,16},{16,20},{20,24},{24,28},{28,32},{32,36}... | collective-permute-start | bytes 884744 | tf_op jit(solution)/shard_map/while/body/eval_jaxpr/ppermute | solution.py:9
  330.0 12.3 %collective-permute-start = (bf16[8,2,3,24,128]{4,3,2,1,0:T(8,128)(2,1)S(1)}, bf16[8,2,3,24,128]{4,3,2,1,0:T(8,128)(2,1)S(1)}, u32[]{:S(2)}, u32[]{:S(2)}) collective-permute-start(bf16[8,2,3,24,128]{4,3,2,1,0:T(8,128)(2,1)S(1)} %get-tuple-element.202), channel_id=1, source_target_pairs={{0,4},{4,8},{8,12},{12,16},{16,20},{20,24},{24,28},{28,32},{32,36}... | collective-permute-start | bytes 884744 | tf_op jit(solution)/shard_map/while/body/eval_jaxpr/ppermute | solution.py:9
  343.6 13.3 %collective-permute-start = (bf16[8,2,3,24,128]{4,3,2,1,0:T(8,128)(2,1)S(1)}, bf16[8,2,3,24,128]{4,3,2,1,0:T(8,128)(2,1)S(1)}, u32[]{:S(2)}, u32[]{:S(2)}) collective-permute-start(bf16[8,2,3,24,128]{4,3,2,1,0:T(8,128)(2,1)S(1)} %get-tuple-element.202), channel_id=1, source_target_pairs={{0,4},{4,8},{8,12},{12,16},{16,20},{20,24},{24,28},{28,32},{32,36}... | collective-permute-start | bytes 884744 | tf_op jit(solution)/shard_map/while/body/eval_jaxpr/ppermute | solution.py:9
  358.2 14.7 %collective-permute-start = (bf16[8,2,3,24,128]{4,3,2,1,0:T(8,128)(2,1)S(1)}, bf16[8,2,3,24,128]{4,3,2,1,0:T(8,128)(2,1)S(1)}, u32[]{:S(2)}, u32[]{:S(2)}) collective-permute-start(bf16[8,2,3,24,128]{4,3,2,1,0:T(8,128)(2,1)S(1)} %get-tuple-element.202), channel_id=1, source_target_pairs={{0,4},{4,8},{8,12},{12,16},{16,20},{20,24},{24,28},{28,32},{32,36}... | collective-permute-start | bytes 884744 | tf_op jit(solution)/shard_map/while/body/eval_jaxpr/ppermute | solution.py:9
  374.2 14.0 %collective-permute-start = (bf16[8,2,3,24,128]{4,3,2,1,0:T(8,128)(2,1)S(1)}, bf16[8,2,3,24,128]{4,3,2,1,0:T(8,128)(2,1)S(1)}, u32[]{:S(2)}, u32[]{:S(2)}) collective-permute-start(bf16[8,2,3,24,128]{4,3,2,1,0:T(8,128)(2,1)S(1)} %get-tuple-element.202), channel_id=1, source_target_pairs={{0,4},{4,8},{8,12},{12,16},{16,20},{20,24},{24,28},{28,32},{32,36}... | collective-permute-start | bytes 884744 | tf_op jit(solution)/shard_map/while/body/eval_jaxpr/ppermute | solution.py:9
  389.5 13.1 %collective-permute-start = (bf16[8,2,3,24,128]{4,3,2,1,0:T(8,128)(2,1)S(1)}, bf16[8,2,3,24,128]{4,3,2,1,0:T(8,128)(2,1)S(1)}, u32[]{:S(2)}, u32[]{:S(2)}) collective-permute-start(bf16[8,2,3,24,128]{4,3,2,1,0:T(8,128)(2,1)S(1)} %get-tuple-element.202), channel_id=1, source_target_pairs={{0,4},{4,8},{8,12},{12,16},{16,20},{20,24},{24,28},{28,32},{32,36}... | collective-permute-start | bytes 884744 | tf_op jit(solution)/shard_map/while/body/eval_jaxpr/ppermute | solution.py:9
  403.9 12.2 %collective-permute-start = (bf16[8,2,3,24,128]{4,3,2,1,0:T(8,128)(2,1)S(1)}, bf16[8,2,3,24,128]{4,3,2,1,0:T(8,128)(2,1)S(1)}, u32[]{:S(2)}, u32[]{:S(2)}) collective-permute-start(bf16[8,2,3,24,128]{4,3,2,1,0:T(8,128)(2,1)S(1)} %get-tuple-element.202), channel_id=1, source_target_pairs={{0,4},{4,8},{8,12},{12,16},{16,20},{20,24},{24,28},{28,32},{32,36}... | collective-permute-start | bytes 884744 | tf_op jit(solution)/shard_map/while/body/eval_jaxpr/ppermute | solution.py:9
  506.1 12.3 %collective-permute-start = (bf16[8,2,3,24,128]{4,3,2,1,0:T(8,128)(2,1)S(1)}, bf16[8,2,3,24,128]{4,3,2,1,0:T(8,128)(2,1)S(1)}, u32[]{:S(2)}, u32[]{:S(2)}) collective-permute-start(bf16[8,2,3,24,128]{4,3,2,1,0:T(8,128)(2,1)S(1)} %get-tuple-element.202), channel_id=1, source_target_pairs={{0,4},{4,8},{8,12},{12,16},{16,20},{20,24},{24,28},{28,32},{32,36}... | collective-permute-start | bytes 884744 | tf_op jit(solution)/shard_map/while/body/eval_jaxpr/ppermute | solution.py:9
  519.8 13.4 %collective-permute-start = (bf16[8,2,3,24,128]{4,3,2,1,0:T(8,128)(2,1)S(1)}, bf16[8,2,3,24,128]{4,3,2,1,0:T(8,128)(2,1)S(1)}, u32[]{:S(2)}, u32[]{:S(2)}) collective-permute-start(bf16[8,2,3,24,128]{4,3,2,1,0:T(8,128)(2,1)S(1)} %get-tuple-element.202), channel_id=1, source_target_pairs={{0,4},{4,8},{8,12},{12,16},{16,20},{20,24},{24,28},{28,32},{32,36}... | collective-permute-start | bytes 884744 | tf_op jit(solution)/shard_map/while/body/eval_jaxpr/ppermute | solution.py:9
  534.5 14.8 %collective-permute-start = (bf16[8,2,3,24,128]{4,3,2,1,0:T(8,128)(2,1)S(1)}, bf16[8,2,3,24,128]{4,3,2,1,0:T(8,128)(2,1)S(1)}, u32[]{:S(2)}, u32[]{:S(2)}) collective-permute-start(bf16[8,2,3,24,128]{4,3,2,1,0:T(8,128)(2,1)S(1)} %get-tuple-element.202), channel_id=1, source_target_pairs={{0,4},{4,8},{8,12},{12,16},{16,20},{20,24},{24,28},{28,32},{32,36}... | collective-permute-start | bytes 884744 | tf_op jit(solution)/shard_map/while/body/eval_jaxpr/ppermute | solution.py:9
  550.6 14.0 %collective-permute-start = (bf16[8,2,3,24,128]{4,3,2,1,0:T(8,128)(2,1)S(1)}, bf16[8,2,3,24,128]{4,3,2,1,0:T(8,128)(2,1)S(1)}, u32[]{:S(2)}, u32[]{:S(2)}) collective-permute-start(bf16[8,2,3,24,128]{4,3,2,1,0:T(8,128)(2,1)S(1)} %get-tuple-element.202), channel_id=1, source_target_pairs={{0,4},{4,8},{8,12},{12,16},{16,20},{20,24},{24,28},{28,32},{32,36}... | collective-permute-start | bytes 884744 | tf_op jit(solution)/shard_map/while/body/eval_jaxpr/ppermute | solution.py:9
  565.9 13.1 %collective-permute-start = (bf16[8,2,3,24,128]{4,3,2,1,0:T(8,128)(2,1)S(1)}, bf16[8,2,3,24,128]{4,3,2,1,0:T(8,128)(2,1)S(1)}, u32[]{:S(2)}, u32[]{:S(2)}) collective-permute-start(bf16[8,2,3,24,128]{4,3,2,1,0:T(8,128)(2,1)S(1)} %get-tuple-element.202), channel_id=1, source_target_pairs={{0,4},{4,8},{8,12},{12,16},{16,20},{20,24},{24,28},{28,32},{32,36}... | collective-permute-start | bytes 884744 | tf_op jit(solution)/shard_map/while/body/eval_jaxpr/ppermute | solution.py:9
  580.3 12.2 %collective-permute-start = (bf16[8,2,3,24,128]{4,3,2,1,0:T(8,128)(2,1)S(1)}, bf16[8,2,3,24,128]{4,3,2,1,0:T(8,128)(2,1)S(1)}, u32[]{:S(2)}, u32[]{:S(2)}) collective-permute-start(bf16[8,2,3,24,128]{4,3,2,1,0:T(8,128)(2,1)S(1)} %get-tuple-element.202), channel_id=1, source_target_pairs={{0,4},{4,8},{8,12},{12,16},{16,20},{20,24},{24,28},{28,32},{32,36}... | collective-permute-start | bytes 884744 | tf_op jit(solution)/shard_map/while/body/eval_jaxpr/ppermute | solution.py:9
  682.5 12.3 %collective-permute-start = (bf16[8,2,3,24,128]{4,3,2,1,0:T(8,128)(2,1)S(1)}, bf16[8,2,3,24,128]{4,3,2,1,0:T(8,128)(2,1)S(1)}, u32[]{:S(2)}, u32[]{:S(2)}) collective-permute-start(bf16[8,2,3,24,128]{4,3,2,1,0:T(8,128)(2,1)S(1)} %get-tuple-element.202), channel_id=1, source_target_pairs={{0,4},{4,8},{8,12},{12,16},{16,20},{20,24},{24,28},{28,32},{32,36}... | collective-permute-start | bytes 884744 | tf_op jit(solution)/shard_map/while/body/eval_jaxpr/ppermute | solution.py:9
  696.1 13.4 %collective-permute-start = (bf16[8,2,3,24,128]{4,3,2,1,0:T(8,128)(2,1)S(1)}, bf16[8,2,3,24,128]{4,3,2,1,0:T(8,128)(2,1)S(1)}, u32[]{:S(2)}, u32[]{:S(2)}) collective-permute-start(bf16[8,2,3,24,128]{4,3,2,1,0:T(8,128)(2,1)S(1)} %get-tuple-element.202), channel_id=1, source_target_pairs={{0,4},{4,8},{8,12},{12,16},{16,20},{20,24},{24,28},{28,32},{32,36}... | collective-permute-start | bytes 884744 | tf_op jit(solution)/shard_map/while/body/eval_jaxpr/ppermute | solution.py:9
  710.8 14.7 %collective-permute-start = (bf16[8,2,3,24,128]{4,3,2,1,0:T(8,128)(2,1)S(1)}, bf16[8,2,3,24,128]{4,3,2,1,0:T(8,128)(2,1)S(1)}, u32[]{:S(2)}, u32[]{:S(2)}) collective-permute-start(bf16[8,2,3,24,128]{4,3,2,1,0:T(8,128)(2,1)S(1)} %get-tuple-element.202), channel_id=1, source_target_pairs={{0,4},{4,8},{8,12},{12,16},{16,20},{20,24},{24,28},{28,32},{32,36}... | collective-permute-start | bytes 884744 | tf_op jit(solution)/shard_map/while/body/eval_jaxpr/ppermute | solution.py:9
  726.9 14.0 %collective-permute-start = (bf16[8,2,3,24,128]{4,3,2,1,0:T(8,128)(2,1)S(1)}, bf16[8,2,3,24,128]{4,3,2,1,0:T(8,128)(2,1)S(1)}, u32[]{:S(2)}, u32[]{:S(2)}) collective-permute-start(bf16[8,2,3,24,128]{4,3,2,1,0:T(8,128)(2,1)S(1)} %get-tuple-element.202), channel_id=1, source_target_pairs={{0,4},{4,8},{8,12},{12,16},{16,20},{20,24},{24,28},{28,32},{32,36}... | collective-permute-start | bytes 884744 | tf_op jit(solution)/shard_map/while/body/eval_jaxpr/ppermute | solution.py:9
  742.1 13.1 %collective-permute-start = (bf16[8,2,3,24,128]{4,3,2,1,0:T(8,128)(2,1)S(1)}, bf16[8,2,3,24,128]{4,3,2,1,0:T(8,128)(2,1)S(1)}, u32[]{:S(2)}, u32[]{:S(2)}) collective-permute-start(bf16[8,2,3,24,128]{4,3,2,1,0:T(8,128)(2,1)S(1)} %get-tuple-element.202), channel_id=1, source_target_pairs={{0,4},{4,8},{8,12},{12,16},{16,20},{20,24},{24,28},{28,32},{32,36}... | collective-permute-start | bytes 884744 | tf_op jit(solution)/shard_map/while/body/eval_jaxpr/ppermute | solution.py:9
  756.5 12.1 %collective-permute-start = (bf16[8,2,3,24,128]{4,3,2,1,0:T(8,128)(2,1)S(1)}, bf16[8,2,3,24,128]{4,3,2,1,0:T(8,128)(2,1)S(1)}, u32[]{:S(2)}, u32[]{:S(2)}) collective-permute-start(bf16[8,2,3,24,128]{4,3,2,1,0:T(8,128)(2,1)S(1)} %get-tuple-element.202), channel_id=1, source_target_pairs={{0,4},{4,8},{8,12},{12,16},{16,20},{20,24},{24,28},{28,32},{32,36}... | collective-permute-start | bytes 884744 | tf_op jit(solution)/shard_map/while/body/eval_jaxpr/ppermute | solution.py:9
  858.7 12.3 %collective-permute-start = (bf16[8,2,3,24,128]{4,3,2,1,0:T(8,128)(2,1)S(1)}, bf16[8,2,3,24,128]{4,3,2,1,0:T(8,128)(2,1)S(1)}, u32[]{:S(2)}, u32[]{:S(2)}) collective-permute-start(bf16[8,2,3,24,128]{4,3,2,1,0:T(8,128)(2,1)S(1)} %get-tuple-element.202), channel_id=1, source_target_pairs={{0,4},{4,8},{8,12},{12,16},{16,20},{20,24},{24,28},{28,32},{32,36}... | collective-permute-start | bytes 884744 | tf_op jit(solution)/shard_map/while/body/eval_jaxpr/ppermute | solution.py:9
  (37 other events, 388.5 us)
Sparse Core Ops, SparseCore 0:
  910.1 101.7 all-reduce.1
where the time goes:
time: 1020 us
  waiting for transfers between devices  862 us (85%)
  local copies, waits for them, and re-layouts  110 us (11%)
  other arithmetic  13.9 us (1%)
  between operations  13.6 us (1%)
    ppermute x63, waiting for transfers between devices, shifted(): lax.ppermute(shard, axis, [(i, (i + by) % size) for i in range(size)])  760 us
    psum x1, waiting for transfers between devices, body(): summed = lax.psum(partial_grams, 'space')  102 us
    dynamic_update_slice x64, local copies, waits for them, and re-layouts, deposit(): return lax.dynamic_update_slice_in_dim(gathered, picked[None], owner, 0)  42.9 us
    gather x64, local copies, waits for them, and re-layouts, deposit(): picked = blocks[wanted]  36.8 us
  transfers between devices with their start and end apart: 64, of which 64 were waited for; matrix products, arithmetic and copies ran while one was open for 0% of the time, Pallas kernels for 0%

commit v1 on v0

v1 whole, which is shorter than its diff:
```python
import functools

import jax
import jax.numpy as jnp
from jax import lax
from jax.experimental import pallas as pl
from jax.experimental.pallas import tpu as pltpu
from jax.sharding import Mesh
from jax.sharding import PartitionSpec as P

F32, BF16 = jnp.float32, jnp.bfloat16
LANES = 128
VMEM_LIMIT = 56 * 1024 * 1024


def split_kernel(place_ref, x_ref, out_ref):
    place = place_ref[0]
    block = lax.broadcasted_iota(jnp.int32, (24, LANES), 1) // 16
    for q in range(6):
        sources = [x_ref[8 * q + s].astype(F32) for s in range(8)]
        for piece in range(8):
            built = None
            for s in range(8):
                shift = (s - piece) % 8 * 16
                moved = pltpu.roll(sources[s], shift, 1) if shift else sources[s]
                built = moved if built is None else jnp.where(block == s, moved, built)
            out_ref[(piece - place) & 7, q] = built.astype(BF16)


def unpack_column(own, sib, bins_ref, first_bin):
    lane = lax.broadcasted_iota(jnp.int32, (24, LANES), 1)
    tiles = [[ref[q].astype(F32) for q in range(6)] for ref in (own, sib)]
    for r in range(8):
        for part in range(2):
            q, offset = divmod(96 * r + 48 * part, LANES)
            halves = []
            for core in range(2):
                picked = tiles[core][q]
                if offset + 48 > LANES:
                    picked = jnp.where(lane >= offset, picked, tiles[core][q + 1])
                shift = (48 * core - offset) % LANES
                halves.append(pltpu.roll(picked, shift, 1) if shift else picked)
            merged = jnp.where(lane < 48, halves[0], halves[1])
            bins_ref[first_bin + r, :, LANES * part : LANES * (part + 1)] = merged.astype(BF16)


def grams_kernel(meta_ref, triads_ref, weights_ref, *refs):
    own_refs, sib_refs = refs[:9], refs[9:18]
    out_ref, bins_ref, w_ref, q_ref = refs[18:]
    place, depth, core = meta_ref[0], meta_ref[1], meta_ref[2]

    for index, turn in enumerate((0, 1, 2, 3, 5, 6, 7)):

        @pl.loop(0, 8)
        def _(d, index=index, turn=turn):
            unpack_column(
                own_refs[index].at[d], sib_refs[index].at[d], bins_ref, turn * 64 + d * 8
            )

    for half in range(2):

        @pl.loop(0, 4)
        def _(d, half=half):
            unpack_column(
                own_refs[7 + half].at[d],
                sib_refs[7 + half].at[d],
                bins_ref,
                4 * 64 + half * 32 + d * 8,
            )

    def slot(which):
        return (
            ((depth - (which & 7)) & 7) * 64
            + ((place - ((which >> 3) & 7)) & 7) * 8
            + (which >> 6)
        )

    weights = weights_ref[0:1, :]
    lane = lax.broadcasted_iota(jnp.int32, (48, LANES), 1)

    @pl.loop(0, 32)
    def _(reader):
        d = reader >> 2
        owner_half = (reader >> 1) & 1
        sub = reader & 1
        row = owner_half * 4 + core * 2 + sub
        owner = (place - d) & 7
        k_bin = row * 64 + owner * 8 + depth
        first = bins_ref[d * 8 + row].astype(F32)
        k_real = first[:, :LANES] * weights
        k_imag = first[:, LANES:] * weights
        for t in range(16):
            l_bin = triads_ref[d, row * 16 + t]
            m_bin = (k_bin + l_bin) & 511
            second = bins_ref[slot(l_bin)].astype(F32)
            l_real, l_imag = second[:, :LANES], second[:, LANES:]
            real = (k_real * l_real - k_imag * l_imag).astype(BF16)
            imag = k_real * l_imag + k_imag * l_real
            plus, minus = imag.astype(BF16), (-imag).astype(BF16)
            w_ref[48 * t : 48 * t + 24, :LANES] = real
            w_ref[48 * t : 48 * t + 24, LANES:] = plus
            w_ref[48 * t + 24 : 48 * t + 48, :LANES] = minus
            w_ref[48 * t + 24 : 48 * t + 48, LANES:] = real
            q_ref[24 * t : 24 * t + 24, :] = bins_ref[slot(m_bin)]
        for n in range(3):
            start = 5 * n
            product = lax.dot_general(
                w_ref[48 * start : 48 * (start + 6), :],
                q_ref[LANES * n : LANES * (n + 1), :],
                (((1,), (1,)), ((), ())),
                preferred_element_type=F32,
            )
            built = product[:48]
            for i in range(1, 6):
                begin = 24 * (start + i) - LANES * n
                built = jnp.where(lane >= begin, product[48 * i : 48 * (i + 1)], built)
            out_ref[owner * 2 + owner_half, sub, :, LANES * n : LANES * (n + 1)] = built.astype(
                BF16
            )


def vmem():
    return pl.BlockSpec(memory_space=pltpu.VMEM)


def smem():
    return pl.BlockSpec(memory_space=pltpu.SMEM)


def step(array, axes, by):
    size = lax.axis_size(axes)
    return lax.ppermute(array, axes, [(i, (i + by) % size) for i in range(size)])


def body(modes, point_weights, triads, counts):
    plane = ("x", "yh")
    place, depth, core = lax.axis_index(plane), lax.axis_index("z"), lax.axis_index("core")
    half = lax.axis_index("yl")

    pieces = pl.pallas_call(
        split_kernel,
        out_shape=jax.ShapeDtypeStruct((8, 6, 24, LANES), BF16),
        in_specs=[smem(), vmem()],
        out_specs=vmem(),
        compiler_params=pltpu.CompilerParams(vmem_limit_bytes=VMEM_LIMIT),
        name="split",
    )(place.astype(jnp.int32)[None], modes.reshape(48, 24, LANES))

    block = jnp.stack([pieces[0]] + [step(pieces[d], plane, d) for d in range(1, 8)])
    lists = triads.reshape(128)
    all_lists = jnp.stack([lists] + [step(lists, plane, d) for d in range(1, 8)])

    own_weights = lax.dynamic_slice_in_dim(point_weights, place * 16, 16)
    sib_weights = step(own_weights, "core", 1)
    lane_weights = jnp.concatenate([own_weights] * 3 + [sib_weights] * 3 + [jnp.zeros(32, F32)])

    ahead, behind = [block], [block]
    for _ in range(3):
        ahead.append(step(ahead[-1], "z", 1))
        behind.append(step(behind[-1], "z", -1))
    far = [step(ahead[3][:4], "z", 1), step(behind[3][4:], "z", -1)]
    own = ahead + behind[:0:-1] + far
    sib = [step(array, "core", 1) for array in own]

    meta = jnp.stack([place, depth, core]).astype(jnp.int32)
    partial = pl.pallas_call(
        grams_kernel,
        out_shape=jax.ShapeDtypeStruct((16, 2, 48, 384), BF16),
        in_specs=[smem(), smem(), vmem()] + [vmem()] * 18,
        out_specs=vmem(),
        scratch_shapes=[
            pltpu.VMEM((512, 24, 256), BF16),
            pltpu.VMEM((768, 256), BF16),
            pltpu.VMEM((384, 256), BF16),
        ],
        compiler_params=pltpu.CompilerParams(vmem_limit_bytes=VMEM_LIMIT),
        name="grams",
    )(meta, all_lists, jnp.broadcast_to(lane_weights, (8, LANES)), *own, *sib)

    received = lax.all_to_all(partial, ("x", "yh", "yl"), 0, 0)
    summed = jnp.sum(received.astype(F32), axis=0) / 24
    rows = summed.reshape(2, 48, 16, 24).transpose(0, 2, 1, 3).reshape(2, 16, 1152)
    live = lax.dynamic_slice_in_dim(counts[:, 0], 4 * half + 2 * core, 2)
    mask = jnp.arange(16, dtype=jnp.int32)[None, :] < live[:, None]
    rows = rows * mask.astype(F32)[:, :, None]
    return lax.all_gather(rows, ("yl", "core")).reshape(8, 1, 16, 1152)


def solution(mesh):
    fine = Mesh(mesh.devices.reshape(4, 2, 8, 2, 2), ("x", "yh", "z", "yl", "core"))
    freq, space = ("x", "yh", "z"), ("yl", "core")
    return jax.shard_map(
        body,
        mesh=fine,
        in_specs=(
            P(None, freq, None, None, None, space),
            P(space),
            P(None, freq, None),
            P(None, freq),
        ),
        out_specs=P(None, freq, None, None),
        check_vma=False,
    )
```

time: 1020 us -> 150 us (0.15)
  waiting for transfers between devices: 862 us -> 53 us
  local copies, waits for them, and re-layouts: 110 us -> 6.89 us
  starting transfers between devices: 7.66 us -> 55.2 us
  Pallas kernels: 0 us -> 25.5 us
  between operations: 13.6 us -> 0.35 us
  other arithmetic: 13.9 us -> 1.58 us
    ppermute x63 -> x32, waiting for transfers between devices: 760 us -> 33.4 us  [step(): lax.ppermute(array, axes, [(i, (i + by) % size) for i in range(size)])]
    psum x1 -> x0, waiting for transfers between devices: 102 us -> none  [body(): summed = lax.psum(partial_grams, 'space')]
    gather x66 -> x0, local copies, waits for them, and re-layouts: 50.8 us -> none  [the longest x64 36.8 us: deposit(): picked = blocks[wanted]]
    ppermute x63 -> x32, starting transfers between devices: 7.66 us -> 51.5 us  [step(): lax.ppermute(array, axes, [(i, (i + by) % size) for i in range(size)])]
    dynamic_update_slice x64 -> x0, local copies, waits for them, and re-layouts: 42.9 us -> none  [deposit(): return lax.dynamic_update_slice_in_dim(gathered, picked[None], owner, 0)]
    pallas_call x0 -> x2, Pallas kernels: none -> 25.5 us  [the longest x1 23.2 us: body(): pl.pallas_call(grams_kernel, out_shape=jax.ShapeDtypeStruct((16, 2, 48, 3...]
    all_to_all x0 -> x1, waiting for transfers between devices: none -> 19.5 us  [body(): received = lax.all_to_all(partial, ('x', 'yh', 'yl'), 0, 0)]
  transfers between devices with their start and end apart: 64 -> 33, of which waited for: 64 -> 11; matrix products, arithmetic and copies ran while one was open for 0% -> 3% of each run, Pallas kernels for 0% -> 0%
where the time goes in v1:
time: 150 us
  starting transfers between devices  55.2 us (37%)
  waiting for transfers between devices  53 us (35%)
  Pallas kernels  25.5 us (17%)
  blocking collectives  7.65 us (5%)
  local copies, waits for them, and re-layouts  6.89 us (5%)
  other arithmetic  1.58 us (1%)
    ppermute x32, starting transfers between devices, step(): lax.ppermute(array, axes, [(i, (i + by) % size) for i in range(size)])  51.5 us
    ppermute x32, waiting for transfers between devices, step(): lax.ppermute(array, axes, [(i, (i + by) % size) for i in range(size)])  33.4 us
    pallas_call x1, Pallas kernels, body(): pl.pallas_call(grams_kernel, out_shape=jax.ShapeDtypeStruct((16, 2, 48, 3...  23.2 us
    all_to_all x1, waiting for transfers between devices, body(): received = lax.all_to_all(partial, ('x', 'yh', 'yl'), 0, 0)  19.5 us
    all_gather x1, blocking collectives, body(): return lax.all_gather(rows, ('yl', 'core')).reshape(8, 1, 16, 1152)  7.65 us
    all_to_all x1, starting transfers between devices, body(): received = lax.all_to_all(partial, ('x', 'yh', 'yl'), 0, 0)  3.7 us
  transfers between devices with their start and end apart: 33, of which 11 were waited for; matrix products, arithmetic and copies ran while one was open for 3% of the time, Pallas kernels for 0%

profile of v1, /device:TPU:1, one launch (start us, length us, event | category | flops | bytes accessed | tf_op | source)
XLA Modules:
  0.0 150.1 jit_solution(16495242593974491441)
XLA Ops:
  0.0 2.3 %split.1 = bf16[8,6,24,128]{3,2,1,0:T(8,128)(2,1)} custom-call(s32[1]{0:T(128)} %bitcast.place_ref, bf16[48,24,128]{2,1,0:T(8,128)(2,1)} %bitcast.52), custom_call_target="tpu_custom_call" | custom-call | tf_op jit(solution)/shard_map/split/pallas_call | solution.py:140
  2.3 0.9 slice_bitcast_fusion
  3.3 3.8 %collective-permute-start.8 = (bf16[6,24,128]{2,1,0:T(8,128)(2,1)S(1)}, bf16[6,24,128]{2,1,0:T(8,128)(2,1)S(1)}, u32[]{:S(2)}, u32[]{:S(2)}) collective-permute-start(bf16[6,24,128]{2,1,0:T(8,128)(2,1)S(1)} %get-tuple-element.11), channel_id=1, source_target_pairs={{0,32},{32,64},{64,96},{96,128},{128,160},{160,192},{192,224},{224... | collective-permute-start | bytes 110600 | tf_op jit(solution)/shard_map/ppermute | solution.py:132
  7.1 2.3 %collective-permute-start.14 = (bf16[6,24,128]{2,1,0:T(8,128)(2,1)S(1)}, bf16[6,24,128]{2,1,0:T(8,128)(2,1)S(1)}, u32[]{:S(2)}, u32[]{:S(2)}) collective-permute-start(bf16[6,24,128]{2,1,0:T(8,128)(2,1)S(1)} %get-tuple-element.5), channel_id=1, source_target_pairs={{0,224},{32,0},{64,32},{96,64},{128,96},{160,128},{192,160},{224,1... | collective-permute-start | bytes 110600 | tf_op jit(solution)/shard_map/ppermute | solution.py:132
  9.4 1.1 collective-permute-start.13
  10.5 2.3 %collective-permute-start.12 = (bf16[6,24,128]{2,1,0:T(8,128)(2,1)S(1)}, bf16[6,24,128]{2,1,0:T(8,128)(2,1)S(1)}, u32[]{:S(2)}, u32[]{:S(2)}) collective-permute-start(bf16[6,24,128]{2,1,0:T(8,128)(2,1)S(1)} %get-tuple-element.7), channel_id=1, source_target_pairs={{0,160},{32,192},{64,224},{96,0},{128,32},{160,64},{192,96},{224,1... | collective-permute-start | bytes 110600 | tf_op jit(solution)/shard_map/ppermute | solution.py:132
  12.8 2.5 %collective-permute-start.11 = (bf16[6,24,128]{2,1,0:T(8,128)(2,1)S(1)}, bf16[6,24,128]{2,1,0:T(8,128)(2,1)S(1)}, u32[]{:S(2)}, u32[]{:S(2)}) collective-permute-start(bf16[6,24,128]{2,1,0:T(8,128)(2,1)S(1)} %get-tuple-element.8), channel_id=1, source_target_pairs={{0,128},{32,160},{64,192},{96,224},{128,0},{160,32},{192,64},{224,... | collective-permute-start | bytes 110600 | tf_op jit(solution)/shard_map/ppermute | solution.py:132
  15.2 4.4 %collective-permute-done.9 = bf16[6,24,128]{2,1,0:T(8,128)(2,1)S(1)} collective-permute-done((bf16[6,24,128]{2,1,0:T(8,128)(2,1)S(1)}, bf16[6,24,128]{2,1,0:T(8,128)(2,1)S(1)}, u32[]{:S(2)}, u32[]{:S(2)}) %collective-permute-start.9) | collective-permute-done | bytes 36896 | tf_op jit(solution)/shard_map/ppermute | solution.py:132
  19.6 6.7 %collective-permute-done.10 = bf16[6,24,128]{2,1,0:T(8,128)(2,1)S(1)} collective-permute-done((bf16[6,24,128]{2,1,0:T(8,128)(2,1)S(1)}, bf16[6,24,128]{2,1,0:T(8,128)(2,1)S(1)}, u32[]{:S(2)}, u32[]{:S(2)}) %collective-permute-start.10) | collective-permute-done | bytes 36896 | tf_op jit(solution)/shard_map/ppermute | solution.py:132
  26.5 5.7 %collective-permute-start.18 = (bf16[8,6,24,128]{3,2,1,0:T(8,128)(2,1)S(1)}, bf16[8,6,24,128]{3,2,1,0:T(8,128)(2,1)S(1)}, u32[]{:S(2)}, u32[]{:S(2)}) collective-permute-start(bf16[8,6,24,128]{3,2,1,0:T(8,128)(2,1)S(1)} %bitcast_dynamic-update-slice_fusion.refs_0_), channel_id=1, source_target_pairs={{0,28},{4,0},{8,4},{12,8},{16,12},{20,16},{24,20},{28,24},{1,29},{... | collective-permute-start | bytes 884744 | tf_op jit(solution)/shard_map/ppermute | solution.py:132
  32.1 3.7 %collective-permute-done.18.refs_6_ = bf16[8,6,24,128]{3,2,1,0:T(8,128)(2,1)S(1)} collective-permute-done((bf16[8,6,24,128]{3,2,1,0:T(8,128)(2,1)S(1)}, bf16[8,6,24,128]{3,2,1,0:T(8,128)(2,1)S(1)}, u32[]{:S(2)}, u32[]{:S(2)}) %collective-permute-start.18) | collective-permute-done | bytes 294944 | tf_op jit(solution)/shard_map/ppermute | solution.py:132
  35.8 3.1 %collective-permute-start.19 = (bf16[8,6,24,128]{3,2,1,0:T(8,128)(2,1)S(1)}, bf16[8,6,24,128]{3,2,1,0:T(8,128)(2,1)S(1)}, u32[]{:S(2)}, u32[]{:S(2)}) collective-permute-start(bf16[8,6,24,128]{3,2,1,0:T(8,128)(2,1)S(1)} %collective-permute-done.18.refs_6_), channel_id=1, source_target_pairs={{0,28},{4,0},{8,4},{12,8},{16,12},{20,16},{24,20},{28,24},{1,29},{... | collective-permute-start | bytes 884744 | tf_op jit(solution)/shard_map/ppermute | solution.py:132
  38.9 4.5 %collective-permute-done.19.refs_5_ = bf16[8,6,24,128]{3,2,1,0:T(8,128)(2,1)S(1)} collective-permute-done((bf16[8,6,24,128]{3,2,1,0:T(8,128)(2,1)S(1)}, bf16[8,6,24,128]{3,2,1,0:T(8,128)(2,1)S(1)}, u32[]{:S(2)}, u32[]{:S(2)}) %collective-permute-start.19) | collective-permute-done | bytes 294944 | tf_op jit(solution)/shard_map/ppermute | solution.py:132
  43.4 3.1 %collective-permute-start.20 = (bf16[8,6,24,128]{3,2,1,0:T(8,128)(2,1)S(1)}, bf16[8,6,24,128]{3,2,1,0:T(8,128)(2,1)S(1)}, u32[]{:S(2)}, u32[]{:S(2)}) collective-permute-start(bf16[8,6,24,128]{3,2,1,0:T(8,128)(2,1)S(1)} %collective-permute-done.19.refs_5_), channel_id=1, source_target_pairs={{0,28},{4,0},{8,4},{12,8},{16,12},{20,16},{24,20},{28,24},{1,29},{... | collective-permute-start | bytes 884744 | tf_op jit(solution)/shard_map/ppermute | solution.py:132
  46.7 8.4 %collective-permute-start.7 = (f32[16]{0:T(128)S(1)}, f32[16]{0:T(128)S(1)}, u32[]{:S(2)}, u32[]{:S(2)}) collective-permute-start(f32[16]{0:T(128)S(1)} %dynamic_slice.8), channel_id=1, source_target_pairs={{0,1},{1,0},{2,3},{3,2},{4,5},{5,4},{6,7},{7,6},{8,9},{9,8},{10,11... | collective-permute-start | bytes 200 | tf_op jit(solution)/shard_map/ppermute | solution.py:132
  55.9 3.1 %collective-permute-start.4 = (s32[128]{0:T(128)S(1)}, s32[128]{0:T(128)S(1)}, u32[]{:S(2)}, u32[]{:S(2)}) collective-permute-start(s32[128]{0:T(128)S(1)} %reshape.51), channel_id=1, source_target_pairs={{0,160},{32,192},{64,224},{96,0},{128,32},{160,64},{192,96},{224,1... | collective-permute-start | bytes 1544 | tf_op jit(solution)/shard_map/ppermute | solution.py:132
  59.1 2.9 %collective-permute-start.3 = (s32[128]{0:T(128)S(1)}, s32[128]{0:T(128)}, u32[]{:S(2)}, u32[]{:S(2)}) collective-permute-start(s32[128]{0:T(128)S(1)} %reshape.51), channel_id=1, source_target_pairs={{0,128},{32,160},{64,192},{96,224},{128,0},{160,32},{192,64},{224,... | collective-permute-start | bytes 1544 | tf_op jit(solution)/shard_map/ppermute | solution.py:132
  63.1 2.2 %collective-permute-start.23 = (bf16[8,6,24,128]{3,2,1,0:T(8,128)(2,1)S(1)}, bf16[8,6,24,128]{3,2,1,0:T(8,128)(2,1)S(1)}, u32[]{:S(2)}, u32[]{:S(2)}) collective-permute-start(bf16[8,6,24,128]{3,2,1,0:T(8,128)(2,1)S(1)} %bitcast_dynamic-update-slice_fusion.refs_0_), channel_id=1, source_target_pairs={{0,1},{1,0},{2,3},{3,2},{4,5},{5,4},{6,7},{7,6},{8,9},{9,8},{10,11... | collective-permute-start | bytes 884744 | tf_op jit(solution)/shard_map/ppermute | solution.py:132
  65.3 3.1 %collective-permute-done.2 = s32[128]{0:T(128)S(1)} collective-permute-done((s32[128]{0:T(128)S(1)}, s32[128]{0:T(128)S(1)}, u32[]{:S(2)}, u32[]{:S(2)}) %collective-permute-start.2) | collective-permute-done | bytes 544 | tf_op jit(solution)/shard_map/ppermute | solution.py:132
  68.3 2.0 %collective-permute-start.29 = (bf16[8,6,24,128]{3,2,1,0:T(8,128)(2,1)S(1)}, bf16[8,6,24,128]{3,2,1,0:T(8,128)(2,1)S(1)}, u32[]{:S(2)}, u32[]{:S(2)}) collective-permute-start(bf16[8,6,24,128]{3,2,1,0:T(8,128)(2,1)S(1)} %collective-permute-done.18.refs_6_), channel_id=1, source_target_pairs={{0,1},{1,0},{2,3},{3,2},{4,5},{5,4},{6,7},{7,6},{8,9},{9,8},{10,11... | collective-permute-start | bytes 884744 | tf_op jit(solution)/shard_map/ppermute | solution.py:132
  70.9 0.9 collective-permute-start
  71.9 5.1 %collective-permute-done = s32[128]{0:T(128)S(1)} collective-permute-done((s32[128]{0:T(128)S(1)}, s32[128]{0:T(128)S(1)}, u32[]{:S(2)}, u32[]{:S(2)}) %collective-permute-start) | collective-permute-done | bytes 544 | tf_op jit(solution)/shard_map/ppermute | solution.py:132
  77.0 1.2 collective-permute-start.25
  78.2 2.9 %collective-permute-start.22 = (bf16[4,6,24,128]{3,2,1,0:T(8,128)(2,1)S(1)}, bf16[4,6,24,128]{3,2,1,0:T(8,128)(2,1)}, u32[]{:S(2)}, u32[]{:S(2)}) collective-permute-start(bf16[4,6,24,128]{3,2,1,0:T(8,128)(2,1)S(1)} %slice.49), channel_id=1, source_target_pairs={{0,28},{4,0},{8,4},{12,8},{16,12},{20,16},{24,20},{28,24},{1,29},{... | collective-permute-start | bytes 442376 | tf_op jit(solution)/shard_map/ppermute | solution.py:132
  81.7 2.6 %collective-permute-done.22.refs_8_ = bf16[4,6,24,128]{3,2,1,0:T(8,128)(2,1)} collective-permute-done((bf16[4,6,24,128]{3,2,1,0:T(8,128)(2,1)S(1)}, bf16[4,6,24,128]{3,2,1,0:T(8,128)(2,1)}, u32[]{:S(2)}, u32[]{:S(2)}) %collective-permute-start.22) | collective-permute-done | bytes 147488 | tf_op jit(solution)/shard_map/ppermute | solution.py:132
  85.2 2.3 %collective-permute-done.21.refs_7_ = bf16[4,6,24,128]{3,2,1,0:T(8,128)(2,1)} collective-permute-done((bf16[4,6,24,128]{3,2,1,0:T(8,128)(2,1)S(1)}, bf16[4,6,24,128]{3,2,1,0:T(8,128)(2,1)}, u32[]{:S(2)}, u32[]{:S(2)}) %collective-permute-start.21) | collective-permute-done | bytes 147488 | tf_op jit(solution)/shard_map/ppermute | solution.py:132
  87.5 1.2 collective-permute-start.30
  91.8 1.3 stack.71.triads_ref
  93.9 23.2 %grams.1 = bf16[16,2,48,384]{3,2,1,0:T(8,128)(2,1)} custom-call(s32[3]{0:T(128)} %pad_add_fusion.meta_ref, s32[8,128]{1,0:T(8,128)} %stack.71.triads_ref, f32[8,128]{1,0:T(8,128)} %broadcast_in_dim.5.weights_ref, bf16[8,6,24,128]{3,2,1,0:T(8,128)(2,1)} %copy-done.3, bf16[8,6,24,128]{3,2,1,0:T(8,128)(2,1)} %copy-done.5, bf16[8,6,24,128]{3,2,1,0:T(8,128)(2,1)} %copy-done.7, ...), custom_call_target="tpu_custom_call" | custom-call | tf_op jit(solution)/shard_map/grams/pallas_call | solution.py:166
  117.2 3.7 %all-to-all-start = ((bf16[16,2,48,384]{3,2,1,0:T(8,128)(2,1)}), bf16[16,2,48,384]{3,2,1,0:T(8,128)(2,1)S(1)}, u32[]{:S(2)}, u32[]{:S(2)}) async-start(bf16[16,2,48,384]{3,2,1,0:T(8,128)(2,1)} %grams.1), calls=%async_computation | async-start | bytes 2359296 | tf_op jit(solution)/shard_map/all_to_all | solution.py:180
  121.0 19.5 %all-to-all-done = bf16[16,2,48,384]{3,2,1,0:T(8,128)(2,1)S(1)} async-done(((bf16[16,2,48,384]{3,2,1,0:T(8,128)(2,1)}), bf16[16,2,48,384]{3,2,1,0:T(8,128)(2,1)S(1)}, u32[]{:S(2)}, u32[]{:S(2)}) %all-to-all-start) | async-done | bytes 1179680 | tf_op jit(solution)/shard_map/all_to_all | solution.py:180
  141.7 7.6 %all_gather.4 = f32[4,2,16,1152]{3,2,1,0:T(8,128)S(1)} all-gather(f32[1,2,16,1152]{3,2,1,0:T(8,128)S(1)} %broadcast_multiply_fusion), channel_id=1, replica_groups=mesh['x'=4,'yh'=2,'z'=8,'yl'=2,'core'=2] {'yl','core'}, dimensions={0}, use_global_device_ids=true | all-gather | bytes 737280 | tf_op jit(solution)/shard_map/all_gather | solution.py:186
  (108 shorter events, 10.2 us)
Async XLA Ops:
  3.3 12.0 %collective-permute-start.8 = (bf16[6,24,128]{2,1,0:T(8,128)(2,1)S(1)}, bf16[6,24,128]{2,1,0:T(8,128)(2,1)S(1)}, u32[]{:S(2)}, u32[]{:S(2)}) collective-permute-start(bf16[6,24,128]{2,1,0:T(8,128)(2,1)S(1)} %get-tuple-element.11), channel_id=1, source_target_pairs={{0,32},{32,64},{64,96},{96,128},{128,160},{160,192},{192,224},{224... | collective-permute-start | bytes 110600 | tf_op jit(solution)/shard_map/ppermute | solution.py:132
  7.1 19.4 %collective-permute-start.14 = (bf16[6,24,128]{2,1,0:T(8,128)(2,1)S(1)}, bf16[6,24,128]{2,1,0:T(8,128)(2,1)S(1)}, u32[]{:S(2)}, u32[]{:S(2)}) collective-permute-start(bf16[6,24,128]{2,1,0:T(8,128)(2,1)S(1)} %get-tuple-element.5), channel_id=1, source_target_pairs={{0,224},{32,0},{64,32},{96,64},{128,96},{160,128},{192,160},{224,1... | collective-permute-start | bytes 110600 | tf_op jit(solution)/shard_map/ppermute | solution.py:132
  9.4 17.1 %collective-permute-start.13 = (bf16[6,24,128]{2,1,0:T(8,128)(2,1)S(1)}, bf16[6,24,128]{2,1,0:T(8,128)(2,1)S(1)}, u32[]{:S(2)}, u32[]{:S(2)}) collective-permute-start(bf16[6,24,128]{2,1,0:T(8,128)(2,1)S(1)} %get-tuple-element.6), channel_id=1, source_target_pairs={{0,192},{32,224},{64,0},{96,32},{128,64},{160,96},{192,128},{224,1... | collective-permute-start | bytes 110600 | tf_op jit(solution)/shard_map/ppermute | solution.py:132
  10.5 15.9 %collective-permute-start.12 = (bf16[6,24,128]{2,1,0:T(8,128)(2,1)S(1)}, bf16[6,24,128]{2,1,0:T(8,128)(2,1)S(1)}, u32[]{:S(2)}, u32[]{:S(2)}) collective-permute-start(bf16[6,24,128]{2,1,0:T(8,128)(2,1)S(1)} %get-tuple-element.7), channel_id=1, source_target_pairs={{0,160},{32,192},{64,224},{96,0},{128,32},{160,64},{192,96},{224,1... | collective-permute-start | bytes 110600 | tf_op jit(solution)/shard_map/ppermute | solution.py:132
  12.8 13.6 %collective-permute-start.11 = (bf16[6,24,128]{2,1,0:T(8,128)(2,1)S(1)}, bf16[6,24,128]{2,1,0:T(8,128)(2,1)S(1)}, u32[]{:S(2)}, u32[]{:S(2)}) collective-permute-start(bf16[6,24,128]{2,1,0:T(8,128)(2,1)S(1)} %get-tuple-element.8), channel_id=1, source_target_pairs={{0,128},{32,160},{64,192},{96,224},{128,0},{160,32},{192,64},{224,... | collective-permute-start | bytes 110600 | tf_op jit(solution)/shard_map/ppermute | solution.py:132
  15.2 4.4 %collective-permute-start.9 = (bf16[6,24,128]{2,1,0:T(8,128)(2,1)S(1)}, bf16[6,24,128]{2,1,0:T(8,128)(2,1)S(1)}, u32[]{:S(2)}, u32[]{:S(2)}) collective-permute-start(bf16[6,24,128]{2,1,0:T(8,128)(2,1)S(1)} %get-tuple-element.10), channel_id=1, source_target_pairs={{0,64},{32,96},{64,128},{96,160},{128,192},{160,224},{192,0},{224,... | collective-permute-start | bytes 110600 | tf_op jit(solution)/shard_map/ppermute | solution.py:132
  19.6 6.7 %collective-permute-start.10 = (bf16[6,24,128]{2,1,0:T(8,128)(2,1)S(1)}, bf16[6,24,128]{2,1,0:T(8,128)(2,1)S(1)}, u32[]{:S(2)}, u32[]{:S(2)}) collective-permute-start(bf16[6,24,128]{2,1,0:T(8,128)(2,1)S(1)} %get-tuple-element.9), channel_id=1, source_target_pairs={{0,96},{32,128},{64,160},{96,192},{128,224},{160,0},{192,32},{224,... | collective-permute-start | bytes 110600 | tf_op jit(solution)/shard_map/ppermute | solution.py:132
  26.5 9.3 %collective-permute-start.18 = (bf16[8,6,24,128]{3,2,1,0:T(8,128)(2,1)S(1)}, bf16[8,6,24,128]{3,2,1,0:T(8,128)(2,1)S(1)}, u32[]{:S(2)}, u32[]{:S(2)}) collective-permute-start(bf16[8,6,24,128]{3,2,1,0:T(8,128)(2,1)S(1)} %bitcast_dynamic-update-slice_fusion.refs_0_), channel_id=1, source_target_pairs={{0,28},{4,0},{8,4},{12,8},{16,12},{20,16},{24,20},{28,24},{1,29},{... | collective-permute-start | bytes 884744 | tf_op jit(solution)/shard_map/ppermute | solution.py:132
  32.1 6.8 %collective-permute-start.15 = (bf16[8,6,24,128]{3,2,1,0:T(8,128)(2,1)S(1)}, bf16[8,6,24,128]{3,2,1,0:T(8,128)(2,1)S(1)}, u32[]{:S(2)}, u32[]{:S(2)}) collective-permute-start(bf16[8,6,24,128]{3,2,1,0:T(8,128)(2,1)S(1)} %bitcast_dynamic-update-slice_fusion.refs_0_), channel_id=1, source_target_pairs={{0,4},{4,8},{8,12},{12,16},{16,20},{20,24},{24,28},{28,0},{1,5},{5... | collective-permute-start | bytes 884744 | tf_op jit(solution)/shard_map/ppermute | solution.py:132
  35.8 7.6 %collective-permute-start.19 = (bf16[8,6,24,128]{3,2,1,0:T(8,128)(2,1)S(1)}, bf16[8,6,24,128]{3,2,1,0:T(8,128)(2,1)S(1)}, u32[]{:S(2)}, u32[]{:S(2)}) collective-permute-start(bf16[8,6,24,128]{3,2,1,0:T(8,128)(2,1)S(1)} %collective-permute-done.18.refs_6_), channel_id=1, source_target_pairs={{0,28},{4,0},{8,4},{12,8},{16,12},{20,16},{24,20},{28,24},{1,29},{... | collective-permute-start | bytes 884744 | tf_op jit(solution)/shard_map/ppermute | solution.py:132
  38.9 20.1 %collective-permute-start.16 = (bf16[8,6,24,128]{3,2,1,0:T(8,128)(2,1)S(1)}, bf16[8,6,24,128]{3,2,1,0:T(8,128)(2,1)S(1)}, u32[]{:S(2)}, u32[]{:S(2)}) collective-permute-start(bf16[8,6,24,128]{3,2,1,0:T(8,128)(2,1)S(1)} %collective-permute-done.15.refs_1_), channel_id=1, source_target_pairs={{0,4},{4,8},{8,12},{12,16},{16,20},{20,24},{24,28},{28,0},{1,5},{5... | collective-permute-start | bytes 884744 | tf_op jit(solution)/shard_map/ppermute | solution.py:132
  43.4 27.0 %collective-permute-start.20 = (bf16[8,6,24,128]{3,2,1,0:T(8,128)(2,1)S(1)}, bf16[8,6,24,128]{3,2,1,0:T(8,128)(2,1)S(1)}, u32[]{:S(2)}, u32[]{:S(2)}) collective-permute-start(bf16[8,6,24,128]{3,2,1,0:T(8,128)(2,1)S(1)} %collective-permute-done.19.refs_5_), channel_id=1, source_target_pairs={{0,28},{4,0},{8,4},{12,8},{16,12},{20,16},{24,20},{28,24},{1,29},{... | collective-permute-start | bytes 884744 | tf_op jit(solution)/shard_map/ppermute | solution.py:132
  46.6 12.5 %collective-permute-start.6 = (s32[128]{0:T(128)S(1)}, s32[128]{0:T(128)}, u32[]{:S(2)}, u32[]{:S(2)}) collective-permute-start(s32[128]{0:T(128)S(1)} %reshape.51), channel_id=1, source_target_pairs={{0,224},{32,0},{64,32},{96,64},{128,96},{160,128},{192,160},{224,1... | collective-permute-start | bytes 1544 | tf_op jit(solution)/shard_map/ppermute | solution.py:132
  46.7 9.2 %collective-permute-start.7 = (f32[16]{0:T(128)S(1)}, f32[16]{0:T(128)S(1)}, u32[]{:S(2)}, u32[]{:S(2)}) collective-permute-start(f32[16]{0:T(128)S(1)} %dynamic_slice.8), channel_id=1, source_target_pairs={{0,1},{1,0},{2,3},{3,2},{4,5},{5,4},{6,7},{7,6},{8,9},{9,8},{10,11... | collective-permute-start | bytes 200 | tf_op jit(solution)/shard_map/ppermute | solution.py:132
  55.1 6.9 %collective-permute-start.5 = (s32[128]{0:T(128)S(1)}, s32[128]{0:T(128)S(1)}, u32[]{:S(2)}, u32[]{:S(2)}) collective-permute-start(s32[128]{0:T(128)S(1)} %reshape.51), channel_id=1, source_target_pairs={{0,192},{32,224},{64,0},{96,32},{128,64},{160,96},{192,128},{224,1... | collective-permute-start | bytes 1544 | tf_op jit(solution)/shard_map/ppermute | solution.py:132
  55.9 6.1 %collective-permute-start.4 = (s32[128]{0:T(128)S(1)}, s32[128]{0:T(128)S(1)}, u32[]{:S(2)}, u32[]{:S(2)}) collective-permute-start(s32[128]{0:T(128)S(1)} %reshape.51), channel_id=1, source_target_pairs={{0,160},{32,192},{64,224},{96,0},{128,32},{160,64},{192,96},{224,1... | collective-permute-start | bytes 1544 | tf_op jit(solution)/shard_map/ppermute | solution.py:132
  59.0 11.8 %collective-permute-start.17 = (bf16[8,6,24,128]{3,2,1,0:T(8,128)(2,1)S(1)}, bf16[8,6,24,128]{3,2,1,0:T(8,128)(2,1)S(1)}, u32[]{:S(2)}, u32[]{:S(2)}) collective-permute-start(bf16[8,6,24,128]{3,2,1,0:T(8,128)(2,1)S(1)} %collective-permute-done.16.refs_2_), channel_id=1, source_target_pairs={{0,4},{4,8},{8,12},{12,16},{16,20},{20,24},{24,28},{28,0},{1,5},{5... | collective-permute-start | bytes 884744 | tf_op jit(solution)/shard_map/ppermute | solution.py:132
  62.0 6.3 %collective-permute-start.2 = (s32[128]{0:T(128)S(1)}, s32[128]{0:T(128)S(1)}, u32[]{:S(2)}, u32[]{:S(2)}) collective-permute-start(s32[128]{0:T(128)S(1)} %reshape.51), channel_id=1, source_target_pairs={{0,96},{32,128},{64,160},{96,192},{128,224},{160,0},{192,32},{224,... | collective-permute-start | bytes 1544 | tf_op jit(solution)/shard_map/ppermute | solution.py:132
  62.1 8.3 %collective-permute-start.1 = (s32[128]{0:T(128)S(1)}, s32[128]{0:T(128)S(1)}, u32[]{:S(2)}, u32[]{:S(2)}) collective-permute-start(s32[128]{0:T(128)S(1)} %reshape.51), channel_id=1, source_target_pairs={{0,64},{32,96},{64,128},{96,160},{128,192},{160,224},{192,0},{224,... | collective-permute-start | bytes 1544 | tf_op jit(solution)/shard_map/ppermute | solution.py:132
  63.1 15.2 %collective-permute-start.23 = (bf16[8,6,24,128]{3,2,1,0:T(8,128)(2,1)S(1)}, bf16[8,6,24,128]{3,2,1,0:T(8,128)(2,1)S(1)}, u32[]{:S(2)}, u32[]{:S(2)}) collective-permute-start(bf16[8,6,24,128]{3,2,1,0:T(8,128)(2,1)S(1)} %bitcast_dynamic-update-slice_fusion.refs_0_), channel_id=1, source_target_pairs={{0,1},{1,0},{2,3},{3,2},{4,5},{5,4},{6,7},{7,6},{8,9},{9,8},{10,11... | collective-permute-start | bytes 884744 | tf_op jit(solution)/shard_map/ppermute | solution.py:132
  68.3 12.8 %collective-permute-start.29 = (bf16[8,6,24,128]{3,2,1,0:T(8,128)(2,1)S(1)}, bf16[8,6,24,128]{3,2,1,0:T(8,128)(2,1)S(1)}, u32[]{:S(2)}, u32[]{:S(2)}) collective-permute-start(bf16[8,6,24,128]{3,2,1,0:T(8,128)(2,1)S(1)} %collective-permute-done.18.refs_6_), channel_id=1, source_target_pairs={{0,1},{1,0},{2,3},{3,2},{4,5},{5,4},{6,7},{7,6},{8,9},{9,8},{10,11... | collective-permute-start | bytes 884744 | tf_op jit(solution)/shard_map/ppermute | solution.py:132
  70.3 10.8 %collective-permute-start.24 = (bf16[8,6,24,128]{3,2,1,0:T(8,128)(2,1)S(1)}, bf16[8,6,24,128]{3,2,1,0:T(8,128)(2,1)S(1)}, u32[]{:S(2)}, u32[]{:S(2)}) collective-permute-start(bf16[8,6,24,128]{3,2,1,0:T(8,128)(2,1)S(1)} %collective-permute-done.15.refs_1_), channel_id=1, source_target_pairs={{0,1},{1,0},{2,3},{3,2},{4,5},{5,4},{6,7},{7,6},{8,9},{9,8},{10,11... | collective-permute-start | bytes 884744 | tf_op jit(solution)/shard_map/ppermute | solution.py:132
  70.5 11.1 %collective-permute-start.28 = (bf16[8,6,24,128]{3,2,1,0:T(8,128)(2,1)S(1)}, bf16[8,6,24,128]{3,2,1,0:T(8,128)(2,1)S(1)}, u32[]{:S(2)}, u32[]{:S(2)}) collective-permute-start(bf16[8,6,24,128]{3,2,1,0:T(8,128)(2,1)S(1)} %collective-permute-done.19.refs_5_), channel_id=1, source_target_pairs={{0,1},{1,0},{2,3},{3,2},{4,5},{5,4},{6,7},{7,6},{8,9},{9,8},{10,11... | collective-permute-start | bytes 884744 | tf_op jit(solution)/shard_map/ppermute | solution.py:132
  70.9 6.1 %collective-permute-start = (s32[128]{0:T(128)S(1)}, s32[128]{0:T(128)S(1)}, u32[]{:S(2)}, u32[]{:S(2)}) collective-permute-start(s32[128]{0:T(128)S(1)} %reshape.51), channel_id=1, source_target_pairs={{0,32},{32,64},{64,96},{96,128},{128,160},{160,192},{192,224},{224... | collective-permute-start | bytes 1544 | tf_op jit(solution)/shard_map/ppermute | solution.py:132
  77.0 16.1 %collective-permute-start.25 = (bf16[8,6,24,128]{3,2,1,0:T(8,128)(2,1)S(1)}, bf16[8,6,24,128]{3,2,1,0:T(8,128)(2,1)S(1)}, u32[]{:S(2)}, u32[]{:S(2)}) collective-permute-start(bf16[8,6,24,128]{3,2,1,0:T(8,128)(2,1)S(1)} %collective-permute-done.16.refs_2_), channel_id=1, source_target_pairs={{0,1},{1,0},{2,3},{3,2},{4,5},{5,4},{6,7},{7,6},{8,9},{9,8},{10,11... | collective-permute-start | bytes 884744 | tf_op jit(solution)/shard_map/ppermute | solution.py:132
  78.2 6.1 %collective-permute-start.22 = (bf16[4,6,24,128]{3,2,1,0:T(8,128)(2,1)S(1)}, bf16[4,6,24,128]{3,2,1,0:T(8,128)(2,1)}, u32[]{:S(2)}, u32[]{:S(2)}) collective-permute-start(bf16[4,6,24,128]{3,2,1,0:T(8,128)(2,1)S(1)} %slice.49), channel_id=1, source_target_pairs={{0,28},{4,0},{8,4},{12,8},{16,12},{20,16},{24,20},{28,24},{1,29},{... | collective-permute-start | bytes 442376 | tf_op jit(solution)/shard_map/ppermute | solution.py:132
  81.1 6.4 %collective-permute-start.21 = (bf16[4,6,24,128]{3,2,1,0:T(8,128)(2,1)S(1)}, bf16[4,6,24,128]{3,2,1,0:T(8,128)(2,1)}, u32[]{:S(2)}, u32[]{:S(2)}) collective-permute-start(bf16[4,6,24,128]{3,2,1,0:T(8,128)(2,1)S(1)} %slice.48), channel_id=1, source_target_pairs={{0,4},{4,8},{8,12},{12,16},{16,20},{20,24},{24,28},{28,0},{1,5},{5... | collective-permute-start | bytes 442376 | tf_op jit(solution)/shard_map/ppermute | solution.py:132
  81.1 12.0 %collective-permute-start.27 = (bf16[8,6,24,128]{3,2,1,0:T(8,128)(2,1)S(1)}, bf16[8,6,24,128]{3,2,1,0:T(8,128)(2,1)}, u32[]{:S(2)}, u32[]{:S(2)}) collective-permute-start(bf16[8,6,24,128]{3,2,1,0:T(8,128)(2,1)S(1)} %collective-permute-done.20.refs_4_), channel_id=1, source_target_pairs={{0,1},{1,0},{2,3},{3,2},{4,5},{5,4},{6,7},{7,6},{8,9},{9,8},{10,11... | collective-permute-start | bytes 884744 | tf_op jit(solution)/shard_map/ppermute | solution.py:132
  81.6 11.6 %collective-permute-start.26 = (bf16[8,6,24,128]{3,2,1,0:T(8,128)(2,1)S(1)}, bf16[8,6,24,128]{3,2,1,0:T(8,128)(2,1)}, u32[]{:S(2)}, u32[]{:S(2)}) collective-permute-start(bf16[8,6,24,128]{3,2,1,0:T(8,128)(2,1)S(1)} %collective-permute-done.17.refs_3_), channel_id=1, source_target_pairs={{0,1},{1,0},{2,3},{3,2},{4,5},{5,4},{6,7},{7,6},{8,9},{9,8},{10,11... | collective-permute-start | bytes 884744 | tf_op jit(solution)/shard_map/ppermute | solution.py:132
  84.3 8.9 %collective-permute-start.31 = (bf16[4,6,24,128]{3,2,1,0:T(8,128)(2,1)}, bf16[4,6,24,128]{3,2,1,0:T(8,128)(2,1)}, u32[]{:S(2)}, u32[]{:S(2)}) collective-permute-start(bf16[4,6,24,128]{3,2,1,0:T(8,128)(2,1)} %collective-permute-done.22.refs_8_), channel_id=1, source_target_pairs={{0,1},{1,0},{2,3},{3,2},{4,5},{5,4},{6,7},{7,6},{8,9},{9,8},{10,11... | collective-permute-start | bytes 442376 | tf_op jit(solution)/shard_map/ppermute | solution.py:132
  87.5 5.7 %collective-permute-start.30 = (bf16[4,6,24,128]{3,2,1,0:T(8,128)(2,1)}, bf16[4,6,24,128]{3,2,1,0:T(8,128)(2,1)}, u32[]{:S(2)}, u32[]{:S(2)}) collective-permute-start(bf16[4,6,24,128]{3,2,1,0:T(8,128)(2,1)} %collective-permute-done.21.refs_7_), channel_id=1, source_target_pairs={{0,1},{1,0},{2,3},{3,2},{4,5},{5,4},{6,7},{7,6},{8,9},{9,8},{10,11... | collective-permute-start | bytes 442376 | tf_op jit(solution)/shard_map/ppermute | solution.py:132
  117.2 23.4 %all-to-all-start = ((bf16[16,2,48,384]{3,2,1,0:T(8,128)(2,1)}), bf16[16,2,48,384]{3,2,1,0:T(8,128)(2,1)S(1)}, u32[]{:S(2)}, u32[]{:S(2)}) async-start(bf16[16,2,48,384]{3,2,1,0:T(8,128)(2,1)} %grams.1), calls=%async_computation | async-start | bytes 2359296 | tf_op jit(solution)/shard_map/all_to_all | solution.py:180
  (22 other events, 602.6 us)

commit v2 on v1

v2 whole, which is shorter than its diff:
```python
import functools

import jax
import jax.numpy as jnp
from jax import lax
from jax.experimental import pallas as pl
from jax.experimental.pallas import tpu as pltpu
from jax.sharding import Mesh
from jax.sharding import PartitionSpec as P

F32, BF16 = jnp.float32, jnp.bfloat16
LANES = 128
VMEM_LIMIT = 56 * 1024 * 1024


def split_kernel(x_ref, triads_ref, weights_ref, out_ref):
    block = lax.broadcasted_iota(jnp.int32, (24, LANES), 1) // 16
    for q in range(6):
        sources = [x_ref[8 * q + s].astype(F32) for s in range(8)]
        for piece in range(8):
            built = None
            for s in range(8):
                shift = (s - piece) % 8 * 16
                moved = pltpu.roll(sources[s], shift, 1) if shift else sources[s]
                built = moved if built is None else jnp.where(block == s, moved, built)
            out_ref[piece, 24 * q : 24 * q + 24] = built.astype(BF16)
    listed = triads_ref[...]
    rest = weights_ref[...]
    parts = []
    for _ in range(3):
        parts.append(rest.astype(BF16))
        rest = rest - parts[-1].astype(F32)
    for piece in range(8):
        tile = [(listed >> 6).astype(F32), (listed & 63).astype(F32)]
        for part in parts:
            own = part[:, 16 * piece : 16 * piece + 16].astype(F32)
            tile.append(jnp.broadcast_to(own, (8, 16)))
        tile.append(jnp.zeros((8, 48), F32))
        out_ref[piece, 144:152] = jnp.concatenate(tile, axis=1).astype(BF16)


def unpack_kernel(own_ref, sib_ref, *refs):
    bins_ref = refs[-1]
    lane = lax.broadcasted_iota(jnp.int32, (24, LANES), 1)

    @pl.loop(0, 8)
    def _(column):
        tiles = [
            [ref[column, 24 * q : 24 * q + 24].astype(F32) for q in range(6)]
            for ref in (own_ref, sib_ref)
        ]
        for r in range(8):
            for part in range(2):
                q, offset = divmod(96 * r + 48 * part, LANES)
                halves = []
                for core in range(2):
                    picked = tiles[core][q]
                    if offset + 48 > LANES:
                        picked = jnp.where(lane >= offset, picked, tiles[core][q + 1])
                    shift = (48 * core - offset) % LANES
                    halves.append(pltpu.roll(picked, shift, 1) if shift else picked)
                merged = jnp.where(lane < 48, halves[0], halves[1])
                lanes = slice(LANES * part, LANES * (part + 1))
                bins_ref[column * 8 + r, :, lanes] = merged.astype(BF16)


def lane_weights(own_ref, sib_ref):
    lane = lax.broadcasted_iota(jnp.int32, (8, LANES), 1)
    total = jnp.zeros((8, LANES), F32)
    for core, ref in enumerate((own_ref, sib_ref)):
        tile = ref[...].astype(F32)
        for component in range(3):
            begin = 48 * core + 16 * component
            inside = (lane >= begin) & (lane < begin + 16)
            value = sum(pltpu.roll(tile, (begin - 32 - 16 * n) % LANES, 1) for n in range(3))
            total = jnp.where(inside, value, total)
    return total[0:1]


def grams_kernel(sub, triads_ref, own_w_ref, sib_w_ref, bins_ref, out_ref, w_ref, q_ref):
    place = lax.axis_index("x") * 2 + lax.axis_index("yh")
    depth, core = lax.axis_index("z"), lax.axis_index("core")
    up = 1 - 2 * core

    def slot(which):
        turn = (up * (depth - (which & 7))) & 7
        return turn * 64 + (which & 56) + (which >> 6)

    weights = lane_weights(own_w_ref, sib_w_ref)
    lane = lax.broadcasted_iota(jnp.int32, (48, LANES), 1)

    @pl.loop(0, 16)
    def _(reader):
        owner = reader >> 1
        row = (reader & 1) * 4 + core * 2 + sub
        k_bin = row * 64 + owner * 8 + depth
        first = bins_ref[owner * 8 + row].astype(F32)
        k_real = first[:, :LANES] * weights
        k_imag = first[:, LANES:] * weights
        for t in range(16):
            l_bin = triads_ref[owner * 8 + row, t]
            m_bin = (k_bin + l_bin) & 511
            second = bins_ref[slot(l_bin)].astype(F32)
            l_real, l_imag = second[:, :LANES], second[:, LANES:]
            real = (k_real * l_real - k_imag * l_imag).astype(BF16)
            imag = k_real * l_imag + k_imag * l_real
            plus, minus = imag.astype(BF16), (-imag).astype(BF16)
            w_ref[48 * t : 48 * t + 24, :LANES] = real
            w_ref[48 * t : 48 * t + 24, LANES:] = plus
            w_ref[48 * t + 24 : 48 * t + 48, :LANES] = minus
            w_ref[48 * t + 24 : 48 * t + 48, LANES:] = real
            q_ref[24 * t : 24 * t + 24, :] = bins_ref[slot(m_bin)]
        for n in range(3):
            start = 5 * n
            product = lax.dot_general(
                w_ref[48 * start : 48 * (start + 6), :],
                q_ref[LANES * n : LANES * (n + 1), :],
                (((1,), (1,)), ((), ())),
                preferred_element_type=F32,
            )
            built = product[:48]
            for i in range(1, 6):
                begin = 24 * (start + i) - LANES * n
                built = jnp.where(lane >= begin, product[48 * i : 48 * (i + 1)], built)
            out_ref[reader, :, LANES * n : LANES * (n + 1)] = built.astype(BF16)


def vmem():
    return pl.BlockSpec(memory_space=pltpu.VMEM)


def smem():
    return pl.BlockSpec(memory_space=pltpu.SMEM)


def step(array, axes, by):
    size = lax.axis_size(axes)
    return lax.ppermute(array, axes, [(i, (i + by) % size) for i in range(size)])


def swap(array):
    return step(array, "core", 1)


def ring(array):
    pairs = []
    for z in range(8):
        pairs += [(2 * z, (2 * z + 2) % 16), (2 * z + 1, (2 * z - 2) % 16 + 1)]
    return lax.ppermute(array, ("z", "core"), pairs)


PARAMS = pltpu.CompilerParams(vmem_limit_bytes=VMEM_LIMIT)
BINS = jax.ShapeDtypeStruct((512, 24, 256), BF16)


def unpack(own, sib, bins, turn):
    operands = [own, sib] + ([] if bins is None else [bins])
    return pl.pallas_call(
        unpack_kernel,
        out_shape=BINS,
        grid=(1,),
        in_specs=[pl.BlockSpec((8, 144, LANES), lambda i: (0, 0, 0))] * 2
        + [pl.BlockSpec(memory_space=pl.ANY)] * (len(operands) - 2),
        out_specs=pl.BlockSpec((64, 24, 256), lambda i: (turn, 0, 0)),
        input_output_aliases={} if bins is None else {2: 0},
        compiler_params=PARAMS,
        cost_estimate=pl.CostEstimate(flops=2000000, bytes_accessed=2000000, transcendentals=0),
        name="unpack",
    )(*operands)


def grams(sub, lists, own_tile, sib_tile, bins):
    return pl.pallas_call(
        functools.partial(grams_kernel, sub),
        out_shape=jax.ShapeDtypeStruct((16, 48, 384), BF16),
        in_specs=[smem()] + [vmem()] * 3,
        out_specs=vmem(),
        scratch_shapes=[pltpu.VMEM((768, 256), BF16), pltpu.VMEM((384, 256), BF16)],
        compiler_params=PARAMS,
        cost_estimate=pl.CostEstimate(
            flops=8000000000, bytes_accessed=8000000, transcendentals=0
        ),
        name="grams",
    )(lists, own_tile, sib_tile, bins)


def body(modes, point_weights, triads, counts):
    core, half = lax.axis_index("core"), lax.axis_index("yl")
    pieces = pl.pallas_call(
        split_kernel,
        out_shape=jax.ShapeDtypeStruct((8, 152, LANES), BF16),
        in_specs=[vmem()] * 3,
        out_specs=vmem(),
        compiler_params=PARAMS,
        name="split",
    )(modes.reshape(48, 24, LANES), triads[:, 0], point_weights[None])
    received = lax.all_to_all(pieces, ("x", "yh"), 0, 0)
    tiles = received[:, 144:]
    codes = tiles[:, :, :32].astype(F32)
    lists = (codes[:, :, :16] * 64 + codes[:, :, 16:]).astype(jnp.int32).reshape(64, 16)

    near = [received[:, :144]]
    sib = [swap(near[0])]
    own_tile, sib_tile = tiles[0], swap(tiles[0])
    for _ in range(3):
        near.append(ring(near[-1]))
        sib.append(ring(sib[-1]))
    near.append(ring(near[-1]))
    bins = unpack(near[0], sib[0], None, 0)
    for s in range(1, 4):
        bins = unpack(near[s], sib[s], bins, s)
        bins = unpack(swap(sib[s]), swap(near[s]), bins, 8 - s)
    bins = unpack(near[4], swap(near[4]), bins, 4)

    live = lax.dynamic_slice_in_dim(counts[:, 0], 4 * half + 2 * core, 2)
    mask = (jnp.arange(16, dtype=jnp.int32)[None, :] < live[:, None]).astype(F32)
    rows = []
    for sub in range(2):
        partial = grams(sub, lists, own_tile, sib_tile, bins)
        parts = lax.all_to_all(partial, ("x", "yh", "yl"), 0, 0)
        summed = jnp.sum(parts.astype(F32), axis=0) / 24
        flat = summed.reshape(48, 16, 24).transpose(1, 0, 2).reshape(16, 1152)
        rows.append(flat * mask[sub][:, None])
    return lax.all_gather(jnp.stack(rows), ("yl", "core")).reshape(8, 1, 16, 1152)


def solution(mesh):
    fine = Mesh(mesh.devices.reshape(4, 2, 8, 2, 2), ("x", "yh", "z", "yl", "core"))
    freq, space = ("x", "yh", "z"), ("yl", "core")
    return jax.shard_map(
        body,
        mesh=fine,
        in_specs=(
            P(None, freq, None, None, None, space),
            P(space),
            P(None, freq, None),
            P(None, freq),
        ),
        out_specs=P(None, freq, None, None),
        check_vma=False,
    )
```

time: 150 us -> 133 us (0.89)
  waiting for transfers between devices: 53 us -> 15.4 us
  Pallas kernels: 25.5 us -> 44 us
  blocking collectives: 7.65 us -> 23.9 us
  starting transfers between devices: 55.2 us -> 42.1 us
    ppermute x32 -> x9, starting transfers between devices: 51.5 us -> 11.6 us  [step(): lax.ppermute(array, axes, [(i, (i + by) % size) for i in range(size)])]
    ppermute x32 -> x9, waiting for transfers between devices: 33.4 us -> 0.02 us  [step(): lax.ppermute(array, axes, [(i, (i + by) % size) for i in range(size)])]
    ppermute x0 -> x7, starting transfers between devices: none -> 21.8 us  [ring(): return lax.ppermute(array, ('z', 'core'), pairs)]
    pallas_call x2 -> x11, Pallas kernels: 25.5 us -> 44 us  [the longest x8 23 us: unpack(): pl.pallas_call(unpack_kernel, out_shape=BINS, grid=(1,), in_specs=[pl.Blo...]
    all_to_all x0 -> x1, blocking collectives: none -> 15.5 us  [body(): received = lax.all_to_all(pieces, ('x', 'yh'), 0, 0)]
    all_to_all x1 -> x2, waiting for transfers between devices: 19.5 us -> 11.9 us  [body(): parts = lax.all_to_all(partial, ('x', 'yh', 'yl'), 0, 0)]
    all_to_all x1 -> x2, starting transfers between devices: 3.7 us -> 8.64 us  [body(): parts = lax.all_to_all(partial, ('x', 'yh', 'yl'), 0, 0)]
    ppermute x0 -> x7, waiting for transfers between devices: none -> 3.52 us  [ring(): return lax.ppermute(array, ('z', 'core'), pairs)]
  transfers between devices with their start and end apart: 33 -> 18, of which waited for: 11 -> 5; matrix products, arithmetic and copies ran while one was open for 3% -> 1% of each run, Pallas kernels for 0% -> 24%
where the time goes in v2:
time: 133 us; the launch traced here: 132 us
  Pallas kernels  44 us (33%)
  starting transfers between devices  42.1 us (32%)
  blocking collectives  23.9 us (18%)
  waiting for transfers between devices  15.4 us (12%)
  local copies, waits for them, and re-layouts  5.42 us (4%)
    pallas_call x8, Pallas kernels, unpack(): pl.pallas_call(unpack_kernel, out_shape=BINS, grid=(1,), in_specs=[pl.Blo...  23 us
    ppermute x7, starting transfers between devices, ring(): return lax.ppermute(array, ('z', 'core'), pairs)  21.8 us
    pallas_call x2, Pallas kernels, grams(): pl.pallas_call(functools.partial(grams_kernel, sub), out_shape=jax.ShapeD...  18.6 us
    all_to_all x1, blocking collectives, body(): received = lax.all_to_all(pieces, ('x', 'yh'), 0, 0)  15.5 us
    all_to_all x2, waiting for transfers between devices, body(): parts = lax.all_to_all(partial, ('x', 'yh', 'yl'), 0, 0)  11.9 us
    ppermute x9, starting transfers between devices, step(): lax.ppermute(array, axes, [(i, (i + by) % size) for i in range(size)])  11.6 us
    all_to_all x2, starting transfers between devices, body(): parts = lax.all_to_all(partial, ('x', 'yh', 'yl'), 0, 0)  8.64 us
    all_gather x1, blocking collectives, body(): lax.all_gather(jnp.stack(rows), ('yl', 'core')).reshape(8, 1, 16, 1152)  8.43 us
  transfers between devices with their start and end apart: 18, of which 5 were waited for; matrix products, arithmetic and copies ran while one was open for 1% of the time, Pallas kernels for 24%

profile of v2, /device:TPU:1, one launch (start us, length us, event | category | flops | bytes accessed | tf_op | source)
XLA Modules:
  0.0 132.1 jit_solution(11730575395716331643)
XLA Ops:
  0.0 2.3 %split.1 = bf16[8,152,128]{2,1,0:T(8,128)(2,1)} custom-call(bf16[48,24,128]{2,1,0:T(8,128)(2,1)} %bitcast.25, s32[8,16]{1,0:T(8,128)} %bitcast.26, f32[1,128]{1,0:T(1,128)} %bitcast.27), custom_call_target="tpu_custom_call" | custom-call | tf_op jit(solution)/shard_map/split/pallas_call | solution.py:189
  2.3 15.5 %all_to_all.15 = bf16[8,152,128]{2,1,0:T(8,128)(2,1)S(1)} all-to-all(bf16[8,152,128]{2,1,0:T(8,128)(2,1)} %split.1), channel_id=1, replica_groups=mesh['x'=4,'yh'=2,'z'=8,'yl'=2,'core'=2] {'x','yh'}, dimensions={0} | all-to-all | bytes 622592 | tf_op jit(solution)/shard_map/all_to_all | solution.py:197
  17.9 2.4 %collective-permute-start.6 = (bf16[8,144,128]{2,1,0:T(8,128)(2,1)S(1)}, bf16[8,144,128]{2,1,0:T(8,128)(2,1)S(1)}, u32[]{:S(2)}, u32[]{:S(2)}) collective-permute-start(bf16[8,144,128]{2,1,0:T(8,128)(2,1)S(1)} %slice.42.own_ref), channel_id=1, source_target_pairs={{0,1},{1,0},{2,3},{3,2},{4,5},{5,4},{6,7},{7,6},{8,9},{9,8},{10,11... | collective-permute-start | bytes 884744 | tf_op jit(solution)/shard_map/ppermute | solution.py:138
  20.3 5.6 %collective-permute-start.1 = (bf16[8,144,128]{2,1,0:T(8,128)(2,1)S(1)}, bf16[8,144,128]{2,1,0:T(8,128)(2,1)S(1)}, u32[]{:S(2)}, u32[]{:S(2)}) collective-permute-start(bf16[8,144,128]{2,1,0:T(8,128)(2,1)S(1)} %slice.42.own_ref), channel_id=1, source_target_pairs={{0,4},{1,29},{4,8},{5,1},{8,12},{9,5},{12,16},{13,9},{16,20},{17,1... | collective-permute-start | bytes 884744 | tf_op jit(solution)/shard_map/ppermute | solution.py:149
  25.9 1.2 collective-permute-start.7
  27.1 2.5 %collective-permute-done.1.own_ref = bf16[8,144,128]{2,1,0:T(8,128)(2,1)S(1)} collective-permute-done((bf16[8,144,128]{2,1,0:T(8,128)(2,1)S(1)}, bf16[8,144,128]{2,1,0:T(8,128)(2,1)S(1)}, u32[]{:S(2)}, u32[]{:S(2)}) %collective-permute-start.1) | collective-permute-done | bytes 294944 | tf_op jit(solution)/shard_map/ppermute | solution.py:149
  29.5 3.1 %collective-permute-start.2 = (bf16[8,144,128]{2,1,0:T(8,128)(2,1)S(1)}, bf16[8,144,128]{2,1,0:T(8,128)(2,1)S(1)}, u32[]{:S(2)}, u32[]{:S(2)}) collective-permute-start(bf16[8,144,128]{2,1,0:T(8,128)(2,1)S(1)} %collective-permute-done.1.own_ref), channel_id=1, source_target_pairs={{0,4},{1,29},{4,8},{5,1},{8,12},{9,5},{12,16},{13,9},{16,20},{17,1... | collective-permute-start | bytes 884744 | tf_op jit(solution)/shard_map/ppermute | solution.py:149
  32.7 3.1 %collective-permute-start.8 = (bf16[8,144,128]{2,1,0:T(8,128)(2,1)S(1)}, bf16[8,144,128]{2,1,0:T(8,128)(2,1)S(1)}, u32[]{:S(2)}, u32[]{:S(2)}) collective-permute-start(bf16[8,144,128]{2,1,0:T(8,128)(2,1)S(1)} %collective-permute-done.7.sib_ref), channel_id=1, source_target_pairs={{0,4},{1,29},{4,8},{5,1},{8,12},{9,5},{12,16},{13,9},{16,20},{17,1... | collective-permute-start | bytes 884744 | tf_op jit(solution)/shard_map/ppermute | solution.py:149
  36.3 3.1 %collective-permute-start.3 = (bf16[8,144,128]{2,1,0:T(8,128)(2,1)S(1)}, bf16[8,144,128]{2,1,0:T(8,128)(2,1)S(1)}, u32[]{:S(2)}, u32[]{:S(2)}) collective-permute-start(bf16[8,144,128]{2,1,0:T(8,128)(2,1)S(1)} %collective-permute-done.2.own_ref), channel_id=1, source_target_pairs={{0,4},{1,29},{4,8},{5,1},{8,12},{9,5},{12,16},{13,9},{16,20},{17,1... | collective-permute-start | bytes 884744 | tf_op jit(solution)/shard_map/ppermute | solution.py:149
  40.0 2.5 %collective-permute-start.9 = (bf16[8,144,128]{2,1,0:T(8,128)(2,1)S(1)}, bf16[8,144,128]{2,1,0:T(8,128)(2,1)S(1)}, u32[]{:S(2)}, u32[]{:S(2)}) collective-permute-start(bf16[8,144,128]{2,1,0:T(8,128)(2,1)S(1)} %collective-permute-done.8.sib_ref), channel_id=1, source_target_pairs={{0,4},{1,29},{4,8},{5,1},{8,12},{9,5},{12,16},{13,9},{16,20},{17,1... | collective-permute-start | bytes 884744 | tf_op jit(solution)/shard_map/ppermute | solution.py:149
  43.1 3.1 %collective-permute-start.4 = (bf16[8,144,128]{2,1,0:T(8,128)(2,1)S(1)}, bf16[8,144,128]{2,1,0:T(8,128)(2,1)S(1)}, u32[]{:S(2)}, u32[]{:S(2)}) collective-permute-start(bf16[8,144,128]{2,1,0:T(8,128)(2,1)S(1)} %collective-permute-done.3.own_ref), channel_id=1, source_target_pairs={{0,4},{1,29},{4,8},{5,1},{8,12},{9,5},{12,16},{13,9},{16,20},{17,1... | collective-permute-start | bytes 884744 | tf_op jit(solution)/shard_map/ppermute | solution.py:149
  47.5 2.4 %collective-permute-start.10 = (bf16[8,144,128]{2,1,0:T(8,128)(2,1)S(1)}, bf16[8,144,128]{2,1,0:T(8,128)(2,1)S(1)}, u32[]{:S(2)}, u32[]{:S(2)}) collective-permute-start(bf16[8,144,128]{2,1,0:T(8,128)(2,1)S(1)} %collective-permute-done.9.sib_ref), channel_id=1, source_target_pairs={{0,1},{1,0},{2,3},{3,2},{4,5},{5,4},{6,7},{7,6},{8,9},{9,8},{10,11... | collective-permute-start | bytes 884744 | tf_op jit(solution)/shard_map/ppermute | solution.py:138
  50.0 4.8 %collective-permute-start.5 = (bf16[8,144,128]{2,1,0:T(8,128)(2,1)S(1)}, bf16[8,144,128]{2,1,0:T(8,128)(2,1)S(1)}, u32[]{:S(2)}, u32[]{:S(2)}) collective-permute-start(bf16[8,144,128]{2,1,0:T(8,128)(2,1)S(1)} %collective-permute-done.4.own_ref), channel_id=1, source_target_pairs={{0,1},{1,0},{2,3},{3,2},{4,5},{5,4},{6,7},{7,6},{8,9},{9,8},{10,11... | collective-permute-start | bytes 884744 | tf_op jit(solution)/shard_map/ppermute | solution.py:138
  55.7 2.9 %unpack.8.refs_0_ = bf16[512,24,256]{2,1,0:T(8,128)(2,1)} custom-call(bf16[8,144,128]{2,1,0:T(8,128)(2,1)} %copy-done.1, bf16[8,144,128]{2,1,0:T(8,128)(2,1)} %copy-done.16), custom_call_target="tpu_custom_call" | custom-call | flops 2000000 | bytes 2000000 | tf_op jit(solution)/shard_map/unpack/pallas_call | solution.py:158
  58.6 2.9 %unpack.9.refs_0_ = bf16[512,24,256]{2,1,0:T(8,128)(2,1)} custom-call(bf16[8,144,128]{2,1,0:T(8,128)(2,1)} %copy-done.2, bf16[8,144,128]{2,1,0:T(8,128)(2,1)} %copy-done.3, bf16[512,24,256]{2,1,0:T(8,128)(2,1)} %unpack.8.refs_0_), custom_call_target="tpu_custom_call", output_to_operand_aliasing={{}: (2, {})} | custom-call | flops 2000000 | bytes 2000000 | tf_op jit(solution)/shard_map/unpack/pallas_call | solution.py:158
  61.6 2.9 %unpack.10.refs_0_ = bf16[512,24,256]{2,1,0:T(8,128)(2,1)} custom-call(bf16[8,144,128]{2,1,0:T(8,128)(2,1)} %copy-done.10, bf16[8,144,128]{2,1,0:T(8,128)(2,1)} %copy-done.9, bf16[512,24,256]{2,1,0:T(8,128)(2,1)} %unpack.9.refs_0_), custom_call_target="tpu_custom_call", output_to_operand_aliasing={{}: (2, {})} | custom-call | flops 2000000 | bytes 2000000 | tf_op jit(solution)/shard_map/unpack/pallas_call | solution.py:158
  64.5 2.9 %unpack.11.refs_0_ = bf16[512,24,256]{2,1,0:T(8,128)(2,1)} custom-call(bf16[8,144,128]{2,1,0:T(8,128)(2,1)} %copy-done.4, bf16[8,144,128]{2,1,0:T(8,128)(2,1)} %copy-done.6, bf16[512,24,256]{2,1,0:T(8,128)(2,1)} %unpack.10.refs_0_), custom_call_target="tpu_custom_call", output_to_operand_aliasing={{}: (2, {})} | custom-call | flops 2000000 | bytes 2000000 | tf_op jit(solution)/shard_map/unpack/pallas_call | solution.py:158
  68.1 2.9 %unpack.12.refs_0_ = bf16[512,24,256]{2,1,0:T(8,128)(2,1)} custom-call(bf16[8,144,128]{2,1,0:T(8,128)(2,1)} %copy-done.13, bf16[8,144,128]{2,1,0:T(8,128)(2,1)} %copy-done.11, bf16[512,24,256]{2,1,0:T(8,128)(2,1)} %unpack.11.refs_0_), custom_call_target="tpu_custom_call", output_to_operand_aliasing={{}: (2, {})} | custom-call | flops 2000000 | bytes 2000000 | tf_op jit(solution)/shard_map/unpack/pallas_call | solution.py:158
  71.0 2.9 %unpack.13.refs_0_ = bf16[512,24,256]{2,1,0:T(8,128)(2,1)} custom-call(bf16[8,144,128]{2,1,0:T(8,128)(2,1)} %copy-done.5, bf16[8,144,128]{2,1,0:T(8,128)(2,1)} %copy-done.8, bf16[512,24,256]{2,1,0:T(8,128)(2,1)} %unpack.12.refs_0_), custom_call_target="tpu_custom_call", output_to_operand_aliasing={{}: (2, {})} | custom-call | flops 2000000 | bytes 2000000 | tf_op jit(solution)/shard_map/unpack/pallas_call | solution.py:158
  73.8 0.7 copy-done.12
  74.6 0.7 copy-done.14
  75.3 2.9 %unpack.14.refs_0_ = bf16[512,24,256]{2,1,0:T(8,128)(2,1)} custom-call(bf16[8,144,128]{2,1,0:T(8,128)(2,1)} %copy-done.14, bf16[8,144,128]{2,1,0:T(8,128)(2,1)} %copy-done.12, bf16[512,24,256]{2,1,0:T(8,128)(2,1)} %unpack.13.refs_0_), custom_call_target="tpu_custom_call", output_to_operand_aliasing={{}: (2, {})} | custom-call | flops 2000000 | bytes 2000000 | tf_op jit(solution)/shard_map/unpack/pallas_call | solution.py:158
  78.2 0.7 copy-done.15
  78.9 2.9 %unpack.15.bins_ref = bf16[512,24,256]{2,1,0:T(8,128)(2,1)} custom-call(bf16[8,144,128]{2,1,0:T(8,128)(2,1)} %copy-done.7, bf16[8,144,128]{2,1,0:T(8,128)(2,1)} %copy-done.15, bf16[512,24,256]{2,1,0:T(8,128)(2,1)} %unpack.14.refs_0_), custom_call_target="tpu_custom_call", output_to_operand_aliasing={{}: (2, {})} | custom-call | flops 2000000 | bytes 2000000 | tf_op jit(solution)/shard_map/unpack/pallas_call | solution.py:158
  82.3 9.3 %grams.2 = bf16[16,48,384]{2,1,0:T(8,128)(2,1)} custom-call(s32[64,16]{1,0:T(8,128)} %fusion.1.triads_ref, bf16[8,128]{1,0:T(8,128)(2,1)} %copy-done.17, bf16[8,128]{1,0:T(8,128)(2,1)} %copy-done.18, bf16[512,24,256]{2,1,0:T(8,128)(2,1)} %unpack.15.bins_ref), custom_call_target="tpu_custom_call" | custom-call | flops 8000000000 | bytes 8000000 | tf_op jit(solution)/shard_map/grams/pallas_call | solution.py:173
  91.6 3.6 %all-to-all-start.1 = ((bf16[16,48,384]{2,1,0:T(8,128)(2,1)}), bf16[16,48,384]{2,1,0:T(8,128)(2,1)S(1)}, u32[]{:S(2)}, u32[]{:S(2)}) async-start(bf16[16,48,384]{2,1,0:T(8,128)(2,1)} %grams.2), calls=%async_computation.1 | async-start | bytes 1179648 | tf_op jit(solution)/shard_map/all_to_all | solution.py:220
  95.2 9.3 %grams.3 = bf16[16,48,384]{2,1,0:T(8,128)(2,1)} custom-call(s32[64,16]{1,0:T(8,128)} %fusion.1.triads_ref, bf16[8,128]{1,0:T(8,128)(2,1)} %copy-done.17, bf16[8,128]{1,0:T(8,128)(2,1)} %copy-done.18, bf16[512,24,256]{2,1,0:T(8,128)(2,1)} %unpack.15.bins_ref), custom_call_target="tpu_custom_call" | custom-call | flops 8000000000 | bytes 8000000 | tf_op jit(solution)/shard_map/grams/pallas_call | solution.py:173
  104.5 1.5 %all-to-all-done.1 = bf16[16,48,384]{2,1,0:T(8,128)(2,1)S(1)} async-done(((bf16[16,48,384]{2,1,0:T(8,128)(2,1)}), bf16[16,48,384]{2,1,0:T(8,128)(2,1)S(1)}, u32[]{:S(2)}, u32[]{:S(2)}) %all-to-all-start.1) | async-done | bytes 589856 | tf_op jit(solution)/shard_map/all_to_all | solution.py:220
  106.1 5.1 %all-to-all-start.2 = ((bf16[16,48,384]{2,1,0:T(8,128)(2,1)}), bf16[16,48,384]{2,1,0:T(8,128)(2,1)S(1)}, u32[]{:S(2)}, u32[]{:S(2)}) async-start(bf16[16,48,384]{2,1,0:T(8,128)(2,1)} %grams.3), calls=%async_computation.2 | async-start | bytes 1179648 | tf_op jit(solution)/shard_map/all_to_all | solution.py:220
  111.8 10.3 %all-to-all-done.2 = bf16[16,48,384]{2,1,0:T(8,128)(2,1)S(1)} async-done(((bf16[16,48,384]{2,1,0:T(8,128)(2,1)}), bf16[16,48,384]{2,1,0:T(8,128)(2,1)S(1)}, u32[]{:S(2)}, u32[]{:S(2)}) %all-to-all-start.2) | async-done | bytes 589856 | tf_op jit(solution)/shard_map/all_to_all | solution.py:220
  122.8 8.4 %all-gather = f32[8,16,1152]{2,1,0:T(8,128)S(1)} all-gather(f32[2,16,1152]{2,1,0:T(8,128)S(1)} %pad_maximum_fusion), channel_id=2, replica_groups=mesh['x'=4,'yh'=2,'z'=8,'yl'=2,'core'=2] {'yl','core'}, dimensions={0}, use_global_device_ids=true | all-gather | bytes 737280 | tf_op jit(solution)/shard_map/all_gather | solution.py:224
  131.2 0.8 copy.28
  (75 shorter events, 6.6 us)
Async XLA Ops:
  0.0 39.4 %copy-start = (s32[8,1]{0,1:T(1,128)S(1)}, s32[8,1]{0,1:T(1,128)}, u32[]{:S(2)}) copy-start(s32[8,1]{0,1:T(1,128)} %param.7) | copy-start | bytes 100
  17.9 37.9 %copy-start.1 = (bf16[8,144,128]{2,1,0:T(8,128)(2,1)}, bf16[8,144,128]{2,1,0:T(8,128)(2,1)S(1)}, u32[]{:S(2)}) copy-start(bf16[8,144,128]{2,1,0:T(8,128)(2,1)S(1)} %slice.42.own_ref) | copy-start | bytes 884740
  17.9 8.0 %collective-permute-start.6 = (bf16[8,144,128]{2,1,0:T(8,128)(2,1)S(1)}, bf16[8,144,128]{2,1,0:T(8,128)(2,1)S(1)}, u32[]{:S(2)}, u32[]{:S(2)}) collective-permute-start(bf16[8,144,128]{2,1,0:T(8,128)(2,1)S(1)} %slice.42.own_ref), channel_id=1, source_target_pairs={{0,1},{1,0},{2,3},{3,2},{4,5},{5,4},{6,7},{7,6},{8,9},{9,8},{10,11... | collective-permute-start | bytes 884744 | tf_op jit(solution)/shard_map/ppermute | solution.py:138
  20.3 9.2 %collective-permute-start.1 = (bf16[8,144,128]{2,1,0:T(8,128)(2,1)S(1)}, bf16[8,144,128]{2,1,0:T(8,128)(2,1)S(1)}, u32[]{:S(2)}, u32[]{:S(2)}) collective-permute-start(bf16[8,144,128]{2,1,0:T(8,128)(2,1)S(1)} %slice.42.own_ref), channel_id=1, source_target_pairs={{0,4},{1,29},{4,8},{5,1},{8,12},{9,5},{12,16},{13,9},{16,20},{17,1... | collective-permute-start | bytes 884744 | tf_op jit(solution)/shard_map/ppermute | solution.py:149
  25.9 29.9 %copy-start.16 = (bf16[8,144,128]{2,1,0:T(8,128)(2,1)}, bf16[8,144,128]{2,1,0:T(8,128)(2,1)S(1)}, u32[]{:S(2)}) copy-start(bf16[8,144,128]{2,1,0:T(8,128)(2,1)S(1)} %collective-permute-done.6.sib_ref) | copy-start | bytes 884740
  25.9 6.8 %collective-permute-start.7 = (bf16[8,144,128]{2,1,0:T(8,128)(2,1)S(1)}, bf16[8,144,128]{2,1,0:T(8,128)(2,1)S(1)}, u32[]{:S(2)}, u32[]{:S(2)}) collective-permute-start(bf16[8,144,128]{2,1,0:T(8,128)(2,1)S(1)} %collective-permute-done.6.sib_ref), channel_id=1, source_target_pairs={{0,4},{1,29},{4,8},{5,1},{8,12},{9,5},{12,16},{13,9},{16,20},{17,1... | collective-permute-start | bytes 884744 | tf_op jit(solution)/shard_map/ppermute | solution.py:149
  29.5 29.1 %copy-start.2 = (bf16[8,144,128]{2,1,0:T(8,128)(2,1)}, bf16[8,144,128]{2,1,0:T(8,128)(2,1)S(1)}, u32[]{:S(2)}) copy-start(bf16[8,144,128]{2,1,0:T(8,128)(2,1)S(1)} %collective-permute-done.1.own_ref) | copy-start | bytes 884740
  29.5 6.8 %collective-permute-start.2 = (bf16[8,144,128]{2,1,0:T(8,128)(2,1)S(1)}, bf16[8,144,128]{2,1,0:T(8,128)(2,1)S(1)}, u32[]{:S(2)}, u32[]{:S(2)}) collective-permute-start(bf16[8,144,128]{2,1,0:T(8,128)(2,1)S(1)} %collective-permute-done.1.own_ref), channel_id=1, source_target_pairs={{0,4},{1,29},{4,8},{5,1},{8,12},{9,5},{12,16},{13,9},{16,20},{17,1... | collective-permute-start | bytes 884744 | tf_op jit(solution)/shard_map/ppermute | solution.py:149
  32.7 25.9 %copy-start.3 = (bf16[8,144,128]{2,1,0:T(8,128)(2,1)}, bf16[8,144,128]{2,1,0:T(8,128)(2,1)S(1)}, u32[]{:S(2)}) copy-start(bf16[8,144,128]{2,1,0:T(8,128)(2,1)S(1)} %collective-permute-done.7.sib_ref) | copy-start | bytes 884740
  32.7 7.4 %collective-permute-start.8 = (bf16[8,144,128]{2,1,0:T(8,128)(2,1)S(1)}, bf16[8,144,128]{2,1,0:T(8,128)(2,1)S(1)}, u32[]{:S(2)}, u32[]{:S(2)}) collective-permute-start(bf16[8,144,128]{2,1,0:T(8,128)(2,1)S(1)} %collective-permute-done.7.sib_ref), channel_id=1, source_target_pairs={{0,4},{1,29},{4,8},{5,1},{8,12},{9,5},{12,16},{13,9},{16,20},{17,1... | collective-permute-start | bytes 884744 | tf_op jit(solution)/shard_map/ppermute | solution.py:149
  36.3 25.2 %copy-start.4 = (bf16[8,144,128]{2,1,0:T(8,128)(2,1)}, bf16[8,144,128]{2,1,0:T(8,128)(2,1)S(1)}, u32[]{:S(2)}) copy-start(bf16[8,144,128]{2,1,0:T(8,128)(2,1)S(1)} %collective-permute-done.2.own_ref) | copy-start | bytes 884740
  36.3 6.8 %collective-permute-start.3 = (bf16[8,144,128]{2,1,0:T(8,128)(2,1)S(1)}, bf16[8,144,128]{2,1,0:T(8,128)(2,1)S(1)}, u32[]{:S(2)}, u32[]{:S(2)}) collective-permute-start(bf16[8,144,128]{2,1,0:T(8,128)(2,1)S(1)} %collective-permute-done.2.own_ref), channel_id=1, source_target_pairs={{0,4},{1,29},{4,8},{5,1},{8,12},{9,5},{12,16},{13,9},{16,20},{17,1... | collective-permute-start | bytes 884744 | tf_op jit(solution)/shard_map/ppermute | solution.py:149
  39.5 7.4 %collective-permute-start.15 = (bf16[8,144,128]{2,1,0:T(8,128)(2,1)S(1)}, bf16[8,144,128]{2,1,0:T(8,128)(2,1)S(1)}, u32[]{:S(2)}, u32[]{:S(2)}) collective-permute-start(bf16[8,144,128]{2,1,0:T(8,128)(2,1)S(1)} %collective-permute-done.1.own_ref), channel_id=1, source_target_pairs={{0,1},{1,0},{2,3},{3,2},{4,5},{5,4},{6,7},{7,6},{8,9},{9,8},{10,11... | collective-permute-start | bytes 884744 | tf_op jit(solution)/shard_map/ppermute | solution.py:138
  39.5 7.5 %collective-permute-start.14 = (bf16[8,144,128]{2,1,0:T(8,128)(2,1)S(1)}, bf16[8,144,128]{2,1,0:T(8,128)(2,1)S(1)}, u32[]{:S(2)}, u32[]{:S(2)}) collective-permute-start(bf16[8,144,128]{2,1,0:T(8,128)(2,1)S(1)} %collective-permute-done.7.sib_ref), channel_id=1, source_target_pairs={{0,1},{1,0},{2,3},{3,2},{4,5},{5,4},{6,7},{7,6},{8,9},{9,8},{10,11... | collective-permute-start | bytes 884744 | tf_op jit(solution)/shard_map/ppermute | solution.py:138
  40.0 21.5 %copy-start.6 = (bf16[8,144,128]{2,1,0:T(8,128)(2,1)}, bf16[8,144,128]{2,1,0:T(8,128)(2,1)S(1)}, u32[]{:S(2)}) copy-start(bf16[8,144,128]{2,1,0:T(8,128)(2,1)S(1)} %collective-permute-done.8.sib_ref) | copy-start | bytes 884740
  40.0 7.5 %collective-permute-start.9 = (bf16[8,144,128]{2,1,0:T(8,128)(2,1)S(1)}, bf16[8,144,128]{2,1,0:T(8,128)(2,1)S(1)}, u32[]{:S(2)}, u32[]{:S(2)}) collective-permute-start(bf16[8,144,128]{2,1,0:T(8,128)(2,1)S(1)} %collective-permute-done.8.sib_ref), channel_id=1, source_target_pairs={{0,4},{1,29},{4,8},{5,1},{8,12},{9,5},{12,16},{13,9},{16,20},{17,1... | collective-permute-start | bytes 884744 | tf_op jit(solution)/shard_map/ppermute | solution.py:149
  43.1 18.4 %copy-start.5 = (bf16[8,144,128]{2,1,0:T(8,128)(2,1)}, bf16[8,144,128]{2,1,0:T(8,128)(2,1)S(1)}, u32[]{:S(2)}) copy-start(bf16[8,144,128]{2,1,0:T(8,128)(2,1)S(1)} %collective-permute-done.3.own_ref) | copy-start | bytes 884740
  43.1 6.9 %collective-permute-start.4 = (bf16[8,144,128]{2,1,0:T(8,128)(2,1)S(1)}, bf16[8,144,128]{2,1,0:T(8,128)(2,1)S(1)}, u32[]{:S(2)}, u32[]{:S(2)}) collective-permute-start(bf16[8,144,128]{2,1,0:T(8,128)(2,1)S(1)} %collective-permute-done.3.own_ref), channel_id=1, source_target_pairs={{0,4},{1,29},{4,8},{5,1},{8,12},{9,5},{12,16},{13,9},{16,20},{17,1... | collective-permute-start | bytes 884744 | tf_op jit(solution)/shard_map/ppermute | solution.py:149
  46.3 8.5 %collective-permute-start.13 = (bf16[8,144,128]{2,1,0:T(8,128)(2,1)S(1)}, bf16[8,144,128]{2,1,0:T(8,128)(2,1)S(1)}, u32[]{:S(2)}, u32[]{:S(2)}) collective-permute-start(bf16[8,144,128]{2,1,0:T(8,128)(2,1)S(1)} %collective-permute-done.2.own_ref), channel_id=1, source_target_pairs={{0,1},{1,0},{2,3},{3,2},{4,5},{5,4},{6,7},{7,6},{8,9},{9,8},{10,11... | collective-permute-start | bytes 884744 | tf_op jit(solution)/shard_map/ppermute | solution.py:138
  46.9 14.6 %copy-start.9 = (bf16[8,144,128]{2,1,0:T(8,128)(2,1)}, bf16[8,144,128]{2,1,0:T(8,128)(2,1)S(1)}, u32[]{:S(2)}) copy-start(bf16[8,144,128]{2,1,0:T(8,128)(2,1)S(1)} %collective-permute-done.15.sib_ref) | copy-start | bytes 884740
  46.9 20.4 %collective-permute-start.12 = (bf16[8,144,128]{2,1,0:T(8,128)(2,1)S(1)}, bf16[8,144,128]{2,1,0:T(8,128)(2,1)S(1)}, u32[]{:S(2)}, u32[]{:S(2)}) collective-permute-start(bf16[8,144,128]{2,1,0:T(8,128)(2,1)S(1)} %collective-permute-done.8.sib_ref), channel_id=1, source_target_pairs={{0,1},{1,0},{2,3},{3,2},{4,5},{5,4},{6,7},{7,6},{8,9},{9,8},{10,11... | collective-permute-start | bytes 884744 | tf_op jit(solution)/shard_map/ppermute | solution.py:138
  47.0 14.5 %copy-start.10 = (bf16[8,144,128]{2,1,0:T(8,128)(2,1)}, bf16[8,144,128]{2,1,0:T(8,128)(2,1)S(1)}, u32[]{:S(2)}) copy-start(bf16[8,144,128]{2,1,0:T(8,128)(2,1)S(1)} %collective-permute-done.14.own_ref) | copy-start | bytes 884740
  47.0 26.8 %collective-permute-start.11 = (bf16[8,144,128]{2,1,0:T(8,128)(2,1)S(1)}, bf16[8,144,128]{2,1,0:T(8,128)(2,1)S(1)}, u32[]{:S(2)}, u32[]{:S(2)}) collective-permute-start(bf16[8,144,128]{2,1,0:T(8,128)(2,1)S(1)} %collective-permute-done.3.own_ref), channel_id=1, source_target_pairs={{0,1},{1,0},{2,3},{3,2},{4,5},{5,4},{6,7},{7,6},{8,9},{9,8},{10,11... | collective-permute-start | bytes 884744 | tf_op jit(solution)/shard_map/ppermute | solution.py:138
  47.5 14.0 %copy-start.8 = (bf16[8,144,128]{2,1,0:T(8,128)(2,1)}, bf16[8,144,128]{2,1,0:T(8,128)(2,1)S(1)}, u32[]{:S(2)}) copy-start(bf16[8,144,128]{2,1,0:T(8,128)(2,1)S(1)} %collective-permute-done.9.sib_ref) | copy-start | bytes 884740
  47.5 26.3 %collective-permute-start.10 = (bf16[8,144,128]{2,1,0:T(8,128)(2,1)S(1)}, bf16[8,144,128]{2,1,0:T(8,128)(2,1)S(1)}, u32[]{:S(2)}, u32[]{:S(2)}) collective-permute-start(bf16[8,144,128]{2,1,0:T(8,128)(2,1)S(1)} %collective-permute-done.9.sib_ref), channel_id=1, source_target_pairs={{0,1},{1,0},{2,3},{3,2},{4,5},{5,4},{6,7},{7,6},{8,9},{9,8},{10,11... | collective-permute-start | bytes 884744 | tf_op jit(solution)/shard_map/ppermute | solution.py:138
  50.0 11.6 %copy-start.7 = (bf16[8,144,128]{2,1,0:T(8,128)(2,1)}, bf16[8,144,128]{2,1,0:T(8,128)(2,1)S(1)}, u32[]{:S(2)}) copy-start(bf16[8,144,128]{2,1,0:T(8,128)(2,1)S(1)} %collective-permute-done.4.own_ref) | copy-start | bytes 884740
  50.0 28.2 %collective-permute-start.5 = (bf16[8,144,128]{2,1,0:T(8,128)(2,1)S(1)}, bf16[8,144,128]{2,1,0:T(8,128)(2,1)S(1)}, u32[]{:S(2)}, u32[]{:S(2)}) collective-permute-start(bf16[8,144,128]{2,1,0:T(8,128)(2,1)S(1)} %collective-permute-done.4.own_ref), channel_id=1, source_target_pairs={{0,1},{1,0},{2,3},{3,2},{4,5},{5,4},{6,7},{7,6},{8,9},{9,8},{10,11... | collective-permute-start | bytes 884744 | tf_op jit(solution)/shard_map/ppermute | solution.py:138
  54.7 6.8 %copy-start.17 = (bf16[8,128]{1,0:T(8,128)(2,1)}, bf16[8,128]{1,0:T(8,128)(2,1)S(1)}, u32[]{:S(2)}) copy-start(bf16[8,128]{1,0:T(8,128)(2,1)S(1)} %slice_bitcast_fusion.own_w_ref) | copy-start | bytes 6148
  54.7 6.8 %copy-start.11 = (bf16[8,144,128]{2,1,0:T(8,128)(2,1)}, bf16[8,144,128]{2,1,0:T(8,128)(2,1)S(1)}, u32[]{:S(2)}) copy-start(bf16[8,144,128]{2,1,0:T(8,128)(2,1)S(1)} %collective-permute-done.13.sib_ref) | copy-start | bytes 884740
  54.8 27.0 %collective-permute-start = (bf16[8,128]{1,0:T(8,128)(2,1)S(1)}, bf16[8,128]{1,0:T(8,128)(2,1)S(1)}, u32[]{:S(2)}, u32[]{:S(2)}) collective-permute-start(bf16[8,128]{1,0:T(8,128)(2,1)S(1)} %slice_bitcast_fusion.own_w_ref), channel_id=1, source_target_pairs={{0,1},{1,0},{2,3},{3,2},{4,5},{5,4},{6,7},{7,6},{8,9},{9,8},{10,11... | collective-permute-start | bytes 6152 | tf_op jit(solution)/shard_map/ppermute | solution.py:138
  91.6 14.4 %all-to-all-start.1 = ((bf16[16,48,384]{2,1,0:T(8,128)(2,1)}), bf16[16,48,384]{2,1,0:T(8,128)(2,1)S(1)}, u32[]{:S(2)}, u32[]{:S(2)}) async-start(bf16[16,48,384]{2,1,0:T(8,128)(2,1)} %grams.2), calls=%async_computation.1 | async-start | bytes 1179648 | tf_op jit(solution)/shard_map/all_to_all | solution.py:220
  106.1 16.0 %all-to-all-start.2 = ((bf16[16,48,384]{2,1,0:T(8,128)(2,1)}), bf16[16,48,384]{2,1,0:T(8,128)(2,1)S(1)}, u32[]{:S(2)}, u32[]{:S(2)}) async-start(bf16[16,48,384]{2,1,0:T(8,128)(2,1)} %grams.3), calls=%async_computation.2 | async-start | bytes 1179648 | tf_op jit(solution)/shard_map/all_to_all | solution.py:220
  (5 other events, 3.4 us)

commit v3 on v2

--- a/solution.py
+++ b/solution.py
@@ -10,7 +10,7 @@
 
 F32, BF16 = jnp.float32, jnp.bfloat16
 LANES = 128
-VMEM_LIMIT = 56 * 1024 * 1024
+MIB = 1024 * 1024
 
 
 def split_kernel(x_ref, triads_ref, weights_ref, out_ref):
@@ -149,7 +149,10 @@
     return lax.ppermute(array, ("z", "core"), pairs)
 
 
-PARAMS = pltpu.CompilerParams(vmem_limit_bytes=VMEM_LIMIT)
+def params(mib):
+    return pltpu.CompilerParams(vmem_limit_bytes=mib * MIB)
+
+
 BINS = jax.ShapeDtypeStruct((512, 24, 256), BF16)
 
 
@@ -163,8 +166,8 @@
         + [pl.BlockSpec(memory_space=pl.ANY)] * (len(operands) - 2),
         out_specs=pl.BlockSpec((64, 24, 256), lambda i: (turn, 0, 0)),
         input_output_aliases={} if bins is None else {2: 0},
-        compiler_params=PARAMS,
-        cost_estimate=pl.CostEstimate(flops=2000000, bytes_accessed=2000000, transcendentals=0),
+        compiler_params=params(8),
+        cost_estimate=pl.CostEstimate(flops=4000000000, bytes_accessed=2000000, transcendentals=0),
         name="unpack",
     )(*operands)
 
@@ -176,7 +179,7 @@
         in_specs=[smem()] + [vmem()] * 3,
         out_specs=vmem(),
         scratch_shapes=[pltpu.VMEM((768, 256), BF16), pltpu.VMEM((384, 256), BF16)],
-        compiler_params=PARAMS,
+        compiler_params=params(16),
         cost_estimate=pl.CostEstimate(
             flops=8000000000, bytes_accessed=8000000, transcendentals=0
         ),
@@ -191,7 +194,7 @@
         out_shape=jax.ShapeDtypeStruct((8, 152, LANES), BF16),
         in_specs=[vmem()] * 3,
         out_specs=vmem(),
-        compiler_params=PARAMS,
+        compiler_params=params(8),
         name="split",
     )(modes.reshape(48, 24, LANES), triads[:, 0], point_weights[None])
     received = lax.all_to_all(pieces, ("x", "yh"), 0, 0)

time: 133 us -> 119 us (0.89)
  Pallas kernels: 44 us -> 24.1 us
  waiting for transfers between devices: 15.4 us -> 34.6 us
  blocking collectives: 23.9 us -> 8.86 us
  local copies, waits for them, and re-layouts: 5.42 us -> 9.69 us
  starting transfers between devices: 42.1 us -> 40.1 us
    pallas_call x8, Pallas kernels: 23 us -> 7.44 us  [unpack(): pl.pallas_call(unpack_kernel, out_shape=BINS, grid=(1,), in_specs=[pl.Blo...]
    all_to_all x1 -> x0, blocking collectives: 15.5 us -> none  [body(): received = lax.all_to_all(pieces, ('x', 'yh'), 0, 0)]
    ppermute x7, waiting for transfers between devices: 3.52 us -> 15.7 us  [ring(): return lax.ppermute(array, ('z', 'core'), pairs)]
    ppermute x7, starting transfers between devices: 21.8 us -> 11.2 us  [ring(): return lax.ppermute(array, ('z', 'core'), pairs)]
    all_to_all x0 -> x1, starting transfers between devices: none -> 7.48 us  [body(): received = lax.all_to_all(pieces, ('x', 'yh'), 0, 0)]
    all_to_all x0 -> x1, waiting for transfers between devices: none -> 7.33 us  [body(): received = lax.all_to_all(pieces, ('x', 'yh'), 0, 0)]
    unnamed x39 -> x13, local copies, waits for them, and re-layouts: 4.3 us -> 8.57 us
    pallas_call x2, Pallas kernels: 18.6 us -> 15.3 us  [grams(): pl.pallas_call(functools.partial(grams_kernel, sub), out_shape=jax.ShapeD...]
  transfers between devices with their start and end apart: 18 -> 19, of which waited for: 5 -> 9; matrix products, arithmetic and copies ran while one was open for 1% -> 1% of each run, Pallas kernels for 24% -> 13%
where the time goes in v3:
time: 119 us; the launch traced here: 118 us
  starting transfers between devices  40.1 us (34%)
  waiting for transfers between devices  34.6 us (29%)
  Pallas kernels  24.1 us (20%)
  local copies, waits for them, and re-layouts  9.69 us (8%)
  blocking collectives  8.86 us (7%)
    ppermute x7, waiting for transfers between devices, ring(): return lax.ppermute(array, ('z', 'core'), pairs)  15.7 us
    pallas_call x2, Pallas kernels, grams(): pl.pallas_call(functools.partial(grams_kernel, sub), out_shape=jax.ShapeD...  15.3 us
    ppermute x9, starting transfers between devices, step(): lax.ppermute(array, axes, [(i, (i + by) % size) for i in range(size)])  12.6 us
    all_to_all x2, waiting for transfers between devices, body(): parts = lax.all_to_all(partial, ('x', 'yh', 'yl'), 0, 0)  11.5 us
    ppermute x7, starting transfers between devices, ring(): return lax.ppermute(array, ('z', 'core'), pairs)  11.2 us
    all_gather x1, blocking collectives, body(): lax.all_gather(jnp.stack(rows), ('yl', 'core')).reshape(8, 1, 16, 1152)  8.86 us
    all_to_all x2, starting transfers between devices, body(): parts = lax.all_to_all(partial, ('x', 'yh', 'yl'), 0, 0)  8.8 us
    unnamed x13, local copies, waits for them, and re-layouts  8.57 us
  transfers between devices with their start and end apart: 19, of which 9 were waited for; matrix products, arithmetic and copies ran while one was open for 1% of the time, Pallas kernels for 13%

profile of v3, /device:TPU:1, one launch (start us, length us, event | category | flops | bytes accessed | tf_op | source)
XLA Modules:
  0.0 118.0 jit_solution(17792165103517794271)
XLA Ops:
  0.0 1.0 copy-done.1
  2.3 1.3 %split.1 = bf16[8,152,128]{2,1,0:T(8,128)(2,1)} custom-call(bf16[48,24,128]{2,1,0:T(8,128)(2,1)S(1)} %bitcast.22, s32[8,16]{1,0:T(8,128)S(1)} %bitcast.23, f32[1,128]{1,0:T(1,128)S(1)} %bitcast.24), custom_call_target="tpu_custom_call" | custom-call | tf_op jit(solution)/shard_map/split/pallas_call | solution.py:192
  3.7 7.5 %all-to-all-start = ((bf16[8,152,128]{2,1,0:T(8,128)(2,1)}), bf16[8,152,128]{2,1,0:T(8,128)(2,1)S(1)}, u32[]{:S(2)}, u32[]{:S(2)}) async-start(bf16[8,152,128]{2,1,0:T(8,128)(2,1)} %split.1), calls=%async_computation | async-start | bytes 622592 | tf_op jit(solution)/shard_map/all_to_all | solution.py:200
  11.3 7.3 %all-to-all-done = bf16[8,152,128]{2,1,0:T(8,128)(2,1)S(1)} async-done(((bf16[8,152,128]{2,1,0:T(8,128)(2,1)}), bf16[8,152,128]{2,1,0:T(8,128)(2,1)S(1)}, u32[]{:S(2)}, u32[]{:S(2)}) %all-to-all-start) | async-done | bytes 311328 | tf_op jit(solution)/shard_map/all_to_all | solution.py:200
  18.6 2.6 %collective-permute-start.6 = (bf16[8,144,128]{2,1,0:T(8,128)(2,1)S(1)}, bf16[8,144,128]{2,1,0:T(8,128)(2,1)S(1)}, u32[]{:S(2)}, u32[]{:S(2)}) collective-permute-start(bf16[8,144,128]{2,1,0:T(8,128)(2,1)S(1)} %slice.42.own_ref), channel_id=1, source_target_pairs={{0,1},{1,0},{2,3},{3,2},{4,5},{5,4},{6,7},{7,6},{8,9},{9,8},{10,11... | collective-permute-start | bytes 884744 | tf_op jit(solution)/shard_map/ppermute | solution.py:138
  21.3 5.6 %collective-permute-start.1 = (bf16[8,144,128]{2,1,0:T(8,128)(2,1)S(1)}, bf16[8,144,128]{2,1,0:T(8,128)(2,1)S(1)}, u32[]{:S(2)}, u32[]{:S(2)}) collective-permute-start(bf16[8,144,128]{2,1,0:T(8,128)(2,1)S(1)} %slice.42.own_ref), channel_id=1, source_target_pairs={{0,4},{1,29},{4,8},{5,1},{8,12},{9,5},{12,16},{13,9},{16,20},{17,1... | collective-permute-start | bytes 884744 | tf_op jit(solution)/shard_map/ppermute | solution.py:149
  26.9 3.6 %collective-permute-done.1.own_ref = bf16[8,144,128]{2,1,0:T(8,128)(2,1)S(1)} collective-permute-done((bf16[8,144,128]{2,1,0:T(8,128)(2,1)S(1)}, bf16[8,144,128]{2,1,0:T(8,128)(2,1)S(1)}, u32[]{:S(2)}, u32[]{:S(2)}) %collective-permute-start.1) | collective-permute-done | bytes 294944 | tf_op jit(solution)/shard_map/ppermute | solution.py:149
  30.5 1.4 %collective-permute-start.15 = (bf16[8,144,128]{2,1,0:T(8,128)(2,1)S(1)}, bf16[8,144,128]{2,1,0:T(8,128)(2,1)S(1)}, u32[]{:S(2)}, u32[]{:S(2)}) collective-permute-start(bf16[8,144,128]{2,1,0:T(8,128)(2,1)S(1)} %collective-permute-done.1.own_ref), channel_id=1, source_target_pairs={{0,1},{1,0},{2,3},{3,2},{4,5},{5,4},{6,7},{7,6},{8,9},{9,8},{10,11... | collective-permute-start | bytes 884744 | tf_op jit(solution)/shard_map/ppermute | solution.py:138
  31.9 1.7 %collective-permute-start.2 = (bf16[8,144,128]{2,1,0:T(8,128)(2,1)S(1)}, bf16[8,144,128]{2,1,0:T(8,128)(2,1)S(1)}, u32[]{:S(2)}, u32[]{:S(2)}) collective-permute-start(bf16[8,144,128]{2,1,0:T(8,128)(2,1)S(1)} %collective-permute-done.1.own_ref), channel_id=1, source_target_pairs={{0,4},{1,29},{4,8},{5,1},{8,12},{9,5},{12,16},{13,9},{16,20},{17,1... | collective-permute-start | bytes 884744 | tf_op jit(solution)/shard_map/ppermute | solution.py:149
  35.3 5.6 %collective-permute-done.7.sib_ref = bf16[8,144,128]{2,1,0:T(8,128)(2,1)S(1)} collective-permute-done((bf16[8,144,128]{2,1,0:T(8,128)(2,1)S(1)}, bf16[8,144,128]{2,1,0:T(8,128)(2,1)S(1)}, u32[]{:S(2)}, u32[]{:S(2)}) %collective-permute-start.7) | collective-permute-done | bytes 294944 | tf_op jit(solution)/shard_map/ppermute | solution.py:149
  40.9 2.1 %collective-permute-start.14 = (bf16[8,144,128]{2,1,0:T(8,128)(2,1)S(1)}, bf16[8,144,128]{2,1,0:T(8,128)(2,1)S(1)}, u32[]{:S(2)}, u32[]{:S(2)}) collective-permute-start(bf16[8,144,128]{2,1,0:T(8,128)(2,1)S(1)} %collective-permute-done.7.sib_ref), channel_id=1, source_target_pairs={{0,1},{1,0},{2,3},{3,2},{4,5},{5,4},{6,7},{7,6},{8,9},{9,8},{10,11... | collective-permute-start | bytes 884744 | tf_op jit(solution)/shard_map/ppermute | solution.py:138
  43.0 1.0 collective-permute-start.8
  45.3 3.6 %collective-permute-done.8.sib_ref = bf16[8,144,128]{2,1,0:T(8,128)(2,1)S(1)} collective-permute-done((bf16[8,144,128]{2,1,0:T(8,128)(2,1)S(1)}, bf16[8,144,128]{2,1,0:T(8,128)(2,1)S(1)}, u32[]{:S(2)}, u32[]{:S(2)}) %collective-permute-start.8) | collective-permute-done | bytes 294944 | tf_op jit(solution)/shard_map/ppermute | solution.py:149
  48.9 2.1 %collective-permute-start.12 = (bf16[8,144,128]{2,1,0:T(8,128)(2,1)S(1)}, bf16[8,144,128]{2,1,0:T(8,128)(2,1)S(1)}, u32[]{:S(2)}, u32[]{:S(2)}) collective-permute-start(bf16[8,144,128]{2,1,0:T(8,128)(2,1)S(1)} %collective-permute-done.8.sib_ref), channel_id=1, source_target_pairs={{0,1},{1,0},{2,3},{3,2},{4,5},{5,4},{6,7},{7,6},{8,9},{9,8},{10,11... | collective-permute-start | bytes 884744 | tf_op jit(solution)/shard_map/ppermute | solution.py:138
  50.9 1.1 collective-permute-done.3.own_ref
  52.0 1.9 %collective-permute-start.4 = (bf16[8,144,128]{2,1,0:T(8,128)(2,1)S(1)}, bf16[8,144,128]{2,1,0:T(8,128)(2,1)S(1)}, u32[]{:S(2)}, u32[]{:S(2)}) collective-permute-start(bf16[8,144,128]{2,1,0:T(8,128)(2,1)S(1)} %collective-permute-done.3.own_ref), channel_id=1, source_target_pairs={{0,4},{1,29},{4,8},{5,1},{8,12},{9,5},{12,16},{13,9},{16,20},{17,1... | collective-permute-start | bytes 884744 | tf_op jit(solution)/shard_map/ppermute | solution.py:149
  54.9 0.9 unpack.11.refs_0_
  56.8 2.1 %collective-permute-start.10 = (bf16[8,144,128]{2,1,0:T(8,128)(2,1)S(1)}, bf16[8,144,128]{2,1,0:T(8,128)(2,1)S(1)}, u32[]{:S(2)}, u32[]{:S(2)}) collective-permute-start(bf16[8,144,128]{2,1,0:T(8,128)(2,1)S(1)} %collective-permute-done.9.sib_ref), channel_id=1, source_target_pairs={{0,1},{1,0},{2,3},{3,2},{4,5},{5,4},{6,7},{7,6},{8,9},{9,8},{10,11... | collective-permute-start | bytes 884744 | tf_op jit(solution)/shard_map/ppermute | solution.py:138
  58.9 1.1 collective-permute-done.4.own_ref
  60.0 2.1 %collective-permute-start.5 = (bf16[8,144,128]{2,1,0:T(8,128)(2,1)S(1)}, bf16[8,144,128]{2,1,0:T(8,128)(2,1)S(1)}, u32[]{:S(2)}, u32[]{:S(2)}) collective-permute-start(bf16[8,144,128]{2,1,0:T(8,128)(2,1)S(1)} %collective-permute-done.4.own_ref), channel_id=1, source_target_pairs={{0,1},{1,0},{2,3},{3,2},{4,5},{5,4},{6,7},{7,6},{8,9},{9,8},{10,11... | collective-permute-start | bytes 884744 | tf_op jit(solution)/shard_map/ppermute | solution.py:138
  63.0 0.9 unpack.13.refs_0_
  63.9 0.9 unpack.14.refs_0_
  64.9 0.9 unpack.15.bins_ref
  65.8 7.7 %grams.2 = bf16[16,48,384]{2,1,0:T(8,128)(2,1)} custom-call(s32[64,16]{1,0:T(8,128)S(1)} %fusion.1.triads_ref, bf16[8,128]{1,0:T(8,128)(2,1)S(1)} %slice_bitcast_fusion.own_w_ref, bf16[8,128]{1,0:T(8,128)(2,1)S(1)} %collective-permute-done.sib_w_ref, bf16[512,24,256]{2,1,0:T(8,128)(2,1)S(1)} %unpack.15.bins_ref), custom_call_target="tpu_custom_call" | custom-call | flops 8000000000 | bytes 8000000 | tf_op jit(solution)/shard_map/grams/pallas_call | solution.py:176
  73.5 2.7 %copy-done.4 = bf16[512,24,256]{2,1,0:T(8,128)(2,1)} copy-done((bf16[512,24,256]{2,1,0:T(8,128)(2,1)}, bf16[512,24,256]{2,1,0:T(8,128)(2,1)S(1)}, u32[]{:S(2)}) %copy-start.4) | copy-done | bytes 6291480
  76.2 3.6 %all-to-all-start.1 = ((bf16[16,48,384]{2,1,0:T(8,128)(2,1)}), bf16[16,48,384]{2,1,0:T(8,128)(2,1)S(1)}, u32[]{:S(2)}, u32[]{:S(2)}) async-start(bf16[16,48,384]{2,1,0:T(8,128)(2,1)} %grams.2), calls=%async_computation.1 | async-start | bytes 1179648 | tf_op jit(solution)/shard_map/all_to_all | solution.py:223
  79.8 2.8 %copy-done.5 = bf16[512,24,256]{2,1,0:T(8,128)(2,1)S(1)} copy-done((bf16[512,24,256]{2,1,0:T(8,128)(2,1)S(1)}, bf16[512,24,256]{2,1,0:T(8,128)(2,1)}, u32[]{:S(2)}) %copy-start.5) | copy-done | bytes 6291480
  82.5 7.7 %grams.3 = bf16[16,48,384]{2,1,0:T(8,128)(2,1)} custom-call(s32[64,16]{1,0:T(8,128)S(1)} %fusion.1.triads_ref, bf16[8,128]{1,0:T(8,128)(2,1)S(1)} %slice_bitcast_fusion.own_w_ref, bf16[8,128]{1,0:T(8,128)(2,1)S(1)} %collective-permute-done.sib_w_ref, bf16[512,24,256]{2,1,0:T(8,128)(2,1)S(1)} %copy-done.5), custom_call_target="tpu_custom_call" | custom-call | flops 8000000000 | bytes 8000000 | tf_op jit(solution)/shard_map/grams/pallas_call | solution.py:176
  90.2 1.4 %all-to-all-done.1 = bf16[16,48,384]{2,1,0:T(8,128)(2,1)S(1)} async-done(((bf16[16,48,384]{2,1,0:T(8,128)(2,1)}), bf16[16,48,384]{2,1,0:T(8,128)(2,1)S(1)}, u32[]{:S(2)}, u32[]{:S(2)}) %all-to-all-start.1) | async-done | bytes 589856 | tf_op jit(solution)/shard_map/all_to_all | solution.py:223
  91.6 5.2 %all-to-all-start.2 = ((bf16[16,48,384]{2,1,0:T(8,128)(2,1)}), bf16[16,48,384]{2,1,0:T(8,128)(2,1)S(1)}, u32[]{:S(2)}, u32[]{:S(2)}) async-start(bf16[16,48,384]{2,1,0:T(8,128)(2,1)} %grams.3), calls=%async_computation.2 | async-start | bytes 1179648 | tf_op jit(solution)/shard_map/all_to_all | solution.py:223
  97.4 10.2 %all-to-all-done.2 = bf16[16,48,384]{2,1,0:T(8,128)(2,1)S(1)} async-done(((bf16[16,48,384]{2,1,0:T(8,128)(2,1)}), bf16[16,48,384]{2,1,0:T(8,128)(2,1)S(1)}, u32[]{:S(2)}, u32[]{:S(2)}) %all-to-all-start.2) | async-done | bytes 589856 | tf_op jit(solution)/shard_map/all_to_all | solution.py:223
  108.3 8.9 %all-gather = f32[8,16,1152]{2,1,0:T(8,128)S(1)} all-gather(f32[2,16,1152]{2,1,0:T(8,128)S(1)} %pad_maximum_fusion), channel_id=2, replica_groups=mesh['x'=4,'yh'=2,'z'=8,'yl'=2,'core'=2] {'yl','core'}, dimensions={0}, use_global_device_ids=true | all-gather | bytes 737280 | tf_op jit(solution)/shard_map/all_gather | solution.py:227
  (50 shorter events, 9.5 us)
Async XLA Ops:
  0.0 11.1 %copy-start = (s32[8,1]{0,1:T(1,128)S(1)}, s32[8,1]{0,1:T(1,128)}, u32[]{:S(2)}) copy-start(s32[8,1]{0,1:T(1,128)} %param.7) | copy-start | bytes 100
  0.0 1.0 copy-start.1
  1.0 0.7 copy-start.2
  1.7 0.7 copy-start.3
  3.7 15.0 %all-to-all-start = ((bf16[8,152,128]{2,1,0:T(8,128)(2,1)}), bf16[8,152,128]{2,1,0:T(8,128)(2,1)S(1)}, u32[]{:S(2)}, u32[]{:S(2)}) async-start(bf16[8,152,128]{2,1,0:T(8,128)(2,1)} %split.1), calls=%async_computation | async-start | bytes 622592 | tf_op jit(solution)/shard_map/all_to_all | solution.py:200
  18.6 15.0 %collective-permute-start.6 = (bf16[8,144,128]{2,1,0:T(8,128)(2,1)S(1)}, bf16[8,144,128]{2,1,0:T(8,128)(2,1)S(1)}, u32[]{:S(2)}, u32[]{:S(2)}) collective-permute-start(bf16[8,144,128]{2,1,0:T(8,128)(2,1)S(1)} %slice.42.own_ref), channel_id=1, source_target_pairs={{0,1},{1,0},{2,3},{3,2},{4,5},{5,4},{6,7},{7,6},{8,9},{9,8},{10,11... | collective-permute-start | bytes 884744 | tf_op jit(solution)/shard_map/ppermute | solution.py:138
  21.3 9.2 %collective-permute-start.1 = (bf16[8,144,128]{2,1,0:T(8,128)(2,1)S(1)}, bf16[8,144,128]{2,1,0:T(8,128)(2,1)S(1)}, u32[]{:S(2)}, u32[]{:S(2)}) collective-permute-start(bf16[8,144,128]{2,1,0:T(8,128)(2,1)S(1)} %slice.42.own_ref), channel_id=1, source_target_pairs={{0,4},{1,29},{4,8},{5,1},{8,12},{9,5},{12,16},{13,9},{16,20},{17,1... | collective-permute-start | bytes 884744 | tf_op jit(solution)/shard_map/ppermute | solution.py:149
  26.8 39.0 %collective-permute-start = (bf16[8,128]{1,0:T(8,128)(2,1)S(1)}, bf16[8,128]{1,0:T(8,128)(2,1)S(1)}, u32[]{:S(2)}, u32[]{:S(2)}) collective-permute-start(bf16[8,128]{1,0:T(8,128)(2,1)S(1)} %slice_bitcast_fusion.own_w_ref), channel_id=1, source_target_pairs={{0,1},{1,0},{2,3},{3,2},{4,5},{5,4},{6,7},{7,6},{8,9},{9,8},{10,11... | collective-permute-start | bytes 6152 | tf_op jit(solution)/shard_map/ppermute | solution.py:138
  30.5 14.7 %collective-permute-start.15 = (bf16[8,144,128]{2,1,0:T(8,128)(2,1)S(1)}, bf16[8,144,128]{2,1,0:T(8,128)(2,1)S(1)}, u32[]{:S(2)}, u32[]{:S(2)}) collective-permute-start(bf16[8,144,128]{2,1,0:T(8,128)(2,1)S(1)} %collective-permute-done.1.own_ref), channel_id=1, source_target_pairs={{0,1},{1,0},{2,3},{3,2},{4,5},{5,4},{6,7},{7,6},{8,9},{9,8},{10,11... | collective-permute-start | bytes 884744 | tf_op jit(solution)/shard_map/ppermute | solution.py:138
  31.9 12.1 %collective-permute-start.2 = (bf16[8,144,128]{2,1,0:T(8,128)(2,1)S(1)}, bf16[8,144,128]{2,1,0:T(8,128)(2,1)S(1)}, u32[]{:S(2)}, u32[]{:S(2)}) collective-permute-start(bf16[8,144,128]{2,1,0:T(8,128)(2,1)S(1)} %collective-permute-done.1.own_ref), channel_id=1, source_target_pairs={{0,4},{1,29},{4,8},{5,1},{8,12},{9,5},{12,16},{13,9},{16,20},{17,1... | collective-permute-start | bytes 884744 | tf_op jit(solution)/shard_map/ppermute | solution.py:149
  33.6 7.3 %collective-permute-start.7 = (bf16[8,144,128]{2,1,0:T(8,128)(2,1)S(1)}, bf16[8,144,128]{2,1,0:T(8,128)(2,1)S(1)}, u32[]{:S(2)}, u32[]{:S(2)}) collective-permute-start(bf16[8,144,128]{2,1,0:T(8,128)(2,1)S(1)} %collective-permute-done.6.sib_ref), channel_id=1, source_target_pairs={{0,4},{1,29},{4,8},{5,1},{8,12},{9,5},{12,16},{13,9},{16,20},{17,1... | collective-permute-start | bytes 884744 | tf_op jit(solution)/shard_map/ppermute | solution.py:149
  40.9 10.0 %collective-permute-start.14 = (bf16[8,144,128]{2,1,0:T(8,128)(2,1)S(1)}, bf16[8,144,128]{2,1,0:T(8,128)(2,1)S(1)}, u32[]{:S(2)}, u32[]{:S(2)}) collective-permute-start(bf16[8,144,128]{2,1,0:T(8,128)(2,1)S(1)} %collective-permute-done.7.sib_ref), channel_id=1, source_target_pairs={{0,1},{1,0},{2,3},{3,2},{4,5},{5,4},{6,7},{7,6},{8,9},{9,8},{10,11... | collective-permute-start | bytes 884744 | tf_op jit(solution)/shard_map/ppermute | solution.py:138
  43.0 5.9 %collective-permute-start.8 = (bf16[8,144,128]{2,1,0:T(8,128)(2,1)S(1)}, bf16[8,144,128]{2,1,0:T(8,128)(2,1)S(1)}, u32[]{:S(2)}, u32[]{:S(2)}) collective-permute-start(bf16[8,144,128]{2,1,0:T(8,128)(2,1)S(1)} %collective-permute-done.7.sib_ref), channel_id=1, source_target_pairs={{0,4},{1,29},{4,8},{5,1},{8,12},{9,5},{12,16},{13,9},{16,20},{17,1... | collective-permute-start | bytes 884744 | tf_op jit(solution)/shard_map/ppermute | solution.py:149
  44.0 8.0 %collective-permute-start.3 = (bf16[8,144,128]{2,1,0:T(8,128)(2,1)S(1)}, bf16[8,144,128]{2,1,0:T(8,128)(2,1)S(1)}, u32[]{:S(2)}, u32[]{:S(2)}) collective-permute-start(bf16[8,144,128]{2,1,0:T(8,128)(2,1)S(1)} %collective-permute-done.2.own_ref), channel_id=1, source_target_pairs={{0,4},{1,29},{4,8},{5,1},{8,12},{9,5},{12,16},{13,9},{16,20},{17,1... | collective-permute-start | bytes 884744 | tf_op jit(solution)/shard_map/ppermute | solution.py:149
  45.2 10.6 %collective-permute-start.13 = (bf16[8,144,128]{2,1,0:T(8,128)(2,1)S(1)}, bf16[8,144,128]{2,1,0:T(8,128)(2,1)S(1)}, u32[]{:S(2)}, u32[]{:S(2)}) collective-permute-start(bf16[8,144,128]{2,1,0:T(8,128)(2,1)S(1)} %collective-permute-done.2.own_ref), channel_id=1, source_target_pairs={{0,1},{1,0},{2,3},{3,2},{4,5},{5,4},{6,7},{7,6},{8,9},{9,8},{10,11... | collective-permute-start | bytes 884744 | tf_op jit(solution)/shard_map/ppermute | solution.py:138
  48.9 13.2 %collective-permute-start.12 = (bf16[8,144,128]{2,1,0:T(8,128)(2,1)S(1)}, bf16[8,144,128]{2,1,0:T(8,128)(2,1)S(1)}, u32[]{:S(2)}, u32[]{:S(2)}) collective-permute-start(bf16[8,144,128]{2,1,0:T(8,128)(2,1)S(1)} %collective-permute-done.8.sib_ref), channel_id=1, source_target_pairs={{0,1},{1,0},{2,3},{3,2},{4,5},{5,4},{6,7},{7,6},{8,9},{9,8},{10,11... | collective-permute-start | bytes 884744 | tf_op jit(solution)/shard_map/ppermute | solution.py:138
  50.9 5.9 %collective-permute-start.9 = (bf16[8,144,128]{2,1,0:T(8,128)(2,1)S(1)}, bf16[8,144,128]{2,1,0:T(8,128)(2,1)S(1)}, u32[]{:S(2)}, u32[]{:S(2)}) collective-permute-start(bf16[8,144,128]{2,1,0:T(8,128)(2,1)S(1)} %collective-permute-done.8.sib_ref), channel_id=1, source_target_pairs={{0,4},{1,29},{4,8},{5,1},{8,12},{9,5},{12,16},{13,9},{16,20},{17,1... | collective-permute-start | bytes 884744 | tf_op jit(solution)/shard_map/ppermute | solution.py:149
  52.0 7.9 %collective-permute-start.4 = (bf16[8,144,128]{2,1,0:T(8,128)(2,1)S(1)}, bf16[8,144,128]{2,1,0:T(8,128)(2,1)S(1)}, u32[]{:S(2)}, u32[]{:S(2)}) collective-permute-start(bf16[8,144,128]{2,1,0:T(8,128)(2,1)S(1)} %collective-permute-done.3.own_ref), channel_id=1, source_target_pairs={{0,4},{1,29},{4,8},{5,1},{8,12},{9,5},{12,16},{13,9},{16,20},{17,1... | collective-permute-start | bytes 884744 | tf_op jit(solution)/shard_map/ppermute | solution.py:149
  55.8 8.1 %collective-permute-start.11 = (bf16[8,144,128]{2,1,0:T(8,128)(2,1)S(1)}, bf16[8,144,128]{2,1,0:T(8,128)(2,1)S(1)}, u32[]{:S(2)}, u32[]{:S(2)}) collective-permute-start(bf16[8,144,128]{2,1,0:T(8,128)(2,1)S(1)} %collective-permute-done.3.own_ref), channel_id=1, source_target_pairs={{0,1},{1,0},{2,3},{3,2},{4,5},{5,4},{6,7},{7,6},{8,9},{9,8},{10,11... | collective-permute-start | bytes 884744 | tf_op jit(solution)/shard_map/ppermute | solution.py:138
  56.8 7.1 %collective-permute-start.10 = (bf16[8,144,128]{2,1,0:T(8,128)(2,1)S(1)}, bf16[8,144,128]{2,1,0:T(8,128)(2,1)S(1)}, u32[]{:S(2)}, u32[]{:S(2)}) collective-permute-start(bf16[8,144,128]{2,1,0:T(8,128)(2,1)S(1)} %collective-permute-done.9.sib_ref), channel_id=1, source_target_pairs={{0,1},{1,0},{2,3},{3,2},{4,5},{5,4},{6,7},{7,6},{8,9},{9,8},{10,11... | collective-permute-start | bytes 884744 | tf_op jit(solution)/shard_map/ppermute | solution.py:138
  60.0 4.9 %collective-permute-start.5 = (bf16[8,144,128]{2,1,0:T(8,128)(2,1)S(1)}, bf16[8,144,128]{2,1,0:T(8,128)(2,1)S(1)}, u32[]{:S(2)}, u32[]{:S(2)}) collective-permute-start(bf16[8,144,128]{2,1,0:T(8,128)(2,1)S(1)} %collective-permute-done.4.own_ref), channel_id=1, source_target_pairs={{0,1},{1,0},{2,3},{3,2},{4,5},{5,4},{6,7},{7,6},{8,9},{9,8},{10,11... | collective-permute-start | bytes 884744 | tf_op jit(solution)/shard_map/ppermute | solution.py:138
  73.5 2.7 %copy-start.4 = (bf16[512,24,256]{2,1,0:T(8,128)(2,1)}, bf16[512,24,256]{2,1,0:T(8,128)(2,1)S(1)}, u32[]{:S(2)}) copy-start(bf16[512,24,256]{2,1,0:T(8,128)(2,1)S(1)} %unpack.15.bins_ref) | copy-start | bytes 18874372
  76.2 15.4 %all-to-all-start.1 = ((bf16[16,48,384]{2,1,0:T(8,128)(2,1)}), bf16[16,48,384]{2,1,0:T(8,128)(2,1)S(1)}, u32[]{:S(2)}, u32[]{:S(2)}) async-start(bf16[16,48,384]{2,1,0:T(8,128)(2,1)} %grams.2), calls=%async_computation.1 | async-start | bytes 1179648 | tf_op jit(solution)/shard_map/all_to_all | solution.py:223
  79.8 2.8 %copy-start.5 = (bf16[512,24,256]{2,1,0:T(8,128)(2,1)S(1)}, bf16[512,24,256]{2,1,0:T(8,128)(2,1)}, u32[]{:S(2)}) copy-start(bf16[512,24,256]{2,1,0:T(8,128)(2,1)} %copy-done.4) | copy-start | bytes 18874372
  91.6 16.0 %all-to-all-start.2 = ((bf16[16,48,384]{2,1,0:T(8,128)(2,1)}), bf16[16,48,384]{2,1,0:T(8,128)(2,1)S(1)}, u32[]{:S(2)}, u32[]{:S(2)}) async-start(bf16[16,48,384]{2,1,0:T(8,128)(2,1)} %grams.3), calls=%async_computation.2 | async-start | bytes 1179648 | tf_op jit(solution)/shard_map/all_to_all | solution.py:223

commit v4 on v3

--- a/solution.py
+++ b/solution.py
@@ -1,5 +1,3 @@
-import functools
-
 import jax
 import jax.numpy as jnp
 from jax import lax
@@ -77,8 +75,8 @@
     return total[0:1]
 
 
-def grams_kernel(sub, triads_ref, own_w_ref, sib_w_ref, bins_ref, out_ref, w_ref, q_ref):
-    place = lax.axis_index("x") * 2 + lax.axis_index("yh")
+def grams_kernel(triads_ref, own_w_ref, sib_w_ref, bins_ref, out_ref, *scratch):
+    buffers = (scratch[0:2], scratch[2:4])
     depth, core = lax.axis_index("z"), lax.axis_index("core")
     up = 1 - 2 * core
 
@@ -89,40 +87,61 @@
     weights = lane_weights(own_w_ref, sib_w_ref)
     lane = lax.broadcasted_iota(jnp.int32, (48, LANES), 1)
 
-    @pl.loop(0, 16)
-    def _(reader):
-        owner = reader >> 1
-        row = (reader & 1) * 4 + core * 2 + sub
+    def prepare(reader, buffer):
+        w_ref, q_ref = buffer
+        owner = reader >> 2
+        row = (reader & 2) * 2 + core * 2 + (reader & 1)
         k_bin = row * 64 + owner * 8 + depth
         first = bins_ref[owner * 8 + row].astype(F32)
         k_real = first[:, :LANES] * weights
         k_imag = first[:, LANES:] * weights
-        for t in range(16):
-            l_bin = triads_ref[owner * 8 + row, t]
-            m_bin = (k_bin + l_bin) & 511
-            second = bins_ref[slot(l_bin)].astype(F32)
-            l_real, l_imag = second[:, :LANES], second[:, LANES:]
-            real = (k_real * l_real - k_imag * l_imag).astype(BF16)
-            imag = k_real * l_imag + k_imag * l_real
-            plus, minus = imag.astype(BF16), (-imag).astype(BF16)
-            w_ref[48 * t : 48 * t + 24, :LANES] = real
-            w_ref[48 * t : 48 * t + 24, LANES:] = plus
-            w_ref[48 * t + 24 : 48 * t + 48, :LANES] = minus
-            w_ref[48 * t + 24 : 48 * t + 48, LANES:] = real
-            q_ref[24 * t : 24 * t + 24, :] = bins_ref[slot(m_bin)]
-        for n in range(3):
-            start = 5 * n
-            product = lax.dot_general(
-                w_ref[48 * start : 48 * (start + 6), :],
-                q_ref[LANES * n : LANES * (n + 1), :],
-                (((1,), (1,)), ((), ())),
-                preferred_element_type=F32,
-            )
-            built = product[:48]
-            for i in range(1, 6):
-                begin = 24 * (start + i) - LANES * n
-                built = jnp.where(lane >= begin, product[48 * i : 48 * (i + 1)], built)
-            out_ref[reader, :, LANES * n : LANES * (n + 1)] = built.astype(BF16)
+
+        def some(triads):
+            for t in triads:
+                l_bin = triads_ref[owner * 8 + row, t]
+                m_bin = (k_bin + l_bin) & 511
+                second = bins_ref[slot(l_bin)].astype(F32)
+                l_real, l_imag = second[:, :LANES], second[:, LANES:]
+                real = (k_real * l_real - k_imag * l_imag).astype(BF16)
+                imag = k_real * l_imag + k_imag * l_real
+                plus, minus = imag.astype(BF16), (-imag).astype(BF16)
+                w_ref[48 * t : 48 * t + 24, :LANES] = real
+                w_ref[48 * t : 48 * t + 24, LANES:] = plus
+                w_ref[48 * t + 24 : 48 * t + 48, :LANES] = minus
+                w_ref[48 * t + 24 : 48 * t + 48, LANES:] = real
+                q_ref[24 * t : 24 * t + 24, :] = bins_ref[slot(m_bin)]
+
+        return some
+
+    def multiply(reader, buffer, n):
+        w_ref, q_ref = buffer
+        start = 5 * n
+        product = lax.dot_general(
+            w_ref[48 * start : 48 * (start + 6), :],
+            q_ref[LANES * n : LANES * (n + 1), :],
+            (((1,), (1,)), ((), ())),
+            preferred_element_type=F32,
+        )
+        built = product[:48]
+        for i in range(1, 6):
+            begin = 24 * (start + i) - LANES * n
+            built = jnp.where(lane >= begin, product[48 * i : 48 * (i + 1)], built)
+        lanes = slice(LANES * n, LANES * (n + 1))
+        out_ref[reader >> 1, reader & 1, :, lanes] = built.astype(BF16)
+
+    thirds = (range(0, 5), range(5, 10), range(10, 16))
+    ready = prepare(0, buffers[0])
+    for third in thirds:
+        ready(third)
+
+    @pl.loop(0, 16)
+    def _(pair):
+        for side in range(2):
+            reader = 2 * pair + side
+            following = prepare((reader + 1) & 31, buffers[1 - side])
+            for n, third in enumerate(thirds):
+                multiply(reader, buffers[side], n)
+                following(third)
 
 
 def vmem():
@@ -142,10 +161,11 @@
     return step(array, "core", 1)
 
 
-def ring(array):
+def ring(array, crossed=False):
     pairs = []
     for z in range(8):
-        pairs += [(2 * z, (2 * z + 2) % 16), (2 * z + 1, (2 * z - 2) % 16 + 1)]
+        up, down = (2 * z + 2) % 16, (2 * z - 2) % 16 + 1
+        pairs += [(2 * z, down), (2 * z + 1, up)] if crossed else [(2 * z, up), (2 * z + 1, down)]
     return lax.ppermute(array, ("z", "core"), pairs)
 
 
@@ -167,21 +187,21 @@
         out_specs=pl.BlockSpec((64, 24, 256), lambda i: (turn, 0, 0)),
         input_output_aliases={} if bins is None else {2: 0},
         compiler_params=params(8),
-        cost_estimate=pl.CostEstimate(flops=4000000000, bytes_accessed=2000000, transcendentals=0),
+        cost_estimate=pl.CostEstimate(flops=1500000000, bytes_accessed=2000000, transcendentals=0),
         name="unpack",
     )(*operands)
 
 
-def grams(sub, lists, own_tile, sib_tile, bins):
+def grams(lists, own_tile, sib_tile, bins):
     return pl.pallas_call(
-        functools.partial(grams_kernel, sub),
-        out_shape=jax.ShapeDtypeStruct((16, 48, 384), BF16),
+        grams_kernel,
+        out_shape=jax.ShapeDtypeStruct((16, 2, 48, 384), BF16),
         in_specs=[smem()] + [vmem()] * 3,
         out_specs=vmem(),
-        scratch_shapes=[pltpu.VMEM((768, 256), BF16), pltpu.VMEM((384, 256), BF16)],
-        compiler_params=params(16),
+        scratch_shapes=[pltpu.VMEM((768, 256), BF16), pltpu.VMEM((384, 256), BF16)] * 2,
+        compiler_params=params(12),
         cost_estimate=pl.CostEstimate(
-            flops=8000000000, bytes_accessed=8000000, transcendentals=0
+            flops=12000000000, bytes_accessed=8000000, transcendentals=0
         ),
         name="grams",
     )(lists, own_tile, sib_tile, bins)
@@ -194,37 +214,39 @@
         out_shape=jax.ShapeDtypeStruct((8, 152, LANES), BF16),
         in_specs=[vmem()] * 3,
         out_specs=vmem(),
-        compiler_params=params(8),
+        compiler_params=params(56),
         name="split",
     )(modes.reshape(48, 24, LANES), triads[:, 0], point_weights[None])
     received = lax.all_to_all(pieces, ("x", "yh"), 0, 0)
-    tiles = received[:, 144:]
-    codes = tiles[:, :, :32].astype(F32)
+    codes = received[:, 144:, :32].astype(F32)
     lists = (codes[:, :, :16] * 64 + codes[:, :, 16:]).astype(jnp.int32).reshape(64, 16)
 
-    near = [received[:, :144]]
-    sib = [swap(near[0])]
-    own_tile, sib_tile = tiles[0], swap(tiles[0])
-    for _ in range(3):
+    beside = swap(received)
+    near, sib = [received[:, :144]], [beside[:, :144]]
+    near.append(ring(near[0]))
+    sib.append(ring(near[0], crossed=True))
+    for _ in range(2):
         near.append(ring(near[-1]))
         sib.append(ring(sib[-1]))
     near.append(ring(near[-1]))
     bins = unpack(near[0], sib[0], None, 0)
-    for s in range(1, 4):
-        bins = unpack(near[s], sib[s], bins, s)
-        bins = unpack(swap(sib[s]), swap(near[s]), bins, 8 - s)
+    passed = [(swap(sib[s]), swap(near[s])) for s in range(1, 4)]
+    bins = unpack(near[1], sib[1], bins, 1)
+    bins = unpack(*passed[0], bins, 7)
+    bins = unpack(near[2], sib[2], bins, 2)
+    bins = unpack(near[3], sib[3], bins, 3)
+    bins = unpack(*passed[1], bins, 6)
+    bins = unpack(*passed[2], bins, 5)
     bins = unpack(near[4], swap(near[4]), bins, 4)
 
     live = lax.dynamic_slice_in_dim(counts[:, 0], 4 * half + 2 * core, 2)
     mask = (jnp.arange(16, dtype=jnp.int32)[None, :] < live[:, None]).astype(F32)
-    rows = []
-    for sub in range(2):
-        partial = grams(sub, lists, own_tile, sib_tile, bins)
-        parts = lax.all_to_all(partial, ("x", "yh", "yl"), 0, 0)
-        summed = jnp.sum(parts.astype(F32), axis=0) / 24
-        flat = summed.reshape(48, 16, 24).transpose(1, 0, 2).reshape(16, 1152)
-        rows.append(flat * mask[sub][:, None])
-    return lax.all_gather(jnp.stack(rows), ("yl", "core")).reshape(8, 1, 16, 1152)
+    partial = grams(lists, received[0, 144:], beside[0, 144:], bins)
+    parts = lax.all_to_all(partial, ("x", "yh", "yl"), 0, 0)
+    summed = jnp.sum(parts.astype(F32), axis=0) / 24
+    rows = summed.reshape(2, 48, 16, 24).transpose(0, 2, 1, 3).reshape(2, 16, 1152)
+    rows = rows * mask[:, :, None]
+    return lax.all_gather(rows, ("yl", "core")).reshape(8, 1, 16, 1152)
 
 
 def solution(mesh):

time: 119 us -> 103 us (0.87)
  blocking collectives: 8.86 us -> 23.2 us
  waiting for transfers between devices: 34.6 us -> 25.6 us
  local copies, waits for them, and re-layouts: 9.69 us -> 1.76 us
  starting transfers between devices: 40.1 us -> 32.2 us
  Pallas kernels: 24.1 us -> 19.7 us
    all_to_all x0 -> x1, blocking collectives: none -> 15.5 us  [body(): received = lax.all_to_all(pieces, ('x', 'yh'), 0, 0)]
    ppermute x7, waiting for transfers between devices: 15.7 us -> 6.19 us  [ring(): return lax.ppermute(array, ('z', 'core'), pairs)]
    ppermute x7, starting transfers between devices: 11.2 us -> 19.1 us  [ring(): return lax.ppermute(array, ('z', 'core'), pairs)]
    all_to_all x2 -> x1, waiting for transfers between devices: 11.5 us -> 19.4 us  [body(): parts = lax.all_to_all(partial, ('x', 'yh', 'yl'), 0, 0)]
    unnamed x13 -> x3, local copies, waits for them, and re-layouts: 8.57 us -> 0.82 us
    all_to_all x1 -> x0, starting transfers between devices: 7.48 us -> none  [body(): received = lax.all_to_all(pieces, ('x', 'yh'), 0, 0)]
    all_to_all x1 -> x0, waiting for transfers between devices: 7.33 us -> none  [body(): received = lax.all_to_all(pieces, ('x', 'yh'), 0, 0)]
    pallas_call x2 -> x1, Pallas kernels: 15.3 us -> 9.95 us  [grams(): pl.pallas_call(grams_kernel, out_shape=jax.ShapeDtypeStruct((16, 2, 48, 3...]
  transfers between devices with their start and end apart: 19 -> 16, of which waited for: 9 -> 3; matrix products, arithmetic and copies ran while one was open for 1% -> 0% of each run, Pallas kernels for 13% -> 6%
where the time goes in v4:
time: 103 us
  starting transfers between devices  32.2 us (31%)
  waiting for transfers between devices  25.6 us (25%)
  blocking collectives  23.2 us (23%)
  Pallas kernels  19.7 us (19%)
  local copies, waits for them, and re-layouts  1.76 us (2%)
    all_to_all x1, waiting for transfers between devices, body(): parts = lax.all_to_all(partial, ('x', 'yh', 'yl'), 0, 0)  19.4 us
    ppermute x7, starting transfers between devices, ring(): return lax.ppermute(array, ('z', 'core'), pairs)  19.1 us
    all_to_all x1, blocking collectives, body(): received = lax.all_to_all(pieces, ('x', 'yh'), 0, 0)  15.5 us
    pallas_call x1, Pallas kernels, grams(): pl.pallas_call(grams_kernel, out_shape=jax.ShapeDtypeStruct((16, 2, 48, 3...  9.95 us
    ppermute x8, starting transfers between devices, step(): lax.ppermute(array, axes, [(i, (i + by) % size) for i in range(size)])  9.43 us
    all_gather x1, blocking collectives, body(): return lax.all_gather(rows, ('yl', 'core')).reshape(8, 1, 16, 1152)  7.65 us
    pallas_call x8, Pallas kernels, unpack(): pl.pallas_call(unpack_kernel, out_shape=BINS, grid=(1,), in_specs=[pl.Blo...  7.45 us
    ppermute x7, waiting for transfers between devices, ring(): return lax.ppermute(array, ('z', 'core'), pairs)  6.19 us
  transfers between devices with their start and end apart: 16, of which 3 were waited for; matrix products, arithmetic and copies ran while one was open for 0% of the time, Pallas kernels for 6%

profile of v4, /device:TPU:1, one launch (start us, length us, event | category | flops | bytes accessed | tf_op | source)
XLA Modules:
  0.0 103.1 jit_solution(16407319041759738335)
XLA Ops:
  0.0 2.3 %split.1 = bf16[8,152,128]{2,1,0:T(8,128)(2,1)} custom-call(bf16[48,24,128]{2,1,0:T(8,128)(2,1)} %bitcast.21, s32[8,16]{1,0:T(8,128)} %bitcast.22, f32[1,128]{1,0:T(1,128)} %bitcast.23), custom_call_target="tpu_custom_call" | custom-call | tf_op jit(solution)/shard_map/split/pallas_call | solution.py:212
  2.3 15.5 %all_to_all.10 = bf16[8,152,128]{2,1,0:T(8,128)(2,1)S(1)} all-to-all(bf16[8,152,128]{2,1,0:T(8,128)(2,1)} %split.1), channel_id=1, replica_groups=mesh['x'=4,'yh'=2,'z'=8,'yl'=2,'core'=2] {'x','yh'}, dimensions={0} | all-to-all | bytes 622592 | tf_op jit(solution)/shard_map/all_to_all | solution.py:220
  17.9 5.7 %collective-permute-start.1 = (bf16[8,144,128]{2,1,0:T(8,128)(2,1)S(1)}, bf16[8,144,128]{2,1,0:T(8,128)(2,1)S(1)}, u32[]{:S(2)}, u32[]{:S(2)}) collective-permute-start(bf16[8,144,128]{2,1,0:T(8,128)(2,1)S(1)} %slice.33.own_ref), channel_id=1, source_target_pairs={{0,4},{1,29},{4,8},{5,1},{8,12},{9,5},{12,16},{13,9},{16,20},{17,1... | collective-permute-start | bytes 884744 | tf_op jit(solution)/shard_map/ppermute | solution.py:169
  23.5 0.2 collective-permute-start.6
  23.7 0.9 collective-permute-start
  24.6 4.4 %collective-permute-done.1.own_ref = bf16[8,144,128]{2,1,0:T(8,128)(2,1)S(1)} collective-permute-done((bf16[8,144,128]{2,1,0:T(8,128)(2,1)S(1)}, bf16[8,144,128]{2,1,0:T(8,128)(2,1)S(1)}, u32[]{:S(2)}, u32[]{:S(2)}) %collective-permute-start.1) | collective-permute-done | bytes 294944 | tf_op jit(solution)/shard_map/ppermute | solution.py:169
  29.0 3.1 %collective-permute-start.2 = (bf16[8,144,128]{2,1,0:T(8,128)(2,1)S(1)}, bf16[8,144,128]{2,1,0:T(8,128)(2,1)S(1)}, u32[]{:S(2)}, u32[]{:S(2)}) collective-permute-start(bf16[8,144,128]{2,1,0:T(8,128)(2,1)S(1)} %collective-permute-done.1.own_ref), channel_id=1, source_target_pairs={{0,4},{1,29},{4,8},{5,1},{8,12},{9,5},{12,16},{13,9},{16,20},{17,1... | collective-permute-start | bytes 884744 | tf_op jit(solution)/shard_map/ppermute | solution.py:169
  32.2 1.3 %collective-permute-start.7 = (bf16[8,144,128]{2,1,0:T(8,128)(2,1)S(1)}, bf16[8,144,128]{2,1,0:T(8,128)(2,1)S(1)}, u32[]{:S(2)}, u32[]{:S(2)}) collective-permute-start(bf16[8,144,128]{2,1,0:T(8,128)(2,1)S(1)} %collective-permute-done.6.sib_ref), channel_id=1, source_target_pairs={{0,4},{1,29},{4,8},{5,1},{8,12},{9,5},{12,16},{13,9},{16,20},{17,1... | collective-permute-start | bytes 884744 | tf_op jit(solution)/shard_map/ppermute | solution.py:169
  33.5 0.5 collective-permute-start.14
  34.0 1.8 %collective-permute-done.2.own_ref = bf16[8,144,128]{2,1,0:T(8,128)(2,1)S(1)} collective-permute-done((bf16[8,144,128]{2,1,0:T(8,128)(2,1)S(1)}, bf16[8,144,128]{2,1,0:T(8,128)(2,1)S(1)}, u32[]{:S(2)}, u32[]{:S(2)}) %collective-permute-start.2) | collective-permute-done | bytes 294944 | tf_op jit(solution)/shard_map/ppermute | solution.py:169
  35.8 3.1 %collective-permute-start.3 = (bf16[8,144,128]{2,1,0:T(8,128)(2,1)S(1)}, bf16[8,144,128]{2,1,0:T(8,128)(2,1)S(1)}, u32[]{:S(2)}, u32[]{:S(2)}) collective-permute-start(bf16[8,144,128]{2,1,0:T(8,128)(2,1)S(1)} %collective-permute-done.2.own_ref), channel_id=1, source_target_pairs={{0,4},{1,29},{4,8},{5,1},{8,12},{9,5},{12,16},{13,9},{16,20},{17,1... | collective-permute-start | bytes 884744 | tf_op jit(solution)/shard_map/ppermute | solution.py:169
  38.9 3.1 %collective-permute-start.8 = (bf16[8,144,128]{2,1,0:T(8,128)(2,1)S(1)}, bf16[8,144,128]{2,1,0:T(8,128)(2,1)S(1)}, u32[]{:S(2)}, u32[]{:S(2)}) collective-permute-start(bf16[8,144,128]{2,1,0:T(8,128)(2,1)S(1)} %collective-permute-done.7.sib_ref), channel_id=1, source_target_pairs={{0,4},{1,29},{4,8},{5,1},{8,12},{9,5},{12,16},{13,9},{16,20},{17,1... | collective-permute-start | bytes 884744 | tf_op jit(solution)/shard_map/ppermute | solution.py:169
  42.1 0.9 unpack.8.refs_0_
  43.0 2.7 %collective-permute-start.4 = (bf16[8,144,128]{2,1,0:T(8,128)(2,1)S(1)}, bf16[8,144,128]{2,1,0:T(8,128)(2,1)S(1)}, u32[]{:S(2)}, u32[]{:S(2)}) collective-permute-start(bf16[8,144,128]{2,1,0:T(8,128)(2,1)S(1)} %collective-permute-done.3.own_ref), channel_id=1, source_target_pairs={{0,4},{1,29},{4,8},{5,1},{8,12},{9,5},{12,16},{13,9},{16,20},{17,1... | collective-permute-start | bytes 884744 | tf_op jit(solution)/shard_map/ppermute | solution.py:169
  45.7 0.9 unpack.9.refs_0_
  46.6 3.0 %collective-permute-start.11 = (bf16[8,144,128]{2,1,0:T(8,128)(2,1)S(1)}, bf16[8,144,128]{2,1,0:T(8,128)(2,1)S(1)}, u32[]{:S(2)}, u32[]{:S(2)}) collective-permute-start(bf16[8,144,128]{2,1,0:T(8,128)(2,1)S(1)} %collective-permute-done.7.sib_ref), channel_id=1, source_target_pairs={{0,1},{1,0},{2,3},{3,2},{4,5},{5,4},{6,7},{7,6},{8,9},{9,8},{10,11... | collective-permute-start | bytes 884744 | tf_op jit(solution)/shard_map/ppermute | solution.py:157
  49.7 0.9 unpack.10.refs_0_
  50.6 0.5 collective-permute-start.10
  51.1 0.6 collective-permute-start.9
  51.7 0.9 unpack.11.refs_0_
  52.7 3.8 %collective-permute-start.5 = (bf16[8,144,128]{2,1,0:T(8,128)(2,1)S(1)}, bf16[8,144,128]{2,1,0:T(8,128)(2,1)S(1)}, u32[]{:S(2)}, u32[]{:S(2)}) collective-permute-start(bf16[8,144,128]{2,1,0:T(8,128)(2,1)S(1)} %collective-permute-done.4.own_ref), channel_id=1, source_target_pairs={{0,1},{1,0},{2,3},{3,2},{4,5},{5,4},{6,7},{7,6},{8,9},{9,8},{10,11... | collective-permute-start | bytes 884744 | tf_op jit(solution)/shard_map/ppermute | solution.py:157
  56.5 0.9 unpack.12.refs_0_
  57.5 0.9 unpack.13.refs_0_
  58.4 0.9 unpack.14.refs_0_
  59.4 0.9 unpack.15.bins_ref
  60.3 10.0 %grams.1 = bf16[16,2,48,384]{3,2,1,0:T(8,128)(2,1)} custom-call(s32[64,16]{1,0:T(8,128)S(1)} %fusion.1.triads_ref, bf16[8,128]{1,0:T(8,128)(2,1)S(1)} %slice_bitcast_fusion.1.own_w_ref, bf16[8,128]{1,0:T(8,128)(2,1)S(1)} %slice_bitcast_fusion.sib_w_ref, bf16[512,24,256]{2,1,0:T(8,128)(2,1)S(1)} %unpack.15.bins_ref), custom_call_target="tpu_custom_call" | custom-call | flops 12000000000 | bytes 8000000 | tf_op jit(solution)/shard_map/grams/pallas_call | solution.py:196
  70.3 3.7 %all-to-all-start.1 = ((bf16[16,2,48,384]{3,2,1,0:T(8,128)(2,1)}), bf16[16,2,48,384]{3,2,1,0:T(8,128)(2,1)S(1)}, u32[]{:S(2)}, u32[]{:S(2)}) async-start(bf16[16,2,48,384]{3,2,1,0:T(8,128)(2,1)} %grams.1), calls=%async_computation.1 | async-start | bytes 2359296 | tf_op jit(solution)/shard_map/all_to_all | solution.py:245
  74.1 19.4 %all-to-all-done.1 = bf16[16,2,48,384]{3,2,1,0:T(8,128)(2,1)S(1)} async-done(((bf16[16,2,48,384]{3,2,1,0:T(8,128)(2,1)}), bf16[16,2,48,384]{3,2,1,0:T(8,128)(2,1)S(1)}, u32[]{:S(2)}, u32[]{:S(2)}) %all-to-all-start.1) | async-done | bytes 1179680 | tf_op jit(solution)/shard_map/all_to_all | solution.py:245
  93.9 0.3 copy.15
  94.2 0.4 reshape.53
  94.6 7.6 %all_gather.4 = f32[4,2,16,1152]{3,2,1,0:T(8,128)S(1)} all-gather(f32[1,2,16,1152]{3,2,1,0:T(8,128)S(1)} %broadcast_multiply_fusion), channel_id=1, replica_groups=mesh['x'=4,'yh'=2,'z'=8,'yl'=2,'core'=2] {'yl','core'}, dimensions={0}, use_global_device_ids=true | all-gather | bytes 737280 | tf_op jit(solution)/shard_map/all_gather | solution.py:249
  102.3 0.8 copy.25
  (29 shorter events, 0.8 us)
Async XLA Ops:
  0.0 74.0 %copy-start = (s32[8,1]{0,1:T(1,128)S(1)}, s32[8,1]{0,1:T(1,128)}, u32[]{:S(2)}) copy-start(s32[8,1]{0,1:T(1,128)} %param.7) | copy-start | bytes 100
  17.9 11.1 %collective-permute-start.1 = (bf16[8,144,128]{2,1,0:T(8,128)(2,1)S(1)}, bf16[8,144,128]{2,1,0:T(8,128)(2,1)S(1)}, u32[]{:S(2)}, u32[]{:S(2)}) collective-permute-start(bf16[8,144,128]{2,1,0:T(8,128)(2,1)S(1)} %slice.33.own_ref), channel_id=1, source_target_pairs={{0,4},{1,29},{4,8},{5,1},{8,12},{9,5},{12,16},{13,9},{16,20},{17,1... | collective-permute-start | bytes 884744 | tf_op jit(solution)/shard_map/ppermute | solution.py:169
  23.5 8.7 %collective-permute-start.6 = (bf16[8,144,128]{2,1,0:T(8,128)(2,1)S(1)}, bf16[8,144,128]{2,1,0:T(8,128)(2,1)S(1)}, u32[]{:S(2)}, u32[]{:S(2)}) collective-permute-start(bf16[8,144,128]{2,1,0:T(8,128)(2,1)S(1)} %slice.33.own_ref), channel_id=1, source_target_pairs={{0,29},{1,4},{4,1},{5,8},{8,5},{9,12},{12,9},{13,16},{16,13},{17,2... | collective-permute-start | bytes 884744 | tf_op jit(solution)/shard_map/ppermute | solution.py:169
  23.7 15.2 %collective-permute-start = (bf16[8,152,128]{2,1,0:T(8,128)(2,1)S(1)}, bf16[8,152,128]{2,1,0:T(8,128)(2,1)S(1)}, u32[]{:S(2)}, u32[]{:S(2)}) collective-permute-start(bf16[8,152,128]{2,1,0:T(8,128)(2,1)S(1)} %all_to_all.10), channel_id=1, source_target_pairs={{0,1},{1,0},{2,3},{3,2},{4,5},{5,4},{6,7},{7,6},{8,9},{9,8},{10,11... | collective-permute-start | bytes 933896 | tf_op jit(solution)/shard_map/ppermute | solution.py:157
  29.0 6.8 %collective-permute-start.2 = (bf16[8,144,128]{2,1,0:T(8,128)(2,1)S(1)}, bf16[8,144,128]{2,1,0:T(8,128)(2,1)S(1)}, u32[]{:S(2)}, u32[]{:S(2)}) collective-permute-start(bf16[8,144,128]{2,1,0:T(8,128)(2,1)S(1)} %collective-permute-done.1.own_ref), channel_id=1, source_target_pairs={{0,4},{1,29},{4,8},{5,1},{8,12},{9,5},{12,16},{13,9},{16,20},{17,1... | collective-permute-start | bytes 884744 | tf_op jit(solution)/shard_map/ppermute | solution.py:169
  32.2 6.7 %collective-permute-start.7 = (bf16[8,144,128]{2,1,0:T(8,128)(2,1)S(1)}, bf16[8,144,128]{2,1,0:T(8,128)(2,1)S(1)}, u32[]{:S(2)}, u32[]{:S(2)}) collective-permute-start(bf16[8,144,128]{2,1,0:T(8,128)(2,1)S(1)} %collective-permute-done.6.sib_ref), channel_id=1, source_target_pairs={{0,4},{1,29},{4,8},{5,1},{8,12},{9,5},{12,16},{13,9},{16,20},{17,1... | collective-permute-start | bytes 884744 | tf_op jit(solution)/shard_map/ppermute | solution.py:169
  33.5 16.1 %collective-permute-start.13 = (bf16[8,144,128]{2,1,0:T(8,128)(2,1)S(1)}, bf16[8,144,128]{2,1,0:T(8,128)(2,1)S(1)}, u32[]{:S(2)}, u32[]{:S(2)}) collective-permute-start(bf16[8,144,128]{2,1,0:T(8,128)(2,1)S(1)} %collective-permute-done.6.sib_ref), channel_id=1, source_target_pairs={{0,1},{1,0},{2,3},{3,2},{4,5},{5,4},{6,7},{7,6},{8,9},{9,8},{10,11... | collective-permute-start | bytes 884744 | tf_op jit(solution)/shard_map/ppermute | solution.py:157
  33.5 16.2 %collective-permute-start.14 = (bf16[8,144,128]{2,1,0:T(8,128)(2,1)S(1)}, bf16[8,144,128]{2,1,0:T(8,128)(2,1)S(1)}, u32[]{:S(2)}, u32[]{:S(2)}) collective-permute-start(bf16[8,144,128]{2,1,0:T(8,128)(2,1)S(1)} %collective-permute-done.1.own_ref), channel_id=1, source_target_pairs={{0,1},{1,0},{2,3},{3,2},{4,5},{5,4},{6,7},{7,6},{8,9},{9,8},{10,11... | collective-permute-start | bytes 884744 | tf_op jit(solution)/shard_map/ppermute | solution.py:157
  35.8 7.2 %collective-permute-start.3 = (bf16[8,144,128]{2,1,0:T(8,128)(2,1)S(1)}, bf16[8,144,128]{2,1,0:T(8,128)(2,1)S(1)}, u32[]{:S(2)}, u32[]{:S(2)}) collective-permute-start(bf16[8,144,128]{2,1,0:T(8,128)(2,1)S(1)} %collective-permute-done.2.own_ref), channel_id=1, source_target_pairs={{0,4},{1,29},{4,8},{5,1},{8,12},{9,5},{12,16},{13,9},{16,20},{17,1... | collective-permute-start | bytes 884744 | tf_op jit(solution)/shard_map/ppermute | solution.py:169
  38.9 12.2 %collective-permute-start.8 = (bf16[8,144,128]{2,1,0:T(8,128)(2,1)S(1)}, bf16[8,144,128]{2,1,0:T(8,128)(2,1)S(1)}, u32[]{:S(2)}, u32[]{:S(2)}) collective-permute-start(bf16[8,144,128]{2,1,0:T(8,128)(2,1)S(1)} %collective-permute-done.7.sib_ref), channel_id=1, source_target_pairs={{0,4},{1,29},{4,8},{5,1},{8,12},{9,5},{12,16},{13,9},{16,20},{17,1... | collective-permute-start | bytes 884744 | tf_op jit(solution)/shard_map/ppermute | solution.py:169
  43.0 9.7 %collective-permute-start.4 = (bf16[8,144,128]{2,1,0:T(8,128)(2,1)S(1)}, bf16[8,144,128]{2,1,0:T(8,128)(2,1)S(1)}, u32[]{:S(2)}, u32[]{:S(2)}) collective-permute-start(bf16[8,144,128]{2,1,0:T(8,128)(2,1)S(1)} %collective-permute-done.3.own_ref), channel_id=1, source_target_pairs={{0,4},{1,29},{4,8},{5,1},{8,12},{9,5},{12,16},{13,9},{16,20},{17,1... | collective-permute-start | bytes 884744 | tf_op jit(solution)/shard_map/ppermute | solution.py:169
  46.6 10.8 %collective-permute-start.11 = (bf16[8,144,128]{2,1,0:T(8,128)(2,1)S(1)}, bf16[8,144,128]{2,1,0:T(8,128)(2,1)S(1)}, u32[]{:S(2)}, u32[]{:S(2)}) collective-permute-start(bf16[8,144,128]{2,1,0:T(8,128)(2,1)S(1)} %collective-permute-done.7.sib_ref), channel_id=1, source_target_pairs={{0,1},{1,0},{2,3},{3,2},{4,5},{5,4},{6,7},{7,6},{8,9},{9,8},{10,11... | collective-permute-start | bytes 884744 | tf_op jit(solution)/shard_map/ppermute | solution.py:157
  49.6 7.9 %collective-permute-start.12 = (bf16[8,144,128]{2,1,0:T(8,128)(2,1)S(1)}, bf16[8,144,128]{2,1,0:T(8,128)(2,1)S(1)}, u32[]{:S(2)}, u32[]{:S(2)}) collective-permute-start(bf16[8,144,128]{2,1,0:T(8,128)(2,1)S(1)} %collective-permute-done.2.own_ref), channel_id=1, source_target_pairs={{0,1},{1,0},{2,3},{3,2},{4,5},{5,4},{6,7},{7,6},{8,9},{9,8},{10,11... | collective-permute-start | bytes 884744 | tf_op jit(solution)/shard_map/ppermute | solution.py:157
  50.6 7.8 %collective-permute-start.10 = (bf16[8,144,128]{2,1,0:T(8,128)(2,1)S(1)}, bf16[8,144,128]{2,1,0:T(8,128)(2,1)S(1)}, u32[]{:S(2)}, u32[]{:S(2)}) collective-permute-start(bf16[8,144,128]{2,1,0:T(8,128)(2,1)S(1)} %collective-permute-done.3.own_ref), channel_id=1, source_target_pairs={{0,1},{1,0},{2,3},{3,2},{4,5},{5,4},{6,7},{7,6},{8,9},{9,8},{10,11... | collective-permute-start | bytes 884744 | tf_op jit(solution)/shard_map/ppermute | solution.py:157
  51.1 7.3 %collective-permute-start.9 = (bf16[8,144,128]{2,1,0:T(8,128)(2,1)S(1)}, bf16[8,144,128]{2,1,0:T(8,128)(2,1)S(1)}, u32[]{:S(2)}, u32[]{:S(2)}) collective-permute-start(bf16[8,144,128]{2,1,0:T(8,128)(2,1)S(1)} %collective-permute-done.8.sib_ref), channel_id=1, source_target_pairs={{0,1},{1,0},{2,3},{3,2},{4,5},{5,4},{6,7},{7,6},{8,9},{9,8},{10,11... | collective-permute-start | bytes 884744 | tf_op jit(solution)/shard_map/ppermute | solution.py:157
  52.7 6.7 %collective-permute-start.5 = (bf16[8,144,128]{2,1,0:T(8,128)(2,1)S(1)}, bf16[8,144,128]{2,1,0:T(8,128)(2,1)S(1)}, u32[]{:S(2)}, u32[]{:S(2)}) collective-permute-start(bf16[8,144,128]{2,1,0:T(8,128)(2,1)S(1)} %collective-permute-done.4.own_ref), channel_id=1, source_target_pairs={{0,1},{1,0},{2,3},{3,2},{4,5},{5,4},{6,7},{7,6},{8,9},{9,8},{10,11... | collective-permute-start | bytes 884744 | tf_op jit(solution)/shard_map/ppermute | solution.py:157
  70.3 23.3 %all-to-all-start.1 = ((bf16[16,2,48,384]{3,2,1,0:T(8,128)(2,1)}), bf16[16,2,48,384]{3,2,1,0:T(8,128)(2,1)S(1)}, u32[]{:S(2)}, u32[]{:S(2)}) async-start(bf16[16,2,48,384]{3,2,1,0:T(8,128)(2,1)} %grams.1), calls=%async_computation.1 | async-start | bytes 2359296 | tf_op jit(solution)/shard_map/all_to_all | solution.py:245

commit v5 on v4

--- a/solution.py
+++ b/solution.py
@@ -85,7 +85,7 @@
         return turn * 64 + (which & 56) + (which >> 6)
 
     weights = lane_weights(own_w_ref, sib_w_ref)
-    lane = lax.broadcasted_iota(jnp.int32, (48, LANES), 1)
+    lane = lax.broadcasted_iota(jnp.int32, (24, LANES), 1)
 
     def prepare(reader, buffer):
         w_ref, q_ref = buffer
@@ -102,14 +102,13 @@
                 m_bin = (k_bin + l_bin) & 511
                 second = bins_ref[slot(l_bin)].astype(F32)
                 l_real, l_imag = second[:, :LANES], second[:, LANES:]
-                real = (k_real * l_real - k_imag * l_imag).astype(BF16)
-                imag = k_real * l_imag + k_imag * l_real
-                plus, minus = imag.astype(BF16), (-imag).astype(BF16)
-                w_ref[48 * t : 48 * t + 24, :LANES] = real
-                w_ref[48 * t : 48 * t + 24, LANES:] = plus
-                w_ref[48 * t + 24 : 48 * t + 48, :LANES] = minus
-                w_ref[48 * t + 24 : 48 * t + 48, LANES:] = real
-                q_ref[24 * t : 24 * t + 24, :] = bins_ref[slot(m_bin)]
+                rows = slice(24 * t, 24 * t + 24)
+                w_ref[rows, :LANES] = (k_real * l_real - k_imag * l_imag).astype(BF16)
+                w_ref[rows, LANES:] = (k_real * l_imag + k_imag * l_real).astype(BF16)
+                third = bins_ref[slot(m_bin)]
+                q_ref[48 * t : 48 * t + 24, :] = third
+                q_ref[48 * t + 24 : 48 * t + 48, :LANES] = third[:, LANES:]
+                q_ref[48 * t + 24 : 48 * t + 48, LANES:] = -third[:, :LANES]
 
         return some
 
@@ -117,17 +116,22 @@
         w_ref, q_ref = buffer
         start = 5 * n
         product = lax.dot_general(
-            w_ref[48 * start : 48 * (start + 6), :],
-            q_ref[LANES * n : LANES * (n + 1), :],
+            w_ref[24 * start : 24 * (start + 6), :],
+            q_ref[256 * n : 256 * (n + 1), :],
             (((1,), (1,)), ((), ())),
             preferred_element_type=F32,
         )
-        built = product[:48]
-        for i in range(1, 6):
-            begin = 24 * (start + i) - LANES * n
-            built = jnp.where(lane >= begin, product[48 * i : 48 * (i + 1)], built)
-        lanes = slice(LANES * n, LANES * (n + 1))
-        out_ref[reader >> 1, reader & 1, :, lanes] = built.astype(BF16)
+        for side in range(2):
+            first_lane = 256 * n + LANES * side
+            lanes = slice(LANES * side, LANES * (side + 1))
+            built = None
+            for i in range(6):
+                begin = 48 * (start + i) - first_lane
+                if begin < LANES and begin + 48 > 0:
+                    part = product[24 * i : 24 * (i + 1), lanes]
+                    built = part if built is None else jnp.where(lane >= begin, part, built)
+            where = slice(first_lane, first_lane + LANES)
+            out_ref[reader >> 1, reader & 1, :, where] = built.astype(BF16)
 
     thirds = (range(0, 5), range(5, 10), range(10, 16))
     ready = prepare(0, buffers[0])
@@ -187,7 +191,7 @@
         out_specs=pl.BlockSpec((64, 24, 256), lambda i: (turn, 0, 0)),
         input_output_aliases={} if bins is None else {2: 0},
         compiler_params=params(8),
-        cost_estimate=pl.CostEstimate(flops=1500000000, bytes_accessed=2000000, transcendentals=0),
+        cost_estimate=pl.CostEstimate(flops=3000000000, bytes_accessed=2000000, transcendentals=0),
         name="unpack",
     )(*operands)
 
@@ -195,10 +199,10 @@
 def grams(lists, own_tile, sib_tile, bins):
     return pl.pallas_call(
         grams_kernel,
-        out_shape=jax.ShapeDtypeStruct((16, 2, 48, 384), BF16),
+        out_shape=jax.ShapeDtypeStruct((16, 2, 24, 768), BF16),
         in_specs=[smem()] + [vmem()] * 3,
         out_specs=vmem(),
-        scratch_shapes=[pltpu.VMEM((768, 256), BF16), pltpu.VMEM((384, 256), BF16)] * 2,
+        scratch_shapes=[pltpu.VMEM((384, 256), BF16), pltpu.VMEM((768, 256), BF16)] * 2,
         compiler_params=params(12),
         cost_estimate=pl.CostEstimate(
             flops=12000000000, bytes_accessed=8000000, transcendentals=0
@@ -244,9 +248,9 @@
     partial = grams(lists, received[0, 144:], beside[0, 144:], bins)
     parts = lax.all_to_all(partial, ("x", "yh", "yl"), 0, 0)
     summed = jnp.sum(parts.astype(F32), axis=0) / 24
-    rows = summed.reshape(2, 48, 16, 24).transpose(0, 2, 1, 3).reshape(2, 16, 1152)
-    rows = rows * mask[:, :, None]
-    return lax.all_gather(rows, ("yl", "core")).reshape(8, 1, 16, 1152)
+    rows = summed.reshape(2, 24, 16, 2, 24).transpose(0, 2, 3, 1, 4).reshape(2, 1, 16, 1152)
+    rows = rows * mask[:, None, :, None]
+    return lax.all_gather(rows, ("yl", "core"), tiled=True)
 
 
 def solution(mesh):

time: 103 us -> 104 us (level)
  local copies, waits for them, and re-layouts: 1.76 us -> 3.08 us
    ppermute x8, starting transfers between devices: 9.43 us -> 10.9 us  [step(): lax.ppermute(array, axes, [(i, (i + by) % size) for i in range(size)])]
    ppermute x7, starting transfers between devices: 19.1 us -> 17.6 us  [ring(): return lax.ppermute(array, ('z', 'core'), pairs)]
    div x1, local copies, waits for them, and re-layouts: 0.16 us -> 1.31 us  [body(): summed = jnp.sum(parts.astype(F32), axis=0) / 24]
where the time goes in v5:
time: 104 us; the launch traced here: 103 us
  starting transfers between devices  32.2 us (31%)
  waiting for transfers between devices  24.8 us (24%)
  blocking collectives  23.2 us (22%)
  Pallas kernels  19.6 us (19%)
  local copies, waits for them, and re-layouts  3.08 us (3%)
    all_to_all x1, waiting for transfers between devices, body(): parts = lax.all_to_all(partial, ('x', 'yh', 'yl'), 0, 0)  19.5 us
    ppermute x7, starting transfers between devices, ring(): return lax.ppermute(array, ('z', 'core'), pairs)  17.6 us
    all_to_all x1, blocking collectives, body(): received = lax.all_to_all(pieces, ('x', 'yh'), 0, 0)  15.5 us
    ppermute x8, starting transfers between devices, step(): lax.ppermute(array, axes, [(i, (i + by) % size) for i in range(size)])  10.9 us
    pallas_call x1, Pallas kernels, grams(): pl.pallas_call(grams_kernel, out_shape=jax.ShapeDtypeStruct((16, 2, 24, 7...  9.81 us
    all_gather x1, blocking collectives, body(): return lax.all_gather(rows, ('yl', 'core'), tiled=True)  7.65 us
    pallas_call x8, Pallas kernels, unpack(): pl.pallas_call(unpack_kernel, out_shape=BINS, grid=(1,), in_specs=[pl.Blo...  7.46 us
    ppermute x7, waiting for transfers between devices, ring(): return lax.ppermute(array, ('z', 'core'), pairs)  5.24 us
  transfers between devices with their start and end apart: 16, of which 3 were waited for; matrix products, arithmetic and copies ran while one was open for 0% of the time, Pallas kernels for 6%

profile of v5, /device:TPU:1, one launch (start us, length us, event | category | flops | bytes accessed | tf_op | source)
XLA Modules:
  0.0 103.5 jit_solution(5772039671646564765)
XLA Ops:
  0.0 2.3 %split.1 = bf16[8,152,128]{2,1,0:T(8,128)(2,1)} custom-call(bf16[48,24,128]{2,1,0:T(8,128)(2,1)} %bitcast.17, s32[8,16]{1,0:T(8,128)} %bitcast.18, f32[1,128]{1,0:T(1,128)} %bitcast.19), custom_call_target="tpu_custom_call" | custom-call | tf_op jit(solution)/shard_map/split/pallas_call | solution.py:216
  2.3 15.5 %all_to_all.10 = bf16[8,152,128]{2,1,0:T(8,128)(2,1)S(1)} all-to-all(bf16[8,152,128]{2,1,0:T(8,128)(2,1)} %split.1), channel_id=1, replica_groups=mesh['x'=4,'yh'=2,'z'=8,'yl'=2,'core'=2] {'x','yh'}, dimensions={0} | all-to-all | bytes 622592 | tf_op jit(solution)/shard_map/all_to_all | solution.py:224
  17.9 5.7 %collective-permute-start.1 = (bf16[8,144,128]{2,1,0:T(8,128)(2,1)S(1)}, bf16[8,144,128]{2,1,0:T(8,128)(2,1)S(1)}, u32[]{:S(2)}, u32[]{:S(2)}) collective-permute-start(bf16[8,144,128]{2,1,0:T(8,128)(2,1)S(1)} %slice.33.own_ref), channel_id=1, source_target_pairs={{0,4},{1,29},{4,8},{5,1},{8,12},{9,5},{12,16},{13,9},{16,20},{17,1... | collective-permute-start | bytes 884744 | tf_op jit(solution)/shard_map/ppermute | solution.py:173
  23.5 0.2 collective-permute-start.6
  23.7 0.9 collective-permute-start
  24.7 4.3 %collective-permute-done.1.own_ref = bf16[8,144,128]{2,1,0:T(8,128)(2,1)S(1)} collective-permute-done((bf16[8,144,128]{2,1,0:T(8,128)(2,1)S(1)}, bf16[8,144,128]{2,1,0:T(8,128)(2,1)S(1)}, u32[]{:S(2)}, u32[]{:S(2)}) %collective-permute-start.1) | collective-permute-done | bytes 294944 | tf_op jit(solution)/shard_map/ppermute | solution.py:173
  29.0 3.7 %collective-permute-start.14 = (bf16[8,144,128]{2,1,0:T(8,128)(2,1)S(1)}, bf16[8,144,128]{2,1,0:T(8,128)(2,1)S(1)}, u32[]{:S(2)}, u32[]{:S(2)}) collective-permute-start(bf16[8,144,128]{2,1,0:T(8,128)(2,1)S(1)} %collective-permute-done.1.own_ref), channel_id=1, source_target_pairs={{0,1},{1,0},{2,3},{3,2},{4,5},{5,4},{6,7},{7,6},{8,9},{9,8},{10,11... | collective-permute-start | bytes 884744 | tf_op jit(solution)/shard_map/ppermute | solution.py:161
  32.7 2.5 %collective-permute-start.2 = (bf16[8,144,128]{2,1,0:T(8,128)(2,1)S(1)}, bf16[8,144,128]{2,1,0:T(8,128)(2,1)S(1)}, u32[]{:S(2)}, u32[]{:S(2)}) collective-permute-start(bf16[8,144,128]{2,1,0:T(8,128)(2,1)S(1)} %collective-permute-done.1.own_ref), channel_id=1, source_target_pairs={{0,4},{1,29},{4,8},{5,1},{8,12},{9,5},{12,16},{13,9},{16,20},{17,1... | collective-permute-start | bytes 884744 | tf_op jit(solution)/shard_map/ppermute | solution.py:173
  35.3 0.8 collective-permute-start.7
  36.1 0.9 unpack.8.refs_0_
  37.1 0.9 unpack.9.refs_0_
  38.0 0.9 collective-permute-done.2.own_ref
  38.9 3.1 %collective-permute-start.3 = (bf16[8,144,128]{2,1,0:T(8,128)(2,1)S(1)}, bf16[8,144,128]{2,1,0:T(8,128)(2,1)S(1)}, u32[]{:S(2)}, u32[]{:S(2)}) collective-permute-start(bf16[8,144,128]{2,1,0:T(8,128)(2,1)S(1)} %collective-permute-done.2.own_ref), channel_id=1, source_target_pairs={{0,4},{1,29},{4,8},{5,1},{8,12},{9,5},{12,16},{13,9},{16,20},{17,1... | collective-permute-start | bytes 884744 | tf_op jit(solution)/shard_map/ppermute | solution.py:173
  42.1 3.1 %collective-permute-start.8 = (bf16[8,144,128]{2,1,0:T(8,128)(2,1)S(1)}, bf16[8,144,128]{2,1,0:T(8,128)(2,1)S(1)}, u32[]{:S(2)}, u32[]{:S(2)}) collective-permute-start(bf16[8,144,128]{2,1,0:T(8,128)(2,1)S(1)} %collective-permute-done.7.sib_ref), channel_id=1, source_target_pairs={{0,4},{1,29},{4,8},{5,1},{8,12},{9,5},{12,16},{13,9},{16,20},{17,1... | collective-permute-start | bytes 884744 | tf_op jit(solution)/shard_map/ppermute | solution.py:173
  45.2 0.5 collective-permute-start.12
  45.7 0.9 unpack.10.refs_0_
  46.7 2.2 %collective-permute-start.4 = (bf16[8,144,128]{2,1,0:T(8,128)(2,1)S(1)}, bf16[8,144,128]{2,1,0:T(8,128)(2,1)S(1)}, u32[]{:S(2)}, u32[]{:S(2)}) collective-permute-start(bf16[8,144,128]{2,1,0:T(8,128)(2,1)S(1)} %collective-permute-done.3.own_ref), channel_id=1, source_target_pairs={{0,4},{1,29},{4,8},{5,1},{8,12},{9,5},{12,16},{13,9},{16,20},{17,1... | collective-permute-start | bytes 884744 | tf_op jit(solution)/shard_map/ppermute | solution.py:173
  48.8 0.9 unpack.11.refs_0_
  49.9 1.9 %collective-permute-start.9 = (bf16[8,144,128]{2,1,0:T(8,128)(2,1)S(1)}, bf16[8,144,128]{2,1,0:T(8,128)(2,1)S(1)}, u32[]{:S(2)}, u32[]{:S(2)}) collective-permute-start(bf16[8,144,128]{2,1,0:T(8,128)(2,1)S(1)} %collective-permute-done.8.sib_ref), channel_id=1, source_target_pairs={{0,1},{1,0},{2,3},{3,2},{4,5},{5,4},{6,7},{7,6},{8,9},{9,8},{10,11... | collective-permute-start | bytes 884744 | tf_op jit(solution)/shard_map/ppermute | solution.py:161
  51.7 0.9 unpack.12.refs_0_
  52.7 3.8 %collective-permute-start.5 = (bf16[8,144,128]{2,1,0:T(8,128)(2,1)S(1)}, bf16[8,144,128]{2,1,0:T(8,128)(2,1)S(1)}, u32[]{:S(2)}, u32[]{:S(2)}) collective-permute-start(bf16[8,144,128]{2,1,0:T(8,128)(2,1)S(1)} %collective-permute-done.4.own_ref), channel_id=1, source_target_pairs={{0,1},{1,0},{2,3},{3,2},{4,5},{5,4},{6,7},{7,6},{8,9},{9,8},{10,11... | collective-permute-start | bytes 884744 | tf_op jit(solution)/shard_map/ppermute | solution.py:161
  56.5 0.9 unpack.13.refs_0_
  57.5 0.9 unpack.14.refs_0_
  58.4 0.9 unpack.15.bins_ref
  59.4 9.8 %grams.1 = bf16[16,2,24,768]{3,2,1,0:T(8,128)(2,1)} custom-call(s32[64,16]{1,0:T(8,128)S(1)} %fusion.1.triads_ref, bf16[8,128]{1,0:T(8,128)(2,1)S(1)} %slice_bitcast_fusion.1.own_w_ref, bf16[8,128]{1,0:T(8,128)(2,1)S(1)} %slice_bitcast_fusion.sib_w_ref, bf16[512,24,256]{2,1,0:T(8,128)(2,1)S(1)} %unpack.15.bins_ref), custom_call_target="tpu_custom_call" | custom-call | flops 12000000000 | bytes 8000000 | tf_op jit(solution)/shard_map/grams/pallas_call | solution.py:200
  69.2 3.7 %all-to-all-start.1 = ((bf16[16,2,24,768]{3,2,1,0:T(8,128)(2,1)}), bf16[16,2,24,768]{3,2,1,0:T(8,128)(2,1)S(1)}, u32[]{:S(2)}, u32[]{:S(2)}) async-start(bf16[16,2,24,768]{3,2,1,0:T(8,128)(2,1)} %grams.1), calls=%async_computation.1 | async-start | bytes 2359296 | tf_op jit(solution)/shard_map/all_to_all | solution.py:249
  73.1 19.5 %all-to-all-done.1 = bf16[16,2,24,768]{3,2,1,0:T(8,128)(2,1)S(1)} async-done(((bf16[16,2,24,768]{3,2,1,0:T(8,128)(2,1)}), bf16[16,2,24,768]{3,2,1,0:T(8,128)(2,1)S(1)}, u32[]{:S(2)}, u32[]{:S(2)}) %all-to-all-start.1) | async-done | bytes 1179680 | tf_op jit(solution)/shard_map/all_to_all | solution.py:249
  92.8 1.3 %div.10 = f32[2,24,16,2,24]{4,3,2,1,0:T(2,128)S(1)} reshape(f32[2,24,768]{2,1,0:T(8,128)S(1)} %broadcast_multiply_fusion) | data formatting | bytes 294912 | tf_op jit(solution)/shard_map/div | solution.py:250
  94.1 0.5 copy.14
  94.6 0.4 reshape.53
  95.0 7.6 %all_gather.3 = f32[8,1,16,1152]{3,2,1,0:T(8,128)S(1)} all-gather(f32[2,1,16,1152]{3,2,1,0:T(8,128)S(1)} %multiply_bitcast_fusion), channel_id=1, replica_groups=mesh['x'=4,'yh'=2,'z'=8,'yl'=2,'core'=2] {'yl','core'}, dimensions={0}, use_global_device_ids=true | all-gather | bytes 737280 | tf_op jit(solution)/shard_map/all_gather | solution.py:253
  102.7 0.8 copy.24
  (29 shorter events, 0.7 us)
Async XLA Ops:
  0.0 72.9 %copy-start = (s32[8,1]{0,1:T(1,128)S(1)}, s32[8,1]{0,1:T(1,128)}, u32[]{:S(2)}) copy-start(s32[8,1]{0,1:T(1,128)} %param.7) | copy-start | bytes 100
  17.9 11.1 %collective-permute-start.1 = (bf16[8,144,128]{2,1,0:T(8,128)(2,1)S(1)}, bf16[8,144,128]{2,1,0:T(8,128)(2,1)S(1)}, u32[]{:S(2)}, u32[]{:S(2)}) collective-permute-start(bf16[8,144,128]{2,1,0:T(8,128)(2,1)S(1)} %slice.33.own_ref), channel_id=1, source_target_pairs={{0,4},{1,29},{4,8},{5,1},{8,12},{9,5},{12,16},{13,9},{16,20},{17,1... | collective-permute-start | bytes 884744 | tf_op jit(solution)/shard_map/ppermute | solution.py:173
  23.5 11.7 %collective-permute-start.6 = (bf16[8,144,128]{2,1,0:T(8,128)(2,1)S(1)}, bf16[8,144,128]{2,1,0:T(8,128)(2,1)S(1)}, u32[]{:S(2)}, u32[]{:S(2)}) collective-permute-start(bf16[8,144,128]{2,1,0:T(8,128)(2,1)S(1)} %slice.33.own_ref), channel_id=1, source_target_pairs={{0,29},{1,4},{4,1},{5,8},{8,5},{9,12},{12,9},{13,16},{16,13},{17,2... | collective-permute-start | bytes 884744 | tf_op jit(solution)/shard_map/ppermute | solution.py:173
  23.7 12.4 %collective-permute-start = (bf16[8,152,128]{2,1,0:T(8,128)(2,1)S(1)}, bf16[8,152,128]{2,1,0:T(8,128)(2,1)S(1)}, u32[]{:S(2)}, u32[]{:S(2)}) collective-permute-start(bf16[8,152,128]{2,1,0:T(8,128)(2,1)S(1)} %all_to_all.10), channel_id=1, source_target_pairs={{0,1},{1,0},{2,3},{3,2},{4,5},{5,4},{6,7},{7,6},{8,9},{9,8},{10,11... | collective-permute-start | bytes 933896 | tf_op jit(solution)/shard_map/ppermute | solution.py:161
  29.0 16.7 %collective-permute-start.14 = (bf16[8,144,128]{2,1,0:T(8,128)(2,1)S(1)}, bf16[8,144,128]{2,1,0:T(8,128)(2,1)S(1)}, u32[]{:S(2)}, u32[]{:S(2)}) collective-permute-start(bf16[8,144,128]{2,1,0:T(8,128)(2,1)S(1)} %collective-permute-done.1.own_ref), channel_id=1, source_target_pairs={{0,1},{1,0},{2,3},{3,2},{4,5},{5,4},{6,7},{7,6},{8,9},{9,8},{10,11... | collective-permute-start | bytes 884744 | tf_op jit(solution)/shard_map/ppermute | solution.py:161
  32.7 6.2 %collective-permute-start.2 = (bf16[8,144,128]{2,1,0:T(8,128)(2,1)S(1)}, bf16[8,144,128]{2,1,0:T(8,128)(2,1)S(1)}, u32[]{:S(2)}, u32[]{:S(2)}) collective-permute-start(bf16[8,144,128]{2,1,0:T(8,128)(2,1)S(1)} %collective-permute-done.1.own_ref), channel_id=1, source_target_pairs={{0,4},{1,29},{4,8},{5,1},{8,12},{9,5},{12,16},{13,9},{16,20},{17,1... | collective-permute-start | bytes 884744 | tf_op jit(solution)/shard_map/ppermute | solution.py:173
  35.2 9.9 %collective-permute-start.13 = (bf16[8,144,128]{2,1,0:T(8,128)(2,1)S(1)}, bf16[8,144,128]{2,1,0:T(8,128)(2,1)S(1)}, u32[]{:S(2)}, u32[]{:S(2)}) collective-permute-start(bf16[8,144,128]{2,1,0:T(8,128)(2,1)S(1)} %collective-permute-done.6.sib_ref), channel_id=1, source_target_pairs={{0,1},{1,0},{2,3},{3,2},{4,5},{5,4},{6,7},{7,6},{8,9},{9,8},{10,11... | collective-permute-start | bytes 884744 | tf_op jit(solution)/shard_map/ppermute | solution.py:161
  35.3 6.8 %collective-permute-start.7 = (bf16[8,144,128]{2,1,0:T(8,128)(2,1)S(1)}, bf16[8,144,128]{2,1,0:T(8,128)(2,1)S(1)}, u32[]{:S(2)}, u32[]{:S(2)}) collective-permute-start(bf16[8,144,128]{2,1,0:T(8,128)(2,1)S(1)} %collective-permute-done.6.sib_ref), channel_id=1, source_target_pairs={{0,4},{1,29},{4,8},{5,1},{8,12},{9,5},{12,16},{13,9},{16,20},{17,1... | collective-permute-start | bytes 884744 | tf_op jit(solution)/shard_map/ppermute | solution.py:173
  38.9 7.7 %collective-permute-start.3 = (bf16[8,144,128]{2,1,0:T(8,128)(2,1)S(1)}, bf16[8,144,128]{2,1,0:T(8,128)(2,1)S(1)}, u32[]{:S(2)}, u32[]{:S(2)}) collective-permute-start(bf16[8,144,128]{2,1,0:T(8,128)(2,1)S(1)} %collective-permute-done.2.own_ref), channel_id=1, source_target_pairs={{0,4},{1,29},{4,8},{5,1},{8,12},{9,5},{12,16},{13,9},{16,20},{17,1... | collective-permute-start | bytes 884744 | tf_op jit(solution)/shard_map/ppermute | solution.py:173
  42.1 7.8 %collective-permute-start.8 = (bf16[8,144,128]{2,1,0:T(8,128)(2,1)S(1)}, bf16[8,144,128]{2,1,0:T(8,128)(2,1)S(1)}, u32[]{:S(2)}, u32[]{:S(2)}) collective-permute-start(bf16[8,144,128]{2,1,0:T(8,128)(2,1)S(1)} %collective-permute-done.7.sib_ref), channel_id=1, source_target_pairs={{0,4},{1,29},{4,8},{5,1},{8,12},{9,5},{12,16},{13,9},{16,20},{17,1... | collective-permute-start | bytes 884744 | tf_op jit(solution)/shard_map/ppermute | solution.py:173
  45.2 11.3 %collective-permute-start.11 = (bf16[8,144,128]{2,1,0:T(8,128)(2,1)S(1)}, bf16[8,144,128]{2,1,0:T(8,128)(2,1)S(1)}, u32[]{:S(2)}, u32[]{:S(2)}) collective-permute-start(bf16[8,144,128]{2,1,0:T(8,128)(2,1)S(1)} %collective-permute-done.7.sib_ref), channel_id=1, source_target_pairs={{0,1},{1,0},{2,3},{3,2},{4,5},{5,4},{6,7},{7,6},{8,9},{9,8},{10,11... | collective-permute-start | bytes 884744 | tf_op jit(solution)/shard_map/ppermute | solution.py:161
  45.2 11.3 %collective-permute-start.12 = (bf16[8,144,128]{2,1,0:T(8,128)(2,1)S(1)}, bf16[8,144,128]{2,1,0:T(8,128)(2,1)S(1)}, u32[]{:S(2)}, u32[]{:S(2)}) collective-permute-start(bf16[8,144,128]{2,1,0:T(8,128)(2,1)S(1)} %collective-permute-done.2.own_ref), channel_id=1, source_target_pairs={{0,1},{1,0},{2,3},{3,2},{4,5},{5,4},{6,7},{7,6},{8,9},{9,8},{10,11... | collective-permute-start | bytes 884744 | tf_op jit(solution)/shard_map/ppermute | solution.py:161
  46.7 6.0 %collective-permute-start.4 = (bf16[8,144,128]{2,1,0:T(8,128)(2,1)S(1)}, bf16[8,144,128]{2,1,0:T(8,128)(2,1)S(1)}, u32[]{:S(2)}, u32[]{:S(2)}) collective-permute-start(bf16[8,144,128]{2,1,0:T(8,128)(2,1)S(1)} %collective-permute-done.3.own_ref), channel_id=1, source_target_pairs={{0,4},{1,29},{4,8},{5,1},{8,12},{9,5},{12,16},{13,9},{16,20},{17,1... | collective-permute-start | bytes 884744 | tf_op jit(solution)/shard_map/ppermute | solution.py:173
  49.8 7.7 %collective-permute-start.10 = (bf16[8,144,128]{2,1,0:T(8,128)(2,1)S(1)}, bf16[8,144,128]{2,1,0:T(8,128)(2,1)S(1)}, u32[]{:S(2)}, u32[]{:S(2)}) collective-permute-start(bf16[8,144,128]{2,1,0:T(8,128)(2,1)S(1)} %collective-permute-done.3.own_ref), channel_id=1, source_target_pairs={{0,1},{1,0},{2,3},{3,2},{4,5},{5,4},{6,7},{7,6},{8,9},{9,8},{10,11... | collective-permute-start | bytes 884744 | tf_op jit(solution)/shard_map/ppermute | solution.py:161
  49.9 7.6 %collective-permute-start.9 = (bf16[8,144,128]{2,1,0:T(8,128)(2,1)S(1)}, bf16[8,144,128]{2,1,0:T(8,128)(2,1)S(1)}, u32[]{:S(2)}, u32[]{:S(2)}) collective-permute-start(bf16[8,144,128]{2,1,0:T(8,128)(2,1)S(1)} %collective-permute-done.8.sib_ref), channel_id=1, source_target_pairs={{0,1},{1,0},{2,3},{3,2},{4,5},{5,4},{6,7},{7,6},{8,9},{9,8},{10,11... | collective-permute-start | bytes 884744 | tf_op jit(solution)/shard_map/ppermute | solution.py:161
  52.7 5.7 %collective-permute-start.5 = (bf16[8,144,128]{2,1,0:T(8,128)(2,1)S(1)}, bf16[8,144,128]{2,1,0:T(8,128)(2,1)S(1)}, u32[]{:S(2)}, u32[]{:S(2)}) collective-permute-start(bf16[8,144,128]{2,1,0:T(8,128)(2,1)S(1)} %collective-permute-done.4.own_ref), channel_id=1, source_target_pairs={{0,1},{1,0},{2,3},{3,2},{4,5},{5,4},{6,7},{7,6},{8,9},{9,8},{10,11... | collective-permute-start | bytes 884744 | tf_op jit(solution)/shard_map/ppermute | solution.py:161
  69.2 23.4 %all-to-all-start.1 = ((bf16[16,2,24,768]{3,2,1,0:T(8,128)(2,1)}), bf16[16,2,24,768]{3,2,1,0:T(8,128)(2,1)S(1)}, u32[]{:S(2)}, u32[]{:S(2)}) async-start(bf16[16,2,24,768]{3,2,1,0:T(8,128)(2,1)} %grams.1), calls=%async_computation.1 | async-start | bytes 2359296 | tf_op jit(solution)/shard_map/all_to_all | solution.py:249

commit v6 on v4

--- a/solution.py
+++ b/solution.py
@@ -134,7 +134,7 @@
     for third in thirds:
         ready(third)
 
-    @pl.loop(0, 16)
+    @pl.loop(0, 16, unroll=2)
     def _(pair):
         for side in range(2):
             reader = 2 * pair + side
@@ -187,7 +187,7 @@
         out_specs=pl.BlockSpec((64, 24, 256), lambda i: (turn, 0, 0)),
         input_output_aliases={} if bins is None else {2: 0},
         compiler_params=params(8),
-        cost_estimate=pl.CostEstimate(flops=1500000000, bytes_accessed=2000000, transcendentals=0),
+        cost_estimate=pl.CostEstimate(flops=3000000000, bytes_accessed=2000000, transcendentals=0),
         name="unpack",
     )(*operands)
 
@@ -208,7 +208,6 @@
 
 
 def body(modes, point_weights, triads, counts):
-    core, half = lax.axis_index("core"), lax.axis_index("yl")
     pieces = pl.pallas_call(
         split_kernel,
         out_shape=jax.ShapeDtypeStruct((8, 152, LANES), BF16),
@@ -239,14 +238,13 @@
     bins = unpack(*passed[2], bins, 5)
     bins = unpack(near[4], swap(near[4]), bins, 4)
 
-    live = lax.dynamic_slice_in_dim(counts[:, 0], 4 * half + 2 * core, 2)
-    mask = (jnp.arange(16, dtype=jnp.int32)[None, :] < live[:, None]).astype(F32)
     partial = grams(lists, received[0, 144:], beside[0, 144:], bins)
     parts = lax.all_to_all(partial, ("x", "yh", "yl"), 0, 0)
     summed = jnp.sum(parts.astype(F32), axis=0) / 24
-    rows = summed.reshape(2, 48, 16, 24).transpose(0, 2, 1, 3).reshape(2, 16, 1152)
-    rows = rows * mask[:, :, None]
-    return lax.all_gather(rows, ("yl", "core")).reshape(8, 1, 16, 1152)
+    rows = summed.reshape(2, 48, 16, 24).transpose(0, 2, 1, 3).reshape(2, 1, 16, 1152)
+    gathered = lax.all_gather(rows, ("yl", "core"), tiled=True)
+    live = jnp.arange(16, dtype=jnp.int32)[None, None, :, None] < counts[:, :, None, None]
+    return jnp.where(live, gathered, 0.0)
 
 
 def solution(mesh):

time: 103 us -> 101 us (0.981)
  Pallas kernels: 19.7 us -> 18.6 us
    ppermute x8, starting transfers between devices: 9.43 us -> 10.9 us  [step(): lax.ppermute(array, axes, [(i, (i + by) % size) for i in range(size)])]
    ppermute x7, starting transfers between devices: 19.1 us -> 17.6 us  [ring(): return lax.ppermute(array, ('z', 'core'), pairs)]
    pallas_call x1, Pallas kernels: 9.95 us -> 8.79 us  [grams(): pl.pallas_call(grams_kernel, out_shape=jax.ShapeDtypeStruct((16, 2, 48, 3...]
where the time goes in v6:
time: 101 us
  starting transfers between devices  32.2 us (32%)
  waiting for transfers between devices  24.8 us (25%)
  blocking collectives  23.2 us (23%)
  Pallas kernels  18.6 us (18%)
  other arithmetic  1.25 us (1%)
    all_to_all x1, waiting for transfers between devices, body(): parts = lax.all_to_all(partial, ('x', 'yh', 'yl'), 0, 0)  19.6 us
    ppermute x7, starting transfers between devices, ring(): return lax.ppermute(array, ('z', 'core'), pairs)  17.6 us
    all_to_all x1, blocking collectives, body(): received = lax.all_to_all(pieces, ('x', 'yh'), 0, 0)  15.5 us
    ppermute x8, starting transfers between devices, step(): lax.ppermute(array, axes, [(i, (i + by) % size) for i in range(size)])  10.9 us
    pallas_call x1, Pallas kernels, grams(): pl.pallas_call(grams_kernel, out_shape=jax.ShapeDtypeStruct((16, 2, 48, 3...  8.79 us
    all_gather x1, blocking collectives, body(): gathered = lax.all_gather(rows, ('yl', 'core'), tiled=True)  7.65 us
    pallas_call x8, Pallas kernels, unpack(): pl.pallas_call(unpack_kernel, out_shape=BINS, grid=(1,), in_specs=[pl.Blo...  7.45 us
    ppermute x7, waiting for transfers between devices, ring(): return lax.ppermute(array, ('z', 'core'), pairs)  5.24 us
  transfers between devices with their start and end apart: 16, of which 3 were waited for; matrix products, arithmetic and copies ran while one was open for 0% of the time, Pallas kernels for 6%

profile of v6, /device:TPU:1, one launch (start us, length us, event | category | flops | bytes accessed | tf_op | source)
XLA Modules:
  0.0 101.1 jit_solution(10787680718061347758)
XLA Ops:
  0.0 2.3 %split.1 = bf16[8,152,128]{2,1,0:T(8,128)(2,1)} custom-call(bf16[48,24,128]{2,1,0:T(8,128)(2,1)} %bitcast.18, s32[8,16]{1,0:T(8,128)} %bitcast.19, f32[1,128]{1,0:T(1,128)} %bitcast.20), custom_call_target="tpu_custom_call" | custom-call | tf_op jit(solution)/shard_map/split/pallas_call | solution.py:211
  2.3 15.5 %all_to_all.10 = bf16[8,152,128]{2,1,0:T(8,128)(2,1)S(1)} all-to-all(bf16[8,152,128]{2,1,0:T(8,128)(2,1)} %split.1), channel_id=1, replica_groups=mesh['x'=4,'yh'=2,'z'=8,'yl'=2,'core'=2] {'x','yh'}, dimensions={0} | all-to-all | bytes 622592 | tf_op jit(solution)/shard_map/all_to_all | solution.py:219
  17.8 5.7 %collective-permute-start.1 = (bf16[8,144,128]{2,1,0:T(8,128)(2,1)S(1)}, bf16[8,144,128]{2,1,0:T(8,128)(2,1)S(1)}, u32[]{:S(2)}, u32[]{:S(2)}) collective-permute-start(bf16[8,144,128]{2,1,0:T(8,128)(2,1)S(1)} %slice.33.own_ref), channel_id=1, source_target_pairs={{0,4},{1,29},{4,8},{5,1},{8,12},{9,5},{12,16},{13,9},{16,20},{17,1... | collective-permute-start | bytes 884744 | tf_op jit(solution)/shard_map/ppermute | solution.py:169
  23.5 0.2 collective-permute-start.6
  23.7 0.9 collective-permute-start
  24.7 4.3 %collective-permute-done.1.own_ref = bf16[8,144,128]{2,1,0:T(8,128)(2,1)S(1)} collective-permute-done((bf16[8,144,128]{2,1,0:T(8,128)(2,1)S(1)}, bf16[8,144,128]{2,1,0:T(8,128)(2,1)S(1)}, u32[]{:S(2)}, u32[]{:S(2)}) %collective-permute-start.1) | collective-permute-done | bytes 294944 | tf_op jit(solution)/shard_map/ppermute | solution.py:169
  29.0 3.7 %collective-permute-start.14 = (bf16[8,144,128]{2,1,0:T(8,128)(2,1)S(1)}, bf16[8,144,128]{2,1,0:T(8,128)(2,1)S(1)}, u32[]{:S(2)}, u32[]{:S(2)}) collective-permute-start(bf16[8,144,128]{2,1,0:T(8,128)(2,1)S(1)} %collective-permute-done.1.own_ref), channel_id=1, source_target_pairs={{0,1},{1,0},{2,3},{3,2},{4,5},{5,4},{6,7},{7,6},{8,9},{9,8},{10,11... | collective-permute-start | bytes 884744 | tf_op jit(solution)/shard_map/ppermute | solution.py:157
  32.7 2.5 %collective-permute-start.2 = (bf16[8,144,128]{2,1,0:T(8,128)(2,1)S(1)}, bf16[8,144,128]{2,1,0:T(8,128)(2,1)S(1)}, u32[]{:S(2)}, u32[]{:S(2)}) collective-permute-start(bf16[8,144,128]{2,1,0:T(8,128)(2,1)S(1)} %collective-permute-done.1.own_ref), channel_id=1, source_target_pairs={{0,4},{1,29},{4,8},{5,1},{8,12},{9,5},{12,16},{13,9},{16,20},{17,1... | collective-permute-start | bytes 884744 | tf_op jit(solution)/shard_map/ppermute | solution.py:169
  35.2 0.8 collective-permute-start.7
  36.1 0.9 unpack.8.refs_0_
  37.0 0.9 unpack.9.refs_0_
  38.0 0.9 collective-permute-done.2.own_ref
  38.9 3.1 %collective-permute-start.3 = (bf16[8,144,128]{2,1,0:T(8,128)(2,1)S(1)}, bf16[8,144,128]{2,1,0:T(8,128)(2,1)S(1)}, u32[]{:S(2)}, u32[]{:S(2)}) collective-permute-start(bf16[8,144,128]{2,1,0:T(8,128)(2,1)S(1)} %collective-permute-done.2.own_ref), channel_id=1, source_target_pairs={{0,4},{1,29},{4,8},{5,1},{8,12},{9,5},{12,16},{13,9},{16,20},{17,1... | collective-permute-start | bytes 884744 | tf_op jit(solution)/shard_map/ppermute | solution.py:169
  42.1 3.1 %collective-permute-start.8 = (bf16[8,144,128]{2,1,0:T(8,128)(2,1)S(1)}, bf16[8,144,128]{2,1,0:T(8,128)(2,1)S(1)}, u32[]{:S(2)}, u32[]{:S(2)}) collective-permute-start(bf16[8,144,128]{2,1,0:T(8,128)(2,1)S(1)} %collective-permute-done.7.sib_ref), channel_id=1, source_target_pairs={{0,4},{1,29},{4,8},{5,1},{8,12},{9,5},{12,16},{13,9},{16,20},{17,1... | collective-permute-start | bytes 884744 | tf_op jit(solution)/shard_map/ppermute | solution.py:169
  45.2 0.5 collective-permute-start.12
  45.7 0.9 unpack.10.refs_0_
  46.6 2.2 %collective-permute-start.4 = (bf16[8,144,128]{2,1,0:T(8,128)(2,1)S(1)}, bf16[8,144,128]{2,1,0:T(8,128)(2,1)S(1)}, u32[]{:S(2)}, u32[]{:S(2)}) collective-permute-start(bf16[8,144,128]{2,1,0:T(8,128)(2,1)S(1)} %collective-permute-done.3.own_ref), channel_id=1, source_target_pairs={{0,4},{1,29},{4,8},{5,1},{8,12},{9,5},{12,16},{13,9},{16,20},{17,1... | collective-permute-start | bytes 884744 | tf_op jit(solution)/shard_map/ppermute | solution.py:169
  48.8 0.9 unpack.11.refs_0_
  49.8 1.9 %collective-permute-start.9 = (bf16[8,144,128]{2,1,0:T(8,128)(2,1)S(1)}, bf16[8,144,128]{2,1,0:T(8,128)(2,1)S(1)}, u32[]{:S(2)}, u32[]{:S(2)}) collective-permute-start(bf16[8,144,128]{2,1,0:T(8,128)(2,1)S(1)} %collective-permute-done.8.sib_ref), channel_id=1, source_target_pairs={{0,1},{1,0},{2,3},{3,2},{4,5},{5,4},{6,7},{7,6},{8,9},{9,8},{10,11... | collective-permute-start | bytes 884744 | tf_op jit(solution)/shard_map/ppermute | solution.py:157
  51.7 0.9 unpack.12.refs_0_
  52.7 3.8 %collective-permute-start.5 = (bf16[8,144,128]{2,1,0:T(8,128)(2,1)S(1)}, bf16[8,144,128]{2,1,0:T(8,128)(2,1)S(1)}, u32[]{:S(2)}, u32[]{:S(2)}) collective-permute-start(bf16[8,144,128]{2,1,0:T(8,128)(2,1)S(1)} %collective-permute-done.4.own_ref), channel_id=1, source_target_pairs={{0,1},{1,0},{2,3},{3,2},{4,5},{5,4},{6,7},{7,6},{8,9},{9,8},{10,11... | collective-permute-start | bytes 884744 | tf_op jit(solution)/shard_map/ppermute | solution.py:157
  56.5 0.9 unpack.13.refs_0_
  57.5 0.9 unpack.14.refs_0_
  58.4 0.9 unpack.15.bins_ref
  59.4 8.8 %grams.1 = bf16[16,2,48,384]{3,2,1,0:T(8,128)(2,1)} custom-call(s32[64,16]{1,0:T(8,128)S(1)} %fusion.1.triads_ref, bf16[8,128]{1,0:T(8,128)(2,1)S(1)} %slice_bitcast_fusion.1.own_w_ref, bf16[8,128]{1,0:T(8,128)(2,1)S(1)} %slice_bitcast_fusion.sib_w_ref, bf16[512,24,256]{2,1,0:T(8,128)(2,1)S(1)} %unpack.15.bins_ref), custom_call_target="tpu_custom_call" | custom-call | flops 12000000000 | bytes 8000000 | tf_op jit(solution)/shard_map/grams/pallas_call | solution.py:196
  68.2 3.7 %all-to-all-start.1 = ((bf16[16,2,48,384]{3,2,1,0:T(8,128)(2,1)}), bf16[16,2,48,384]{3,2,1,0:T(8,128)(2,1)S(1)}, u32[]{:S(2)}, u32[]{:S(2)}) async-start(bf16[16,2,48,384]{3,2,1,0:T(8,128)(2,1)} %grams.1), calls=%async_computation.1 | async-start | bytes 2359296 | tf_op jit(solution)/shard_map/all_to_all | solution.py:242
  71.9 19.6 %all-to-all-done.1 = bf16[16,2,48,384]{3,2,1,0:T(8,128)(2,1)S(1)} async-done(((bf16[16,2,48,384]{3,2,1,0:T(8,128)(2,1)}), bf16[16,2,48,384]{3,2,1,0:T(8,128)(2,1)S(1)}, u32[]{:S(2)}, u32[]{:S(2)}) %all-to-all-start.1) | async-done | bytes 1179680 | tf_op jit(solution)/shard_map/all_to_all | solution.py:242
  91.7 0.2 copy.14
  91.9 0.3 copy.15
  92.2 0.4 reshape.43
  92.5 7.6 %all_gather.3 = f32[8,1,16,1152]{3,2,1,0:T(8,128)S(1)} all-gather(f32[2,1,16,1152]{3,2,1,0:T(8,128)S(1)} %bitcast.17), channel_id=1, replica_groups=mesh['x'=4,'yh'=2,'z'=8,'yl'=2,'core'=2] {'yl','core'}, dimensions={0}, use_global_device_ids=true | all-gather | bytes 737280 | tf_op jit(solution)/shard_map/all_gather | solution.py:245
  100.2 0.9 broadcast_select_fusion
  (27 shorter events, 0.5 us)
Async XLA Ops:
  17.8 11.1 %collective-permute-start.1 = (bf16[8,144,128]{2,1,0:T(8,128)(2,1)S(1)}, bf16[8,144,128]{2,1,0:T(8,128)(2,1)S(1)}, u32[]{:S(2)}, u32[]{:S(2)}) collective-permute-start(bf16[8,144,128]{2,1,0:T(8,128)(2,1)S(1)} %slice.33.own_ref), channel_id=1, source_target_pairs={{0,4},{1,29},{4,8},{5,1},{8,12},{9,5},{12,16},{13,9},{16,20},{17,1... | collective-permute-start | bytes 884744 | tf_op jit(solution)/shard_map/ppermute | solution.py:169
  23.5 11.7 %collective-permute-start.6 = (bf16[8,144,128]{2,1,0:T(8,128)(2,1)S(1)}, bf16[8,144,128]{2,1,0:T(8,128)(2,1)S(1)}, u32[]{:S(2)}, u32[]{:S(2)}) collective-permute-start(bf16[8,144,128]{2,1,0:T(8,128)(2,1)S(1)} %slice.33.own_ref), channel_id=1, source_target_pairs={{0,29},{1,4},{4,1},{5,8},{8,5},{9,12},{12,9},{13,16},{16,13},{17,2... | collective-permute-start | bytes 884744 | tf_op jit(solution)/shard_map/ppermute | solution.py:169
  23.7 12.4 %collective-permute-start = (bf16[8,152,128]{2,1,0:T(8,128)(2,1)S(1)}, bf16[8,152,128]{2,1,0:T(8,128)(2,1)S(1)}, u32[]{:S(2)}, u32[]{:S(2)}) collective-permute-start(bf16[8,152,128]{2,1,0:T(8,128)(2,1)S(1)} %all_to_all.10), channel_id=1, source_target_pairs={{0,1},{1,0},{2,3},{3,2},{4,5},{5,4},{6,7},{7,6},{8,9},{9,8},{10,11... | collective-permute-start | bytes 933896 | tf_op jit(solution)/shard_map/ppermute | solution.py:157
  29.0 16.7 %collective-permute-start.14 = (bf16[8,144,128]{2,1,0:T(8,128)(2,1)S(1)}, bf16[8,144,128]{2,1,0:T(8,128)(2,1)S(1)}, u32[]{:S(2)}, u32[]{:S(2)}) collective-permute-start(bf16[8,144,128]{2,1,0:T(8,128)(2,1)S(1)} %collective-permute-done.1.own_ref), channel_id=1, source_target_pairs={{0,1},{1,0},{2,3},{3,2},{4,5},{5,4},{6,7},{7,6},{8,9},{9,8},{10,11... | collective-permute-start | bytes 884744 | tf_op jit(solution)/shard_map/ppermute | solution.py:157
  32.7 6.2 %collective-permute-start.2 = (bf16[8,144,128]{2,1,0:T(8,128)(2,1)S(1)}, bf16[8,144,128]{2,1,0:T(8,128)(2,1)S(1)}, u32[]{:S(2)}, u32[]{:S(2)}) collective-permute-start(bf16[8,144,128]{2,1,0:T(8,128)(2,1)S(1)} %collective-permute-done.1.own_ref), channel_id=1, source_target_pairs={{0,4},{1,29},{4,8},{5,1},{8,12},{9,5},{12,16},{13,9},{16,20},{17,1... | collective-permute-start | bytes 884744 | tf_op jit(solution)/shard_map/ppermute | solution.py:169
  35.2 9.9 %collective-permute-start.13 = (bf16[8,144,128]{2,1,0:T(8,128)(2,1)S(1)}, bf16[8,144,128]{2,1,0:T(8,128)(2,1)S(1)}, u32[]{:S(2)}, u32[]{:S(2)}) collective-permute-start(bf16[8,144,128]{2,1,0:T(8,128)(2,1)S(1)} %collective-permute-done.6.sib_ref), channel_id=1, source_target_pairs={{0,1},{1,0},{2,3},{3,2},{4,5},{5,4},{6,7},{7,6},{8,9},{9,8},{10,11... | collective-permute-start | bytes 884744 | tf_op jit(solution)/shard_map/ppermute | solution.py:157
  35.2 6.8 %collective-permute-start.7 = (bf16[8,144,128]{2,1,0:T(8,128)(2,1)S(1)}, bf16[8,144,128]{2,1,0:T(8,128)(2,1)S(1)}, u32[]{:S(2)}, u32[]{:S(2)}) collective-permute-start(bf16[8,144,128]{2,1,0:T(8,128)(2,1)S(1)} %collective-permute-done.6.sib_ref), channel_id=1, source_target_pairs={{0,4},{1,29},{4,8},{5,1},{8,12},{9,5},{12,16},{13,9},{16,20},{17,1... | collective-permute-start | bytes 884744 | tf_op jit(solution)/shard_map/ppermute | solution.py:169
  38.9 7.7 %collective-permute-start.3 = (bf16[8,144,128]{2,1,0:T(8,128)(2,1)S(1)}, bf16[8,144,128]{2,1,0:T(8,128)(2,1)S(1)}, u32[]{:S(2)}, u32[]{:S(2)}) collective-permute-start(bf16[8,144,128]{2,1,0:T(8,128)(2,1)S(1)} %collective-permute-done.2.own_ref), channel_id=1, source_target_pairs={{0,4},{1,29},{4,8},{5,1},{8,12},{9,5},{12,16},{13,9},{16,20},{17,1... | collective-permute-start | bytes 884744 | tf_op jit(solution)/shard_map/ppermute | solution.py:169
  42.1 7.8 %collective-permute-start.8 = (bf16[8,144,128]{2,1,0:T(8,128)(2,1)S(1)}, bf16[8,144,128]{2,1,0:T(8,128)(2,1)S(1)}, u32[]{:S(2)}, u32[]{:S(2)}) collective-permute-start(bf16[8,144,128]{2,1,0:T(8,128)(2,1)S(1)} %collective-permute-done.7.sib_ref), channel_id=1, source_target_pairs={{0,4},{1,29},{4,8},{5,1},{8,12},{9,5},{12,16},{13,9},{16,20},{17,1... | collective-permute-start | bytes 884744 | tf_op jit(solution)/shard_map/ppermute | solution.py:169
  45.2 11.3 %collective-permute-start.11 = (bf16[8,144,128]{2,1,0:T(8,128)(2,1)S(1)}, bf16[8,144,128]{2,1,0:T(8,128)(2,1)S(1)}, u32[]{:S(2)}, u32[]{:S(2)}) collective-permute-start(bf16[8,144,128]{2,1,0:T(8,128)(2,1)S(1)} %collective-permute-done.7.sib_ref), channel_id=1, source_target_pairs={{0,1},{1,0},{2,3},{3,2},{4,5},{5,4},{6,7},{7,6},{8,9},{9,8},{10,11... | collective-permute-start | bytes 884744 | tf_op jit(solution)/shard_map/ppermute | solution.py:157
  45.2 11.3 %collective-permute-start.12 = (bf16[8,144,128]{2,1,0:T(8,128)(2,1)S(1)}, bf16[8,144,128]{2,1,0:T(8,128)(2,1)S(1)}, u32[]{:S(2)}, u32[]{:S(2)}) collective-permute-start(bf16[8,144,128]{2,1,0:T(8,128)(2,1)S(1)} %collective-permute-done.2.own_ref), channel_id=1, source_target_pairs={{0,1},{1,0},{2,3},{3,2},{4,5},{5,4},{6,7},{7,6},{8,9},{9,8},{10,11... | collective-permute-start | bytes 884744 | tf_op jit(solution)/shard_map/ppermute | solution.py:157
  46.6 6.0 %collective-permute-start.4 = (bf16[8,144,128]{2,1,0:T(8,128)(2,1)S(1)}, bf16[8,144,128]{2,1,0:T(8,128)(2,1)S(1)}, u32[]{:S(2)}, u32[]{:S(2)}) collective-permute-start(bf16[8,144,128]{2,1,0:T(8,128)(2,1)S(1)} %collective-permute-done.3.own_ref), channel_id=1, source_target_pairs={{0,4},{1,29},{4,8},{5,1},{8,12},{9,5},{12,16},{13,9},{16,20},{17,1... | collective-permute-start | bytes 884744 | tf_op jit(solution)/shard_map/ppermute | solution.py:169
  49.7 7.7 %collective-permute-start.10 = (bf16[8,144,128]{2,1,0:T(8,128)(2,1)S(1)}, bf16[8,144,128]{2,1,0:T(8,128)(2,1)S(1)}, u32[]{:S(2)}, u32[]{:S(2)}) collective-permute-start(bf16[8,144,128]{2,1,0:T(8,128)(2,1)S(1)} %collective-permute-done.3.own_ref), channel_id=1, source_target_pairs={{0,1},{1,0},{2,3},{3,2},{4,5},{5,4},{6,7},{7,6},{8,9},{9,8},{10,11... | collective-permute-start | bytes 884744 | tf_op jit(solution)/shard_map/ppermute | solution.py:157
  49.8 7.6 %collective-permute-start.9 = (bf16[8,144,128]{2,1,0:T(8,128)(2,1)S(1)}, bf16[8,144,128]{2,1,0:T(8,128)(2,1)S(1)}, u32[]{:S(2)}, u32[]{:S(2)}) collective-permute-start(bf16[8,144,128]{2,1,0:T(8,128)(2,1)S(1)} %collective-permute-done.8.sib_ref), channel_id=1, source_target_pairs={{0,1},{1,0},{2,3},{3,2},{4,5},{5,4},{6,7},{7,6},{8,9},{9,8},{10,11... | collective-permute-start | bytes 884744 | tf_op jit(solution)/shard_map/ppermute | solution.py:157
  52.7 5.7 %collective-permute-start.5 = (bf16[8,144,128]{2,1,0:T(8,128)(2,1)S(1)}, bf16[8,144,128]{2,1,0:T(8,128)(2,1)S(1)}, u32[]{:S(2)}, u32[]{:S(2)}) collective-permute-start(bf16[8,144,128]{2,1,0:T(8,128)(2,1)S(1)} %collective-permute-done.4.own_ref), channel_id=1, source_target_pairs={{0,1},{1,0},{2,3},{3,2},{4,5},{5,4},{6,7},{7,6},{8,9},{9,8},{10,11... | collective-permute-start | bytes 884744 | tf_op jit(solution)/shard_map/ppermute | solution.py:157
  59.4 12.5 %copy-start = (s32[8,1]{0,1:T(1,128)S(1)}, s32[8,1]{0,1:T(1,128)}, u32[]{:S(2)}) copy-start(s32[8,1]{0,1:T(1,128)} %param.7) | copy-start | bytes 100
  68.2 23.4 %all-to-all-start.1 = ((bf16[16,2,48,384]{3,2,1,0:T(8,128)(2,1)}), bf16[16,2,48,384]{3,2,1,0:T(8,128)(2,1)S(1)}, u32[]{:S(2)}, u32[]{:S(2)}) async-start(bf16[16,2,48,384]{3,2,1,0:T(8,128)(2,1)} %grams.1), calls=%async_computation.1 | async-start | bytes 2359296 | tf_op jit(solution)/shard_map/all_to_all | solution.py:242

commit v7 on v6

--- a/solution.py
+++ b/solution.py
@@ -187,7 +187,7 @@
         out_specs=pl.BlockSpec((64, 24, 256), lambda i: (turn, 0, 0)),
         input_output_aliases={} if bins is None else {2: 0},
         compiler_params=params(8),
-        cost_estimate=pl.CostEstimate(flops=3000000000, bytes_accessed=2000000, transcendentals=0),
+        cost_estimate=pl.CostEstimate(flops=1500000000, bytes_accessed=2000000, transcendentals=0),
         name="unpack",
     )(*operands)
 
@@ -229,14 +229,19 @@
         sib.append(ring(sib[-1]))
     near.append(ring(near[-1]))
     bins = unpack(near[0], sib[0], None, 0)
-    passed = [(swap(sib[s]), swap(near[s])) for s in range(1, 4)]
+    passed = []
+    for s in range(1, 4):
+        pair = lax.optimization_barrier((sib[s], near[s]))
+        passed.append((swap(pair[0]), swap(pair[1])))
     bins = unpack(near[1], sib[1], bins, 1)
     bins = unpack(*passed[0], bins, 7)
     bins = unpack(near[2], sib[2], bins, 2)
+    bins = unpack(*passed[1], bins, 6)
     bins = unpack(near[3], sib[3], bins, 3)
-    bins = unpack(*passed[1], bins, 6)
+    last, bins = lax.optimization_barrier((near[4], bins))
+    last_passed = swap(last)
     bins = unpack(*passed[2], bins, 5)
-    bins = unpack(near[4], swap(near[4]), bins, 4)
+    bins = unpack(last, last_passed, bins, 4)
 
     partial = grams(lists, received[0, 144:], beside[0, 144:], bins)
     parts = lax.all_to_all(partial, ("x", "yh", "yl"), 0, 0)

time: 101 us -> 100 us (0.990)
  waiting for transfers between devices: 24.8 us -> 23.7 us
    all_to_all x1, waiting for transfers between devices: 19.6 us -> 18.3 us  [body(): parts = lax.all_to_all(partial, ('x', 'yh', 'yl'), 0, 0)]
  transfers between devices with their start and end apart: 16 -> 16, of which waited for: 3 -> 4; matrix products, arithmetic and copies ran while one was open for 0% -> 0% of each run, Pallas kernels for 6% -> 7%
where the time goes in v7:
time: 100 us; the launch traced here: 99.9 us
  starting transfers between devices  31.4 us (31%)
  blocking collectives  23.9 us (24%)
  waiting for transfers between devices  23.7 us (24%)
  Pallas kernels  18.6 us (19%)
  other arithmetic  1.25 us (1%)
    all_to_all x1, waiting for transfers between devices, body(): parts = lax.all_to_all(partial, ('x', 'yh', 'yl'), 0, 0)  18.3 us
    ppermute x7, starting transfers between devices, ring(): return lax.ppermute(array, ('z', 'core'), pairs)  17.1 us
    all_to_all x1, blocking collectives, body(): received = lax.all_to_all(pieces, ('x', 'yh'), 0, 0)  15.5 us
    ppermute x8, starting transfers between devices, step(): lax.ppermute(array, axes, [(i, (i + by) % size) for i in range(size)])  10.6 us
    pallas_call x1, Pallas kernels, grams(): pl.pallas_call(grams_kernel, out_shape=jax.ShapeDtypeStruct((16, 2, 48, 3...  8.8 us
    all_gather x1, blocking collectives, body(): gathered = lax.all_gather(rows, ('yl', 'core'), tiled=True)  8.37 us
    pallas_call x8, Pallas kernels, unpack(): pl.pallas_call(unpack_kernel, out_shape=BINS, grid=(1,), in_specs=[pl.Blo...  7.47 us
    ppermute x7, waiting for transfers between devices, ring(): return lax.ppermute(array, ('z', 'core'), pairs)  5.15 us
  transfers between devices with their start and end apart: 16, of which 4 were waited for; matrix products, arithmetic and copies ran while one was open for 0% of the time, Pallas kernels for 7%

profile of v7, /device:TPU:1, one launch (start us, length us, event | category | flops | bytes accessed | tf_op | source)
XLA Modules:
  0.0 99.9 jit_solution(15156142174181329577)
XLA Ops:
  0.0 2.3 %split.1 = bf16[8,152,128]{2,1,0:T(8,128)(2,1)} custom-call(bf16[48,24,128]{2,1,0:T(8,128)(2,1)} %bitcast.18, s32[8,16]{1,0:T(8,128)} %bitcast.19, f32[1,128]{1,0:T(1,128)} %bitcast.20), custom_call_target="tpu_custom_call" | custom-call | tf_op jit(solution)/shard_map/split/pallas_call | solution.py:211
  2.3 15.5 %all_to_all.10 = bf16[8,152,128]{2,1,0:T(8,128)(2,1)S(1)} all-to-all(bf16[8,152,128]{2,1,0:T(8,128)(2,1)} %split.1), channel_id=1, replica_groups=mesh['x'=4,'yh'=2,'z'=8,'yl'=2,'core'=2] {'x','yh'}, dimensions={0} | all-to-all | bytes 622592 | tf_op jit(solution)/shard_map/all_to_all | solution.py:219
  17.8 5.7 %collective-permute-start.1 = (bf16[8,144,128]{2,1,0:T(8,128)(2,1)S(1)}, bf16[8,144,128]{2,1,0:T(8,128)(2,1)S(1)}, u32[]{:S(2)}, u32[]{:S(2)}) collective-permute-start(bf16[8,144,128]{2,1,0:T(8,128)(2,1)S(1)} %slice.33.own_ref), channel_id=1, source_target_pairs={{0,4},{1,29},{4,8},{5,1},{8,12},{9,5},{12,16},{13,9},{16,20},{17,1... | collective-permute-start | bytes 884744 | tf_op jit(solution)/shard_map/ppermute | solution.py:169
  23.5 0.2 collective-permute-start.5
  23.7 0.9 collective-permute-start
  24.6 4.4 %collective-permute-done.1.own_ref = bf16[8,144,128]{2,1,0:T(8,128)(2,1)S(1)} collective-permute-done((bf16[8,144,128]{2,1,0:T(8,128)(2,1)S(1)}, bf16[8,144,128]{2,1,0:T(8,128)(2,1)S(1)}, u32[]{:S(2)}, u32[]{:S(2)}) %collective-permute-start.1) | collective-permute-done | bytes 294944 | tf_op jit(solution)/shard_map/ppermute | solution.py:169
  29.0 3.1 %collective-permute-start.2 = (bf16[8,144,128]{2,1,0:T(8,128)(2,1)S(1)}, bf16[8,144,128]{2,1,0:T(8,128)(2,1)S(1)}, u32[]{:S(2)}, u32[]{:S(2)}) collective-permute-start(bf16[8,144,128]{2,1,0:T(8,128)(2,1)S(1)} %collective-permute-done.1.own_ref), channel_id=1, source_target_pairs={{0,4},{1,29},{4,8},{5,1},{8,12},{9,5},{12,16},{13,9},{16,20},{17,1... | collective-permute-start | bytes 884744 | tf_op jit(solution)/shard_map/ppermute | solution.py:169
  32.2 0.7 collective-permute-start.10
  33.0 3.0 %collective-permute-start.6 = (bf16[8,144,128]{2,1,0:T(8,128)(2,1)S(1)}, bf16[8,144,128]{2,1,0:T(8,128)(2,1)S(1)}, u32[]{:S(2)}, u32[]{:S(2)}) collective-permute-start(bf16[8,144,128]{2,1,0:T(8,128)(2,1)S(1)} %collective-permute-done.5.sib_ref), channel_id=1, source_target_pairs={{0,4},{1,29},{4,8},{5,1},{8,12},{9,5},{12,16},{13,9},{16,20},{17,1... | collective-permute-start | bytes 884744 | tf_op jit(solution)/shard_map/ppermute | solution.py:169
  36.0 2.9 %collective-permute-start.3 = (bf16[8,144,128]{2,1,0:T(8,128)(2,1)S(1)}, bf16[8,144,128]{2,1,0:T(8,128)(2,1)S(1)}, u32[]{:S(2)}, u32[]{:S(2)}) collective-permute-start(bf16[8,144,128]{2,1,0:T(8,128)(2,1)S(1)} %collective-permute-done.2.own_ref), channel_id=1, source_target_pairs={{0,4},{1,29},{4,8},{5,1},{8,12},{9,5},{12,16},{13,9},{16,20},{17,1... | collective-permute-start | bytes 884744 | tf_op jit(solution)/shard_map/ppermute | solution.py:169
  38.9 0.9 unpack.8.refs_0_
  39.8 3.9 %collective-permute-start.8 = (bf16[8,144,128]{2,1,0:T(8,128)(2,1)S(1)}, bf16[8,144,128]{2,1,0:T(8,128)(2,1)S(1)}, u32[]{:S(2)}, u32[]{:S(2)}) collective-permute-start(bf16[8,144,128]{2,1,0:T(8,128)(2,1)S(1)} %collective-permute-done.6.sib_ref), channel_id=1, source_target_pairs={{0,1},{1,0},{2,3},{3,2},{4,5},{5,4},{6,7},{7,6},{8,9},{9,8},{10,11... | collective-permute-start | bytes 884744 | tf_op jit(solution)/shard_map/ppermute | solution.py:157
  43.8 1.3 %collective-permute-start.7 = (bf16[8,144,128]{2,1,0:T(8,128)(2,1)S(1)}, bf16[8,144,128]{2,1,0:T(8,128)(2,1)S(1)}, u32[]{:S(2)}, u32[]{:S(2)}) collective-permute-start(bf16[8,144,128]{2,1,0:T(8,128)(2,1)S(1)} %collective-permute-done.6.sib_ref), channel_id=1, source_target_pairs={{0,4},{1,29},{4,8},{5,1},{8,12},{9,5},{12,16},{13,9},{16,20},{17,1... | collective-permute-start | bytes 884744 | tf_op jit(solution)/shard_map/ppermute | solution.py:169
  45.1 0.9 unpack.9.refs_0_
  46.1 0.9 unpack.10.refs_0_
  47.0 0.9 collective-permute-start.4
  47.9 0.9 unpack.11.refs_0_
  48.9 0.8 collective-permute-done.7.sib_ref
  49.7 2.6 %collective-permute-start.13 = (bf16[8,144,128]{2,1,0:T(8,128)(2,1)S(1)}, bf16[8,144,128]{2,1,0:T(8,128)(2,1)S(1)}, u32[]{:S(2)}, u32[]{:S(2)}) collective-permute-start(bf16[8,144,128]{2,1,0:T(8,128)(2,1)S(1)} %collective-permute-done.7.sib_ref), channel_id=1, source_target_pairs={{0,1},{1,0},{2,3},{3,2},{4,5},{5,4},{6,7},{7,6},{8,9},{9,8},{10,11... | collective-permute-start | bytes 884744 | tf_op jit(solution)/shard_map/ppermute | solution.py:157
  52.2 0.9 unpack.12.refs_0_
  53.2 0.9 unpack.13.refs_0_
  54.1 2.4 %collective-permute-start.12 = (bf16[8,144,128]{2,1,0:T(8,128)(2,1)S(1)}, bf16[8,144,128]{2,1,0:T(8,128)(2,1)S(1)}, u32[]{:S(2)}, u32[]{:S(2)}) collective-permute-start(bf16[8,144,128]{2,1,0:T(8,128)(2,1)S(1)} %collective-permute-done.4.own_ref), channel_id=1, source_target_pairs={{0,1},{1,0},{2,3},{3,2},{4,5},{5,4},{6,7},{7,6},{8,9},{9,8},{10,11... | collective-permute-start | bytes 884744 | tf_op jit(solution)/shard_map/ppermute | solution.py:157
  56.5 0.9 unpack.14.refs_0_
  57.4 0.3 collective-permute-done.12.sib_ref
  57.7 0.9 unpack.15.bins_ref
  58.7 8.8 %grams.1 = bf16[16,2,48,384]{3,2,1,0:T(8,128)(2,1)} custom-call(s32[64,16]{1,0:T(8,128)S(1)} %fusion.1.triads_ref, bf16[8,128]{1,0:T(8,128)(2,1)S(1)} %slice_bitcast_fusion.1.own_w_ref, bf16[8,128]{1,0:T(8,128)(2,1)S(1)} %slice_bitcast_fusion.sib_w_ref, bf16[512,24,256]{2,1,0:T(8,128)(2,1)S(1)} %unpack.15.bins_ref), custom_call_target="tpu_custom_call" | custom-call | flops 12000000000 | bytes 8000000 | tf_op jit(solution)/shard_map/grams/pallas_call | solution.py:196
  67.5 3.7 %all-to-all-start.1 = ((bf16[16,2,48,384]{3,2,1,0:T(8,128)(2,1)}), bf16[16,2,48,384]{3,2,1,0:T(8,128)(2,1)S(1)}, u32[]{:S(2)}, u32[]{:S(2)}) async-start(bf16[16,2,48,384]{3,2,1,0:T(8,128)(2,1)} %grams.1), calls=%async_computation.1 | async-start | bytes 2359296 | tf_op jit(solution)/shard_map/all_to_all | solution.py:247
  71.2 18.3 %all-to-all-done.1 = bf16[16,2,48,384]{3,2,1,0:T(8,128)(2,1)S(1)} async-done(((bf16[16,2,48,384]{3,2,1,0:T(8,128)(2,1)}), bf16[16,2,48,384]{3,2,1,0:T(8,128)(2,1)S(1)}, u32[]{:S(2)}, u32[]{:S(2)}) %all-to-all-start.1) | async-done | bytes 1179680 | tf_op jit(solution)/shard_map/all_to_all | solution.py:247
  89.9 0.3 copy.15
  90.2 0.4 reshape.43
  90.6 8.4 %all_gather.3 = f32[8,1,16,1152]{3,2,1,0:T(8,128)S(1)} all-gather(f32[2,1,16,1152]{3,2,1,0:T(8,128)S(1)} %bitcast.17), channel_id=1, replica_groups=mesh['x'=4,'yh'=2,'z'=8,'yl'=2,'core'=2] {'yl','core'}, dimensions={0}, use_global_device_ids=true | all-gather | bytes 737280 | tf_op jit(solution)/shard_map/all_gather | solution.py:250
  98.9 0.9 broadcast_select_fusion
  (27 shorter events, 0.7 us)
Async XLA Ops:
  17.8 11.1 %collective-permute-start.1 = (bf16[8,144,128]{2,1,0:T(8,128)(2,1)S(1)}, bf16[8,144,128]{2,1,0:T(8,128)(2,1)S(1)}, u32[]{:S(2)}, u32[]{:S(2)}) collective-permute-start(bf16[8,144,128]{2,1,0:T(8,128)(2,1)S(1)} %slice.33.own_ref), channel_id=1, source_target_pairs={{0,4},{1,29},{4,8},{5,1},{8,12},{9,5},{12,16},{13,9},{16,20},{17,1... | collective-permute-start | bytes 884744 | tf_op jit(solution)/shard_map/ppermute | solution.py:169
  23.5 8.7 %collective-permute-start.5 = (bf16[8,144,128]{2,1,0:T(8,128)(2,1)S(1)}, bf16[8,144,128]{2,1,0:T(8,128)(2,1)S(1)}, u32[]{:S(2)}, u32[]{:S(2)}) collective-permute-start(bf16[8,144,128]{2,1,0:T(8,128)(2,1)S(1)} %slice.33.own_ref), channel_id=1, source_target_pairs={{0,29},{1,4},{4,1},{5,8},{8,5},{9,12},{12,9},{13,16},{16,13},{17,2... | collective-permute-start | bytes 884744 | tf_op jit(solution)/shard_map/ppermute | solution.py:169
  23.7 12.2 %collective-permute-start = (bf16[8,152,128]{2,1,0:T(8,128)(2,1)S(1)}, bf16[8,152,128]{2,1,0:T(8,128)(2,1)S(1)}, u32[]{:S(2)}, u32[]{:S(2)}) collective-permute-start(bf16[8,152,128]{2,1,0:T(8,128)(2,1)S(1)} %all_to_all.10), channel_id=1, source_target_pairs={{0,1},{1,0},{2,3},{3,2},{4,5},{5,4},{6,7},{7,6},{8,9},{9,8},{10,11... | collective-permute-start | bytes 933896 | tf_op jit(solution)/shard_map/ppermute | solution.py:157
  29.0 7.0 %collective-permute-start.2 = (bf16[8,144,128]{2,1,0:T(8,128)(2,1)S(1)}, bf16[8,144,128]{2,1,0:T(8,128)(2,1)S(1)}, u32[]{:S(2)}, u32[]{:S(2)}) collective-permute-start(bf16[8,144,128]{2,1,0:T(8,128)(2,1)S(1)} %collective-permute-done.1.own_ref), channel_id=1, source_target_pairs={{0,4},{1,29},{4,8},{5,1},{8,12},{9,5},{12,16},{13,9},{16,20},{17,1... | collective-permute-start | bytes 884744 | tf_op jit(solution)/shard_map/ppermute | solution.py:169
  32.2 11.6 %collective-permute-start.10 = (bf16[8,144,128]{2,1,0:T(8,128)(2,1)S(1)}, bf16[8,144,128]{2,1,0:T(8,128)(2,1)S(1)}, u32[]{:S(2)}, u32[]{:S(2)}) collective-permute-start(bf16[8,144,128]{2,1,0:T(8,128)(2,1)S(1)} %collective-permute-done.5.sib_ref), channel_id=1, source_target_pairs={{0,1},{1,0},{2,3},{3,2},{4,5},{5,4},{6,7},{7,6},{8,9},{9,8},{10,11... | collective-permute-start | bytes 884744 | tf_op jit(solution)/shard_map/ppermute | solution.py:157
  32.9 13.2 %collective-permute-start.11 = (bf16[8,144,128]{2,1,0:T(8,128)(2,1)S(1)}, bf16[8,144,128]{2,1,0:T(8,128)(2,1)S(1)}, u32[]{:S(2)}, u32[]{:S(2)}) collective-permute-start(bf16[8,144,128]{2,1,0:T(8,128)(2,1)S(1)} %collective-permute-done.1.own_ref), channel_id=1, source_target_pairs={{0,1},{1,0},{2,3},{3,2},{4,5},{5,4},{6,7},{7,6},{8,9},{9,8},{10,11... | collective-permute-start | bytes 884744 | tf_op jit(solution)/shard_map/ppermute | solution.py:157
  33.0 6.9 %collective-permute-start.6 = (bf16[8,144,128]{2,1,0:T(8,128)(2,1)S(1)}, bf16[8,144,128]{2,1,0:T(8,128)(2,1)S(1)}, u32[]{:S(2)}, u32[]{:S(2)}) collective-permute-start(bf16[8,144,128]{2,1,0:T(8,128)(2,1)S(1)} %collective-permute-done.5.sib_ref), channel_id=1, source_target_pairs={{0,4},{1,29},{4,8},{5,1},{8,12},{9,5},{12,16},{13,9},{16,20},{17,1... | collective-permute-start | bytes 884744 | tf_op jit(solution)/shard_map/ppermute | solution.py:169
  36.0 11.1 %collective-permute-start.3 = (bf16[8,144,128]{2,1,0:T(8,128)(2,1)S(1)}, bf16[8,144,128]{2,1,0:T(8,128)(2,1)S(1)}, u32[]{:S(2)}, u32[]{:S(2)}) collective-permute-start(bf16[8,144,128]{2,1,0:T(8,128)(2,1)S(1)} %collective-permute-done.2.own_ref), channel_id=1, source_target_pairs={{0,4},{1,29},{4,8},{5,1},{8,12},{9,5},{12,16},{13,9},{16,20},{17,1... | collective-permute-start | bytes 884744 | tf_op jit(solution)/shard_map/ppermute | solution.py:169
  39.8 12.4 %collective-permute-start.8 = (bf16[8,144,128]{2,1,0:T(8,128)(2,1)S(1)}, bf16[8,144,128]{2,1,0:T(8,128)(2,1)S(1)}, u32[]{:S(2)}, u32[]{:S(2)}) collective-permute-start(bf16[8,144,128]{2,1,0:T(8,128)(2,1)S(1)} %collective-permute-done.6.sib_ref), channel_id=1, source_target_pairs={{0,1},{1,0},{2,3},{3,2},{4,5},{5,4},{6,7},{7,6},{8,9},{9,8},{10,11... | collective-permute-start | bytes 884744 | tf_op jit(solution)/shard_map/ppermute | solution.py:157
  43.8 8.5 %collective-permute-start.9 = (bf16[8,144,128]{2,1,0:T(8,128)(2,1)S(1)}, bf16[8,144,128]{2,1,0:T(8,128)(2,1)S(1)}, u32[]{:S(2)}, u32[]{:S(2)}) collective-permute-start(bf16[8,144,128]{2,1,0:T(8,128)(2,1)S(1)} %collective-permute-done.2.own_ref), channel_id=1, source_target_pairs={{0,1},{1,0},{2,3},{3,2},{4,5},{5,4},{6,7},{7,6},{8,9},{9,8},{10,11... | collective-permute-start | bytes 884744 | tf_op jit(solution)/shard_map/ppermute | solution.py:157
  43.8 5.9 %collective-permute-start.7 = (bf16[8,144,128]{2,1,0:T(8,128)(2,1)S(1)}, bf16[8,144,128]{2,1,0:T(8,128)(2,1)S(1)}, u32[]{:S(2)}, u32[]{:S(2)}) collective-permute-start(bf16[8,144,128]{2,1,0:T(8,128)(2,1)S(1)} %collective-permute-done.6.sib_ref), channel_id=1, source_target_pairs={{0,4},{1,29},{4,8},{5,1},{8,12},{9,5},{12,16},{13,9},{16,20},{17,1... | collective-permute-start | bytes 884744 | tf_op jit(solution)/shard_map/ppermute | solution.py:169
  47.0 7.1 %collective-permute-start.4 = (bf16[8,144,128]{2,1,0:T(8,128)(2,1)S(1)}, bf16[8,144,128]{2,1,0:T(8,128)(2,1)S(1)}, u32[]{:S(2)}, u32[]{:S(2)}) collective-permute-start(bf16[8,144,128]{2,1,0:T(8,128)(2,1)S(1)} %collective-permute-done.3.own_ref), channel_id=1, source_target_pairs={{0,4},{1,29},{4,8},{5,1},{8,12},{9,5},{12,16},{13,9},{16,20},{17,1... | collective-permute-start | bytes 884744 | tf_op jit(solution)/shard_map/ppermute | solution.py:169
  49.7 6.8 %collective-permute-start.13 = (bf16[8,144,128]{2,1,0:T(8,128)(2,1)S(1)}, bf16[8,144,128]{2,1,0:T(8,128)(2,1)S(1)}, u32[]{:S(2)}, u32[]{:S(2)}) collective-permute-start(bf16[8,144,128]{2,1,0:T(8,128)(2,1)S(1)} %collective-permute-done.7.sib_ref), channel_id=1, source_target_pairs={{0,1},{1,0},{2,3},{3,2},{4,5},{5,4},{6,7},{7,6},{8,9},{9,8},{10,11... | collective-permute-start | bytes 884744 | tf_op jit(solution)/shard_map/ppermute | solution.py:157
  52.2 4.3 %collective-permute-start.14 = (bf16[8,144,128]{2,1,0:T(8,128)(2,1)S(1)}, bf16[8,144,128]{2,1,0:T(8,128)(2,1)S(1)}, u32[]{:S(2)}, u32[]{:S(2)}) collective-permute-start(bf16[8,144,128]{2,1,0:T(8,128)(2,1)S(1)} %collective-permute-done.3.own_ref), channel_id=1, source_target_pairs={{0,1},{1,0},{2,3},{3,2},{4,5},{5,4},{6,7},{7,6},{8,9},{9,8},{10,11... | collective-permute-start | bytes 884744 | tf_op jit(solution)/shard_map/ppermute | solution.py:157
  54.1 3.6 %collective-permute-start.12 = (bf16[8,144,128]{2,1,0:T(8,128)(2,1)S(1)}, bf16[8,144,128]{2,1,0:T(8,128)(2,1)S(1)}, u32[]{:S(2)}, u32[]{:S(2)}) collective-permute-start(bf16[8,144,128]{2,1,0:T(8,128)(2,1)S(1)} %collective-permute-done.4.own_ref), channel_id=1, source_target_pairs={{0,1},{1,0},{2,3},{3,2},{4,5},{5,4},{6,7},{7,6},{8,9},{9,8},{10,11... | collective-permute-start | bytes 884744 | tf_op jit(solution)/shard_map/ppermute | solution.py:157
  58.6 12.5 %copy-start = (s32[8,1]{0,1:T(1,128)S(1)}, s32[8,1]{0,1:T(1,128)}, u32[]{:S(2)}) copy-start(s32[8,1]{0,1:T(1,128)} %param.7) | copy-start | bytes 100
  67.5 22.1 %all-to-all-start.1 = ((bf16[16,2,48,384]{3,2,1,0:T(8,128)(2,1)}), bf16[16,2,48,384]{3,2,1,0:T(8,128)(2,1)S(1)}, u32[]{:S(2)}, u32[]{:S(2)}) async-start(bf16[16,2,48,384]{3,2,1,0:T(8,128)(2,1)} %grams.1), calls=%async_computation.1 | async-start | bytes 2359296 | tf_op jit(solution)/shard_map/all_to_all | solution.py:247

commit v8 on v7

--- a/solution.py
+++ b/solution.py
@@ -245,6 +245,7 @@
 
     partial = grams(lists, received[0, 144:], beside[0, 144:], bins)
     parts = lax.all_to_all(partial, ("x", "yh", "yl"), 0, 0)
+    parts, counts = lax.optimization_barrier((parts, counts))
     summed = jnp.sum(parts.astype(F32), axis=0) / 24
     rows = summed.reshape(2, 48, 16, 24).transpose(0, 2, 1, 3).reshape(2, 1, 16, 1152)
     gathered = lax.all_gather(rows, ("yl", "core"), tiled=True)

time: 100 us -> 97.1 us (0.971)
  blocking collectives: 23.9 us -> 43.9 us
  waiting for transfers between devices: 23.7 us -> 5.42 us
  starting transfers between devices: 31.4 us -> 27.7 us
  Pallas kernels: 18.6 us -> 17.6 us
    all_to_all x0 -> x1, blocking collectives: none -> 20.5 us  [body(): parts = lax.all_to_all(partial, ('x', 'yh', 'yl'), 0, 0)]
    all_to_all x1 -> x0, waiting for transfers between devices: 18.3 us -> none  [body(): parts = lax.all_to_all(partial, ('x', 'yh', 'yl'), 0, 0)]
    all_to_all x1 -> x0, starting transfers between devices: 3.7 us -> none  [body(): parts = lax.all_to_all(partial, ('x', 'yh', 'yl'), 0, 0)]
    pallas_call x1, Pallas kernels: 8.8 us -> 7.78 us  [grams(): pl.pallas_call(grams_kernel, out_shape=jax.ShapeDtypeStruct((16, 2, 48, 3...]
  transfers between devices with their start and end apart: 16 -> 15, of which waited for: 4 -> 3; matrix products, arithmetic and copies ran while one was open for 0% -> 0% of each run, Pallas kernels for 7% -> 7%
where the time goes in v8:
time: 97.1 us; the launch traced here: 96.9 us
  blocking collectives  43.9 us (45%)
  starting transfers between devices  27.7 us (29%)
  Pallas kernels  17.6 us (18%)
  waiting for transfers between devices  5.42 us (6%)
  other arithmetic  1.25 us (1%)
    all_to_all x1, blocking collectives, body(): parts = lax.all_to_all(partial, ('x', 'yh', 'yl'), 0, 0)  20.5 us
    ppermute x7, starting transfers between devices, ring(): return lax.ppermute(array, ('z', 'core'), pairs)  17.1 us
    all_to_all x1, blocking collectives, body(): received = lax.all_to_all(pieces, ('x', 'yh'), 0, 0)  15.5 us
    ppermute x8, starting transfers between devices, step(): lax.ppermute(array, axes, [(i, (i + by) % size) for i in range(size)])  10.6 us
    all_gather x1, blocking collectives, body(): gathered = lax.all_gather(rows, ('yl', 'core'), tiled=True)  7.95 us
    pallas_call x1, Pallas kernels, grams(): pl.pallas_call(grams_kernel, out_shape=jax.ShapeDtypeStruct((16, 2, 48, 3...  7.78 us
    pallas_call x8, Pallas kernels, unpack(): pl.pallas_call(unpack_kernel, out_shape=BINS, grid=(1,), in_specs=[pl.Blo...  7.47 us
    ppermute x7, waiting for transfers between devices, ring(): return lax.ppermute(array, ('z', 'core'), pairs)  5.15 us
  transfers between devices with their start and end apart: 15, of which 3 were waited for; matrix products, arithmetic and copies ran while one was open for 0% of the time, Pallas kernels for 7%

profile of v8, /device:TPU:1, one launch (start us, length us, event | category | flops | bytes accessed | tf_op | source)
XLA Modules:
  0.0 96.9 jit_solution(14516300011741067490)
XLA Ops:
  0.0 2.3 %split.1 = bf16[8,152,128]{2,1,0:T(8,128)(2,1)} custom-call(bf16[48,24,128]{2,1,0:T(8,128)(2,1)} %bitcast.18, s32[8,16]{1,0:T(8,128)} %bitcast.19, f32[1,128]{1,0:T(1,128)} %bitcast.20), custom_call_target="tpu_custom_call" | custom-call | tf_op jit(solution)/shard_map/split/pallas_call | solution.py:211
  2.3 15.5 %all_to_all.10 = bf16[8,152,128]{2,1,0:T(8,128)(2,1)S(1)} all-to-all(bf16[8,152,128]{2,1,0:T(8,128)(2,1)} %split.1), channel_id=1, replica_groups=mesh['x'=4,'yh'=2,'z'=8,'yl'=2,'core'=2] {'x','yh'}, dimensions={0} | all-to-all | bytes 622592 | tf_op jit(solution)/shard_map/all_to_all | solution.py:219
  17.8 5.7 %collective-permute-start.1 = (bf16[8,144,128]{2,1,0:T(8,128)(2,1)S(1)}, bf16[8,144,128]{2,1,0:T(8,128)(2,1)S(1)}, u32[]{:S(2)}, u32[]{:S(2)}) collective-permute-start(bf16[8,144,128]{2,1,0:T(8,128)(2,1)S(1)} %slice.33.own_ref), channel_id=1, source_target_pairs={{0,4},{1,29},{4,8},{5,1},{8,12},{9,5},{12,16},{13,9},{16,20},{17,1... | collective-permute-start | bytes 884744 | tf_op jit(solution)/shard_map/ppermute | solution.py:169
  23.5 0.2 collective-permute-start.5
  23.7 0.9 collective-permute-start
  24.6 4.4 %collective-permute-done.1.own_ref = bf16[8,144,128]{2,1,0:T(8,128)(2,1)S(1)} collective-permute-done((bf16[8,144,128]{2,1,0:T(8,128)(2,1)S(1)}, bf16[8,144,128]{2,1,0:T(8,128)(2,1)S(1)}, u32[]{:S(2)}, u32[]{:S(2)}) %collective-permute-start.1) | collective-permute-done | bytes 294944 | tf_op jit(solution)/shard_map/ppermute | solution.py:169
  29.0 3.1 %collective-permute-start.2 = (bf16[8,144,128]{2,1,0:T(8,128)(2,1)S(1)}, bf16[8,144,128]{2,1,0:T(8,128)(2,1)S(1)}, u32[]{:S(2)}, u32[]{:S(2)}) collective-permute-start(bf16[8,144,128]{2,1,0:T(8,128)(2,1)S(1)} %collective-permute-done.1.own_ref), channel_id=1, source_target_pairs={{0,4},{1,29},{4,8},{5,1},{8,12},{9,5},{12,16},{13,9},{16,20},{17,1... | collective-permute-start | bytes 884744 | tf_op jit(solution)/shard_map/ppermute | solution.py:169
  32.2 0.7 collective-permute-start.10
  33.0 3.0 %collective-permute-start.6 = (bf16[8,144,128]{2,1,0:T(8,128)(2,1)S(1)}, bf16[8,144,128]{2,1,0:T(8,128)(2,1)S(1)}, u32[]{:S(2)}, u32[]{:S(2)}) collective-permute-start(bf16[8,144,128]{2,1,0:T(8,128)(2,1)S(1)} %collective-permute-done.5.sib_ref), channel_id=1, source_target_pairs={{0,4},{1,29},{4,8},{5,1},{8,12},{9,5},{12,16},{13,9},{16,20},{17,1... | collective-permute-start | bytes 884744 | tf_op jit(solution)/shard_map/ppermute | solution.py:169
  36.0 2.9 %collective-permute-start.3 = (bf16[8,144,128]{2,1,0:T(8,128)(2,1)S(1)}, bf16[8,144,128]{2,1,0:T(8,128)(2,1)S(1)}, u32[]{:S(2)}, u32[]{:S(2)}) collective-permute-start(bf16[8,144,128]{2,1,0:T(8,128)(2,1)S(1)} %collective-permute-done.2.own_ref), channel_id=1, source_target_pairs={{0,4},{1,29},{4,8},{5,1},{8,12},{9,5},{12,16},{13,9},{16,20},{17,1... | collective-permute-start | bytes 884744 | tf_op jit(solution)/shard_map/ppermute | solution.py:169
  38.9 0.9 unpack.8.refs_0_
  39.8 3.9 %collective-permute-start.8 = (bf16[8,144,128]{2,1,0:T(8,128)(2,1)S(1)}, bf16[8,144,128]{2,1,0:T(8,128)(2,1)S(1)}, u32[]{:S(2)}, u32[]{:S(2)}) collective-permute-start(bf16[8,144,128]{2,1,0:T(8,128)(2,1)S(1)} %collective-permute-done.6.sib_ref), channel_id=1, source_target_pairs={{0,1},{1,0},{2,3},{3,2},{4,5},{5,4},{6,7},{7,6},{8,9},{9,8},{10,11... | collective-permute-start | bytes 884744 | tf_op jit(solution)/shard_map/ppermute | solution.py:157
  43.8 1.3 %collective-permute-start.7 = (bf16[8,144,128]{2,1,0:T(8,128)(2,1)S(1)}, bf16[8,144,128]{2,1,0:T(8,128)(2,1)S(1)}, u32[]{:S(2)}, u32[]{:S(2)}) collective-permute-start(bf16[8,144,128]{2,1,0:T(8,128)(2,1)S(1)} %collective-permute-done.6.sib_ref), channel_id=1, source_target_pairs={{0,4},{1,29},{4,8},{5,1},{8,12},{9,5},{12,16},{13,9},{16,20},{17,1... | collective-permute-start | bytes 884744 | tf_op jit(solution)/shard_map/ppermute | solution.py:169
  45.1 0.9 unpack.9.refs_0_
  46.1 0.9 unpack.10.refs_0_
  47.0 0.9 collective-permute-start.4
  47.9 0.9 unpack.11.refs_0_
  48.9 0.8 collective-permute-done.7.sib_ref
  49.7 2.6 %collective-permute-start.13 = (bf16[8,144,128]{2,1,0:T(8,128)(2,1)S(1)}, bf16[8,144,128]{2,1,0:T(8,128)(2,1)S(1)}, u32[]{:S(2)}, u32[]{:S(2)}) collective-permute-start(bf16[8,144,128]{2,1,0:T(8,128)(2,1)S(1)} %collective-permute-done.7.sib_ref), channel_id=1, source_target_pairs={{0,1},{1,0},{2,3},{3,2},{4,5},{5,4},{6,7},{7,6},{8,9},{9,8},{10,11... | collective-permute-start | bytes 884744 | tf_op jit(solution)/shard_map/ppermute | solution.py:157
  52.2 0.9 unpack.12.refs_0_
  53.2 0.9 unpack.13.refs_0_
  54.1 2.4 %collective-permute-start.12 = (bf16[8,144,128]{2,1,0:T(8,128)(2,1)S(1)}, bf16[8,144,128]{2,1,0:T(8,128)(2,1)S(1)}, u32[]{:S(2)}, u32[]{:S(2)}) collective-permute-start(bf16[8,144,128]{2,1,0:T(8,128)(2,1)S(1)} %collective-permute-done.4.own_ref), channel_id=1, source_target_pairs={{0,1},{1,0},{2,3},{3,2},{4,5},{5,4},{6,7},{7,6},{8,9},{9,8},{10,11... | collective-permute-start | bytes 884744 | tf_op jit(solution)/shard_map/ppermute | solution.py:157
  56.5 0.9 unpack.14.refs_0_
  57.4 0.3 collective-permute-done.12.sib_ref
  57.7 0.9 unpack.15.bins_ref
  58.6 7.8 %grams.1 = bf16[16,2,48,384]{3,2,1,0:T(8,128)(2,1)S(1)} custom-call(s32[64,16]{1,0:T(8,128)S(1)} %fusion.1.triads_ref, bf16[8,128]{1,0:T(8,128)(2,1)S(1)} %slice_bitcast_fusion.1.own_w_ref, bf16[8,128]{1,0:T(8,128)(2,1)S(1)} %slice_bitcast_fusion.sib_w_ref, bf16[512,24,256]{2,1,0:T(8,128)(2,1)S(1)} %unpack.15.bins_ref), custom_call_target="tpu_custom_call" | custom-call | flops 12000000000 | bytes 8000000 | tf_op jit(solution)/shard_map/grams/pallas_call | solution.py:196
  66.4 20.5 %all_to_all.11 = bf16[16,2,48,384]{3,2,1,0:T(8,128)(2,1)S(1)} all-to-all(bf16[16,2,48,384]{3,2,1,0:T(8,128)(2,1)S(1)} %grams.1), channel_id=1, replica_groups=mesh['x'=4,'yh'=2,'z'=8,'yl'=2,'core'=2] {'x','yh','yl'}, dimensions={0} | all-to-all | bytes 2359296 | tf_op jit(solution)/shard_map/all_to_all | solution.py:247
  87.1 0.2 copy.14
  87.3 0.3 copy.15
  87.6 0.4 reshape.43
  87.9 8.0 %all_gather.3 = f32[8,1,16,1152]{3,2,1,0:T(8,128)S(1)} all-gather(f32[2,1,16,1152]{3,2,1,0:T(8,128)S(1)} %bitcast.17), channel_id=1, replica_groups=mesh['x'=4,'yh'=2,'z'=8,'yl'=2,'core'=2] {'yl','core'}, dimensions={0}, use_global_device_ids=true | all-gather | bytes 737280 | tf_op jit(solution)/shard_map/all_gather | solution.py:251
  96.0 0.9 broadcast_select_fusion
  (26 shorter events, 0.5 us)
Async XLA Ops:
  17.8 11.1 %collective-permute-start.1 = (bf16[8,144,128]{2,1,0:T(8,128)(2,1)S(1)}, bf16[8,144,128]{2,1,0:T(8,128)(2,1)S(1)}, u32[]{:S(2)}, u32[]{:S(2)}) collective-permute-start(bf16[8,144,128]{2,1,0:T(8,128)(2,1)S(1)} %slice.33.own_ref), channel_id=1, source_target_pairs={{0,4},{1,29},{4,8},{5,1},{8,12},{9,5},{12,16},{13,9},{16,20},{17,1... | collective-permute-start | bytes 884744 | tf_op jit(solution)/shard_map/ppermute | solution.py:169
  23.5 8.7 %collective-permute-start.5 = (bf16[8,144,128]{2,1,0:T(8,128)(2,1)S(1)}, bf16[8,144,128]{2,1,0:T(8,128)(2,1)S(1)}, u32[]{:S(2)}, u32[]{:S(2)}) collective-permute-start(bf16[8,144,128]{2,1,0:T(8,128)(2,1)S(1)} %slice.33.own_ref), channel_id=1, source_target_pairs={{0,29},{1,4},{4,1},{5,8},{8,5},{9,12},{12,9},{13,16},{16,13},{17,2... | collective-permute-start | bytes 884744 | tf_op jit(solution)/shard_map/ppermute | solution.py:169
  23.7 12.2 %collective-permute-start = (bf16[8,152,128]{2,1,0:T(8,128)(2,1)S(1)}, bf16[8,152,128]{2,1,0:T(8,128)(2,1)S(1)}, u32[]{:S(2)}, u32[]{:S(2)}) collective-permute-start(bf16[8,152,128]{2,1,0:T(8,128)(2,1)S(1)} %all_to_all.10), channel_id=1, source_target_pairs={{0,1},{1,0},{2,3},{3,2},{4,5},{5,4},{6,7},{7,6},{8,9},{9,8},{10,11... | collective-permute-start | bytes 933896 | tf_op jit(solution)/shard_map/ppermute | solution.py:157
  29.0 7.0 %collective-permute-start.2 = (bf16[8,144,128]{2,1,0:T(8,128)(2,1)S(1)}, bf16[8,144,128]{2,1,0:T(8,128)(2,1)S(1)}, u32[]{:S(2)}, u32[]{:S(2)}) collective-permute-start(bf16[8,144,128]{2,1,0:T(8,128)(2,1)S(1)} %collective-permute-done.1.own_ref), channel_id=1, source_target_pairs={{0,4},{1,29},{4,8},{5,1},{8,12},{9,5},{12,16},{13,9},{16,20},{17,1... | collective-permute-start | bytes 884744 | tf_op jit(solution)/shard_map/ppermute | solution.py:169
  32.2 11.6 %collective-permute-start.10 = (bf16[8,144,128]{2,1,0:T(8,128)(2,1)S(1)}, bf16[8,144,128]{2,1,0:T(8,128)(2,1)S(1)}, u32[]{:S(2)}, u32[]{:S(2)}) collective-permute-start(bf16[8,144,128]{2,1,0:T(8,128)(2,1)S(1)} %collective-permute-done.5.sib_ref), channel_id=1, source_target_pairs={{0,1},{1,0},{2,3},{3,2},{4,5},{5,4},{6,7},{7,6},{8,9},{9,8},{10,11... | collective-permute-start | bytes 884744 | tf_op jit(solution)/shard_map/ppermute | solution.py:157
  32.9 13.2 %collective-permute-start.11 = (bf16[8,144,128]{2,1,0:T(8,128)(2,1)S(1)}, bf16[8,144,128]{2,1,0:T(8,128)(2,1)S(1)}, u32[]{:S(2)}, u32[]{:S(2)}) collective-permute-start(bf16[8,144,128]{2,1,0:T(8,128)(2,1)S(1)} %collective-permute-done.1.own_ref), channel_id=1, source_target_pairs={{0,1},{1,0},{2,3},{3,2},{4,5},{5,4},{6,7},{7,6},{8,9},{9,8},{10,11... | collective-permute-start | bytes 884744 | tf_op jit(solution)/shard_map/ppermute | solution.py:157
  33.0 6.9 %collective-permute-start.6 = (bf16[8,144,128]{2,1,0:T(8,128)(2,1)S(1)}, bf16[8,144,128]{2,1,0:T(8,128)(2,1)S(1)}, u32[]{:S(2)}, u32[]{:S(2)}) collective-permute-start(bf16[8,144,128]{2,1,0:T(8,128)(2,1)S(1)} %collective-permute-done.5.sib_ref), channel_id=1, source_target_pairs={{0,4},{1,29},{4,8},{5,1},{8,12},{9,5},{12,16},{13,9},{16,20},{17,1... | collective-permute-start | bytes 884744 | tf_op jit(solution)/shard_map/ppermute | solution.py:169
  36.0 11.1 %collective-permute-start.3 = (bf16[8,144,128]{2,1,0:T(8,128)(2,1)S(1)}, bf16[8,144,128]{2,1,0:T(8,128)(2,1)S(1)}, u32[]{:S(2)}, u32[]{:S(2)}) collective-permute-start(bf16[8,144,128]{2,1,0:T(8,128)(2,1)S(1)} %collective-permute-done.2.own_ref), channel_id=1, source_target_pairs={{0,4},{1,29},{4,8},{5,1},{8,12},{9,5},{12,16},{13,9},{16,20},{17,1... | collective-permute-start | bytes 884744 | tf_op jit(solution)/shard_map/ppermute | solution.py:169
  39.8 12.4 %collective-permute-start.8 = (bf16[8,144,128]{2,1,0:T(8,128)(2,1)S(1)}, bf16[8,144,128]{2,1,0:T(8,128)(2,1)S(1)}, u32[]{:S(2)}, u32[]{:S(2)}) collective-permute-start(bf16[8,144,128]{2,1,0:T(8,128)(2,1)S(1)} %collective-permute-done.6.sib_ref), channel_id=1, source_target_pairs={{0,1},{1,0},{2,3},{3,2},{4,5},{5,4},{6,7},{7,6},{8,9},{9,8},{10,11... | collective-permute-start | bytes 884744 | tf_op jit(solution)/shard_map/ppermute | solution.py:157
  43.8 8.5 %collective-permute-start.9 = (bf16[8,144,128]{2,1,0:T(8,128)(2,1)S(1)}, bf16[8,144,128]{2,1,0:T(8,128)(2,1)S(1)}, u32[]{:S(2)}, u32[]{:S(2)}) collective-permute-start(bf16[8,144,128]{2,1,0:T(8,128)(2,1)S(1)} %collective-permute-done.2.own_ref), channel_id=1, source_target_pairs={{0,1},{1,0},{2,3},{3,2},{4,5},{5,4},{6,7},{7,6},{8,9},{9,8},{10,11... | collective-permute-start | bytes 884744 | tf_op jit(solution)/shard_map/ppermute | solution.py:157
  43.8 5.9 %collective-permute-start.7 = (bf16[8,144,128]{2,1,0:T(8,128)(2,1)S(1)}, bf16[8,144,128]{2,1,0:T(8,128)(2,1)S(1)}, u32[]{:S(2)}, u32[]{:S(2)}) collective-permute-start(bf16[8,144,128]{2,1,0:T(8,128)(2,1)S(1)} %collective-permute-done.6.sib_ref), channel_id=1, source_target_pairs={{0,4},{1,29},{4,8},{5,1},{8,12},{9,5},{12,16},{13,9},{16,20},{17,1... | collective-permute-start | bytes 884744 | tf_op jit(solution)/shard_map/ppermute | solution.py:169
  47.0 7.1 %collective-permute-start.4 = (bf16[8,144,128]{2,1,0:T(8,128)(2,1)S(1)}, bf16[8,144,128]{2,1,0:T(8,128)(2,1)S(1)}, u32[]{:S(2)}, u32[]{:S(2)}) collective-permute-start(bf16[8,144,128]{2,1,0:T(8,128)(2,1)S(1)} %collective-permute-done.3.own_ref), channel_id=1, source_target_pairs={{0,4},{1,29},{4,8},{5,1},{8,12},{9,5},{12,16},{13,9},{16,20},{17,1... | collective-permute-start | bytes 884744 | tf_op jit(solution)/shard_map/ppermute | solution.py:169
  49.7 6.8 %collective-permute-start.13 = (bf16[8,144,128]{2,1,0:T(8,128)(2,1)S(1)}, bf16[8,144,128]{2,1,0:T(8,128)(2,1)S(1)}, u32[]{:S(2)}, u32[]{:S(2)}) collective-permute-start(bf16[8,144,128]{2,1,0:T(8,128)(2,1)S(1)} %collective-permute-done.7.sib_ref), channel_id=1, source_target_pairs={{0,1},{1,0},{2,3},{3,2},{4,5},{5,4},{6,7},{7,6},{8,9},{9,8},{10,11... | collective-permute-start | bytes 884744 | tf_op jit(solution)/shard_map/ppermute | solution.py:157
  52.2 4.3 %collective-permute-start.14 = (bf16[8,144,128]{2,1,0:T(8,128)(2,1)S(1)}, bf16[8,144,128]{2,1,0:T(8,128)(2,1)S(1)}, u32[]{:S(2)}, u32[]{:S(2)}) collective-permute-start(bf16[8,144,128]{2,1,0:T(8,128)(2,1)S(1)} %collective-permute-done.3.own_ref), channel_id=1, source_target_pairs={{0,1},{1,0},{2,3},{3,2},{4,5},{5,4},{6,7},{7,6},{8,9},{9,8},{10,11... | collective-permute-start | bytes 884744 | tf_op jit(solution)/shard_map/ppermute | solution.py:157
  54.1 3.6 %collective-permute-start.12 = (bf16[8,144,128]{2,1,0:T(8,128)(2,1)S(1)}, bf16[8,144,128]{2,1,0:T(8,128)(2,1)S(1)}, u32[]{:S(2)}, u32[]{:S(2)}) collective-permute-start(bf16[8,144,128]{2,1,0:T(8,128)(2,1)S(1)} %collective-permute-done.4.own_ref), channel_id=1, source_target_pairs={{0,1},{1,0},{2,3},{3,2},{4,5},{5,4},{6,7},{7,6},{8,9},{9,8},{10,11... | collective-permute-start | bytes 884744 | tf_op jit(solution)/shard_map/ppermute | solution.py:157
  66.4 29.5 %copy-start = (s32[8,1]{0,1:T(1,128)S(1)}, s32[8,1]{0,1:T(1,128)}, u32[]{:S(2)}) copy-start(s32[8,1]{0,1:T(1,128)} %param.7) | copy-start | bytes 100

commit v9 on v8

--- a/solution.py
+++ b/solution.py
@@ -41,7 +41,7 @@
     bins_ref = refs[-1]
     lane = lax.broadcasted_iota(jnp.int32, (24, LANES), 1)
 
-    @pl.loop(0, 8)
+    @pl.loop(0, 8, unroll=4)
     def _(column):
         tiles = [
             [ref[column, 24 * q : 24 * q + 24].astype(F32) for q in range(6)]
@@ -134,7 +134,7 @@
     for third in thirds:
         ready(third)
 
-    @pl.loop(0, 16, unroll=2)
+    @pl.loop(0, 16, unroll=8)
     def _(pair):
         for side in range(2):
             reader = 2 * pair + side

time: 97.1 us -> 94.9 us (0.977)
  Pallas kernels: 17.6 us -> 12.3 us
  waiting for transfers between devices: 5.42 us -> 7.33 us
  starting transfers between devices: 27.7 us -> 28.8 us
    pallas_call x8, Pallas kernels: 7.47 us -> 3.99 us  [unpack(): pl.pallas_call(unpack_kernel, out_shape=BINS, grid=(1,), in_specs=[pl.Blo...]
    pallas_call x1, Pallas kernels: 7.78 us -> 5.97 us  [grams(): pl.pallas_call(grams_kernel, out_shape=jax.ShapeDtypeStruct((16, 2, 48, 3...]
    ppermute x7, waiting for transfers between devices: 5.15 us -> 6.63 us  [ring(): return lax.ppermute(array, ('z', 'core'), pairs)]
    ppermute x8, starting transfers between devices: 10.6 us -> 11.7 us  [step(): lax.ppermute(array, axes, [(i, (i + by) % size) for i in range(size)])]
  transfers between devices with their start and end apart: 15 -> 15, of which waited for: 3 -> 4; matrix products, arithmetic and copies ran while one was open for 0% -> 0% of each run, Pallas kernels for 7% -> 4%
where the time goes in v9:
time: 94.9 us; the launch traced here: 94.6 us
  blocking collectives  43.9 us (46%)
  starting transfers between devices  28.8 us (30%)
  Pallas kernels  12.3 us (13%)
  waiting for transfers between devices  7.33 us (8%)
  other arithmetic  1.25 us (1%)
    all_to_all x1, blocking collectives, body(): parts = lax.all_to_all(partial, ('x', 'yh', 'yl'), 0, 0)  20.5 us
    ppermute x7, starting transfers between devices, ring(): return lax.ppermute(array, ('z', 'core'), pairs)  17.1 us
    all_to_all x1, blocking collectives, body(): received = lax.all_to_all(pieces, ('x', 'yh'), 0, 0)  15.5 us
    ppermute x8, starting transfers between devices, step(): lax.ppermute(array, axes, [(i, (i + by) % size) for i in range(size)])  11.7 us
    all_gather x1, blocking collectives, body(): gathered = lax.all_gather(rows, ('yl', 'core'), tiled=True)  7.96 us
    ppermute x7, waiting for transfers between devices, ring(): return lax.ppermute(array, ('z', 'core'), pairs)  6.63 us
    pallas_call x1, Pallas kernels, grams(): pl.pallas_call(grams_kernel, out_shape=jax.ShapeDtypeStruct((16, 2, 48, 3...  5.97 us
    pallas_call x8, Pallas kernels, unpack(): pl.pallas_call(unpack_kernel, out_shape=BINS, grid=(1,), in_specs=[pl.Blo...  3.99 us
  transfers between devices with their start and end apart: 15, of which 4 were waited for; matrix products, arithmetic and copies ran while one was open for 0% of the time, Pallas kernels for 4%

profile of v9, /device:TPU:1, one launch (start us, length us, event | category | flops | bytes accessed | tf_op | source)
XLA Modules:
  0.0 94.6 jit_solution(13162436370098754225)
XLA Ops:
  0.0 2.3 %split.1 = bf16[8,152,128]{2,1,0:T(8,128)(2,1)} custom-call(bf16[48,24,128]{2,1,0:T(8,128)(2,1)} %bitcast.18, s32[8,16]{1,0:T(8,128)} %bitcast.19, f32[1,128]{1,0:T(1,128)} %bitcast.20), custom_call_target="tpu_custom_call" | custom-call | tf_op jit(solution)/shard_map/split/pallas_call | solution.py:211
  2.3 15.5 %all_to_all.10 = bf16[8,152,128]{2,1,0:T(8,128)(2,1)S(1)} all-to-all(bf16[8,152,128]{2,1,0:T(8,128)(2,1)} %split.1), channel_id=1, replica_groups=mesh['x'=4,'yh'=2,'z'=8,'yl'=2,'core'=2] {'x','yh'}, dimensions={0} | all-to-all | bytes 622592 | tf_op jit(solution)/shard_map/all_to_all | solution.py:219
  17.8 5.7 %collective-permute-start.1 = (bf16[8,144,128]{2,1,0:T(8,128)(2,1)S(1)}, bf16[8,144,128]{2,1,0:T(8,128)(2,1)S(1)}, u32[]{:S(2)}, u32[]{:S(2)}) collective-permute-start(bf16[8,144,128]{2,1,0:T(8,128)(2,1)S(1)} %slice.33.own_ref), channel_id=1, source_target_pairs={{0,4},{1,29},{4,8},{5,1},{8,12},{9,5},{12,16},{13,9},{16,20},{17,1... | collective-permute-start | bytes 884744 | tf_op jit(solution)/shard_map/ppermute | solution.py:169
  23.5 0.2 collective-permute-start.5
  23.7 0.9 collective-permute-start
  24.6 4.4 %collective-permute-done.1.own_ref = bf16[8,144,128]{2,1,0:T(8,128)(2,1)S(1)} collective-permute-done((bf16[8,144,128]{2,1,0:T(8,128)(2,1)S(1)}, bf16[8,144,128]{2,1,0:T(8,128)(2,1)S(1)}, u32[]{:S(2)}, u32[]{:S(2)}) %collective-permute-start.1) | collective-permute-done | bytes 294944 | tf_op jit(solution)/shard_map/ppermute | solution.py:169
  29.0 3.1 %collective-permute-start.2 = (bf16[8,144,128]{2,1,0:T(8,128)(2,1)S(1)}, bf16[8,144,128]{2,1,0:T(8,128)(2,1)S(1)}, u32[]{:S(2)}, u32[]{:S(2)}) collective-permute-start(bf16[8,144,128]{2,1,0:T(8,128)(2,1)S(1)} %collective-permute-done.1.own_ref), channel_id=1, source_target_pairs={{0,4},{1,29},{4,8},{5,1},{8,12},{9,5},{12,16},{13,9},{16,20},{17,1... | collective-permute-start | bytes 884744 | tf_op jit(solution)/shard_map/ppermute | solution.py:169
  32.2 0.7 collective-permute-start.10
  33.0 3.0 %collective-permute-start.6 = (bf16[8,144,128]{2,1,0:T(8,128)(2,1)S(1)}, bf16[8,144,128]{2,1,0:T(8,128)(2,1)S(1)}, u32[]{:S(2)}, u32[]{:S(2)}) collective-permute-start(bf16[8,144,128]{2,1,0:T(8,128)(2,1)S(1)} %collective-permute-done.5.sib_ref), channel_id=1, source_target_pairs={{0,4},{1,29},{4,8},{5,1},{8,12},{9,5},{12,16},{13,9},{16,20},{17,1... | collective-permute-start | bytes 884744 | tf_op jit(solution)/shard_map/ppermute | solution.py:169
  36.0 2.9 %collective-permute-start.3 = (bf16[8,144,128]{2,1,0:T(8,128)(2,1)S(1)}, bf16[8,144,128]{2,1,0:T(8,128)(2,1)S(1)}, u32[]{:S(2)}, u32[]{:S(2)}) collective-permute-start(bf16[8,144,128]{2,1,0:T(8,128)(2,1)S(1)} %collective-permute-done.2.own_ref), channel_id=1, source_target_pairs={{0,4},{1,29},{4,8},{5,1},{8,12},{9,5},{12,16},{13,9},{16,20},{17,1... | collective-permute-start | bytes 884744 | tf_op jit(solution)/shard_map/ppermute | solution.py:169
  38.9 0.5 unpack.8.refs_0_
  39.4 0.2 collective-permute-done.6.sib_ref
  39.6 4.2 %collective-permute-start.8 = (bf16[8,144,128]{2,1,0:T(8,128)(2,1)S(1)}, bf16[8,144,128]{2,1,0:T(8,128)(2,1)S(1)}, u32[]{:S(2)}, u32[]{:S(2)}) collective-permute-start(bf16[8,144,128]{2,1,0:T(8,128)(2,1)S(1)} %collective-permute-done.6.sib_ref), channel_id=1, source_target_pairs={{0,1},{1,0},{2,3},{3,2},{4,5},{5,4},{6,7},{7,6},{8,9},{9,8},{10,11... | collective-permute-start | bytes 884744 | tf_op jit(solution)/shard_map/ppermute | solution.py:157
  43.8 1.3 %collective-permute-start.7 = (bf16[8,144,128]{2,1,0:T(8,128)(2,1)S(1)}, bf16[8,144,128]{2,1,0:T(8,128)(2,1)S(1)}, u32[]{:S(2)}, u32[]{:S(2)}) collective-permute-start(bf16[8,144,128]{2,1,0:T(8,128)(2,1)S(1)} %collective-permute-done.6.sib_ref), channel_id=1, source_target_pairs={{0,4},{1,29},{4,8},{5,1},{8,12},{9,5},{12,16},{13,9},{16,20},{17,1... | collective-permute-start | bytes 884744 | tf_op jit(solution)/shard_map/ppermute | solution.py:169
  45.1 0.5 unpack.9.refs_0_
  45.6 0.5 unpack.10.refs_0_
  46.2 0.9 collective-permute-start.4
  47.1 0.5 unpack.11.refs_0_
  47.6 2.1 %collective-permute-done.7.sib_ref = bf16[8,144,128]{2,1,0:T(8,128)(2,1)S(1)} collective-permute-done((bf16[8,144,128]{2,1,0:T(8,128)(2,1)S(1)}, bf16[8,144,128]{2,1,0:T(8,128)(2,1)S(1)}, u32[]{:S(2)}, u32[]{:S(2)}) %collective-permute-start.7) | collective-permute-done | bytes 294944 | tf_op jit(solution)/shard_map/ppermute | solution.py:169
  49.7 2.6 %collective-permute-start.13 = (bf16[8,144,128]{2,1,0:T(8,128)(2,1)S(1)}, bf16[8,144,128]{2,1,0:T(8,128)(2,1)S(1)}, u32[]{:S(2)}, u32[]{:S(2)}) collective-permute-start(bf16[8,144,128]{2,1,0:T(8,128)(2,1)S(1)} %collective-permute-done.7.sib_ref), channel_id=1, source_target_pairs={{0,1},{1,0},{2,3},{3,2},{4,5},{5,4},{6,7},{7,6},{8,9},{9,8},{10,11... | collective-permute-start | bytes 884744 | tf_op jit(solution)/shard_map/ppermute | solution.py:157
  52.2 0.5 unpack.12.refs_0_
  52.7 0.5 unpack.13.refs_0_
  53.3 3.2 %collective-permute-start.12 = (bf16[8,144,128]{2,1,0:T(8,128)(2,1)S(1)}, bf16[8,144,128]{2,1,0:T(8,128)(2,1)S(1)}, u32[]{:S(2)}, u32[]{:S(2)}) collective-permute-start(bf16[8,144,128]{2,1,0:T(8,128)(2,1)S(1)} %collective-permute-done.4.own_ref), channel_id=1, source_target_pairs={{0,1},{1,0},{2,3},{3,2},{4,5},{5,4},{6,7},{7,6},{8,9},{9,8},{10,11... | collective-permute-start | bytes 884744 | tf_op jit(solution)/shard_map/ppermute | solution.py:157
  56.5 0.5 unpack.14.refs_0_
  57.0 0.7 collective-permute-done.12.sib_ref
  57.7 0.5 unpack.15.bins_ref
  58.2 6.0 %grams.1 = bf16[16,2,48,384]{3,2,1,0:T(8,128)(2,1)S(1)} custom-call(s32[64,16]{1,0:T(8,128)S(1)} %fusion.1.triads_ref, bf16[8,128]{1,0:T(8,128)(2,1)S(1)} %slice_bitcast_fusion.1.own_w_ref, bf16[8,128]{1,0:T(8,128)(2,1)S(1)} %slice_bitcast_fusion.sib_w_ref, bf16[512,24,256]{2,1,0:T(8,128)(2,1)S(1)} %unpack.15.bins_ref), custom_call_target="tpu_custom_call" | custom-call | flops 12000000000 | bytes 8000000 | tf_op jit(solution)/shard_map/grams/pallas_call | solution.py:196
  64.2 20.5 %all_to_all.11 = bf16[16,2,48,384]{3,2,1,0:T(8,128)(2,1)S(1)} all-to-all(bf16[16,2,48,384]{3,2,1,0:T(8,128)(2,1)S(1)} %grams.1), channel_id=1, replica_groups=mesh['x'=4,'yh'=2,'z'=8,'yl'=2,'core'=2] {'x','yh','yl'}, dimensions={0} | all-to-all | bytes 2359296 | tf_op jit(solution)/shard_map/all_to_all | solution.py:247
  85.0 0.3 copy.15
  85.3 0.4 reshape.43
  85.7 8.0 %all_gather.3 = f32[8,1,16,1152]{3,2,1,0:T(8,128)S(1)} all-gather(f32[2,1,16,1152]{3,2,1,0:T(8,128)S(1)} %bitcast.17), channel_id=1, replica_groups=mesh['x'=4,'yh'=2,'z'=8,'yl'=2,'core'=2] {'yl','core'}, dimensions={0}, use_global_device_ids=true | all-gather | bytes 737280 | tf_op jit(solution)/shard_map/all_gather | solution.py:251
  93.7 0.9 broadcast_select_fusion
  (26 shorter events, 0.7 us)
Async XLA Ops:
  17.8 11.1 %collective-permute-start.1 = (bf16[8,144,128]{2,1,0:T(8,128)(2,1)S(1)}, bf16[8,144,128]{2,1,0:T(8,128)(2,1)S(1)}, u32[]{:S(2)}, u32[]{:S(2)}) collective-permute-start(bf16[8,144,128]{2,1,0:T(8,128)(2,1)S(1)} %slice.33.own_ref), channel_id=1, source_target_pairs={{0,4},{1,29},{4,8},{5,1},{8,12},{9,5},{12,16},{13,9},{16,20},{17,1... | collective-permute-start | bytes 884744 | tf_op jit(solution)/shard_map/ppermute | solution.py:169
  23.5 8.7 %collective-permute-start.5 = (bf16[8,144,128]{2,1,0:T(8,128)(2,1)S(1)}, bf16[8,144,128]{2,1,0:T(8,128)(2,1)S(1)}, u32[]{:S(2)}, u32[]{:S(2)}) collective-permute-start(bf16[8,144,128]{2,1,0:T(8,128)(2,1)S(1)} %slice.33.own_ref), channel_id=1, source_target_pairs={{0,29},{1,4},{4,1},{5,8},{8,5},{9,12},{12,9},{13,16},{16,13},{17,2... | collective-permute-start | bytes 884744 | tf_op jit(solution)/shard_map/ppermute | solution.py:169
  23.7 12.2 %collective-permute-start = (bf16[8,152,128]{2,1,0:T(8,128)(2,1)S(1)}, bf16[8,152,128]{2,1,0:T(8,128)(2,1)S(1)}, u32[]{:S(2)}, u32[]{:S(2)}) collective-permute-start(bf16[8,152,128]{2,1,0:T(8,128)(2,1)S(1)} %all_to_all.10), channel_id=1, source_target_pairs={{0,1},{1,0},{2,3},{3,2},{4,5},{5,4},{6,7},{7,6},{8,9},{9,8},{10,11... | collective-permute-start | bytes 933896 | tf_op jit(solution)/shard_map/ppermute | solution.py:157
  29.0 7.0 %collective-permute-start.2 = (bf16[8,144,128]{2,1,0:T(8,128)(2,1)S(1)}, bf16[8,144,128]{2,1,0:T(8,128)(2,1)S(1)}, u32[]{:S(2)}, u32[]{:S(2)}) collective-permute-start(bf16[8,144,128]{2,1,0:T(8,128)(2,1)S(1)} %collective-permute-done.1.own_ref), channel_id=1, source_target_pairs={{0,4},{1,29},{4,8},{5,1},{8,12},{9,5},{12,16},{13,9},{16,20},{17,1... | collective-permute-start | bytes 884744 | tf_op jit(solution)/shard_map/ppermute | solution.py:169
  32.2 11.6 %collective-permute-start.10 = (bf16[8,144,128]{2,1,0:T(8,128)(2,1)S(1)}, bf16[8,144,128]{2,1,0:T(8,128)(2,1)S(1)}, u32[]{:S(2)}, u32[]{:S(2)}) collective-permute-start(bf16[8,144,128]{2,1,0:T(8,128)(2,1)S(1)} %collective-permute-done.5.sib_ref), channel_id=1, source_target_pairs={{0,1},{1,0},{2,3},{3,2},{4,5},{5,4},{6,7},{7,6},{8,9},{9,8},{10,11... | collective-permute-start | bytes 884744 | tf_op jit(solution)/shard_map/ppermute | solution.py:157
  32.9 12.8 %collective-permute-start.11 = (bf16[8,144,128]{2,1,0:T(8,128)(2,1)S(1)}, bf16[8,144,128]{2,1,0:T(8,128)(2,1)S(1)}, u32[]{:S(2)}, u32[]{:S(2)}) collective-permute-start(bf16[8,144,128]{2,1,0:T(8,128)(2,1)S(1)} %collective-permute-done.1.own_ref), channel_id=1, source_target_pairs={{0,1},{1,0},{2,3},{3,2},{4,5},{5,4},{6,7},{7,6},{8,9},{9,8},{10,11... | collective-permute-start | bytes 884744 | tf_op jit(solution)/shard_map/ppermute | solution.py:157
  33.0 6.6 %collective-permute-start.6 = (bf16[8,144,128]{2,1,0:T(8,128)(2,1)S(1)}, bf16[8,144,128]{2,1,0:T(8,128)(2,1)S(1)}, u32[]{:S(2)}, u32[]{:S(2)}) collective-permute-start(bf16[8,144,128]{2,1,0:T(8,128)(2,1)S(1)} %collective-permute-done.5.sib_ref), channel_id=1, source_target_pairs={{0,4},{1,29},{4,8},{5,1},{8,12},{9,5},{12,16},{13,9},{16,20},{17,1... | collective-permute-start | bytes 884744 | tf_op jit(solution)/shard_map/ppermute | solution.py:169
  36.0 10.2 %collective-permute-start.3 = (bf16[8,144,128]{2,1,0:T(8,128)(2,1)S(1)}, bf16[8,144,128]{2,1,0:T(8,128)(2,1)S(1)}, u32[]{:S(2)}, u32[]{:S(2)}) collective-permute-start(bf16[8,144,128]{2,1,0:T(8,128)(2,1)S(1)} %collective-permute-done.2.own_ref), channel_id=1, source_target_pairs={{0,4},{1,29},{4,8},{5,1},{8,12},{9,5},{12,16},{13,9},{16,20},{17,1... | collective-permute-start | bytes 884744 | tf_op jit(solution)/shard_map/ppermute | solution.py:169
  39.6 12.7 %collective-permute-start.8 = (bf16[8,144,128]{2,1,0:T(8,128)(2,1)S(1)}, bf16[8,144,128]{2,1,0:T(8,128)(2,1)S(1)}, u32[]{:S(2)}, u32[]{:S(2)}) collective-permute-start(bf16[8,144,128]{2,1,0:T(8,128)(2,1)S(1)} %collective-permute-done.6.sib_ref), channel_id=1, source_target_pairs={{0,1},{1,0},{2,3},{3,2},{4,5},{5,4},{6,7},{7,6},{8,9},{9,8},{10,11... | collective-permute-start | bytes 884744 | tf_op jit(solution)/shard_map/ppermute | solution.py:157
  43.8 8.5 %collective-permute-start.9 = (bf16[8,144,128]{2,1,0:T(8,128)(2,1)S(1)}, bf16[8,144,128]{2,1,0:T(8,128)(2,1)S(1)}, u32[]{:S(2)}, u32[]{:S(2)}) collective-permute-start(bf16[8,144,128]{2,1,0:T(8,128)(2,1)S(1)} %collective-permute-done.2.own_ref), channel_id=1, source_target_pairs={{0,1},{1,0},{2,3},{3,2},{4,5},{5,4},{6,7},{7,6},{8,9},{9,8},{10,11... | collective-permute-start | bytes 884744 | tf_op jit(solution)/shard_map/ppermute | solution.py:157
  43.8 5.9 %collective-permute-start.7 = (bf16[8,144,128]{2,1,0:T(8,128)(2,1)S(1)}, bf16[8,144,128]{2,1,0:T(8,128)(2,1)S(1)}, u32[]{:S(2)}, u32[]{:S(2)}) collective-permute-start(bf16[8,144,128]{2,1,0:T(8,128)(2,1)S(1)} %collective-permute-done.6.sib_ref), channel_id=1, source_target_pairs={{0,4},{1,29},{4,8},{5,1},{8,12},{9,5},{12,16},{13,9},{16,20},{17,1... | collective-permute-start | bytes 884744 | tf_op jit(solution)/shard_map/ppermute | solution.py:169
  46.2 7.1 %collective-permute-start.4 = (bf16[8,144,128]{2,1,0:T(8,128)(2,1)S(1)}, bf16[8,144,128]{2,1,0:T(8,128)(2,1)S(1)}, u32[]{:S(2)}, u32[]{:S(2)}) collective-permute-start(bf16[8,144,128]{2,1,0:T(8,128)(2,1)S(1)} %collective-permute-done.3.own_ref), channel_id=1, source_target_pairs={{0,4},{1,29},{4,8},{5,1},{8,12},{9,5},{12,16},{13,9},{16,20},{17,1... | collective-permute-start | bytes 884744 | tf_op jit(solution)/shard_map/ppermute | solution.py:169
  49.7 6.8 %collective-permute-start.13 = (bf16[8,144,128]{2,1,0:T(8,128)(2,1)S(1)}, bf16[8,144,128]{2,1,0:T(8,128)(2,1)S(1)}, u32[]{:S(2)}, u32[]{:S(2)}) collective-permute-start(bf16[8,144,128]{2,1,0:T(8,128)(2,1)S(1)} %collective-permute-done.7.sib_ref), channel_id=1, source_target_pairs={{0,1},{1,0},{2,3},{3,2},{4,5},{5,4},{6,7},{7,6},{8,9},{9,8},{10,11... | collective-permute-start | bytes 884744 | tf_op jit(solution)/shard_map/ppermute | solution.py:157
  52.2 4.3 %collective-permute-start.14 = (bf16[8,144,128]{2,1,0:T(8,128)(2,1)S(1)}, bf16[8,144,128]{2,1,0:T(8,128)(2,1)S(1)}, u32[]{:S(2)}, u32[]{:S(2)}) collective-permute-start(bf16[8,144,128]{2,1,0:T(8,128)(2,1)S(1)} %collective-permute-done.3.own_ref), channel_id=1, source_target_pairs={{0,1},{1,0},{2,3},{3,2},{4,5},{5,4},{6,7},{7,6},{8,9},{9,8},{10,11... | collective-permute-start | bytes 884744 | tf_op jit(solution)/shard_map/ppermute | solution.py:157
  53.3 4.4 %collective-permute-start.12 = (bf16[8,144,128]{2,1,0:T(8,128)(2,1)S(1)}, bf16[8,144,128]{2,1,0:T(8,128)(2,1)S(1)}, u32[]{:S(2)}, u32[]{:S(2)}) collective-permute-start(bf16[8,144,128]{2,1,0:T(8,128)(2,1)S(1)} %collective-permute-done.4.own_ref), channel_id=1, source_target_pairs={{0,1},{1,0},{2,3},{3,2},{4,5},{5,4},{6,7},{7,6},{8,9},{9,8},{10,11... | collective-permute-start | bytes 884744 | tf_op jit(solution)/shard_map/ppermute | solution.py:157
  64.2 29.5 %copy-start = (s32[8,1]{0,1:T(1,128)S(1)}, s32[8,1]{0,1:T(1,128)}, u32[]{:S(2)}) copy-start(s32[8,1]{0,1:T(1,128)} %param.7) | copy-start | bytes 100

commit v10 on v9

--- a/solution.py
+++ b/solution.py
@@ -37,29 +37,30 @@
         out_ref[piece, 144:152] = jnp.concatenate(tile, axis=1).astype(BF16)
 
 
-def unpack_kernel(own_ref, sib_ref, *refs):
+def unpack_kernel(*refs):
     bins_ref = refs[-1]
     lane = lax.broadcasted_iota(jnp.int32, (24, LANES), 1)
-
-    @pl.loop(0, 8, unroll=4)
-    def _(column):
-        tiles = [
-            [ref[column, 24 * q : 24 * q + 24].astype(F32) for q in range(6)]
-            for ref in (own_ref, sib_ref)
-        ]
-        for r in range(8):
-            for part in range(2):
-                q, offset = divmod(96 * r + 48 * part, LANES)
-                halves = []
-                for core in range(2):
-                    picked = tiles[core][q]
-                    if offset + 48 > LANES:
-                        picked = jnp.where(lane >= offset, picked, tiles[core][q + 1])
-                    shift = (48 * core - offset) % LANES
-                    halves.append(pltpu.roll(picked, shift, 1) if shift else picked)
-                merged = jnp.where(lane < 48, halves[0], halves[1])
-                lanes = slice(LANES * part, LANES * (part + 1))
-                bins_ref[column * 8 + r, :, lanes] = merged.astype(BF16)
+    for half in range(2):
+
+        @pl.loop(0, 4, unroll=2)
+        def _(column, half=half):
+            tiles = [
+                [ref[column, 24 * q : 24 * q + 24].astype(F32) for q in range(6)]
+                for ref in (refs[half], refs[2 + half])
+            ]
+            for r in range(8):
+                for part in range(2):
+                    q, offset = divmod(96 * r + 48 * part, LANES)
+                    pair = []
+                    for core in range(2):
+                        picked = tiles[core][q]
+                        if offset + 48 > LANES:
+                            picked = jnp.where(lane >= offset, picked, tiles[core][q + 1])
+                        shift = (48 * core - offset) % LANES
+                        pair.append(pltpu.roll(picked, shift, 1) if shift else picked)
+                    merged = jnp.where(lane < 48, pair[0], pair[1])
+                    lanes = slice(LANES * part, LANES * (part + 1))
+                    bins_ref[(half * 4 + column) * 8 + r, :, lanes] = merged.astype(BF16)
 
 
 def lane_weights(own_ref, sib_ref):
@@ -78,10 +79,9 @@
 def grams_kernel(triads_ref, own_w_ref, sib_w_ref, bins_ref, out_ref, *scratch):
     buffers = (scratch[0:2], scratch[2:4])
     depth, core = lax.axis_index("z"), lax.axis_index("core")
-    up = 1 - 2 * core
 
     def slot(which):
-        turn = (up * (depth - (which & 7))) & 7
+        turn = (depth - (which & 7)) & 7
         return turn * 64 + (which & 56) + (which >> 6)
 
     weights = lane_weights(own_w_ref, sib_w_ref)
@@ -161,14 +161,6 @@
     return step(array, "core", 1)
 
 
-def ring(array, crossed=False):
-    pairs = []
-    for z in range(8):
-        up, down = (2 * z + 2) % 16, (2 * z - 2) % 16 + 1
-        pairs += [(2 * z, down), (2 * z + 1, up)] if crossed else [(2 * z, up), (2 * z + 1, down)]
-    return lax.ppermute(array, ("z", "core"), pairs)
-
-
 def params(mib):
     return pltpu.CompilerParams(vmem_limit_bytes=mib * MIB)
 
@@ -176,16 +168,16 @@
 BINS = jax.ShapeDtypeStruct((512, 24, 256), BF16)
 
 
-def unpack(own, sib, bins, turn):
-    operands = [own, sib] + ([] if bins is None else [bins])
+def unpack(parts, bins, turn):
+    specs = [pl.BlockSpec((4, 144, LANES), lambda i, at=at: (at, 0, 0)) for _, at in parts]
+    operands = [array for array, _ in parts] + ([] if bins is None else [bins])
     return pl.pallas_call(
         unpack_kernel,
         out_shape=BINS,
         grid=(1,),
-        in_specs=[pl.BlockSpec((8, 144, LANES), lambda i: (0, 0, 0))] * 2
-        + [pl.BlockSpec(memory_space=pl.ANY)] * (len(operands) - 2),
+        in_specs=specs + [pl.BlockSpec(memory_space=pl.ANY)] * (len(operands) - 4),
         out_specs=pl.BlockSpec((64, 24, 256), lambda i: (turn, 0, 0)),
-        input_output_aliases={} if bins is None else {2: 0},
+        input_output_aliases={} if bins is None else {4: 0},
         compiler_params=params(8),
         cost_estimate=pl.CostEstimate(flops=1500000000, bytes_accessed=2000000, transcendentals=0),
         name="unpack",
@@ -221,27 +213,24 @@
     lists = (codes[:, :, :16] * 64 + codes[:, :, 16:]).astype(jnp.int32).reshape(64, 16)
 
     beside = swap(received)
-    near, sib = [received[:, :144]], [beside[:, :144]]
-    near.append(ring(near[0]))
-    sib.append(ring(near[0], crossed=True))
-    for _ in range(2):
-        near.append(ring(near[-1]))
-        sib.append(ring(sib[-1]))
-    near.append(ring(near[-1]))
-    bins = unpack(near[0], sib[0], None, 0)
+    own, sib = received[:, :144], beside[:, :144]
+    up, down = [[own[:4], own[4:]]], [[own[:4], own[4:]]]
     passed = []
-    for s in range(1, 4):
-        pair = lax.optimization_barrier((sib[s], near[s]))
-        passed.append((swap(pair[0]), swap(pair[1])))
-    bins = unpack(near[1], sib[1], bins, 1)
-    bins = unpack(*passed[0], bins, 7)
-    bins = unpack(near[2], sib[2], bins, 2)
-    bins = unpack(*passed[1], bins, 6)
-    bins = unpack(near[3], sib[3], bins, 3)
-    last, bins = lax.optimization_barrier((near[4], bins))
-    last_passed = swap(last)
-    bins = unpack(*passed[2], bins, 5)
-    bins = unpack(last, last_passed, bins, 4)
+    for s in range(3):
+        up.append([step(part, "z", 1) for part in up[s]])
+        down.append([step(part, "z", -1) for part in down[s]])
+        passed.append(swap(jnp.concatenate(up[-1] + down[-1])))
+    far = [step(up[3][0], "z", 1), step(down[3][1], "z", -1)]
+    bins = unpack([(own, 0), (own, 1), (sib, 0), (sib, 1)], None, 0)
+    for s in range(3):
+        if s == 2:
+            far[0], far[1], bins = lax.optimization_barrier((far[0], far[1], bins))
+            last = swap(jnp.concatenate(far))
+        mine, theirs = up[s + 1] + down[s + 1], passed[s]
+        for way, turn in ((0, s + 1), (2, 7 - s)):
+            operands = [(mine[way], 0), (mine[way + 1], 0), (theirs, way), (theirs, way + 1)]
+            bins = unpack(operands, bins, turn)
+    bins = unpack([(far[0], 0), (far[1], 0), (last, 0), (last, 1)], bins, 4)
 
     partial = grams(lists, received[0, 144:], beside[0, 144:], bins)
     parts = lax.all_to_all(partial, ("x", "yh", "yl"), 0, 0)

time: 94.9 us -> 103 us (1.085)
  starting transfers between devices: 28.8 us -> 33 us
  waiting for transfers between devices: 7.33 us -> 9.84 us
  Pallas kernels: 12.3 us -> 13.6 us
    ppermute x8 -> x19, starting transfers between devices: 11.7 us -> 33 us  [step(): lax.ppermute(array, axes, [(i, (i + by) % size) for i in range(size)])]
    ppermute x7 -> x0, starting transfers between devices: 17.1 us -> none  [ring(): return lax.ppermute(array, ('z', 'core'), pairs)]
    ppermute x8 -> x19, waiting for transfers between devices: 0.7 us -> 9.84 us  [step(): lax.ppermute(array, axes, [(i, (i + by) % size) for i in range(size)])]
    ppermute x7 -> x0, waiting for transfers between devices: 6.63 us -> none  [ring(): return lax.ppermute(array, ('z', 'core'), pairs)]
    pallas_call x8, Pallas kernels: 3.99 us -> 5.16 us  [unpack(): pl.pallas_call(unpack_kernel, out_shape=BINS, grid=(1,), in_specs=specs +...]
  transfers between devices with their start and end apart: 15 -> 19, of which waited for: 4 -> 5; matrix products, arithmetic and copies ran while one was open for 0% -> 0% of each run, Pallas kernels for 4% -> 4%
where the time goes in v10:
time: 103 us
  blocking collectives  43.9 us (43%)
  starting transfers between devices  33 us (32%)
  Pallas kernels  13.6 us (13%)
  waiting for transfers between devices  9.84 us (10%)
  other arithmetic  1.51 us (1%)
    ppermute x19, starting transfers between devices, step(): lax.ppermute(array, axes, [(i, (i + by) % size) for i in range(size)])  33 us
    all_to_all x1, blocking collectives, body(): parts = lax.all_to_all(partial, ('x', 'yh', 'yl'), 0, 0)  20.4 us
    all_to_all x1, blocking collectives, body(): received = lax.all_to_all(pieces, ('x', 'yh'), 0, 0)  15.5 us
    ppermute x19, waiting for transfers between devices, step(): lax.ppermute(array, axes, [(i, (i + by) % size) for i in range(size)])  9.84 us
    all_gather x1, blocking collectives, body(): gathered = lax.all_gather(rows, ('yl', 'core'), tiled=True)  8.04 us
    pallas_call x1, Pallas kernels, grams(): pl.pallas_call(grams_kernel, out_shape=jax.ShapeDtypeStruct((16, 2, 48, 3...  6.11 us
    pallas_call x8, Pallas kernels, unpack(): pl.pallas_call(unpack_kernel, out_shape=BINS, grid=(1,), in_specs=specs +...  5.16 us
    pallas_call x1, Pallas kernels, body(): pl.pallas_call(split_kernel, out_shape=jax.ShapeDtypeStruct((8, 152, LANE...  2.31 us
  transfers between devices with their start and end apart: 19, of which 5 were waited for; matrix products, arithmetic and copies ran while one was open for 0% of the time, Pallas kernels for 4%

profile of v10, /device:TPU:1, one launch (start us, length us, event | category | flops | bytes accessed | tf_op | source)
XLA Modules:
  0.0 102.9 jit_solution(13279078912933105864)
XLA Ops:
  0.0 2.3 %split.1 = bf16[8,152,128]{2,1,0:T(8,128)(2,1)} custom-call(bf16[48,24,128]{2,1,0:T(8,128)(2,1)} %bitcast.18, s32[8,16]{1,0:T(8,128)} %bitcast.19, f32[1,128]{1,0:T(1,128)} %bitcast.20), custom_call_target="tpu_custom_call" | custom-call | tf_op jit(solution)/shard_map/split/pallas_call | solution.py:203
  2.3 15.5 %all_to_all.10 = bf16[8,152,128]{2,1,0:T(8,128)(2,1)S(1)} all-to-all(bf16[8,152,128]{2,1,0:T(8,128)(2,1)} %split.1), channel_id=1, replica_groups=mesh['x'=4,'yh'=2,'z'=8,'yl'=2,'core'=2] {'x','yh'}, dimensions={0} | all-to-all | bytes 622592 | tf_op jit(solution)/shard_map/all_to_all | solution.py:211
  17.8 1.7 %collective-permute-start.11 = (bf16[4,144,128]{2,1,0:T(8,128)(2,1)S(1)}, bf16[4,144,128]{2,1,0:T(8,128)(2,1)S(1)}, u32[]{:S(2)}, u32[]{:S(2)}) collective-permute-start(bf16[4,144,128]{2,1,0:T(8,128)(2,1)S(1)} %get-tuple-element.15), channel_id=1, source_target_pairs={{0,4},{4,8},{8,12},{12,16},{16,20},{20,24},{24,28},{28,0},{1,5},{5... | collective-permute-start | bytes 442376 | tf_op jit(solution)/shard_map/ppermute | solution.py:157
  19.6 4.0 %collective-permute-start.5 = (bf16[4,144,128]{2,1,0:T(8,128)(2,1)S(1)}, bf16[4,144,128]{2,1,0:T(8,128)(2,1)S(1)}, u32[]{:S(2)}, u32[]{:S(2)}) collective-permute-start(bf16[4,144,128]{2,1,0:T(8,128)(2,1)S(1)} %get-tuple-element.15), channel_id=1, source_target_pairs={{0,28},{4,0},{8,4},{12,8},{16,12},{20,16},{24,20},{28,24},{1,29},{... | collective-permute-start | bytes 442376 | tf_op jit(solution)/shard_map/ppermute | solution.py:157
  23.6 2.7 %collective-permute-start.9 = (bf16[4,144,128]{2,1,0:T(8,128)(2,1)S(1)}, bf16[4,144,128]{2,1,0:T(8,128)(2,1)S(1)}, u32[]{:S(2)}, u32[]{:S(2)}) collective-permute-start(bf16[4,144,128]{2,1,0:T(8,128)(2,1)S(1)} %get-tuple-element.16), channel_id=1, source_target_pairs={{0,28},{4,0},{8,4},{12,8},{16,12},{20,16},{24,20},{28,24},{1,29},{... | collective-permute-start | bytes 442376 | tf_op jit(solution)/shard_map/ppermute | solution.py:157
  26.3 3.2 %collective-permute-start = (bf16[8,152,128]{2,1,0:T(8,128)(2,1)S(1)}, bf16[8,152,128]{2,1,0:T(8,128)(2,1)S(1)}, u32[]{:S(2)}, u32[]{:S(2)}) collective-permute-start(bf16[8,152,128]{2,1,0:T(8,128)(2,1)S(1)} %all_to_all.10), channel_id=1, source_target_pairs={{0,1},{1,0},{2,3},{3,2},{4,5},{5,4},{6,7},{7,6},{8,9},{9,8},{10,11... | collective-permute-start | bytes 933896 | tf_op jit(solution)/shard_map/ppermute | solution.py:157
  29.4 0.4 collective-permute-done.9.refs_0_
  29.8 3.4 %collective-permute-start.10 = (bf16[4,144,128]{2,1,0:T(8,128)(2,1)S(1)}, bf16[4,144,128]{2,1,0:T(8,128)(2,1)S(1)}, u32[]{:S(2)}, u32[]{:S(2)}) collective-permute-start(bf16[4,144,128]{2,1,0:T(8,128)(2,1)S(1)} %collective-permute-done.9.refs_0_), channel_id=1, source_target_pairs={{0,28},{4,0},{8,4},{12,8},{16,12},{20,16},{24,20},{28,24},{1,29},{... | collective-permute-start | bytes 442376 | tf_op jit(solution)/shard_map/ppermute | solution.py:157
  33.4 2.7 %collective-permute-start.6 = (bf16[4,144,128]{2,1,0:T(8,128)(2,1)S(1)}, bf16[4,144,128]{2,1,0:T(8,128)(2,1)S(1)}, u32[]{:S(2)}, u32[]{:S(2)}) collective-permute-start(bf16[4,144,128]{2,1,0:T(8,128)(2,1)S(1)} %collective-permute-done.5.refs_1_), channel_id=1, source_target_pairs={{0,28},{4,0},{8,4},{12,8},{16,12},{20,16},{24,20},{28,24},{1,29},{... | collective-permute-start | bytes 442376 | tf_op jit(solution)/shard_map/ppermute | solution.py:157
  36.1 4.3 %collective-permute-done.2.refs_0_ = bf16[4,144,128]{2,1,0:T(8,128)(2,1)S(1)} collective-permute-done((bf16[4,144,128]{2,1,0:T(8,128)(2,1)S(1)}, bf16[4,144,128]{2,1,0:T(8,128)(2,1)S(1)}, u32[]{:S(2)}, u32[]{:S(2)}) %collective-permute-start.2) | collective-permute-done | bytes 147488 | tf_op jit(solution)/shard_map/ppermute | solution.py:157
  40.5 3.5 %collective-permute-start.14 = (bf16[16,144,128]{2,1,0:T(8,128)(2,1)S(1)}, bf16[16,144,128]{2,1,0:T(8,128)(2,1)S(1)}, u32[]{:S(2)}, u32[]{:S(2)}) collective-permute-start(bf16[16,144,128]{2,1,0:T(8,128)(2,1)S(1)} %pad_maximum_fusion.1), channel_id=1, source_target_pairs={{0,1},{1,0},{2,3},{3,2},{4,5},{5,4},{6,7},{7,6},{8,9},{9,8},{10,11... | collective-permute-start | bytes 1769480 | tf_op jit(solution)/shard_map/ppermute | solution.py:157
  44.3 3.0 %collective-permute-start.7 = (bf16[4,144,128]{2,1,0:T(8,128)(2,1)S(1)}, bf16[4,144,128]{2,1,0:T(8,128)(2,1)S(1)}, u32[]{:S(2)}, u32[]{:S(2)}) collective-permute-start(bf16[4,144,128]{2,1,0:T(8,128)(2,1)S(1)} %collective-permute-done.6.refs_1_), channel_id=1, source_target_pairs={{0,28},{4,0},{8,4},{12,8},{16,12},{20,16},{24,20},{28,24},{1,29},{... | collective-permute-start | bytes 442376 | tf_op jit(solution)/shard_map/ppermute | solution.py:157
  47.4 1.4 %collective-permute-start.17 = (bf16[4,144,128]{2,1,0:T(8,128)(2,1)S(1)}, bf16[4,144,128]{2,1,0:T(8,128)(2,1)S(1)}, u32[]{:S(2)}, u32[]{:S(2)}) collective-permute-start(bf16[4,144,128]{2,1,0:T(8,128)(2,1)S(1)} %collective-permute-done.12.refs_1_), channel_id=1, source_target_pairs={{0,4},{4,8},{8,12},{12,16},{16,20},{20,24},{24,28},{28,0},{1,5},{5... | collective-permute-start | bytes 442376 | tf_op jit(solution)/shard_map/ppermute | solution.py:157
  48.8 0.6 unpack.8.refs_4_
  49.5 0.6 collective-permute-done.7.refs_1_
  50.1 3.2 %collective-permute-done.16.refs_0_ = bf16[4,144,128]{2,1,0:T(8,128)(2,1)S(1)} collective-permute-done((bf16[4,144,128]{2,1,0:T(8,128)(2,1)S(1)}, bf16[4,144,128]{2,1,0:T(8,128)(2,1)S(1)}, u32[]{:S(2)}, u32[]{:S(2)}) %collective-permute-start.16) | collective-permute-done | bytes 147488 | tf_op jit(solution)/shard_map/ppermute | solution.py:157
  53.3 3.4 %collective-permute-start.18 = (bf16[16,144,128]{2,1,0:T(8,128)(2,1)S(1)}, bf16[16,144,128]{2,1,0:T(8,128)(2,1)S(1)}, u32[]{:S(2)}, u32[]{:S(2)}) collective-permute-start(bf16[16,144,128]{2,1,0:T(8,128)(2,1)S(1)} %pad_maximum_fusion.2), channel_id=1, source_target_pairs={{0,1},{1,0},{2,3},{3,2},{4,5},{5,4},{6,7},{7,6},{8,9},{9,8},{10,11... | collective-permute-start | bytes 1769480 | tf_op jit(solution)/shard_map/ppermute | solution.py:157
  56.8 2.7 %collective-permute-start.8 = (bf16[4,144,128]{2,1,0:T(8,128)(2,1)S(1)}, bf16[4,144,128]{2,1,0:T(8,128)(2,1)S(1)}, u32[]{:S(2)}, u32[]{:S(2)}) collective-permute-start(bf16[4,144,128]{2,1,0:T(8,128)(2,1)S(1)} %collective-permute-done.7.refs_1_), channel_id=1, source_target_pairs={{0,28},{4,0},{8,4},{12,8},{16,12},{20,16},{24,20},{28,24},{1,29},{... | collective-permute-start | bytes 442376 | tf_op jit(solution)/shard_map/ppermute | solution.py:157
  59.5 0.6 unpack.9.refs_4_
  60.1 0.6 unpack.10.refs_4_
  60.8 0.6 unpack.11.refs_4_
  61.4 0.6 unpack.12.refs_4_
  62.1 1.3 %collective-permute-done.4.refs_0_ = bf16[4,144,128]{2,1,0:T(8,128)(2,1)S(1)} collective-permute-done((bf16[4,144,128]{2,1,0:T(8,128)(2,1)S(1)}, bf16[4,144,128]{2,1,0:T(8,128)(2,1)S(1)}, u32[]{:S(2)}, u32[]{:S(2)}) %collective-permute-start.4) | collective-permute-done | bytes 147488 | tf_op jit(solution)/shard_map/ppermute | solution.py:157
  63.4 1.0 collective-permute-start.15
  64.4 0.6 unpack.13.refs_4_
  65.0 0.6 unpack.14.refs_4_
  65.7 0.6 unpack.15.bins_ref
  66.3 6.1 %grams.1 = bf16[16,2,48,384]{3,2,1,0:T(8,128)(2,1)S(1)} custom-call(s32[64,16]{1,0:T(8,128)S(1)} %fusion.1.triads_ref, bf16[8,128]{1,0:T(8,128)(2,1)S(1)} %slice_bitcast_fusion.1.own_w_ref, bf16[8,128]{1,0:T(8,128)(2,1)S(1)} %slice_bitcast_fusion.sib_w_ref, bf16[512,24,256]{2,1,0:T(8,128)(2,1)S(1)} %unpack.15.bins_ref), custom_call_target="tpu_custom_call" | custom-call | flops 12000000000 | bytes 8000000 | tf_op jit(solution)/shard_map/grams/pallas_call | solution.py:188
  72.5 20.4 %all_to_all.11 = bf16[16,2,48,384]{3,2,1,0:T(8,128)(2,1)S(1)} all-to-all(bf16[16,2,48,384]{3,2,1,0:T(8,128)(2,1)S(1)} %grams.1), channel_id=1, replica_groups=mesh['x'=4,'yh'=2,'z'=8,'yl'=2,'core'=2] {'x','yh','yl'}, dimensions={0} | all-to-all | bytes 2359296 | tf_op jit(solution)/shard_map/all_to_all | solution.py:236
  93.5 0.4 reshape.43
  93.9 8.0 %all_gather.3 = f32[8,1,16,1152]{3,2,1,0:T(8,128)S(1)} all-gather(f32[2,1,16,1152]{3,2,1,0:T(8,128)S(1)} %bitcast.17), channel_id=1, replica_groups=mesh['x'=4,'yh'=2,'z'=8,'yl'=2,'core'=2] {'yl','core'}, dimensions={0}, use_global_device_ids=true | all-gather | bytes 737280 | tf_op jit(solution)/shard_map/all_gather | solution.py:240
  102.0 0.9 broadcast_select_fusion
  (39 shorter events, 1.5 us)
Async XLA Ops:
  17.8 15.4 %collective-permute-start.11 = (bf16[4,144,128]{2,1,0:T(8,128)(2,1)S(1)}, bf16[4,144,128]{2,1,0:T(8,128)(2,1)S(1)}, u32[]{:S(2)}, u32[]{:S(2)}) collective-permute-start(bf16[4,144,128]{2,1,0:T(8,128)(2,1)S(1)} %get-tuple-element.15), channel_id=1, source_target_pairs={{0,4},{4,8},{8,12},{12,16},{16,20},{20,24},{24,28},{28,0},{1,5},{5... | collective-permute-start | bytes 442376 | tf_op jit(solution)/shard_map/ppermute | solution.py:157
  19.6 13.8 %collective-permute-start.5 = (bf16[4,144,128]{2,1,0:T(8,128)(2,1)S(1)}, bf16[4,144,128]{2,1,0:T(8,128)(2,1)S(1)}, u32[]{:S(2)}, u32[]{:S(2)}) collective-permute-start(bf16[4,144,128]{2,1,0:T(8,128)(2,1)S(1)} %get-tuple-element.15), channel_id=1, source_target_pairs={{0,28},{4,0},{8,4},{12,8},{16,12},{20,16},{24,20},{28,24},{1,29},{... | collective-permute-start | bytes 442376 | tf_op jit(solution)/shard_map/ppermute | solution.py:157
  23.6 9.7 %collective-permute-start.1 = (bf16[4,144,128]{2,1,0:T(8,128)(2,1)S(1)}, bf16[4,144,128]{2,1,0:T(8,128)(2,1)S(1)}, u32[]{:S(2)}, u32[]{:S(2)}) collective-permute-start(bf16[4,144,128]{2,1,0:T(8,128)(2,1)S(1)} %get-tuple-element.16), channel_id=1, source_target_pairs={{0,4},{4,8},{8,12},{12,16},{16,20},{20,24},{24,28},{28,0},{1,5},{5... | collective-permute-start | bytes 442376 | tf_op jit(solution)/shard_map/ppermute | solution.py:157
  23.6 6.2 %collective-permute-start.9 = (bf16[4,144,128]{2,1,0:T(8,128)(2,1)S(1)}, bf16[4,144,128]{2,1,0:T(8,128)(2,1)S(1)}, u32[]{:S(2)}, u32[]{:S(2)}) collective-permute-start(bf16[4,144,128]{2,1,0:T(8,128)(2,1)S(1)} %get-tuple-element.16), channel_id=1, source_target_pairs={{0,28},{4,0},{8,4},{12,8},{16,12},{20,16},{24,20},{28,24},{1,29},{... | collective-permute-start | bytes 442376 | tf_op jit(solution)/shard_map/ppermute | solution.py:157
  26.3 21.0 %collective-permute-start = (bf16[8,152,128]{2,1,0:T(8,128)(2,1)S(1)}, bf16[8,152,128]{2,1,0:T(8,128)(2,1)S(1)}, u32[]{:S(2)}, u32[]{:S(2)}) collective-permute-start(bf16[8,152,128]{2,1,0:T(8,128)(2,1)S(1)} %all_to_all.10), channel_id=1, source_target_pairs={{0,1},{1,0},{2,3},{3,2},{4,5},{5,4},{6,7},{7,6},{8,9},{9,8},{10,11... | collective-permute-start | bytes 933896 | tf_op jit(solution)/shard_map/ppermute | solution.py:157
  29.8 10.7 %collective-permute-start.10 = (bf16[4,144,128]{2,1,0:T(8,128)(2,1)S(1)}, bf16[4,144,128]{2,1,0:T(8,128)(2,1)S(1)}, u32[]{:S(2)}, u32[]{:S(2)}) collective-permute-start(bf16[4,144,128]{2,1,0:T(8,128)(2,1)S(1)} %collective-permute-done.9.refs_0_), channel_id=1, source_target_pairs={{0,28},{4,0},{8,4},{12,8},{16,12},{20,16},{24,20},{28,24},{1,29},{... | collective-permute-start | bytes 442376 | tf_op jit(solution)/shard_map/ppermute | solution.py:157
  33.2 10.8 %collective-permute-start.12 = (bf16[4,144,128]{2,1,0:T(8,128)(2,1)S(1)}, bf16[4,144,128]{2,1,0:T(8,128)(2,1)S(1)}, u32[]{:S(2)}, u32[]{:S(2)}) collective-permute-start(bf16[4,144,128]{2,1,0:T(8,128)(2,1)S(1)} %collective-permute-done.11.refs_1_), channel_id=1, source_target_pairs={{0,4},{4,8},{8,12},{12,16},{16,20},{20,24},{24,28},{28,0},{1,5},{5... | collective-permute-start | bytes 442376 | tf_op jit(solution)/shard_map/ppermute | solution.py:157
  33.3 7.2 %collective-permute-start.2 = (bf16[4,144,128]{2,1,0:T(8,128)(2,1)S(1)}, bf16[4,144,128]{2,1,0:T(8,128)(2,1)S(1)}, u32[]{:S(2)}, u32[]{:S(2)}) collective-permute-start(bf16[4,144,128]{2,1,0:T(8,128)(2,1)S(1)} %collective-permute-done.1.refs_0_), channel_id=1, source_target_pairs={{0,4},{4,8},{8,12},{12,16},{16,20},{20,24},{24,28},{28,0},{1,5},{5... | collective-permute-start | bytes 442376 | tf_op jit(solution)/shard_map/ppermute | solution.py:157
  33.4 10.7 %collective-permute-start.6 = (bf16[4,144,128]{2,1,0:T(8,128)(2,1)S(1)}, bf16[4,144,128]{2,1,0:T(8,128)(2,1)S(1)}, u32[]{:S(2)}, u32[]{:S(2)}) collective-permute-start(bf16[4,144,128]{2,1,0:T(8,128)(2,1)S(1)} %collective-permute-done.5.refs_1_), channel_id=1, source_target_pairs={{0,28},{4,0},{8,4},{12,8},{16,12},{20,16},{24,20},{28,24},{1,29},{... | collective-permute-start | bytes 442376 | tf_op jit(solution)/shard_map/ppermute | solution.py:157
  40.4 7.0 %collective-permute-start.3 = (bf16[4,144,128]{2,1,0:T(8,128)(2,1)S(1)}, bf16[4,144,128]{2,1,0:T(8,128)(2,1)S(1)}, u32[]{:S(2)}, u32[]{:S(2)}) collective-permute-start(bf16[4,144,128]{2,1,0:T(8,128)(2,1)S(1)} %collective-permute-done.2.refs_0_), channel_id=1, source_target_pairs={{0,4},{4,8},{8,12},{12,16},{16,20},{20,24},{24,28},{28,0},{1,5},{5... | collective-permute-start | bytes 442376 | tf_op jit(solution)/shard_map/ppermute | solution.py:157
  40.5 18.9 %collective-permute-start.14 = (bf16[16,144,128]{2,1,0:T(8,128)(2,1)S(1)}, bf16[16,144,128]{2,1,0:T(8,128)(2,1)S(1)}, u32[]{:S(2)}, u32[]{:S(2)}) collective-permute-start(bf16[16,144,128]{2,1,0:T(8,128)(2,1)S(1)} %pad_maximum_fusion.1), channel_id=1, source_target_pairs={{0,1},{1,0},{2,3},{3,2},{4,5},{5,4},{6,7},{7,6},{8,9},{9,8},{10,11... | collective-permute-start | bytes 1769480 | tf_op jit(solution)/shard_map/ppermute | solution.py:157
  44.2 16.6 %collective-permute-start.13 = (bf16[16,144,128]{2,1,0:T(8,128)(2,1)S(1)}, bf16[16,144,128]{2,1,0:T(8,128)(2,1)S(1)}, u32[]{:S(2)}, u32[]{:S(2)}) collective-permute-start(bf16[16,144,128]{2,1,0:T(8,128)(2,1)S(1)} %pad_maximum_fusion), channel_id=1, source_target_pairs={{0,1},{1,0},{2,3},{3,2},{4,5},{5,4},{6,7},{7,6},{8,9},{9,8},{10,11... | collective-permute-start | bytes 1769480 | tf_op jit(solution)/shard_map/ppermute | solution.py:157
  44.3 5.8 %collective-permute-start.7 = (bf16[4,144,128]{2,1,0:T(8,128)(2,1)S(1)}, bf16[4,144,128]{2,1,0:T(8,128)(2,1)S(1)}, u32[]{:S(2)}, u32[]{:S(2)}) collective-permute-start(bf16[4,144,128]{2,1,0:T(8,128)(2,1)S(1)} %collective-permute-done.6.refs_1_), channel_id=1, source_target_pairs={{0,28},{4,0},{8,4},{12,8},{16,12},{20,16},{24,20},{28,24},{1,29},{... | collective-permute-start | bytes 442376 | tf_op jit(solution)/shard_map/ppermute | solution.py:157
  47.3 6.0 %collective-permute-start.16 = (bf16[4,144,128]{2,1,0:T(8,128)(2,1)S(1)}, bf16[4,144,128]{2,1,0:T(8,128)(2,1)S(1)}, u32[]{:S(2)}, u32[]{:S(2)}) collective-permute-start(bf16[4,144,128]{2,1,0:T(8,128)(2,1)S(1)} %collective-permute-done.10.refs_0_), channel_id=1, source_target_pairs={{0,28},{4,0},{8,4},{12,8},{16,12},{20,16},{24,20},{28,24},{1,29},{... | collective-permute-start | bytes 442376 | tf_op jit(solution)/shard_map/ppermute | solution.py:157
  47.4 5.9 %collective-permute-start.17 = (bf16[4,144,128]{2,1,0:T(8,128)(2,1)S(1)}, bf16[4,144,128]{2,1,0:T(8,128)(2,1)S(1)}, u32[]{:S(2)}, u32[]{:S(2)}) collective-permute-start(bf16[4,144,128]{2,1,0:T(8,128)(2,1)S(1)} %collective-permute-done.12.refs_1_), channel_id=1, source_target_pairs={{0,4},{4,8},{8,12},{12,16},{16,20},{20,24},{24,28},{28,0},{1,5},{5... | collective-permute-start | bytes 442376 | tf_op jit(solution)/shard_map/ppermute | solution.py:157
  53.3 11.0 %collective-permute-start.18 = (bf16[16,144,128]{2,1,0:T(8,128)(2,1)S(1)}, bf16[16,144,128]{2,1,0:T(8,128)(2,1)S(1)}, u32[]{:S(2)}, u32[]{:S(2)}) collective-permute-start(bf16[16,144,128]{2,1,0:T(8,128)(2,1)S(1)} %pad_maximum_fusion.2), channel_id=1, source_target_pairs={{0,1},{1,0},{2,3},{3,2},{4,5},{5,4},{6,7},{7,6},{8,9},{9,8},{10,11... | collective-permute-start | bytes 1769480 | tf_op jit(solution)/shard_map/ppermute | solution.py:157
  56.8 6.6 %collective-permute-start.4 = (bf16[4,144,128]{2,1,0:T(8,128)(2,1)S(1)}, bf16[4,144,128]{2,1,0:T(8,128)(2,1)S(1)}, u32[]{:S(2)}, u32[]{:S(2)}) collective-permute-start(bf16[4,144,128]{2,1,0:T(8,128)(2,1)S(1)} %collective-permute-done.3.refs_0_), channel_id=1, source_target_pairs={{0,4},{4,8},{8,12},{12,16},{16,20},{20,24},{24,28},{28,0},{1,5},{5... | collective-permute-start | bytes 442376 | tf_op jit(solution)/shard_map/ppermute | solution.py:157
  56.8 6.6 %collective-permute-start.8 = (bf16[4,144,128]{2,1,0:T(8,128)(2,1)S(1)}, bf16[4,144,128]{2,1,0:T(8,128)(2,1)S(1)}, u32[]{:S(2)}, u32[]{:S(2)}) collective-permute-start(bf16[4,144,128]{2,1,0:T(8,128)(2,1)S(1)} %collective-permute-done.7.refs_1_), channel_id=1, source_target_pairs={{0,28},{4,0},{8,4},{12,8},{16,12},{20,16},{24,20},{28,24},{1,29},{... | collective-permute-start | bytes 442376 | tf_op jit(solution)/shard_map/ppermute | solution.py:157
  63.4 2.3 %collective-permute-start.15 = (bf16[8,144,128]{2,1,0:T(8,128)(2,1)S(1)}, bf16[8,144,128]{2,1,0:T(8,128)(2,1)S(1)}, u32[]{:S(2)}, u32[]{:S(2)}) collective-permute-start(bf16[8,144,128]{2,1,0:T(8,128)(2,1)S(1)} %pad_maximum_fusion.3), channel_id=1, source_target_pairs={{0,1},{1,0},{2,3},{3,2},{4,5},{5,4},{6,7},{7,6},{8,9},{9,8},{10,11... | collective-permute-start | bytes 884744 | tf_op jit(solution)/shard_map/ppermute | solution.py:157
  72.5 29.5 %copy-start = (s32[8,1]{0,1:T(1,128)S(1)}, s32[8,1]{0,1:T(1,128)}, u32[]{:S(2)}) copy-start(s32[8,1]{0,1:T(1,128)} %param.7) | copy-start | bytes 100

commit v11 on v9

--- a/solution.py
+++ b/solution.py
@@ -82,7 +82,7 @@
 
     def slot(which):
         turn = (up * (depth - (which & 7))) & 7
-        return turn * 64 + (which & 56) + (which >> 6)
+        return turn * 64 + (which & 8) * 4 + (which & 48) // 2 + (which >> 6)
 
     weights = lane_weights(own_w_ref, sib_w_ref)
     lane = lax.broadcasted_iota(jnp.int32, (48, LANES), 1)
@@ -91,7 +91,7 @@
         w_ref, q_ref = buffer
         owner = reader >> 2
         row = (reader & 2) * 2 + core * 2 + (reader & 1)
-        k_bin = row * 64 + owner * 8 + depth
+        k_bin = row * 64 + (owner & 3) * 16 + (owner >> 2) * 8 + depth
         first = bins_ref[owner * 8 + row].astype(F32)
         k_real = first[:, :LANES] * weights
         k_imag = first[:, LANES:] * weights
@@ -127,7 +127,8 @@
             begin = 24 * (start + i) - LANES * n
             built = jnp.where(lane >= begin, product[48 * i : 48 * (i + 1)], built)
         lanes = slice(LANES * n, LANES * (n + 1))
-        out_ref[reader >> 1, reader & 1, :, lanes] = built.astype(BF16)
+        place = ((reader >> 2) & 3) * 4 + (reader & 2) + (reader >> 4)
+        out_ref[place, reader & 1, :, lanes] = built.astype(BF16)
 
     thirds = (range(0, 5), range(5, 10), range(10, 16))
     ready = prepare(0, buffers[0])
@@ -216,7 +217,7 @@
         compiler_params=params(56),
         name="split",
     )(modes.reshape(48, 24, LANES), triads[:, 0], point_weights[None])
-    received = lax.all_to_all(pieces, ("x", "yh"), 0, 0)
+    received = lax.all_to_all(pieces, ("yh", "x"), 0, 0)
     codes = received[:, 144:, :32].astype(F32)
     lists = (codes[:, :, :16] * 64 + codes[:, :, 16:]).astype(jnp.int32).reshape(64, 16)
 
@@ -244,7 +245,7 @@
     bins = unpack(last, last_passed, bins, 4)
 
     partial = grams(lists, received[0, 144:], beside[0, 144:], bins)
-    parts = lax.all_to_all(partial, ("x", "yh", "yl"), 0, 0)
+    parts = lax.all_to_all(partial, ("x", "yl", "yh"), 0, 0)
     parts, counts = lax.optimization_barrier((parts, counts))
     summed = jnp.sum(parts.astype(F32), axis=0) / 24
     rows = summed.reshape(2, 48, 16, 24).transpose(0, 2, 1, 3).reshape(2, 1, 16, 1152)

time: 94.9 us -> 99.7 us (1.051)
  Pallas kernels: 12.3 us -> 16.4 us
    pallas_call x1, Pallas kernels: 5.97 us -> 10.1 us  [grams(): pl.pallas_call(grams_kernel, out_shape=jax.ShapeDtypeStruct((16, 2, 48, 3...]
where the time goes in v11:
time: 99.7 us; the launch traced here: 99.5 us
  blocking collectives  44.7 us (45%)
  starting transfers between devices  28.8 us (29%)
  Pallas kernels  16.4 us (16%)
  waiting for transfers between devices  7.29 us (7%)
  other arithmetic  1.25 us (1%)
    all_to_all x1, blocking collectives, body(): parts = lax.all_to_all(partial, ('x', 'yl', 'yh'), 0, 0)  20.8 us
    ppermute x7, starting transfers between devices, ring(): return lax.ppermute(array, ('z', 'core'), pairs)  17.1 us
    all_to_all x1, blocking collectives, body(): received = lax.all_to_all(pieces, ('yh', 'x'), 0, 0)  15.6 us
    ppermute x8, starting transfers between devices, step(): lax.ppermute(array, axes, [(i, (i + by) % size) for i in range(size)])  11.7 us
    pallas_call x1, Pallas kernels, grams(): pl.pallas_call(grams_kernel, out_shape=jax.ShapeDtypeStruct((16, 2, 48, 3...  10.1 us
    all_gather x1, blocking collectives, body(): gathered = lax.all_gather(rows, ('yl', 'core'), tiled=True)  8.21 us
    ppermute x7, waiting for transfers between devices, ring(): return lax.ppermute(array, ('z', 'core'), pairs)  6.58 us
    pallas_call x8, Pallas kernels, unpack(): pl.pallas_call(unpack_kernel, out_shape=BINS, grid=(1,), in_specs=[pl.Blo...  3.99 us
  transfers between devices with their start and end apart: 15, of which 4 were waited for; matrix products, arithmetic and copies ran while one was open for 0% of the time, Pallas kernels for 4%

profile of v11, /device:TPU:1, one launch (start us, length us, event | category | flops | bytes accessed | tf_op | source)
XLA Modules:
  0.0 99.5 jit_solution(3163602969611136556)
XLA Ops:
  0.0 2.3 %split.1 = bf16[8,152,128]{2,1,0:T(8,128)(2,1)} custom-call(bf16[48,24,128]{2,1,0:T(8,128)(2,1)} %bitcast.18, s32[8,16]{1,0:T(8,128)} %bitcast.19, f32[1,128]{1,0:T(1,128)} %bitcast.20), custom_call_target="tpu_custom_call" | custom-call | tf_op jit(solution)/shard_map/split/pallas_call | solution.py:212
  2.3 15.6 %all_to_all.10 = bf16[8,152,128]{2,1,0:T(8,128)(2,1)S(1)} all-to-all(bf16[8,152,128]{2,1,0:T(8,128)(2,1)} %split.1), channel_id=1, replica_groups=mesh['x'=4,'yh'=2,'z'=8,'yl'=2,'core'=2] {'yh','x'}, dimensions={0} | all-to-all | bytes 622592 | tf_op jit(solution)/shard_map/all_to_all | solution.py:220
  18.0 5.7 %collective-permute-start.1 = (bf16[8,144,128]{2,1,0:T(8,128)(2,1)S(1)}, bf16[8,144,128]{2,1,0:T(8,128)(2,1)S(1)}, u32[]{:S(2)}, u32[]{:S(2)}) collective-permute-start(bf16[8,144,128]{2,1,0:T(8,128)(2,1)S(1)} %slice.33.own_ref), channel_id=1, source_target_pairs={{0,4},{1,29},{4,8},{5,1},{8,12},{9,5},{12,16},{13,9},{16,20},{17,1... | collective-permute-start | bytes 884744 | tf_op jit(solution)/shard_map/ppermute | solution.py:170
  23.8 1.0 collective-permute-start
  24.7 4.4 %collective-permute-done.1.own_ref = bf16[8,144,128]{2,1,0:T(8,128)(2,1)S(1)} collective-permute-done((bf16[8,144,128]{2,1,0:T(8,128)(2,1)S(1)}, bf16[8,144,128]{2,1,0:T(8,128)(2,1)S(1)}, u32[]{:S(2)}, u32[]{:S(2)}) %collective-permute-start.1) | collective-permute-done | bytes 294944 | tf_op jit(solution)/shard_map/ppermute | solution.py:170
  29.1 3.1 %collective-permute-start.2 = (bf16[8,144,128]{2,1,0:T(8,128)(2,1)S(1)}, bf16[8,144,128]{2,1,0:T(8,128)(2,1)S(1)}, u32[]{:S(2)}, u32[]{:S(2)}) collective-permute-start(bf16[8,144,128]{2,1,0:T(8,128)(2,1)S(1)} %collective-permute-done.1.own_ref), channel_id=1, source_target_pairs={{0,4},{1,29},{4,8},{5,1},{8,12},{9,5},{12,16},{13,9},{16,20},{17,1... | collective-permute-start | bytes 884744 | tf_op jit(solution)/shard_map/ppermute | solution.py:170
  32.3 0.6 collective-permute-start.10
  33.0 3.0 %collective-permute-start.6 = (bf16[8,144,128]{2,1,0:T(8,128)(2,1)S(1)}, bf16[8,144,128]{2,1,0:T(8,128)(2,1)S(1)}, u32[]{:S(2)}, u32[]{:S(2)}) collective-permute-start(bf16[8,144,128]{2,1,0:T(8,128)(2,1)S(1)} %collective-permute-done.5.sib_ref), channel_id=1, source_target_pairs={{0,4},{1,29},{4,8},{5,1},{8,12},{9,5},{12,16},{13,9},{16,20},{17,1... | collective-permute-start | bytes 884744 | tf_op jit(solution)/shard_map/ppermute | solution.py:170
  36.0 3.0 %collective-permute-start.3 = (bf16[8,144,128]{2,1,0:T(8,128)(2,1)S(1)}, bf16[8,144,128]{2,1,0:T(8,128)(2,1)S(1)}, u32[]{:S(2)}, u32[]{:S(2)}) collective-permute-start(bf16[8,144,128]{2,1,0:T(8,128)(2,1)S(1)} %collective-permute-done.2.own_ref), channel_id=1, source_target_pairs={{0,4},{1,29},{4,8},{5,1},{8,12},{9,5},{12,16},{13,9},{16,20},{17,1... | collective-permute-start | bytes 884744 | tf_op jit(solution)/shard_map/ppermute | solution.py:170
  39.0 0.5 unpack.8.refs_0_
  39.6 4.2 %collective-permute-start.8 = (bf16[8,144,128]{2,1,0:T(8,128)(2,1)S(1)}, bf16[8,144,128]{2,1,0:T(8,128)(2,1)S(1)}, u32[]{:S(2)}, u32[]{:S(2)}) collective-permute-start(bf16[8,144,128]{2,1,0:T(8,128)(2,1)S(1)} %collective-permute-done.6.sib_ref), channel_id=1, source_target_pairs={{0,1},{1,0},{2,3},{3,2},{4,5},{5,4},{6,7},{7,6},{8,9},{9,8},{10,11... | collective-permute-start | bytes 884744 | tf_op jit(solution)/shard_map/ppermute | solution.py:158
  43.9 1.3 %collective-permute-start.7 = (bf16[8,144,128]{2,1,0:T(8,128)(2,1)S(1)}, bf16[8,144,128]{2,1,0:T(8,128)(2,1)S(1)}, u32[]{:S(2)}, u32[]{:S(2)}) collective-permute-start(bf16[8,144,128]{2,1,0:T(8,128)(2,1)S(1)} %collective-permute-done.6.sib_ref), channel_id=1, source_target_pairs={{0,4},{1,29},{4,8},{5,1},{8,12},{9,5},{12,16},{13,9},{16,20},{17,1... | collective-permute-start | bytes 884744 | tf_op jit(solution)/shard_map/ppermute | solution.py:170
  45.2 0.5 unpack.9.refs_0_
  45.7 0.5 unpack.10.refs_0_
  46.2 0.9 collective-permute-start.4
  47.1 0.5 unpack.11.refs_0_
  47.6 2.1 %collective-permute-done.7.sib_ref = bf16[8,144,128]{2,1,0:T(8,128)(2,1)S(1)} collective-permute-done((bf16[8,144,128]{2,1,0:T(8,128)(2,1)S(1)}, bf16[8,144,128]{2,1,0:T(8,128)(2,1)S(1)}, u32[]{:S(2)}, u32[]{:S(2)}) %collective-permute-start.7) | collective-permute-done | bytes 294944 | tf_op jit(solution)/shard_map/ppermute | solution.py:170
  49.7 2.6 %collective-permute-start.13 = (bf16[8,144,128]{2,1,0:T(8,128)(2,1)S(1)}, bf16[8,144,128]{2,1,0:T(8,128)(2,1)S(1)}, u32[]{:S(2)}, u32[]{:S(2)}) collective-permute-start(bf16[8,144,128]{2,1,0:T(8,128)(2,1)S(1)} %collective-permute-done.7.sib_ref), channel_id=1, source_target_pairs={{0,1},{1,0},{2,3},{3,2},{4,5},{5,4},{6,7},{7,6},{8,9},{9,8},{10,11... | collective-permute-start | bytes 884744 | tf_op jit(solution)/shard_map/ppermute | solution.py:158
  52.3 0.5 unpack.12.refs_0_
  52.8 0.5 unpack.13.refs_0_
  53.3 3.2 %collective-permute-start.12 = (bf16[8,144,128]{2,1,0:T(8,128)(2,1)S(1)}, bf16[8,144,128]{2,1,0:T(8,128)(2,1)S(1)}, u32[]{:S(2)}, u32[]{:S(2)}) collective-permute-start(bf16[8,144,128]{2,1,0:T(8,128)(2,1)S(1)} %collective-permute-done.4.own_ref), channel_id=1, source_target_pairs={{0,1},{1,0},{2,3},{3,2},{4,5},{5,4},{6,7},{7,6},{8,9},{9,8},{10,11... | collective-permute-start | bytes 884744 | tf_op jit(solution)/shard_map/ppermute | solution.py:158
  56.6 0.5 unpack.14.refs_0_
  57.1 0.7 collective-permute-done.12.sib_ref
  57.8 0.5 unpack.15.bins_ref
  58.3 10.1 %grams.1 = bf16[16,2,48,384]{3,2,1,0:T(8,128)(2,1)S(1)} custom-call(s32[64,16]{1,0:T(8,128)S(1)} %fusion.1.triads_ref, bf16[8,128]{1,0:T(8,128)(2,1)S(1)} %slice_bitcast_fusion.1.own_w_ref, bf16[8,128]{1,0:T(8,128)(2,1)S(1)} %slice_bitcast_fusion.sib_w_ref, bf16[512,24,256]{2,1,0:T(8,128)(2,1)S(1)} %unpack.15.bins_ref), custom_call_target="tpu_custom_call" | custom-call | flops 12000000000 | bytes 8000000 | tf_op jit(solution)/shard_map/grams/pallas_call | solution.py:197
  68.4 20.8 %all_to_all.11 = bf16[16,2,48,384]{3,2,1,0:T(8,128)(2,1)S(1)} all-to-all(bf16[16,2,48,384]{3,2,1,0:T(8,128)(2,1)S(1)} %grams.1), channel_id=1, replica_groups=mesh['x'=4,'yh'=2,'z'=8,'yl'=2,'core'=2] {'x','yl','yh'}, dimensions={0} | all-to-all | bytes 2359296 | tf_op jit(solution)/shard_map/all_to_all | solution.py:248
  89.3 0.2 convert_reduce_fusion
  89.4 0.2 copy.14
  89.6 0.3 copy.15
  89.9 0.4 reshape.43
  90.3 8.2 %all_gather.3 = f32[8,1,16,1152]{3,2,1,0:T(8,128)S(1)} all-gather(f32[2,1,16,1152]{3,2,1,0:T(8,128)S(1)} %bitcast.17), channel_id=1, replica_groups=mesh['x'=4,'yh'=2,'z'=8,'yl'=2,'core'=2] {'yl','core'}, dimensions={0}, use_global_device_ids=true | all-gather | bytes 737280 | tf_op jit(solution)/shard_map/all_gather | solution.py:252
  98.6 0.9 broadcast_select_fusion
  (26 shorter events, 0.6 us)
Async XLA Ops:
  18.0 11.1 %collective-permute-start.1 = (bf16[8,144,128]{2,1,0:T(8,128)(2,1)S(1)}, bf16[8,144,128]{2,1,0:T(8,128)(2,1)S(1)}, u32[]{:S(2)}, u32[]{:S(2)}) collective-permute-start(bf16[8,144,128]{2,1,0:T(8,128)(2,1)S(1)} %slice.33.own_ref), channel_id=1, source_target_pairs={{0,4},{1,29},{4,8},{5,1},{8,12},{9,5},{12,16},{13,9},{16,20},{17,1... | collective-permute-start | bytes 884744 | tf_op jit(solution)/shard_map/ppermute | solution.py:170
  23.6 8.7 %collective-permute-start.5 = (bf16[8,144,128]{2,1,0:T(8,128)(2,1)S(1)}, bf16[8,144,128]{2,1,0:T(8,128)(2,1)S(1)}, u32[]{:S(2)}, u32[]{:S(2)}) collective-permute-start(bf16[8,144,128]{2,1,0:T(8,128)(2,1)S(1)} %slice.33.own_ref), channel_id=1, source_target_pairs={{0,29},{1,4},{4,1},{5,8},{8,5},{9,12},{12,9},{13,16},{16,13},{17,2... | collective-permute-start | bytes 884744 | tf_op jit(solution)/shard_map/ppermute | solution.py:170
  23.8 12.2 %collective-permute-start = (bf16[8,152,128]{2,1,0:T(8,128)(2,1)S(1)}, bf16[8,152,128]{2,1,0:T(8,128)(2,1)S(1)}, u32[]{:S(2)}, u32[]{:S(2)}) collective-permute-start(bf16[8,152,128]{2,1,0:T(8,128)(2,1)S(1)} %all_to_all.10), channel_id=1, source_target_pairs={{0,1},{1,0},{2,3},{3,2},{4,5},{5,4},{6,7},{7,6},{8,9},{9,8},{10,11... | collective-permute-start | bytes 933896 | tf_op jit(solution)/shard_map/ppermute | solution.py:158
  29.1 6.9 %collective-permute-start.2 = (bf16[8,144,128]{2,1,0:T(8,128)(2,1)S(1)}, bf16[8,144,128]{2,1,0:T(8,128)(2,1)S(1)}, u32[]{:S(2)}, u32[]{:S(2)}) collective-permute-start(bf16[8,144,128]{2,1,0:T(8,128)(2,1)S(1)} %collective-permute-done.1.own_ref), channel_id=1, source_target_pairs={{0,4},{1,29},{4,8},{5,1},{8,12},{9,5},{12,16},{13,9},{16,20},{17,1... | collective-permute-start | bytes 884744 | tf_op jit(solution)/shard_map/ppermute | solution.py:170
  32.3 11.5 %collective-permute-start.10 = (bf16[8,144,128]{2,1,0:T(8,128)(2,1)S(1)}, bf16[8,144,128]{2,1,0:T(8,128)(2,1)S(1)}, u32[]{:S(2)}, u32[]{:S(2)}) collective-permute-start(bf16[8,144,128]{2,1,0:T(8,128)(2,1)S(1)} %collective-permute-done.5.sib_ref), channel_id=1, source_target_pairs={{0,1},{1,0},{2,3},{3,2},{4,5},{5,4},{6,7},{7,6},{8,9},{9,8},{10,11... | collective-permute-start | bytes 884744 | tf_op jit(solution)/shard_map/ppermute | solution.py:158
  32.9 12.8 %collective-permute-start.11 = (bf16[8,144,128]{2,1,0:T(8,128)(2,1)S(1)}, bf16[8,144,128]{2,1,0:T(8,128)(2,1)S(1)}, u32[]{:S(2)}, u32[]{:S(2)}) collective-permute-start(bf16[8,144,128]{2,1,0:T(8,128)(2,1)S(1)} %collective-permute-done.1.own_ref), channel_id=1, source_target_pairs={{0,1},{1,0},{2,3},{3,2},{4,5},{5,4},{6,7},{7,6},{8,9},{9,8},{10,11... | collective-permute-start | bytes 884744 | tf_op jit(solution)/shard_map/ppermute | solution.py:158
  33.0 6.6 %collective-permute-start.6 = (bf16[8,144,128]{2,1,0:T(8,128)(2,1)S(1)}, bf16[8,144,128]{2,1,0:T(8,128)(2,1)S(1)}, u32[]{:S(2)}, u32[]{:S(2)}) collective-permute-start(bf16[8,144,128]{2,1,0:T(8,128)(2,1)S(1)} %collective-permute-done.5.sib_ref), channel_id=1, source_target_pairs={{0,4},{1,29},{4,8},{5,1},{8,12},{9,5},{12,16},{13,9},{16,20},{17,1... | collective-permute-start | bytes 884744 | tf_op jit(solution)/shard_map/ppermute | solution.py:170
  36.0 10.2 %collective-permute-start.3 = (bf16[8,144,128]{2,1,0:T(8,128)(2,1)S(1)}, bf16[8,144,128]{2,1,0:T(8,128)(2,1)S(1)}, u32[]{:S(2)}, u32[]{:S(2)}) collective-permute-start(bf16[8,144,128]{2,1,0:T(8,128)(2,1)S(1)} %collective-permute-done.2.own_ref), channel_id=1, source_target_pairs={{0,4},{1,29},{4,8},{5,1},{8,12},{9,5},{12,16},{13,9},{16,20},{17,1... | collective-permute-start | bytes 884744 | tf_op jit(solution)/shard_map/ppermute | solution.py:170
  39.6 12.7 %collective-permute-start.8 = (bf16[8,144,128]{2,1,0:T(8,128)(2,1)S(1)}, bf16[8,144,128]{2,1,0:T(8,128)(2,1)S(1)}, u32[]{:S(2)}, u32[]{:S(2)}) collective-permute-start(bf16[8,144,128]{2,1,0:T(8,128)(2,1)S(1)} %collective-permute-done.6.sib_ref), channel_id=1, source_target_pairs={{0,1},{1,0},{2,3},{3,2},{4,5},{5,4},{6,7},{7,6},{8,9},{9,8},{10,11... | collective-permute-start | bytes 884744 | tf_op jit(solution)/shard_map/ppermute | solution.py:158
  43.8 8.5 %collective-permute-start.9 = (bf16[8,144,128]{2,1,0:T(8,128)(2,1)S(1)}, bf16[8,144,128]{2,1,0:T(8,128)(2,1)S(1)}, u32[]{:S(2)}, u32[]{:S(2)}) collective-permute-start(bf16[8,144,128]{2,1,0:T(8,128)(2,1)S(1)} %collective-permute-done.2.own_ref), channel_id=1, source_target_pairs={{0,1},{1,0},{2,3},{3,2},{4,5},{5,4},{6,7},{7,6},{8,9},{9,8},{10,11... | collective-permute-start | bytes 884744 | tf_op jit(solution)/shard_map/ppermute | solution.py:158
  43.9 5.9 %collective-permute-start.7 = (bf16[8,144,128]{2,1,0:T(8,128)(2,1)S(1)}, bf16[8,144,128]{2,1,0:T(8,128)(2,1)S(1)}, u32[]{:S(2)}, u32[]{:S(2)}) collective-permute-start(bf16[8,144,128]{2,1,0:T(8,128)(2,1)S(1)} %collective-permute-done.6.sib_ref), channel_id=1, source_target_pairs={{0,4},{1,29},{4,8},{5,1},{8,12},{9,5},{12,16},{13,9},{16,20},{17,1... | collective-permute-start | bytes 884744 | tf_op jit(solution)/shard_map/ppermute | solution.py:170
  46.2 7.1 %collective-permute-start.4 = (bf16[8,144,128]{2,1,0:T(8,128)(2,1)S(1)}, bf16[8,144,128]{2,1,0:T(8,128)(2,1)S(1)}, u32[]{:S(2)}, u32[]{:S(2)}) collective-permute-start(bf16[8,144,128]{2,1,0:T(8,128)(2,1)S(1)} %collective-permute-done.3.own_ref), channel_id=1, source_target_pairs={{0,4},{1,29},{4,8},{5,1},{8,12},{9,5},{12,16},{13,9},{16,20},{17,1... | collective-permute-start | bytes 884744 | tf_op jit(solution)/shard_map/ppermute | solution.py:170
  49.7 6.8 %collective-permute-start.13 = (bf16[8,144,128]{2,1,0:T(8,128)(2,1)S(1)}, bf16[8,144,128]{2,1,0:T(8,128)(2,1)S(1)}, u32[]{:S(2)}, u32[]{:S(2)}) collective-permute-start(bf16[8,144,128]{2,1,0:T(8,128)(2,1)S(1)} %collective-permute-done.7.sib_ref), channel_id=1, source_target_pairs={{0,1},{1,0},{2,3},{3,2},{4,5},{5,4},{6,7},{7,6},{8,9},{9,8},{10,11... | collective-permute-start | bytes 884744 | tf_op jit(solution)/shard_map/ppermute | solution.py:158
  52.3 4.3 %collective-permute-start.14 = (bf16[8,144,128]{2,1,0:T(8,128)(2,1)S(1)}, bf16[8,144,128]{2,1,0:T(8,128)(2,1)S(1)}, u32[]{:S(2)}, u32[]{:S(2)}) collective-permute-start(bf16[8,144,128]{2,1,0:T(8,128)(2,1)S(1)} %collective-permute-done.3.own_ref), channel_id=1, source_target_pairs={{0,1},{1,0},{2,3},{3,2},{4,5},{5,4},{6,7},{7,6},{8,9},{9,8},{10,11... | collective-permute-start | bytes 884744 | tf_op jit(solution)/shard_map/ppermute | solution.py:158
  53.3 4.4 %collective-permute-start.12 = (bf16[8,144,128]{2,1,0:T(8,128)(2,1)S(1)}, bf16[8,144,128]{2,1,0:T(8,128)(2,1)S(1)}, u32[]{:S(2)}, u32[]{:S(2)}) collective-permute-start(bf16[8,144,128]{2,1,0:T(8,128)(2,1)S(1)} %collective-permute-done.4.own_ref), channel_id=1, source_target_pairs={{0,1},{1,0},{2,3},{3,2},{4,5},{5,4},{6,7},{7,6},{8,9},{9,8},{10,11... | collective-permute-start | bytes 884744 | tf_op jit(solution)/shard_map/ppermute | solution.py:158
  68.4 30.1 %copy-start = (s32[8,1]{0,1:T(1,128)S(1)}, s32[8,1]{0,1:T(1,128)}, u32[]{:S(2)}) copy-start(s32[8,1]{0,1:T(1,128)} %param.7) | copy-start | bytes 100

commit v12 on v9

--- a/solution.py
+++ b/solution.py
@@ -75,15 +75,9 @@
     return total[0:1]
 
 
-def grams_kernel(triads_ref, own_w_ref, sib_w_ref, bins_ref, out_ref, *scratch):
+def grams_kernel(slots_ref, own_w_ref, sib_w_ref, bins_ref, out_ref, *scratch):
     buffers = (scratch[0:2], scratch[2:4])
-    depth, core = lax.axis_index("z"), lax.axis_index("core")
-    up = 1 - 2 * core
-
-    def slot(which):
-        turn = (up * (depth - (which & 7))) & 7
-        return turn * 64 + (which & 56) + (which >> 6)
-
+    core = lax.axis_index("core")
     weights = lane_weights(own_w_ref, sib_w_ref)
     lane = lax.broadcasted_iota(jnp.int32, (48, LANES), 1)
 
@@ -91,16 +85,14 @@
         w_ref, q_ref = buffer
         owner = reader >> 2
         row = (reader & 2) * 2 + core * 2 + (reader & 1)
-        k_bin = row * 64 + owner * 8 + depth
-        first = bins_ref[owner * 8 + row].astype(F32)
+        listed = owner * 8 + row
+        first = bins_ref[listed].astype(F32)
         k_real = first[:, :LANES] * weights
         k_imag = first[:, LANES:] * weights
 
         def some(triads):
             for t in triads:
-                l_bin = triads_ref[owner * 8 + row, t]
-                m_bin = (k_bin + l_bin) & 511
-                second = bins_ref[slot(l_bin)].astype(F32)
+                second = bins_ref[slots_ref[listed, t]].astype(F32)
                 l_real, l_imag = second[:, :LANES], second[:, LANES:]
                 real = (k_real * l_real - k_imag * l_imag).astype(BF16)
                 imag = k_real * l_imag + k_imag * l_real
@@ -109,7 +101,7 @@
                 w_ref[48 * t : 48 * t + 24, LANES:] = plus
                 w_ref[48 * t + 24 : 48 * t + 48, :LANES] = minus
                 w_ref[48 * t + 24 : 48 * t + 48, LANES:] = real
-                q_ref[24 * t : 24 * t + 24, :] = bins_ref[slot(m_bin)]
+                q_ref[24 * t : 24 * t + 24, :] = bins_ref[slots_ref[listed, 16 + t]]
 
         return some
 
@@ -192,7 +184,7 @@
     )(*operands)
 
 
-def grams(lists, own_tile, sib_tile, bins):
+def grams(slots, own_tile, sib_tile, bins):
     return pl.pallas_call(
         grams_kernel,
         out_shape=jax.ShapeDtypeStruct((16, 2, 48, 384), BF16),
@@ -204,7 +196,7 @@
             flops=12000000000, bytes_accessed=8000000, transcendentals=0
         ),
         name="grams",
-    )(lists, own_tile, sib_tile, bins)
+    )(slots, own_tile, sib_tile, bins)
 
 
 def body(modes, point_weights, triads, counts):
@@ -218,7 +210,14 @@
     )(modes.reshape(48, 24, LANES), triads[:, 0], point_weights[None])
     received = lax.all_to_all(pieces, ("x", "yh"), 0, 0)
     codes = received[:, 144:, :32].astype(F32)
-    lists = (codes[:, :, :16] * 64 + codes[:, :, 16:]).astype(jnp.int32).reshape(64, 16)
+    seconds = (codes[:, :, :16] * 64 + codes[:, :, 16:]).astype(jnp.int32)
+    depth, core = lax.axis_index("z"), lax.axis_index("core")
+    shape = (8, 8, 1)
+    firsts = lax.broadcasted_iota(jnp.int32, shape, 1) * 64
+    firsts = firsts + lax.broadcasted_iota(jnp.int32, shape, 0) * 8 + depth
+    both = jnp.concatenate([seconds, (firsts + seconds) & 511], axis=2)
+    turn = ((1 - 2 * core) * (depth - (both & 7))) & 7
+    slots = (turn * 64 + (both & 56) + (both >> 6)).reshape(64, 32)
 
     beside = swap(received)
     near, sib = [received[:, :144]], [beside[:, :144]]
@@ -243,7 +242,7 @@
     bins = unpack(*passed[2], bins, 5)
     bins = unpack(last, last_passed, bins, 4)
 
-    partial = grams(lists, received[0, 144:], beside[0, 144:], bins)
+    partial = grams(slots, received[0, 144:], beside[0, 144:], bins)
     parts = lax.all_to_all(partial, ("x", "yh", "yl"), 0, 0)
     parts, counts = lax.optimization_barrier((parts, counts))
     summed = jnp.sum(parts.astype(F32), axis=0) / 24

time: 94.9 us -> 95 us (level)
  blocking collectives: 43.9 us -> 29.1 us
  waiting for transfers between devices: 7.33 us -> 15.9 us
  starting transfers between devices: 28.8 us -> 35.1 us
    all_to_all x1 -> x0, blocking collectives: 15.5 us -> none  [body(): received = lax.all_to_all(pieces, ('x', 'yh'), 0, 0)]
    all_to_all x0 -> x1, starting transfers between devices: none -> 7.48 us  [body(): received = lax.all_to_all(pieces, ('x', 'yh'), 0, 0)]
    all_to_all x0 -> x1, waiting for transfers between devices: none -> 7.4 us  [body(): received = lax.all_to_all(pieces, ('x', 'yh'), 0, 0)]
    ppermute x7, waiting for transfers between devices: 6.63 us -> 7.81 us  [ring(): return lax.ppermute(array, ('z', 'core'), pairs)]
  transfers between devices with their start and end apart: 15 -> 16, of which waited for: 4 -> 6; matrix products, arithmetic and copies ran while one was open for 0% -> 0% of each run, Pallas kernels for 4% -> 4%
where the time goes in v12:
time: 95 us; the launch traced here: 94.8 us
  starting transfers between devices  35.1 us (37%)
  blocking collectives  29.1 us (31%)
  waiting for transfers between devices  15.9 us (17%)
  Pallas kernels  12.1 us (13%)
  other arithmetic  1.5 us (2%)
    all_to_all x1, blocking collectives, body(): parts = lax.all_to_all(partial, ('x', 'yh', 'yl'), 0, 0)  20.8 us
    ppermute x7, starting transfers between devices, ring(): return lax.ppermute(array, ('z', 'core'), pairs)  16.9 us
    ppermute x8, starting transfers between devices, step(): lax.ppermute(array, axes, [(i, (i + by) % size) for i in range(size)])  10.8 us
    all_gather x1, blocking collectives, body(): gathered = lax.all_gather(rows, ('yl', 'core'), tiled=True)  8.26 us
    ppermute x7, waiting for transfers between devices, ring(): return lax.ppermute(array, ('z', 'core'), pairs)  7.81 us
    all_to_all x1, starting transfers between devices, body(): received = lax.all_to_all(pieces, ('x', 'yh'), 0, 0)  7.48 us
    all_to_all x1, waiting for transfers between devices, body(): received = lax.all_to_all(pieces, ('x', 'yh'), 0, 0)  7.4 us
    pallas_call x1, Pallas kernels, grams(): pl.pallas_call(grams_kernel, out_shape=jax.ShapeDtypeStruct((16, 2, 48, 3...  5.79 us
  transfers between devices with their start and end apart: 16, of which 6 were waited for; matrix products, arithmetic and copies ran while one was open for 0% of the time, Pallas kernels for 4%

profile of v12, /device:TPU:1, one launch (start us, length us, event | category | flops | bytes accessed | tf_op | source)
XLA Modules:
  0.0 94.8 jit_solution(15965550723083196744)
XLA Ops:
  0.0 2.3 %split.1 = bf16[8,152,128]{2,1,0:T(8,128)(2,1)} custom-call(bf16[48,24,128]{2,1,0:T(8,128)(2,1)} %bitcast.20, s32[8,16]{1,0:T(8,128)} %bitcast.21, f32[1,128]{1,0:T(1,128)} %bitcast.22), custom_call_target="tpu_custom_call" | custom-call | tf_op jit(solution)/shard_map/split/pallas_call | solution.py:203
  2.3 7.5 %all-to-all-start = ((bf16[8,152,128]{2,1,0:T(8,128)(2,1)}), bf16[8,152,128]{2,1,0:T(8,128)(2,1)S(1)}, u32[]{:S(2)}, u32[]{:S(2)}) async-start(bf16[8,152,128]{2,1,0:T(8,128)(2,1)} %split.1), calls=%async_computation | async-start | bytes 622592 | tf_op jit(solution)/shard_map/all_to_all | solution.py:211
  9.9 7.4 %all-to-all-done = bf16[8,152,128]{2,1,0:T(8,128)(2,1)S(1)} async-done(((bf16[8,152,128]{2,1,0:T(8,128)(2,1)}), bf16[8,152,128]{2,1,0:T(8,128)(2,1)S(1)}, u32[]{:S(2)}, u32[]{:S(2)}) %all-to-all-start) | async-done | bytes 311328 | tf_op jit(solution)/shard_map/all_to_all | solution.py:211
  17.3 5.7 %collective-permute-start.1 = (bf16[8,144,128]{2,1,0:T(8,128)(2,1)S(1)}, bf16[8,144,128]{2,1,0:T(8,128)(2,1)S(1)}, u32[]{:S(2)}, u32[]{:S(2)}) collective-permute-start(bf16[8,144,128]{2,1,0:T(8,128)(2,1)S(1)} %slice.33.own_ref), channel_id=1, source_target_pairs={{0,4},{1,29},{4,8},{5,1},{8,12},{9,5},{12,16},{13,9},{16,20},{17,1... | collective-permute-start | bytes 884744 | tf_op jit(solution)/shard_map/ppermute | solution.py:161
  23.0 0.4 collective-permute-start.5
  23.4 0.8 collective-permute-start
  24.3 4.2 %collective-permute-done.1.own_ref = bf16[8,144,128]{2,1,0:T(8,128)(2,1)S(1)} collective-permute-done((bf16[8,144,128]{2,1,0:T(8,128)(2,1)S(1)}, bf16[8,144,128]{2,1,0:T(8,128)(2,1)S(1)}, u32[]{:S(2)}, u32[]{:S(2)}) %collective-permute-start.1) | collective-permute-done | bytes 294944 | tf_op jit(solution)/shard_map/ppermute | solution.py:161
  28.4 1.0 %collective-permute-done.5.sib_ref = bf16[8,144,128]{2,1,0:T(8,128)(2,1)S(1)} collective-permute-done((bf16[8,144,128]{2,1,0:T(8,128)(2,1)S(1)}, bf16[8,144,128]{2,1,0:T(8,128)(2,1)S(1)}, u32[]{:S(2)}, u32[]{:S(2)}) %collective-permute-start.5) | collective-permute-done | bytes 294944 | tf_op jit(solution)/shard_map/ppermute | solution.py:161
  29.4 2.9 %collective-permute-start.10 = (bf16[8,144,128]{2,1,0:T(8,128)(2,1)S(1)}, bf16[8,144,128]{2,1,0:T(8,128)(2,1)S(1)}, u32[]{:S(2)}, u32[]{:S(2)}) collective-permute-start(bf16[8,144,128]{2,1,0:T(8,128)(2,1)S(1)} %collective-permute-done.5.sib_ref), channel_id=1, source_target_pairs={{0,1},{1,0},{2,3},{3,2},{4,5},{5,4},{6,7},{7,6},{8,9},{9,8},{10,11... | collective-permute-start | bytes 884744 | tf_op jit(solution)/shard_map/ppermute | solution.py:149
  32.3 2.5 %collective-permute-start.2 = (bf16[8,144,128]{2,1,0:T(8,128)(2,1)S(1)}, bf16[8,144,128]{2,1,0:T(8,128)(2,1)S(1)}, u32[]{:S(2)}, u32[]{:S(2)}) collective-permute-start(bf16[8,144,128]{2,1,0:T(8,128)(2,1)S(1)} %collective-permute-done.1.own_ref), channel_id=1, source_target_pairs={{0,4},{1,29},{4,8},{5,1},{8,12},{9,5},{12,16},{13,9},{16,20},{17,1... | collective-permute-start | bytes 884744 | tf_op jit(solution)/shard_map/ppermute | solution.py:161
  34.9 1.2 %collective-permute-start.6 = (bf16[8,144,128]{2,1,0:T(8,128)(2,1)S(1)}, bf16[8,144,128]{2,1,0:T(8,128)(2,1)S(1)}, u32[]{:S(2)}, u32[]{:S(2)}) collective-permute-start(bf16[8,144,128]{2,1,0:T(8,128)(2,1)S(1)} %collective-permute-done.5.sib_ref), channel_id=1, source_target_pairs={{0,4},{1,29},{4,8},{5,1},{8,12},{9,5},{12,16},{13,9},{16,20},{17,1... | collective-permute-start | bytes 884744 | tf_op jit(solution)/shard_map/ppermute | solution.py:161
  36.2 2.3 %collective-permute-done.2.own_ref = bf16[8,144,128]{2,1,0:T(8,128)(2,1)S(1)} collective-permute-done((bf16[8,144,128]{2,1,0:T(8,128)(2,1)S(1)}, bf16[8,144,128]{2,1,0:T(8,128)(2,1)S(1)}, u32[]{:S(2)}, u32[]{:S(2)}) %collective-permute-start.2) | collective-permute-done | bytes 294944 | tf_op jit(solution)/shard_map/ppermute | solution.py:161
  38.6 3.1 %collective-permute-start.3 = (bf16[8,144,128]{2,1,0:T(8,128)(2,1)S(1)}, bf16[8,144,128]{2,1,0:T(8,128)(2,1)S(1)}, u32[]{:S(2)}, u32[]{:S(2)}) collective-permute-start(bf16[8,144,128]{2,1,0:T(8,128)(2,1)S(1)} %collective-permute-done.2.own_ref), channel_id=1, source_target_pairs={{0,4},{1,29},{4,8},{5,1},{8,12},{9,5},{12,16},{13,9},{16,20},{17,1... | collective-permute-start | bytes 884744 | tf_op jit(solution)/shard_map/ppermute | solution.py:161
  41.7 0.5 unpack.8.refs_0_
  42.2 1.2 %collective-permute-start.8 = (bf16[8,144,128]{2,1,0:T(8,128)(2,1)S(1)}, bf16[8,144,128]{2,1,0:T(8,128)(2,1)S(1)}, u32[]{:S(2)}, u32[]{:S(2)}) collective-permute-start(bf16[8,144,128]{2,1,0:T(8,128)(2,1)S(1)} %collective-permute-done.6.sib_ref), channel_id=1, source_target_pairs={{0,1},{1,0},{2,3},{3,2},{4,5},{5,4},{6,7},{7,6},{8,9},{9,8},{10,11... | collective-permute-start | bytes 884744 | tf_op jit(solution)/shard_map/ppermute | solution.py:149
  43.5 1.9 %collective-permute-start.7 = (bf16[8,144,128]{2,1,0:T(8,128)(2,1)S(1)}, bf16[8,144,128]{2,1,0:T(8,128)(2,1)S(1)}, u32[]{:S(2)}, u32[]{:S(2)}) collective-permute-start(bf16[8,144,128]{2,1,0:T(8,128)(2,1)S(1)} %collective-permute-done.6.sib_ref), channel_id=1, source_target_pairs={{0,4},{1,29},{4,8},{5,1},{8,12},{9,5},{12,16},{13,9},{16,20},{17,1... | collective-permute-start | bytes 884744 | tf_op jit(solution)/shard_map/ppermute | solution.py:161
  45.4 0.5 unpack.9.refs_0_
  45.9 0.5 unpack.10.refs_0_
  46.4 2.1 %collective-permute-start.4 = (bf16[8,144,128]{2,1,0:T(8,128)(2,1)S(1)}, bf16[8,144,128]{2,1,0:T(8,128)(2,1)S(1)}, u32[]{:S(2)}, u32[]{:S(2)}) collective-permute-start(bf16[8,144,128]{2,1,0:T(8,128)(2,1)S(1)} %collective-permute-done.3.own_ref), channel_id=1, source_target_pairs={{0,4},{1,29},{4,8},{5,1},{8,12},{9,5},{12,16},{13,9},{16,20},{17,1... | collective-permute-start | bytes 884744 | tf_op jit(solution)/shard_map/ppermute | solution.py:161
  48.5 0.5 unpack.11.refs_0_
  49.3 2.6 %collective-permute-start.13 = (bf16[8,144,128]{2,1,0:T(8,128)(2,1)S(1)}, bf16[8,144,128]{2,1,0:T(8,128)(2,1)S(1)}, u32[]{:S(2)}, u32[]{:S(2)}) collective-permute-start(bf16[8,144,128]{2,1,0:T(8,128)(2,1)S(1)} %collective-permute-done.7.sib_ref), channel_id=1, source_target_pairs={{0,1},{1,0},{2,3},{3,2},{4,5},{5,4},{6,7},{7,6},{8,9},{9,8},{10,11... | collective-permute-start | bytes 884744 | tf_op jit(solution)/shard_map/ppermute | solution.py:149
  51.9 0.5 unpack.12.refs_0_
  52.4 0.5 unpack.13.refs_0_
  52.9 3.2 %collective-permute-start.12 = (bf16[8,144,128]{2,1,0:T(8,128)(2,1)S(1)}, bf16[8,144,128]{2,1,0:T(8,128)(2,1)S(1)}, u32[]{:S(2)}, u32[]{:S(2)}) collective-permute-start(bf16[8,144,128]{2,1,0:T(8,128)(2,1)S(1)} %collective-permute-done.4.own_ref), channel_id=1, source_target_pairs={{0,1},{1,0},{2,3},{3,2},{4,5},{5,4},{6,7},{7,6},{8,9},{9,8},{10,11... | collective-permute-start | bytes 884744 | tf_op jit(solution)/shard_map/ppermute | solution.py:149
  56.2 0.5 unpack.14.refs_0_
  56.7 0.7 collective-permute-done.12.sib_ref
  57.4 0.5 unpack.15.bins_ref
  57.9 5.8 %grams.1 = bf16[16,2,48,384]{3,2,1,0:T(8,128)(2,1)S(1)} custom-call(s32[64,32]{1,0:T(8,128)S(1)} %shift-right-arithmetic_add_fusion.slots_ref, bf16[8,128]{1,0:T(8,128)(2,1)S(1)} %slice_bitcast_fusion.1.own_w_ref, bf16[8,128]{1,0:T(8,128)(2,1)S(1)} %slice_bitcast_fusion.sib_w_ref, bf16[512,24,256]{2,1,0:T(8,128)(2,1)S(1)} %unpack.15.bins_ref), custom_call_target="tpu_custom_call" | custom-call | flops 12000000000 | bytes 8000000 | tf_op jit(solution)/shard_map/grams/pallas_call | solution.py:188
  63.7 20.8 %all_to_all.10 = bf16[16,2,48,384]{3,2,1,0:T(8,128)(2,1)S(1)} all-to-all(bf16[16,2,48,384]{3,2,1,0:T(8,128)(2,1)S(1)} %grams.1), channel_id=1, replica_groups=mesh['x'=4,'yh'=2,'z'=8,'yl'=2,'core'=2] {'x','yh','yl'}, dimensions={0} | all-to-all | bytes 2359296 | tf_op jit(solution)/shard_map/all_to_all | solution.py:246
  85.2 0.4 reshape.68
  85.5 8.3 %all_gather.3 = f32[8,1,16,1152]{3,2,1,0:T(8,128)S(1)} all-gather(f32[2,1,16,1152]{3,2,1,0:T(8,128)S(1)} %bitcast.19), channel_id=1, replica_groups=mesh['x'=4,'yh'=2,'z'=8,'yl'=2,'core'=2] {'yl','core'}, dimensions={0}, use_global_device_ids=true | all-gather | bytes 737280 | tf_op jit(solution)/shard_map/all_gather | solution.py:250
  93.9 0.9 broadcast_select_fusion
  (31 shorter events, 1.5 us)
Async XLA Ops:
  2.3 15.0 %all-to-all-start = ((bf16[8,152,128]{2,1,0:T(8,128)(2,1)}), bf16[8,152,128]{2,1,0:T(8,128)(2,1)S(1)}, u32[]{:S(2)}, u32[]{:S(2)}) async-start(bf16[8,152,128]{2,1,0:T(8,128)(2,1)} %split.1), calls=%async_computation | async-start | bytes 622592 | tf_op jit(solution)/shard_map/all_to_all | solution.py:211
  17.3 11.1 %collective-permute-start.1 = (bf16[8,144,128]{2,1,0:T(8,128)(2,1)S(1)}, bf16[8,144,128]{2,1,0:T(8,128)(2,1)S(1)}, u32[]{:S(2)}, u32[]{:S(2)}) collective-permute-start(bf16[8,144,128]{2,1,0:T(8,128)(2,1)S(1)} %slice.33.own_ref), channel_id=1, source_target_pairs={{0,4},{1,29},{4,8},{5,1},{8,12},{9,5},{12,16},{13,9},{16,20},{17,1... | collective-permute-start | bytes 884744 | tf_op jit(solution)/shard_map/ppermute | solution.py:161
  23.0 6.4 %collective-permute-start.5 = (bf16[8,144,128]{2,1,0:T(8,128)(2,1)S(1)}, bf16[8,144,128]{2,1,0:T(8,128)(2,1)S(1)}, u32[]{:S(2)}, u32[]{:S(2)}) collective-permute-start(bf16[8,144,128]{2,1,0:T(8,128)(2,1)S(1)} %slice.33.own_ref), channel_id=1, source_target_pairs={{0,29},{1,4},{4,1},{5,8},{8,5},{9,12},{12,9},{13,16},{16,13},{17,2... | collective-permute-start | bytes 884744 | tf_op jit(solution)/shard_map/ppermute | solution.py:161
  23.4 12.8 %collective-permute-start = (bf16[8,152,128]{2,1,0:T(8,128)(2,1)S(1)}, bf16[8,152,128]{2,1,0:T(8,128)(2,1)S(1)}, u32[]{:S(2)}, u32[]{:S(2)}) collective-permute-start(bf16[8,152,128]{2,1,0:T(8,128)(2,1)S(1)} %all-to-all-done), channel_id=1, source_target_pairs={{0,1},{1,0},{2,3},{3,2},{4,5},{5,4},{6,7},{7,6},{8,9},{9,8},{10,11... | collective-permute-start | bytes 933896 | tf_op jit(solution)/shard_map/ppermute | solution.py:149
  29.4 14.0 %collective-permute-start.10 = (bf16[8,144,128]{2,1,0:T(8,128)(2,1)S(1)}, bf16[8,144,128]{2,1,0:T(8,128)(2,1)S(1)}, u32[]{:S(2)}, u32[]{:S(2)}) collective-permute-start(bf16[8,144,128]{2,1,0:T(8,128)(2,1)S(1)} %collective-permute-done.5.sib_ref), channel_id=1, source_target_pairs={{0,1},{1,0},{2,3},{3,2},{4,5},{5,4},{6,7},{7,6},{8,9},{9,8},{10,11... | collective-permute-start | bytes 884744 | tf_op jit(solution)/shard_map/ppermute | solution.py:149
  32.3 6.2 %collective-permute-start.2 = (bf16[8,144,128]{2,1,0:T(8,128)(2,1)S(1)}, bf16[8,144,128]{2,1,0:T(8,128)(2,1)S(1)}, u32[]{:S(2)}, u32[]{:S(2)}) collective-permute-start(bf16[8,144,128]{2,1,0:T(8,128)(2,1)S(1)} %collective-permute-done.1.own_ref), channel_id=1, source_target_pairs={{0,4},{1,29},{4,8},{5,1},{8,12},{9,5},{12,16},{13,9},{16,20},{17,1... | collective-permute-start | bytes 884744 | tf_op jit(solution)/shard_map/ppermute | solution.py:161
  34.9 7.3 %collective-permute-start.6 = (bf16[8,144,128]{2,1,0:T(8,128)(2,1)S(1)}, bf16[8,144,128]{2,1,0:T(8,128)(2,1)S(1)}, u32[]{:S(2)}, u32[]{:S(2)}) collective-permute-start(bf16[8,144,128]{2,1,0:T(8,128)(2,1)S(1)} %collective-permute-done.5.sib_ref), channel_id=1, source_target_pairs={{0,4},{1,29},{4,8},{5,1},{8,12},{9,5},{12,16},{13,9},{16,20},{17,1... | collective-permute-start | bytes 884744 | tf_op jit(solution)/shard_map/ppermute | solution.py:161
  36.1 9.8 %collective-permute-start.11 = (bf16[8,144,128]{2,1,0:T(8,128)(2,1)S(1)}, bf16[8,144,128]{2,1,0:T(8,128)(2,1)S(1)}, u32[]{:S(2)}, u32[]{:S(2)}) collective-permute-start(bf16[8,144,128]{2,1,0:T(8,128)(2,1)S(1)} %collective-permute-done.1.own_ref), channel_id=1, source_target_pairs={{0,1},{1,0},{2,3},{3,2},{4,5},{5,4},{6,7},{7,6},{8,9},{9,8},{10,11... | collective-permute-start | bytes 884744 | tf_op jit(solution)/shard_map/ppermute | solution.py:149
  38.6 7.8 %collective-permute-start.3 = (bf16[8,144,128]{2,1,0:T(8,128)(2,1)S(1)}, bf16[8,144,128]{2,1,0:T(8,128)(2,1)S(1)}, u32[]{:S(2)}, u32[]{:S(2)}) collective-permute-start(bf16[8,144,128]{2,1,0:T(8,128)(2,1)S(1)} %collective-permute-done.2.own_ref), channel_id=1, source_target_pairs={{0,4},{1,29},{4,8},{5,1},{8,12},{9,5},{12,16},{13,9},{16,20},{17,1... | collective-permute-start | bytes 884744 | tf_op jit(solution)/shard_map/ppermute | solution.py:161
  42.2 9.7 %collective-permute-start.8 = (bf16[8,144,128]{2,1,0:T(8,128)(2,1)S(1)}, bf16[8,144,128]{2,1,0:T(8,128)(2,1)S(1)}, u32[]{:S(2)}, u32[]{:S(2)}) collective-permute-start(bf16[8,144,128]{2,1,0:T(8,128)(2,1)S(1)} %collective-permute-done.6.sib_ref), channel_id=1, source_target_pairs={{0,1},{1,0},{2,3},{3,2},{4,5},{5,4},{6,7},{7,6},{8,9},{9,8},{10,11... | collective-permute-start | bytes 884744 | tf_op jit(solution)/shard_map/ppermute | solution.py:149
  43.4 8.5 %collective-permute-start.9 = (bf16[8,144,128]{2,1,0:T(8,128)(2,1)S(1)}, bf16[8,144,128]{2,1,0:T(8,128)(2,1)S(1)}, u32[]{:S(2)}, u32[]{:S(2)}) collective-permute-start(bf16[8,144,128]{2,1,0:T(8,128)(2,1)S(1)} %collective-permute-done.2.own_ref), channel_id=1, source_target_pairs={{0,1},{1,0},{2,3},{3,2},{4,5},{5,4},{6,7},{7,6},{8,9},{9,8},{10,11... | collective-permute-start | bytes 884744 | tf_op jit(solution)/shard_map/ppermute | solution.py:149
  43.5 5.9 %collective-permute-start.7 = (bf16[8,144,128]{2,1,0:T(8,128)(2,1)S(1)}, bf16[8,144,128]{2,1,0:T(8,128)(2,1)S(1)}, u32[]{:S(2)}, u32[]{:S(2)}) collective-permute-start(bf16[8,144,128]{2,1,0:T(8,128)(2,1)S(1)} %collective-permute-done.6.sib_ref), channel_id=1, source_target_pairs={{0,4},{1,29},{4,8},{5,1},{8,12},{9,5},{12,16},{13,9},{16,20},{17,1... | collective-permute-start | bytes 884744 | tf_op jit(solution)/shard_map/ppermute | solution.py:161
  46.4 6.5 %collective-permute-start.4 = (bf16[8,144,128]{2,1,0:T(8,128)(2,1)S(1)}, bf16[8,144,128]{2,1,0:T(8,128)(2,1)S(1)}, u32[]{:S(2)}, u32[]{:S(2)}) collective-permute-start(bf16[8,144,128]{2,1,0:T(8,128)(2,1)S(1)} %collective-permute-done.3.own_ref), channel_id=1, source_target_pairs={{0,4},{1,29},{4,8},{5,1},{8,12},{9,5},{12,16},{13,9},{16,20},{17,1... | collective-permute-start | bytes 884744 | tf_op jit(solution)/shard_map/ppermute | solution.py:161
  49.3 6.8 %collective-permute-start.13 = (bf16[8,144,128]{2,1,0:T(8,128)(2,1)S(1)}, bf16[8,144,128]{2,1,0:T(8,128)(2,1)S(1)}, u32[]{:S(2)}, u32[]{:S(2)}) collective-permute-start(bf16[8,144,128]{2,1,0:T(8,128)(2,1)S(1)} %collective-permute-done.7.sib_ref), channel_id=1, source_target_pairs={{0,1},{1,0},{2,3},{3,2},{4,5},{5,4},{6,7},{7,6},{8,9},{9,8},{10,11... | collective-permute-start | bytes 884744 | tf_op jit(solution)/shard_map/ppermute | solution.py:149
  51.9 4.3 %collective-permute-start.14 = (bf16[8,144,128]{2,1,0:T(8,128)(2,1)S(1)}, bf16[8,144,128]{2,1,0:T(8,128)(2,1)S(1)}, u32[]{:S(2)}, u32[]{:S(2)}) collective-permute-start(bf16[8,144,128]{2,1,0:T(8,128)(2,1)S(1)} %collective-permute-done.3.own_ref), channel_id=1, source_target_pairs={{0,1},{1,0},{2,3},{3,2},{4,5},{5,4},{6,7},{7,6},{8,9},{9,8},{10,11... | collective-permute-start | bytes 884744 | tf_op jit(solution)/shard_map/ppermute | solution.py:149
  52.9 4.4 %collective-permute-start.12 = (bf16[8,144,128]{2,1,0:T(8,128)(2,1)S(1)}, bf16[8,144,128]{2,1,0:T(8,128)(2,1)S(1)}, u32[]{:S(2)}, u32[]{:S(2)}) collective-permute-start(bf16[8,144,128]{2,1,0:T(8,128)(2,1)S(1)} %collective-permute-done.4.own_ref), channel_id=1, source_target_pairs={{0,1},{1,0},{2,3},{3,2},{4,5},{5,4},{6,7},{7,6},{8,9},{9,8},{10,11... | collective-permute-start | bytes 884744 | tf_op jit(solution)/shard_map/ppermute | solution.py:149
  63.7 30.1 %copy-start = (s32[8,1]{0,1:T(1,128)S(1)}, s32[8,1]{0,1:T(1,128)}, u32[]{:S(2)}) copy-start(s32[8,1]{0,1:T(1,128)} %param.7) | copy-start | bytes 100

commit v13 on v12

--- a/solution.py
+++ b/solution.py
@@ -179,7 +179,7 @@
         out_specs=pl.BlockSpec((64, 24, 256), lambda i: (turn, 0, 0)),
         input_output_aliases={} if bins is None else {2: 0},
         compiler_params=params(8),
-        cost_estimate=pl.CostEstimate(flops=1500000000, bytes_accessed=2000000, transcendentals=0),
+        cost_estimate=pl.CostEstimate(flops=1000000000, bytes_accessed=2000000, transcendentals=0),
         name="unpack",
     )(*operands)
 

time: 95 us -> 95 us (level)
  transfers between devices with their start and end apart: 16 -> 16, of which waited for: 6 -> 5; matrix products, arithmetic and copies ran while one was open for 0% -> 0% of each run, Pallas kernels for 4% -> 4%
where the time goes in v13:
time: 95 us; the launch traced here: 94.8 us
  starting transfers between devices  35.6 us (37%)
  blocking collectives  29.1 us (31%)
  waiting for transfers between devices  15.4 us (16%)
  Pallas kernels  12.1 us (13%)
  other arithmetic  1.5 us (2%)
    all_to_all x1, blocking collectives, body(): parts = lax.all_to_all(partial, ('x', 'yh', 'yl'), 0, 0)  20.9 us
    ppermute x7, starting transfers between devices, ring(): return lax.ppermute(array, ('z', 'core'), pairs)  17.2 us
    ppermute x8, starting transfers between devices, step(): lax.ppermute(array, axes, [(i, (i + by) % size) for i in range(size)])  11 us
    all_gather x1, blocking collectives, body(): gathered = lax.all_gather(rows, ('yl', 'core'), tiled=True)  8.24 us
    all_to_all x1, starting transfers between devices, body(): received = lax.all_to_all(pieces, ('x', 'yh'), 0, 0)  7.48 us
    all_to_all x1, waiting for transfers between devices, body(): received = lax.all_to_all(pieces, ('x', 'yh'), 0, 0)  7.4 us
    ppermute x7, waiting for transfers between devices, ring(): return lax.ppermute(array, ('z', 'core'), pairs)  7.29 us
    pallas_call x1, Pallas kernels, grams(): pl.pallas_call(grams_kernel, out_shape=jax.ShapeDtypeStruct((16, 2, 48, 3...  5.79 us
  transfers between devices with their start and end apart: 16, of which 5 were waited for; matrix products, arithmetic and copies ran while one was open for 0% of the time, Pallas kernels for 4%

profile of v13, /device:TPU:1, one launch (start us, length us, event | category | flops | bytes accessed | tf_op | source)
XLA Modules:
  0.0 94.8 jit_solution(10027137181072108422)
XLA Ops:
  0.0 2.3 %split.1 = bf16[8,152,128]{2,1,0:T(8,128)(2,1)} custom-call(bf16[48,24,128]{2,1,0:T(8,128)(2,1)} %bitcast.20, s32[8,16]{1,0:T(8,128)} %bitcast.21, f32[1,128]{1,0:T(1,128)} %bitcast.22), custom_call_target="tpu_custom_call" | custom-call | tf_op jit(solution)/shard_map/split/pallas_call | solution.py:203
  2.3 7.5 %all-to-all-start = ((bf16[8,152,128]{2,1,0:T(8,128)(2,1)}), bf16[8,152,128]{2,1,0:T(8,128)(2,1)S(1)}, u32[]{:S(2)}, u32[]{:S(2)}) async-start(bf16[8,152,128]{2,1,0:T(8,128)(2,1)} %split.1), calls=%async_computation | async-start | bytes 622592 | tf_op jit(solution)/shard_map/all_to_all | solution.py:211
  9.9 7.4 %all-to-all-done = bf16[8,152,128]{2,1,0:T(8,128)(2,1)S(1)} async-done(((bf16[8,152,128]{2,1,0:T(8,128)(2,1)}), bf16[8,152,128]{2,1,0:T(8,128)(2,1)S(1)}, u32[]{:S(2)}, u32[]{:S(2)}) %all-to-all-start) | async-done | bytes 311328 | tf_op jit(solution)/shard_map/all_to_all | solution.py:211
  17.3 5.7 %collective-permute-start.1 = (bf16[8,144,128]{2,1,0:T(8,128)(2,1)S(1)}, bf16[8,144,128]{2,1,0:T(8,128)(2,1)S(1)}, u32[]{:S(2)}, u32[]{:S(2)}) collective-permute-start(bf16[8,144,128]{2,1,0:T(8,128)(2,1)S(1)} %slice.33.own_ref), channel_id=1, source_target_pairs={{0,4},{1,29},{4,8},{5,1},{8,12},{9,5},{12,16},{13,9},{16,20},{17,1... | collective-permute-start | bytes 884744 | tf_op jit(solution)/shard_map/ppermute | solution.py:161
  23.0 0.4 collective-permute-start.5
  23.4 5.0 %collective-permute-done.1.own_ref = bf16[8,144,128]{2,1,0:T(8,128)(2,1)S(1)} collective-permute-done((bf16[8,144,128]{2,1,0:T(8,128)(2,1)S(1)}, bf16[8,144,128]{2,1,0:T(8,128)(2,1)S(1)}, u32[]{:S(2)}, u32[]{:S(2)}) %collective-permute-start.1) | collective-permute-done | bytes 294944 | tf_op jit(solution)/shard_map/ppermute | solution.py:161
  28.4 3.1 %collective-permute-start.2 = (bf16[8,144,128]{2,1,0:T(8,128)(2,1)S(1)}, bf16[8,144,128]{2,1,0:T(8,128)(2,1)S(1)}, u32[]{:S(2)}, u32[]{:S(2)}) collective-permute-start(bf16[8,144,128]{2,1,0:T(8,128)(2,1)S(1)} %collective-permute-done.1.own_ref), channel_id=1, source_target_pairs={{0,4},{1,29},{4,8},{5,1},{8,12},{9,5},{12,16},{13,9},{16,20},{17,1... | collective-permute-start | bytes 884744 | tf_op jit(solution)/shard_map/ppermute | solution.py:161
  31.6 0.8 collective-permute-start
  32.6 3.0 %collective-permute-start.6 = (bf16[8,144,128]{2,1,0:T(8,128)(2,1)S(1)}, bf16[8,144,128]{2,1,0:T(8,128)(2,1)S(1)}, u32[]{:S(2)}, u32[]{:S(2)}) collective-permute-start(bf16[8,144,128]{2,1,0:T(8,128)(2,1)S(1)} %collective-permute-done.5.sib_ref), channel_id=1, source_target_pairs={{0,4},{1,29},{4,8},{5,1},{8,12},{9,5},{12,16},{13,9},{16,20},{17,1... | collective-permute-start | bytes 884744 | tf_op jit(solution)/shard_map/ppermute | solution.py:161
  35.5 2.8 %collective-permute-start.3 = (bf16[8,144,128]{2,1,0:T(8,128)(2,1)S(1)}, bf16[8,144,128]{2,1,0:T(8,128)(2,1)S(1)}, u32[]{:S(2)}, u32[]{:S(2)}) collective-permute-start(bf16[8,144,128]{2,1,0:T(8,128)(2,1)S(1)} %collective-permute-done.2.own_ref), channel_id=1, source_target_pairs={{0,4},{1,29},{4,8},{5,1},{8,12},{9,5},{12,16},{13,9},{16,20},{17,1... | collective-permute-start | bytes 884744 | tf_op jit(solution)/shard_map/ppermute | solution.py:161
  38.5 0.7 collective-permute-done.6.sib_ref
  39.2 4.3 %collective-permute-start.8 = (bf16[8,144,128]{2,1,0:T(8,128)(2,1)S(1)}, bf16[8,144,128]{2,1,0:T(8,128)(2,1)S(1)}, u32[]{:S(2)}, u32[]{:S(2)}) collective-permute-start(bf16[8,144,128]{2,1,0:T(8,128)(2,1)S(1)} %collective-permute-done.6.sib_ref), channel_id=1, source_target_pairs={{0,1},{1,0},{2,3},{3,2},{4,5},{5,4},{6,7},{7,6},{8,9},{9,8},{10,11... | collective-permute-start | bytes 884744 | tf_op jit(solution)/shard_map/ppermute | solution.py:149
  43.4 1.3 %collective-permute-start.7 = (bf16[8,144,128]{2,1,0:T(8,128)(2,1)S(1)}, bf16[8,144,128]{2,1,0:T(8,128)(2,1)S(1)}, u32[]{:S(2)}, u32[]{:S(2)}) collective-permute-start(bf16[8,144,128]{2,1,0:T(8,128)(2,1)S(1)} %collective-permute-done.6.sib_ref), channel_id=1, source_target_pairs={{0,4},{1,29},{4,8},{5,1},{8,12},{9,5},{12,16},{13,9},{16,20},{17,1... | collective-permute-start | bytes 884744 | tf_op jit(solution)/shard_map/ppermute | solution.py:161
  44.8 0.5 unpack.8.refs_0_
  45.3 0.5 unpack.9.refs_0_
  45.8 0.9 collective-permute-start.4
  46.7 0.5 unpack.10.refs_0_
  47.2 0.5 unpack.11.refs_0_
  47.7 1.6 %collective-permute-done.7.sib_ref = bf16[8,144,128]{2,1,0:T(8,128)(2,1)S(1)} collective-permute-done((bf16[8,144,128]{2,1,0:T(8,128)(2,1)S(1)}, bf16[8,144,128]{2,1,0:T(8,128)(2,1)S(1)}, u32[]{:S(2)}, u32[]{:S(2)}) %collective-permute-start.7) | collective-permute-done | bytes 294944 | tf_op jit(solution)/shard_map/ppermute | solution.py:161
  49.3 2.6 %collective-permute-start.13 = (bf16[8,144,128]{2,1,0:T(8,128)(2,1)S(1)}, bf16[8,144,128]{2,1,0:T(8,128)(2,1)S(1)}, u32[]{:S(2)}, u32[]{:S(2)}) collective-permute-start(bf16[8,144,128]{2,1,0:T(8,128)(2,1)S(1)} %collective-permute-done.7.sib_ref), channel_id=1, source_target_pairs={{0,1},{1,0},{2,3},{3,2},{4,5},{5,4},{6,7},{7,6},{8,9},{9,8},{10,11... | collective-permute-start | bytes 884744 | tf_op jit(solution)/shard_map/ppermute | solution.py:149
  51.9 0.5 unpack.12.refs_0_
  52.4 0.5 unpack.13.refs_0_
  52.9 3.2 %collective-permute-start.12 = (bf16[8,144,128]{2,1,0:T(8,128)(2,1)S(1)}, bf16[8,144,128]{2,1,0:T(8,128)(2,1)S(1)}, u32[]{:S(2)}, u32[]{:S(2)}) collective-permute-start(bf16[8,144,128]{2,1,0:T(8,128)(2,1)S(1)} %collective-permute-done.4.own_ref), channel_id=1, source_target_pairs={{0,1},{1,0},{2,3},{3,2},{4,5},{5,4},{6,7},{7,6},{8,9},{9,8},{10,11... | collective-permute-start | bytes 884744 | tf_op jit(solution)/shard_map/ppermute | solution.py:149
  56.2 0.5 unpack.14.refs_0_
  56.7 0.7 collective-permute-done.12.sib_ref
  57.4 0.5 unpack.15.bins_ref
  57.9 5.8 %grams.1 = bf16[16,2,48,384]{3,2,1,0:T(8,128)(2,1)S(1)} custom-call(s32[64,32]{1,0:T(8,128)S(1)} %shift-right-arithmetic_add_fusion.slots_ref, bf16[8,128]{1,0:T(8,128)(2,1)S(1)} %slice_bitcast_fusion.1.own_w_ref, bf16[8,128]{1,0:T(8,128)(2,1)S(1)} %slice_bitcast_fusion.sib_w_ref, bf16[512,24,256]{2,1,0:T(8,128)(2,1)S(1)} %unpack.15.bins_ref), custom_call_target="tpu_custom_call" | custom-call | flops 12000000000 | bytes 8000000 | tf_op jit(solution)/shard_map/grams/pallas_call | solution.py:188
  63.7 20.9 %all_to_all.10 = bf16[16,2,48,384]{3,2,1,0:T(8,128)(2,1)S(1)} all-to-all(bf16[16,2,48,384]{3,2,1,0:T(8,128)(2,1)S(1)} %grams.1), channel_id=1, replica_groups=mesh['x'=4,'yh'=2,'z'=8,'yl'=2,'core'=2] {'x','yh','yl'}, dimensions={0} | all-to-all | bytes 2359296 | tf_op jit(solution)/shard_map/all_to_all | solution.py:246
  84.9 0.3 copy.19
  85.2 0.4 reshape.68
  85.5 8.2 %all_gather.3 = f32[8,1,16,1152]{3,2,1,0:T(8,128)S(1)} all-gather(f32[2,1,16,1152]{3,2,1,0:T(8,128)S(1)} %bitcast.19), channel_id=1, replica_groups=mesh['x'=4,'yh'=2,'z'=8,'yl'=2,'core'=2] {'yl','core'}, dimensions={0}, use_global_device_ids=true | all-gather | bytes 737280 | tf_op jit(solution)/shard_map/all_gather | solution.py:250
  93.9 0.9 broadcast_select_fusion
  (31 shorter events, 0.9 us)
Async XLA Ops:
  2.3 15.0 %all-to-all-start = ((bf16[8,152,128]{2,1,0:T(8,128)(2,1)}), bf16[8,152,128]{2,1,0:T(8,128)(2,1)S(1)}, u32[]{:S(2)}, u32[]{:S(2)}) async-start(bf16[8,152,128]{2,1,0:T(8,128)(2,1)} %split.1), calls=%async_computation | async-start | bytes 622592 | tf_op jit(solution)/shard_map/all_to_all | solution.py:211
  17.3 11.1 %collective-permute-start.1 = (bf16[8,144,128]{2,1,0:T(8,128)(2,1)S(1)}, bf16[8,144,128]{2,1,0:T(8,128)(2,1)S(1)}, u32[]{:S(2)}, u32[]{:S(2)}) collective-permute-start(bf16[8,144,128]{2,1,0:T(8,128)(2,1)S(1)} %slice.33.own_ref), channel_id=1, source_target_pairs={{0,4},{1,29},{4,8},{5,1},{8,12},{9,5},{12,16},{13,9},{16,20},{17,1... | collective-permute-start | bytes 884744 | tf_op jit(solution)/shard_map/ppermute | solution.py:161
  23.0 9.5 %collective-permute-start.5 = (bf16[8,144,128]{2,1,0:T(8,128)(2,1)S(1)}, bf16[8,144,128]{2,1,0:T(8,128)(2,1)S(1)}, u32[]{:S(2)}, u32[]{:S(2)}) collective-permute-start(bf16[8,144,128]{2,1,0:T(8,128)(2,1)S(1)} %slice.33.own_ref), channel_id=1, source_target_pairs={{0,29},{1,4},{4,1},{5,8},{8,5},{9,12},{12,9},{13,16},{16,13},{17,2... | collective-permute-start | bytes 884744 | tf_op jit(solution)/shard_map/ppermute | solution.py:161
  28.4 7.1 %collective-permute-start.2 = (bf16[8,144,128]{2,1,0:T(8,128)(2,1)S(1)}, bf16[8,144,128]{2,1,0:T(8,128)(2,1)S(1)}, u32[]{:S(2)}, u32[]{:S(2)}) collective-permute-start(bf16[8,144,128]{2,1,0:T(8,128)(2,1)S(1)} %collective-permute-done.1.own_ref), channel_id=1, source_target_pairs={{0,4},{1,29},{4,8},{5,1},{8,12},{9,5},{12,16},{13,9},{16,20},{17,1... | collective-permute-start | bytes 884744 | tf_op jit(solution)/shard_map/ppermute | solution.py:161
  31.6 6.8 %collective-permute-start = (bf16[8,152,128]{2,1,0:T(8,128)(2,1)S(1)}, bf16[8,152,128]{2,1,0:T(8,128)(2,1)S(1)}, u32[]{:S(2)}, u32[]{:S(2)}) collective-permute-start(bf16[8,152,128]{2,1,0:T(8,128)(2,1)S(1)} %all-to-all-done), channel_id=1, source_target_pairs={{0,1},{1,0},{2,3},{3,2},{4,5},{5,4},{6,7},{7,6},{8,9},{9,8},{10,11... | collective-permute-start | bytes 933896 | tf_op jit(solution)/shard_map/ppermute | solution.py:149
  32.5 11.0 %collective-permute-start.10 = (bf16[8,144,128]{2,1,0:T(8,128)(2,1)S(1)}, bf16[8,144,128]{2,1,0:T(8,128)(2,1)S(1)}, u32[]{:S(2)}, u32[]{:S(2)}) collective-permute-start(bf16[8,144,128]{2,1,0:T(8,128)(2,1)S(1)} %collective-permute-done.5.sib_ref), channel_id=1, source_target_pairs={{0,1},{1,0},{2,3},{3,2},{4,5},{5,4},{6,7},{7,6},{8,9},{9,8},{10,11... | collective-permute-start | bytes 884744 | tf_op jit(solution)/shard_map/ppermute | solution.py:149
  32.6 6.6 %collective-permute-start.6 = (bf16[8,144,128]{2,1,0:T(8,128)(2,1)S(1)}, bf16[8,144,128]{2,1,0:T(8,128)(2,1)S(1)}, u32[]{:S(2)}, u32[]{:S(2)}) collective-permute-start(bf16[8,144,128]{2,1,0:T(8,128)(2,1)S(1)} %collective-permute-done.5.sib_ref), channel_id=1, source_target_pairs={{0,4},{1,29},{4,8},{5,1},{8,12},{9,5},{12,16},{13,9},{16,20},{17,1... | collective-permute-start | bytes 884744 | tf_op jit(solution)/shard_map/ppermute | solution.py:161
  35.5 11.2 %collective-permute-start.11 = (bf16[8,144,128]{2,1,0:T(8,128)(2,1)S(1)}, bf16[8,144,128]{2,1,0:T(8,128)(2,1)S(1)}, u32[]{:S(2)}, u32[]{:S(2)}) collective-permute-start(bf16[8,144,128]{2,1,0:T(8,128)(2,1)S(1)} %collective-permute-done.1.own_ref), channel_id=1, source_target_pairs={{0,1},{1,0},{2,3},{3,2},{4,5},{5,4},{6,7},{7,6},{8,9},{9,8},{10,11... | collective-permute-start | bytes 884744 | tf_op jit(solution)/shard_map/ppermute | solution.py:149
  35.5 10.3 %collective-permute-start.3 = (bf16[8,144,128]{2,1,0:T(8,128)(2,1)S(1)}, bf16[8,144,128]{2,1,0:T(8,128)(2,1)S(1)}, u32[]{:S(2)}, u32[]{:S(2)}) collective-permute-start(bf16[8,144,128]{2,1,0:T(8,128)(2,1)S(1)} %collective-permute-done.2.own_ref), channel_id=1, source_target_pairs={{0,4},{1,29},{4,8},{5,1},{8,12},{9,5},{12,16},{13,9},{16,20},{17,1... | collective-permute-start | bytes 884744 | tf_op jit(solution)/shard_map/ppermute | solution.py:161
  39.2 12.7 %collective-permute-start.8 = (bf16[8,144,128]{2,1,0:T(8,128)(2,1)S(1)}, bf16[8,144,128]{2,1,0:T(8,128)(2,1)S(1)}, u32[]{:S(2)}, u32[]{:S(2)}) collective-permute-start(bf16[8,144,128]{2,1,0:T(8,128)(2,1)S(1)} %collective-permute-done.6.sib_ref), channel_id=1, source_target_pairs={{0,1},{1,0},{2,3},{3,2},{4,5},{5,4},{6,7},{7,6},{8,9},{9,8},{10,11... | collective-permute-start | bytes 884744 | tf_op jit(solution)/shard_map/ppermute | solution.py:149
  43.4 8.5 %collective-permute-start.9 = (bf16[8,144,128]{2,1,0:T(8,128)(2,1)S(1)}, bf16[8,144,128]{2,1,0:T(8,128)(2,1)S(1)}, u32[]{:S(2)}, u32[]{:S(2)}) collective-permute-start(bf16[8,144,128]{2,1,0:T(8,128)(2,1)S(1)} %collective-permute-done.2.own_ref), channel_id=1, source_target_pairs={{0,1},{1,0},{2,3},{3,2},{4,5},{5,4},{6,7},{7,6},{8,9},{9,8},{10,11... | collective-permute-start | bytes 884744 | tf_op jit(solution)/shard_map/ppermute | solution.py:149
  43.4 5.9 %collective-permute-start.7 = (bf16[8,144,128]{2,1,0:T(8,128)(2,1)S(1)}, bf16[8,144,128]{2,1,0:T(8,128)(2,1)S(1)}, u32[]{:S(2)}, u32[]{:S(2)}) collective-permute-start(bf16[8,144,128]{2,1,0:T(8,128)(2,1)S(1)} %collective-permute-done.6.sib_ref), channel_id=1, source_target_pairs={{0,4},{1,29},{4,8},{5,1},{8,12},{9,5},{12,16},{13,9},{16,20},{17,1... | collective-permute-start | bytes 884744 | tf_op jit(solution)/shard_map/ppermute | solution.py:161
  45.8 7.1 %collective-permute-start.4 = (bf16[8,144,128]{2,1,0:T(8,128)(2,1)S(1)}, bf16[8,144,128]{2,1,0:T(8,128)(2,1)S(1)}, u32[]{:S(2)}, u32[]{:S(2)}) collective-permute-start(bf16[8,144,128]{2,1,0:T(8,128)(2,1)S(1)} %collective-permute-done.3.own_ref), channel_id=1, source_target_pairs={{0,4},{1,29},{4,8},{5,1},{8,12},{9,5},{12,16},{13,9},{16,20},{17,1... | collective-permute-start | bytes 884744 | tf_op jit(solution)/shard_map/ppermute | solution.py:161
  49.3 6.8 %collective-permute-start.13 = (bf16[8,144,128]{2,1,0:T(8,128)(2,1)S(1)}, bf16[8,144,128]{2,1,0:T(8,128)(2,1)S(1)}, u32[]{:S(2)}, u32[]{:S(2)}) collective-permute-start(bf16[8,144,128]{2,1,0:T(8,128)(2,1)S(1)} %collective-permute-done.7.sib_ref), channel_id=1, source_target_pairs={{0,1},{1,0},{2,3},{3,2},{4,5},{5,4},{6,7},{7,6},{8,9},{9,8},{10,11... | collective-permute-start | bytes 884744 | tf_op jit(solution)/shard_map/ppermute | solution.py:149
  51.9 4.3 %collective-permute-start.14 = (bf16[8,144,128]{2,1,0:T(8,128)(2,1)S(1)}, bf16[8,144,128]{2,1,0:T(8,128)(2,1)S(1)}, u32[]{:S(2)}, u32[]{:S(2)}) collective-permute-start(bf16[8,144,128]{2,1,0:T(8,128)(2,1)S(1)} %collective-permute-done.3.own_ref), channel_id=1, source_target_pairs={{0,1},{1,0},{2,3},{3,2},{4,5},{5,4},{6,7},{7,6},{8,9},{9,8},{10,11... | collective-permute-start | bytes 884744 | tf_op jit(solution)/shard_map/ppermute | solution.py:149
  52.9 4.4 %collective-permute-start.12 = (bf16[8,144,128]{2,1,0:T(8,128)(2,1)S(1)}, bf16[8,144,128]{2,1,0:T(8,128)(2,1)S(1)}, u32[]{:S(2)}, u32[]{:S(2)}) collective-permute-start(bf16[8,144,128]{2,1,0:T(8,128)(2,1)S(1)} %collective-permute-done.4.own_ref), channel_id=1, source_target_pairs={{0,1},{1,0},{2,3},{3,2},{4,5},{5,4},{6,7},{7,6},{8,9},{9,8},{10,11... | collective-permute-start | bytes 884744 | tf_op jit(solution)/shard_map/ppermute | solution.py:149
  63.7 30.1 %copy-start = (s32[8,1]{0,1:T(1,128)S(1)}, s32[8,1]{0,1:T(1,128)}, u32[]{:S(2)}) copy-start(s32[8,1]{0,1:T(1,128)} %param.7) | copy-start | bytes 100

commit v14 on v12

--- a/solution.py
+++ b/solution.py
@@ -15,13 +15,17 @@
     block = lax.broadcasted_iota(jnp.int32, (24, LANES), 1) // 16
     for q in range(6):
         sources = [x_ref[8 * q + s].astype(F32) for s in range(8)]
+        for bit in (1, 2, 4):
+            high = (block & bit) > 0
+            for s in range(8):
+                if not s & bit:
+                    low_part, high_part = sources[s], sources[s | bit]
+                    raised = pltpu.roll(high_part, 16 * bit, 1)
+                    lowered = pltpu.roll(low_part, LANES - 16 * bit, 1)
+                    sources[s] = jnp.where(high, raised, low_part)
+                    sources[s | bit] = jnp.where(high, high_part, lowered)
         for piece in range(8):
-            built = None
-            for s in range(8):
-                shift = (s - piece) % 8 * 16
-                moved = pltpu.roll(sources[s], shift, 1) if shift else sources[s]
-                built = moved if built is None else jnp.where(block == s, moved, built)
-            out_ref[piece, 24 * q : 24 * q + 24] = built.astype(BF16)
+            out_ref[piece, 24 * q : 24 * q + 24] = sources[piece].astype(BF16)
     listed = triads_ref[...]
     rest = weights_ref[...]
     parts = []

time: 95 us -> 95.1 us (level)
  no operation moved by 1% of the time
where the time goes in v14:
time: 95.1 us; the launch traced here: 94.9 us
  starting transfers between devices  35.1 us (37%)
  blocking collectives  29.1 us (31%)
  waiting for transfers between devices  15.9 us (17%)
  Pallas kernels  12.2 us (13%)
  other arithmetic  1.5 us (2%)
    all_to_all x1, blocking collectives, body(): parts = lax.all_to_all(partial, ('x', 'yh', 'yl'), 0, 0)  20.9 us
    ppermute x7, starting transfers between devices, ring(): return lax.ppermute(array, ('z', 'core'), pairs)  16.9 us
    ppermute x8, starting transfers between devices, step(): lax.ppermute(array, axes, [(i, (i + by) % size) for i in range(size)])  10.8 us
    all_gather x1, blocking collectives, body(): gathered = lax.all_gather(rows, ('yl', 'core'), tiled=True)  8.24 us
    ppermute x7, waiting for transfers between devices, ring(): return lax.ppermute(array, ('z', 'core'), pairs)  7.81 us
    all_to_all x1, starting transfers between devices, body(): received = lax.all_to_all(pieces, ('x', 'yh'), 0, 0)  7.48 us
    all_to_all x1, waiting for transfers between devices, body(): received = lax.all_to_all(pieces, ('x', 'yh'), 0, 0)  7.4 us
    pallas_call x1, Pallas kernels, grams(): pl.pallas_call(grams_kernel, out_shape=jax.ShapeDtypeStruct((16, 2, 48, 3...  5.79 us
  transfers between devices with their start and end apart: 16, of which 6 were waited for; matrix products, arithmetic and copies ran while one was open for 0% of the time, Pallas kernels for 4%

profile of v14, /device:TPU:1, one launch (start us, length us, event | category | flops | bytes accessed | tf_op | source)
XLA Modules:
  0.0 94.9 jit_solution(2558923546634593623)
XLA Ops:
  0.0 2.4 %split.1 = bf16[8,152,128]{2,1,0:T(8,128)(2,1)} custom-call(bf16[48,24,128]{2,1,0:T(8,128)(2,1)} %bitcast.20, s32[8,16]{1,0:T(8,128)} %bitcast.21, f32[1,128]{1,0:T(1,128)} %bitcast.22), custom_call_target="tpu_custom_call" | custom-call | tf_op jit(solution)/shard_map/split/pallas_call | solution.py:207
  2.4 7.5 %all-to-all-start = ((bf16[8,152,128]{2,1,0:T(8,128)(2,1)}), bf16[8,152,128]{2,1,0:T(8,128)(2,1)S(1)}, u32[]{:S(2)}, u32[]{:S(2)}) async-start(bf16[8,152,128]{2,1,0:T(8,128)(2,1)} %split.1), calls=%async_computation | async-start | bytes 622592 | tf_op jit(solution)/shard_map/all_to_all | solution.py:215
  10.0 7.4 %all-to-all-done = bf16[8,152,128]{2,1,0:T(8,128)(2,1)S(1)} async-done(((bf16[8,152,128]{2,1,0:T(8,128)(2,1)}), bf16[8,152,128]{2,1,0:T(8,128)(2,1)S(1)}, u32[]{:S(2)}, u32[]{:S(2)}) %all-to-all-start) | async-done | bytes 311328 | tf_op jit(solution)/shard_map/all_to_all | solution.py:215
  17.4 5.7 %collective-permute-start.1 = (bf16[8,144,128]{2,1,0:T(8,128)(2,1)S(1)}, bf16[8,144,128]{2,1,0:T(8,128)(2,1)S(1)}, u32[]{:S(2)}, u32[]{:S(2)}) collective-permute-start(bf16[8,144,128]{2,1,0:T(8,128)(2,1)S(1)} %slice.33.own_ref), channel_id=1, source_target_pairs={{0,4},{1,29},{4,8},{5,1},{8,12},{9,5},{12,16},{13,9},{16,20},{17,1... | collective-permute-start | bytes 884744 | tf_op jit(solution)/shard_map/ppermute | solution.py:165
  23.0 0.4 collective-permute-start.5
  23.5 0.8 collective-permute-start
  24.4 4.2 %collective-permute-done.1.own_ref = bf16[8,144,128]{2,1,0:T(8,128)(2,1)S(1)} collective-permute-done((bf16[8,144,128]{2,1,0:T(8,128)(2,1)S(1)}, bf16[8,144,128]{2,1,0:T(8,128)(2,1)S(1)}, u32[]{:S(2)}, u32[]{:S(2)}) %collective-permute-start.1) | collective-permute-done | bytes 294944 | tf_op jit(solution)/shard_map/ppermute | solution.py:165
  28.5 1.0 %collective-permute-done.5.sib_ref = bf16[8,144,128]{2,1,0:T(8,128)(2,1)S(1)} collective-permute-done((bf16[8,144,128]{2,1,0:T(8,128)(2,1)S(1)}, bf16[8,144,128]{2,1,0:T(8,128)(2,1)S(1)}, u32[]{:S(2)}, u32[]{:S(2)}) %collective-permute-start.5) | collective-permute-done | bytes 294944 | tf_op jit(solution)/shard_map/ppermute | solution.py:165
  29.5 2.9 %collective-permute-start.10 = (bf16[8,144,128]{2,1,0:T(8,128)(2,1)S(1)}, bf16[8,144,128]{2,1,0:T(8,128)(2,1)S(1)}, u32[]{:S(2)}, u32[]{:S(2)}) collective-permute-start(bf16[8,144,128]{2,1,0:T(8,128)(2,1)S(1)} %collective-permute-done.5.sib_ref), channel_id=1, source_target_pairs={{0,1},{1,0},{2,3},{3,2},{4,5},{5,4},{6,7},{7,6},{8,9},{9,8},{10,11... | collective-permute-start | bytes 884744 | tf_op jit(solution)/shard_map/ppermute | solution.py:153
  32.4 2.5 %collective-permute-start.2 = (bf16[8,144,128]{2,1,0:T(8,128)(2,1)S(1)}, bf16[8,144,128]{2,1,0:T(8,128)(2,1)S(1)}, u32[]{:S(2)}, u32[]{:S(2)}) collective-permute-start(bf16[8,144,128]{2,1,0:T(8,128)(2,1)S(1)} %collective-permute-done.1.own_ref), channel_id=1, source_target_pairs={{0,4},{1,29},{4,8},{5,1},{8,12},{9,5},{12,16},{13,9},{16,20},{17,1... | collective-permute-start | bytes 884744 | tf_op jit(solution)/shard_map/ppermute | solution.py:165
  35.0 1.2 %collective-permute-start.6 = (bf16[8,144,128]{2,1,0:T(8,128)(2,1)S(1)}, bf16[8,144,128]{2,1,0:T(8,128)(2,1)S(1)}, u32[]{:S(2)}, u32[]{:S(2)}) collective-permute-start(bf16[8,144,128]{2,1,0:T(8,128)(2,1)S(1)} %collective-permute-done.5.sib_ref), channel_id=1, source_target_pairs={{0,4},{1,29},{4,8},{5,1},{8,12},{9,5},{12,16},{13,9},{16,20},{17,1... | collective-permute-start | bytes 884744 | tf_op jit(solution)/shard_map/ppermute | solution.py:165
  36.3 2.3 %collective-permute-done.2.own_ref = bf16[8,144,128]{2,1,0:T(8,128)(2,1)S(1)} collective-permute-done((bf16[8,144,128]{2,1,0:T(8,128)(2,1)S(1)}, bf16[8,144,128]{2,1,0:T(8,128)(2,1)S(1)}, u32[]{:S(2)}, u32[]{:S(2)}) %collective-permute-start.2) | collective-permute-done | bytes 294944 | tf_op jit(solution)/shard_map/ppermute | solution.py:165
  38.6 3.1 %collective-permute-start.3 = (bf16[8,144,128]{2,1,0:T(8,128)(2,1)S(1)}, bf16[8,144,128]{2,1,0:T(8,128)(2,1)S(1)}, u32[]{:S(2)}, u32[]{:S(2)}) collective-permute-start(bf16[8,144,128]{2,1,0:T(8,128)(2,1)S(1)} %collective-permute-done.2.own_ref), channel_id=1, source_target_pairs={{0,4},{1,29},{4,8},{5,1},{8,12},{9,5},{12,16},{13,9},{16,20},{17,1... | collective-permute-start | bytes 884744 | tf_op jit(solution)/shard_map/ppermute | solution.py:165
  41.7 0.5 unpack.8.refs_0_
  42.3 1.2 %collective-permute-start.8 = (bf16[8,144,128]{2,1,0:T(8,128)(2,1)S(1)}, bf16[8,144,128]{2,1,0:T(8,128)(2,1)S(1)}, u32[]{:S(2)}, u32[]{:S(2)}) collective-permute-start(bf16[8,144,128]{2,1,0:T(8,128)(2,1)S(1)} %collective-permute-done.6.sib_ref), channel_id=1, source_target_pairs={{0,1},{1,0},{2,3},{3,2},{4,5},{5,4},{6,7},{7,6},{8,9},{9,8},{10,11... | collective-permute-start | bytes 884744 | tf_op jit(solution)/shard_map/ppermute | solution.py:153
  43.5 1.9 %collective-permute-start.7 = (bf16[8,144,128]{2,1,0:T(8,128)(2,1)S(1)}, bf16[8,144,128]{2,1,0:T(8,128)(2,1)S(1)}, u32[]{:S(2)}, u32[]{:S(2)}) collective-permute-start(bf16[8,144,128]{2,1,0:T(8,128)(2,1)S(1)} %collective-permute-done.6.sib_ref), channel_id=1, source_target_pairs={{0,4},{1,29},{4,8},{5,1},{8,12},{9,5},{12,16},{13,9},{16,20},{17,1... | collective-permute-start | bytes 884744 | tf_op jit(solution)/shard_map/ppermute | solution.py:165
  45.4 0.5 unpack.9.refs_0_
  45.9 0.5 unpack.10.refs_0_
  46.5 2.1 %collective-permute-start.4 = (bf16[8,144,128]{2,1,0:T(8,128)(2,1)S(1)}, bf16[8,144,128]{2,1,0:T(8,128)(2,1)S(1)}, u32[]{:S(2)}, u32[]{:S(2)}) collective-permute-start(bf16[8,144,128]{2,1,0:T(8,128)(2,1)S(1)} %collective-permute-done.3.own_ref), channel_id=1, source_target_pairs={{0,4},{1,29},{4,8},{5,1},{8,12},{9,5},{12,16},{13,9},{16,20},{17,1... | collective-permute-start | bytes 884744 | tf_op jit(solution)/shard_map/ppermute | solution.py:165
  48.5 0.5 unpack.11.refs_0_
  49.4 2.6 %collective-permute-start.13 = (bf16[8,144,128]{2,1,0:T(8,128)(2,1)S(1)}, bf16[8,144,128]{2,1,0:T(8,128)(2,1)S(1)}, u32[]{:S(2)}, u32[]{:S(2)}) collective-permute-start(bf16[8,144,128]{2,1,0:T(8,128)(2,1)S(1)} %collective-permute-done.7.sib_ref), channel_id=1, source_target_pairs={{0,1},{1,0},{2,3},{3,2},{4,5},{5,4},{6,7},{7,6},{8,9},{9,8},{10,11... | collective-permute-start | bytes 884744 | tf_op jit(solution)/shard_map/ppermute | solution.py:153
  52.0 0.5 unpack.12.refs_0_
  52.5 0.5 unpack.13.refs_0_
  53.0 3.2 %collective-permute-start.12 = (bf16[8,144,128]{2,1,0:T(8,128)(2,1)S(1)}, bf16[8,144,128]{2,1,0:T(8,128)(2,1)S(1)}, u32[]{:S(2)}, u32[]{:S(2)}) collective-permute-start(bf16[8,144,128]{2,1,0:T(8,128)(2,1)S(1)} %collective-permute-done.4.own_ref), channel_id=1, source_target_pairs={{0,1},{1,0},{2,3},{3,2},{4,5},{5,4},{6,7},{7,6},{8,9},{9,8},{10,11... | collective-permute-start | bytes 884744 | tf_op jit(solution)/shard_map/ppermute | solution.py:153
  56.2 0.5 unpack.14.refs_0_
  56.7 0.7 collective-permute-done.12.sib_ref
  57.4 0.5 unpack.15.bins_ref
  57.9 5.8 %grams.1 = bf16[16,2,48,384]{3,2,1,0:T(8,128)(2,1)S(1)} custom-call(s32[64,32]{1,0:T(8,128)S(1)} %shift-right-arithmetic_add_fusion.slots_ref, bf16[8,128]{1,0:T(8,128)(2,1)S(1)} %slice_bitcast_fusion.1.own_w_ref, bf16[8,128]{1,0:T(8,128)(2,1)S(1)} %slice_bitcast_fusion.sib_w_ref, bf16[512,24,256]{2,1,0:T(8,128)(2,1)S(1)} %unpack.15.bins_ref), custom_call_target="tpu_custom_call" | custom-call | flops 12000000000 | bytes 8000000 | tf_op jit(solution)/shard_map/grams/pallas_call | solution.py:192
  63.7 20.9 %all_to_all.10 = bf16[16,2,48,384]{3,2,1,0:T(8,128)(2,1)S(1)} all-to-all(bf16[16,2,48,384]{3,2,1,0:T(8,128)(2,1)S(1)} %grams.1), channel_id=1, replica_groups=mesh['x'=4,'yh'=2,'z'=8,'yl'=2,'core'=2] {'x','yh','yl'}, dimensions={0} | all-to-all | bytes 2359296 | tf_op jit(solution)/shard_map/all_to_all | solution.py:250
  85.3 0.4 reshape.68
  85.6 8.2 %all_gather.3 = f32[8,1,16,1152]{3,2,1,0:T(8,128)S(1)} all-gather(f32[2,1,16,1152]{3,2,1,0:T(8,128)S(1)} %bitcast.19), channel_id=1, replica_groups=mesh['x'=4,'yh'=2,'z'=8,'yl'=2,'core'=2] {'yl','core'}, dimensions={0}, use_global_device_ids=true | all-gather | bytes 737280 | tf_op jit(solution)/shard_map/all_gather | solution.py:254
  93.9 0.9 broadcast_select_fusion
  (31 shorter events, 1.5 us)
Async XLA Ops:
  2.4 15.0 %all-to-all-start = ((bf16[8,152,128]{2,1,0:T(8,128)(2,1)}), bf16[8,152,128]{2,1,0:T(8,128)(2,1)S(1)}, u32[]{:S(2)}, u32[]{:S(2)}) async-start(bf16[8,152,128]{2,1,0:T(8,128)(2,1)} %split.1), calls=%async_computation | async-start | bytes 622592 | tf_op jit(solution)/shard_map/all_to_all | solution.py:215
  17.4 11.1 %collective-permute-start.1 = (bf16[8,144,128]{2,1,0:T(8,128)(2,1)S(1)}, bf16[8,144,128]{2,1,0:T(8,128)(2,1)S(1)}, u32[]{:S(2)}, u32[]{:S(2)}) collective-permute-start(bf16[8,144,128]{2,1,0:T(8,128)(2,1)S(1)} %slice.33.own_ref), channel_id=1, source_target_pairs={{0,4},{1,29},{4,8},{5,1},{8,12},{9,5},{12,16},{13,9},{16,20},{17,1... | collective-permute-start | bytes 884744 | tf_op jit(solution)/shard_map/ppermute | solution.py:165
  23.0 6.4 %collective-permute-start.5 = (bf16[8,144,128]{2,1,0:T(8,128)(2,1)S(1)}, bf16[8,144,128]{2,1,0:T(8,128)(2,1)S(1)}, u32[]{:S(2)}, u32[]{:S(2)}) collective-permute-start(bf16[8,144,128]{2,1,0:T(8,128)(2,1)S(1)} %slice.33.own_ref), channel_id=1, source_target_pairs={{0,29},{1,4},{4,1},{5,8},{8,5},{9,12},{12,9},{13,16},{16,13},{17,2... | collective-permute-start | bytes 884744 | tf_op jit(solution)/shard_map/ppermute | solution.py:165
  23.5 12.8 %collective-permute-start = (bf16[8,152,128]{2,1,0:T(8,128)(2,1)S(1)}, bf16[8,152,128]{2,1,0:T(8,128)(2,1)S(1)}, u32[]{:S(2)}, u32[]{:S(2)}) collective-permute-start(bf16[8,152,128]{2,1,0:T(8,128)(2,1)S(1)} %all-to-all-done), channel_id=1, source_target_pairs={{0,1},{1,0},{2,3},{3,2},{4,5},{5,4},{6,7},{7,6},{8,9},{9,8},{10,11... | collective-permute-start | bytes 933896 | tf_op jit(solution)/shard_map/ppermute | solution.py:153
  29.5 14.0 %collective-permute-start.10 = (bf16[8,144,128]{2,1,0:T(8,128)(2,1)S(1)}, bf16[8,144,128]{2,1,0:T(8,128)(2,1)S(1)}, u32[]{:S(2)}, u32[]{:S(2)}) collective-permute-start(bf16[8,144,128]{2,1,0:T(8,128)(2,1)S(1)} %collective-permute-done.5.sib_ref), channel_id=1, source_target_pairs={{0,1},{1,0},{2,3},{3,2},{4,5},{5,4},{6,7},{7,6},{8,9},{9,8},{10,11... | collective-permute-start | bytes 884744 | tf_op jit(solution)/shard_map/ppermute | solution.py:153
  32.4 6.2 %collective-permute-start.2 = (bf16[8,144,128]{2,1,0:T(8,128)(2,1)S(1)}, bf16[8,144,128]{2,1,0:T(8,128)(2,1)S(1)}, u32[]{:S(2)}, u32[]{:S(2)}) collective-permute-start(bf16[8,144,128]{2,1,0:T(8,128)(2,1)S(1)} %collective-permute-done.1.own_ref), channel_id=1, source_target_pairs={{0,4},{1,29},{4,8},{5,1},{8,12},{9,5},{12,16},{13,9},{16,20},{17,1... | collective-permute-start | bytes 884744 | tf_op jit(solution)/shard_map/ppermute | solution.py:165
  35.0 7.3 %collective-permute-start.6 = (bf16[8,144,128]{2,1,0:T(8,128)(2,1)S(1)}, bf16[8,144,128]{2,1,0:T(8,128)(2,1)S(1)}, u32[]{:S(2)}, u32[]{:S(2)}) collective-permute-start(bf16[8,144,128]{2,1,0:T(8,128)(2,1)S(1)} %collective-permute-done.5.sib_ref), channel_id=1, source_target_pairs={{0,4},{1,29},{4,8},{5,1},{8,12},{9,5},{12,16},{13,9},{16,20},{17,1... | collective-permute-start | bytes 884744 | tf_op jit(solution)/shard_map/ppermute | solution.py:165
  36.2 9.8 %collective-permute-start.11 = (bf16[8,144,128]{2,1,0:T(8,128)(2,1)S(1)}, bf16[8,144,128]{2,1,0:T(8,128)(2,1)S(1)}, u32[]{:S(2)}, u32[]{:S(2)}) collective-permute-start(bf16[8,144,128]{2,1,0:T(8,128)(2,1)S(1)} %collective-permute-done.1.own_ref), channel_id=1, source_target_pairs={{0,1},{1,0},{2,3},{3,2},{4,5},{5,4},{6,7},{7,6},{8,9},{9,8},{10,11... | collective-permute-start | bytes 884744 | tf_op jit(solution)/shard_map/ppermute | solution.py:153
  38.6 7.8 %collective-permute-start.3 = (bf16[8,144,128]{2,1,0:T(8,128)(2,1)S(1)}, bf16[8,144,128]{2,1,0:T(8,128)(2,1)S(1)}, u32[]{:S(2)}, u32[]{:S(2)}) collective-permute-start(bf16[8,144,128]{2,1,0:T(8,128)(2,1)S(1)} %collective-permute-done.2.own_ref), channel_id=1, source_target_pairs={{0,4},{1,29},{4,8},{5,1},{8,12},{9,5},{12,16},{13,9},{16,20},{17,1... | collective-permute-start | bytes 884744 | tf_op jit(solution)/shard_map/ppermute | solution.py:165
  42.3 9.7 %collective-permute-start.8 = (bf16[8,144,128]{2,1,0:T(8,128)(2,1)S(1)}, bf16[8,144,128]{2,1,0:T(8,128)(2,1)S(1)}, u32[]{:S(2)}, u32[]{:S(2)}) collective-permute-start(bf16[8,144,128]{2,1,0:T(8,128)(2,1)S(1)} %collective-permute-done.6.sib_ref), channel_id=1, source_target_pairs={{0,1},{1,0},{2,3},{3,2},{4,5},{5,4},{6,7},{7,6},{8,9},{9,8},{10,11... | collective-permute-start | bytes 884744 | tf_op jit(solution)/shard_map/ppermute | solution.py:153
  43.5 8.5 %collective-permute-start.9 = (bf16[8,144,128]{2,1,0:T(8,128)(2,1)S(1)}, bf16[8,144,128]{2,1,0:T(8,128)(2,1)S(1)}, u32[]{:S(2)}, u32[]{:S(2)}) collective-permute-start(bf16[8,144,128]{2,1,0:T(8,128)(2,1)S(1)} %collective-permute-done.2.own_ref), channel_id=1, source_target_pairs={{0,1},{1,0},{2,3},{3,2},{4,5},{5,4},{6,7},{7,6},{8,9},{9,8},{10,11... | collective-permute-start | bytes 884744 | tf_op jit(solution)/shard_map/ppermute | solution.py:153
  43.5 5.9 %collective-permute-start.7 = (bf16[8,144,128]{2,1,0:T(8,128)(2,1)S(1)}, bf16[8,144,128]{2,1,0:T(8,128)(2,1)S(1)}, u32[]{:S(2)}, u32[]{:S(2)}) collective-permute-start(bf16[8,144,128]{2,1,0:T(8,128)(2,1)S(1)} %collective-permute-done.6.sib_ref), channel_id=1, source_target_pairs={{0,4},{1,29},{4,8},{5,1},{8,12},{9,5},{12,16},{13,9},{16,20},{17,1... | collective-permute-start | bytes 884744 | tf_op jit(solution)/shard_map/ppermute | solution.py:165
  46.5 6.5 %collective-permute-start.4 = (bf16[8,144,128]{2,1,0:T(8,128)(2,1)S(1)}, bf16[8,144,128]{2,1,0:T(8,128)(2,1)S(1)}, u32[]{:S(2)}, u32[]{:S(2)}) collective-permute-start(bf16[8,144,128]{2,1,0:T(8,128)(2,1)S(1)} %collective-permute-done.3.own_ref), channel_id=1, source_target_pairs={{0,4},{1,29},{4,8},{5,1},{8,12},{9,5},{12,16},{13,9},{16,20},{17,1... | collective-permute-start | bytes 884744 | tf_op jit(solution)/shard_map/ppermute | solution.py:165
  49.4 6.8 %collective-permute-start.13 = (bf16[8,144,128]{2,1,0:T(8,128)(2,1)S(1)}, bf16[8,144,128]{2,1,0:T(8,128)(2,1)S(1)}, u32[]{:S(2)}, u32[]{:S(2)}) collective-permute-start(bf16[8,144,128]{2,1,0:T(8,128)(2,1)S(1)} %collective-permute-done.7.sib_ref), channel_id=1, source_target_pairs={{0,1},{1,0},{2,3},{3,2},{4,5},{5,4},{6,7},{7,6},{8,9},{9,8},{10,11... | collective-permute-start | bytes 884744 | tf_op jit(solution)/shard_map/ppermute | solution.py:153
  52.0 4.3 %collective-permute-start.14 = (bf16[8,144,128]{2,1,0:T(8,128)(2,1)S(1)}, bf16[8,144,128]{2,1,0:T(8,128)(2,1)S(1)}, u32[]{:S(2)}, u32[]{:S(2)}) collective-permute-start(bf16[8,144,128]{2,1,0:T(8,128)(2,1)S(1)} %collective-permute-done.3.own_ref), channel_id=1, source_target_pairs={{0,1},{1,0},{2,3},{3,2},{4,5},{5,4},{6,7},{7,6},{8,9},{9,8},{10,11... | collective-permute-start | bytes 884744 | tf_op jit(solution)/shard_map/ppermute | solution.py:153
  53.0 4.4 %collective-permute-start.12 = (bf16[8,144,128]{2,1,0:T(8,128)(2,1)S(1)}, bf16[8,144,128]{2,1,0:T(8,128)(2,1)S(1)}, u32[]{:S(2)}, u32[]{:S(2)}) collective-permute-start(bf16[8,144,128]{2,1,0:T(8,128)(2,1)S(1)} %collective-permute-done.4.own_ref), channel_id=1, source_target_pairs={{0,1},{1,0},{2,3},{3,2},{4,5},{5,4},{6,7},{7,6},{8,9},{9,8},{10,11... | collective-permute-start | bytes 884744 | tf_op jit(solution)/shard_map/ppermute | solution.py:153
  63.7 30.1 %copy-start = (s32[8,1]{0,1:T(1,128)S(1)}, s32[8,1]{0,1:T(1,128)}, u32[]{:S(2)}) copy-start(s32[8,1]{0,1:T(1,128)} %param.7) | copy-start | bytes 100

commit v15 on v14

--- a/solution.py
+++ b/solution.py
@@ -209,7 +209,7 @@
         out_shape=jax.ShapeDtypeStruct((8, 152, LANES), BF16),
         in_specs=[vmem()] * 3,
         out_specs=vmem(),
-        compiler_params=params(56),
+        compiler_params=params(8),
         name="split",
     )(modes.reshape(48, 24, LANES), triads[:, 0], point_weights[None])
     received = lax.all_to_all(pieces, ("x", "yh"), 0, 0)

time: 95.1 us -> 96.5 us (1.015)
  local copies, waits for them, and re-layouts: 0.88 us -> 3.18 us
  Pallas kernels: 12.2 us -> 11.2 us
    unnamed x2 -> x8, local copies, waits for them, and re-layouts: 0.01 us -> 2.31 us
    pallas_call x1, Pallas kernels: 2.38 us -> 1.41 us  [body(): pl.pallas_call(split_kernel, out_shape=jax.ShapeDtypeStruct((8, 152, LANE...]
where the time goes in v15:
time: 96.5 us; the launch traced here: 96.2 us
  starting transfers between devices  35.1 us (36%)
  blocking collectives  29.1 us (30%)
  waiting for transfers between devices  15.9 us (16%)
  Pallas kernels  11.2 us (12%)
  local copies, waits for them, and re-layouts  3.18 us (3%)
  other arithmetic  1.5 us (2%)
    all_to_all x1, blocking collectives, body(): parts = lax.all_to_all(partial, ('x', 'yh', 'yl'), 0, 0)  20.9 us
    ppermute x7, starting transfers between devices, ring(): return lax.ppermute(array, ('z', 'core'), pairs)  16.9 us
    ppermute x8, starting transfers between devices, step(): lax.ppermute(array, axes, [(i, (i + by) % size) for i in range(size)])  10.8 us
    all_gather x1, blocking collectives, body(): gathered = lax.all_gather(rows, ('yl', 'core'), tiled=True)  8.25 us
    ppermute x7, waiting for transfers between devices, ring(): return lax.ppermute(array, ('z', 'core'), pairs)  7.81 us
    all_to_all x1, starting transfers between devices, body(): received = lax.all_to_all(pieces, ('x', 'yh'), 0, 0)  7.48 us
    all_to_all x1, waiting for transfers between devices, body(): received = lax.all_to_all(pieces, ('x', 'yh'), 0, 0)  7.4 us
    pallas_call x1, Pallas kernels, grams(): pl.pallas_call(grams_kernel, out_shape=jax.ShapeDtypeStruct((16, 2, 48, 3...  5.79 us
  transfers between devices with their start and end apart: 16, of which 6 were waited for; matrix products, arithmetic and copies ran while one was open for 0% of the time, Pallas kernels for 4%

profile of v15, /device:TPU:1, one launch (start us, length us, event | category | flops | bytes accessed | tf_op | source)
XLA Modules:
  0.0 96.2 jit_solution(7298707207109217295)
XLA Ops:
  0.0 1.0 copy-done
  1.0 0.7 copy-done.1
  1.7 0.7 copy-done.2
  2.3 1.4 %split.1 = bf16[8,152,128]{2,1,0:T(8,128)(2,1)} custom-call(bf16[48,24,128]{2,1,0:T(8,128)(2,1)S(1)} %bitcast.18, s32[8,16]{1,0:T(8,128)S(1)} %bitcast.19, f32[1,128]{1,0:T(1,128)S(1)} %bitcast.20), custom_call_target="tpu_custom_call" | custom-call | tf_op jit(solution)/shard_map/split/pallas_call | solution.py:207
  3.7 7.5 %all-to-all-start = ((bf16[8,152,128]{2,1,0:T(8,128)(2,1)}), bf16[8,152,128]{2,1,0:T(8,128)(2,1)S(1)}, u32[]{:S(2)}, u32[]{:S(2)}) async-start(bf16[8,152,128]{2,1,0:T(8,128)(2,1)} %split.1), calls=%async_computation | async-start | bytes 622592 | tf_op jit(solution)/shard_map/all_to_all | solution.py:215
  11.3 7.4 %all-to-all-done = bf16[8,152,128]{2,1,0:T(8,128)(2,1)S(1)} async-done(((bf16[8,152,128]{2,1,0:T(8,128)(2,1)}), bf16[8,152,128]{2,1,0:T(8,128)(2,1)S(1)}, u32[]{:S(2)}, u32[]{:S(2)}) %all-to-all-start) | async-done | bytes 311328 | tf_op jit(solution)/shard_map/all_to_all | solution.py:215
  18.7 5.7 %collective-permute-start.1 = (bf16[8,144,128]{2,1,0:T(8,128)(2,1)S(1)}, bf16[8,144,128]{2,1,0:T(8,128)(2,1)S(1)}, u32[]{:S(2)}, u32[]{:S(2)}) collective-permute-start(bf16[8,144,128]{2,1,0:T(8,128)(2,1)S(1)} %slice.33.own_ref), channel_id=1, source_target_pairs={{0,4},{1,29},{4,8},{5,1},{8,12},{9,5},{12,16},{13,9},{16,20},{17,1... | collective-permute-start | bytes 884744 | tf_op jit(solution)/shard_map/ppermute | solution.py:165
  24.8 0.8 collective-permute-start
  25.7 4.2 %collective-permute-done.1.own_ref = bf16[8,144,128]{2,1,0:T(8,128)(2,1)S(1)} collective-permute-done((bf16[8,144,128]{2,1,0:T(8,128)(2,1)S(1)}, bf16[8,144,128]{2,1,0:T(8,128)(2,1)S(1)}, u32[]{:S(2)}, u32[]{:S(2)}) %collective-permute-start.1) | collective-permute-done | bytes 294944 | tf_op jit(solution)/shard_map/ppermute | solution.py:165
  29.8 1.0 collective-permute-done.5.sib_ref
  30.8 2.9 %collective-permute-start.10 = (bf16[8,144,128]{2,1,0:T(8,128)(2,1)S(1)}, bf16[8,144,128]{2,1,0:T(8,128)(2,1)S(1)}, u32[]{:S(2)}, u32[]{:S(2)}) collective-permute-start(bf16[8,144,128]{2,1,0:T(8,128)(2,1)S(1)} %collective-permute-done.5.sib_ref), channel_id=1, source_target_pairs={{0,1},{1,0},{2,3},{3,2},{4,5},{5,4},{6,7},{7,6},{8,9},{9,8},{10,11... | collective-permute-start | bytes 884744 | tf_op jit(solution)/shard_map/ppermute | solution.py:153
  33.7 2.5 %collective-permute-start.2 = (bf16[8,144,128]{2,1,0:T(8,128)(2,1)S(1)}, bf16[8,144,128]{2,1,0:T(8,128)(2,1)S(1)}, u32[]{:S(2)}, u32[]{:S(2)}) collective-permute-start(bf16[8,144,128]{2,1,0:T(8,128)(2,1)S(1)} %collective-permute-done.1.own_ref), channel_id=1, source_target_pairs={{0,4},{1,29},{4,8},{5,1},{8,12},{9,5},{12,16},{13,9},{16,20},{17,1... | collective-permute-start | bytes 884744 | tf_op jit(solution)/shard_map/ppermute | solution.py:165
  36.3 1.2 %collective-permute-start.6 = (bf16[8,144,128]{2,1,0:T(8,128)(2,1)S(1)}, bf16[8,144,128]{2,1,0:T(8,128)(2,1)S(1)}, u32[]{:S(2)}, u32[]{:S(2)}) collective-permute-start(bf16[8,144,128]{2,1,0:T(8,128)(2,1)S(1)} %collective-permute-done.5.sib_ref), channel_id=1, source_target_pairs={{0,4},{1,29},{4,8},{5,1},{8,12},{9,5},{12,16},{13,9},{16,20},{17,1... | collective-permute-start | bytes 884744 | tf_op jit(solution)/shard_map/ppermute | solution.py:165
  37.6 2.3 %collective-permute-done.2.own_ref = bf16[8,144,128]{2,1,0:T(8,128)(2,1)S(1)} collective-permute-done((bf16[8,144,128]{2,1,0:T(8,128)(2,1)S(1)}, bf16[8,144,128]{2,1,0:T(8,128)(2,1)S(1)}, u32[]{:S(2)}, u32[]{:S(2)}) %collective-permute-start.2) | collective-permute-done | bytes 294944 | tf_op jit(solution)/shard_map/ppermute | solution.py:165
  40.0 3.1 %collective-permute-start.3 = (bf16[8,144,128]{2,1,0:T(8,128)(2,1)S(1)}, bf16[8,144,128]{2,1,0:T(8,128)(2,1)S(1)}, u32[]{:S(2)}, u32[]{:S(2)}) collective-permute-start(bf16[8,144,128]{2,1,0:T(8,128)(2,1)S(1)} %collective-permute-done.2.own_ref), channel_id=1, source_target_pairs={{0,4},{1,29},{4,8},{5,1},{8,12},{9,5},{12,16},{13,9},{16,20},{17,1... | collective-permute-start | bytes 884744 | tf_op jit(solution)/shard_map/ppermute | solution.py:165
  43.6 1.2 %collective-permute-start.8 = (bf16[8,144,128]{2,1,0:T(8,128)(2,1)S(1)}, bf16[8,144,128]{2,1,0:T(8,128)(2,1)S(1)}, u32[]{:S(2)}, u32[]{:S(2)}) collective-permute-start(bf16[8,144,128]{2,1,0:T(8,128)(2,1)S(1)} %collective-permute-done.6.sib_ref), channel_id=1, source_target_pairs={{0,1},{1,0},{2,3},{3,2},{4,5},{5,4},{6,7},{7,6},{8,9},{9,8},{10,11... | collective-permute-start | bytes 884744 | tf_op jit(solution)/shard_map/ppermute | solution.py:153
  44.8 1.9 %collective-permute-start.7 = (bf16[8,144,128]{2,1,0:T(8,128)(2,1)S(1)}, bf16[8,144,128]{2,1,0:T(8,128)(2,1)S(1)}, u32[]{:S(2)}, u32[]{:S(2)}) collective-permute-start(bf16[8,144,128]{2,1,0:T(8,128)(2,1)S(1)} %collective-permute-done.6.sib_ref), channel_id=1, source_target_pairs={{0,4},{1,29},{4,8},{5,1},{8,12},{9,5},{12,16},{13,9},{16,20},{17,1... | collective-permute-start | bytes 884744 | tf_op jit(solution)/shard_map/ppermute | solution.py:165
  46.8 0.5 unpack.9.refs_0_
  47.3 0.5 unpack.10.refs_0_
  47.8 2.1 %collective-permute-start.4 = (bf16[8,144,128]{2,1,0:T(8,128)(2,1)S(1)}, bf16[8,144,128]{2,1,0:T(8,128)(2,1)S(1)}, u32[]{:S(2)}, u32[]{:S(2)}) collective-permute-start(bf16[8,144,128]{2,1,0:T(8,128)(2,1)S(1)} %collective-permute-done.3.own_ref), channel_id=1, source_target_pairs={{0,4},{1,29},{4,8},{5,1},{8,12},{9,5},{12,16},{13,9},{16,20},{17,1... | collective-permute-start | bytes 884744 | tf_op jit(solution)/shard_map/ppermute | solution.py:165
  49.9 0.5 unpack.11.refs_0_
  50.7 2.6 %collective-permute-start.13 = (bf16[8,144,128]{2,1,0:T(8,128)(2,1)S(1)}, bf16[8,144,128]{2,1,0:T(8,128)(2,1)S(1)}, u32[]{:S(2)}, u32[]{:S(2)}) collective-permute-start(bf16[8,144,128]{2,1,0:T(8,128)(2,1)S(1)} %collective-permute-done.7.sib_ref), channel_id=1, source_target_pairs={{0,1},{1,0},{2,3},{3,2},{4,5},{5,4},{6,7},{7,6},{8,9},{9,8},{10,11... | collective-permute-start | bytes 884744 | tf_op jit(solution)/shard_map/ppermute | solution.py:153
  53.3 0.5 unpack.12.refs_0_
  53.8 0.5 unpack.13.refs_0_
  54.3 3.2 %collective-permute-start.12 = (bf16[8,144,128]{2,1,0:T(8,128)(2,1)S(1)}, bf16[8,144,128]{2,1,0:T(8,128)(2,1)S(1)}, u32[]{:S(2)}, u32[]{:S(2)}) collective-permute-start(bf16[8,144,128]{2,1,0:T(8,128)(2,1)S(1)} %collective-permute-done.4.own_ref), channel_id=1, source_target_pairs={{0,1},{1,0},{2,3},{3,2},{4,5},{5,4},{6,7},{7,6},{8,9},{9,8},{10,11... | collective-permute-start | bytes 884744 | tf_op jit(solution)/shard_map/ppermute | solution.py:153
  57.6 0.5 unpack.14.refs_0_
  58.1 0.7 collective-permute-done.12.sib_ref
  58.8 0.5 unpack.15.bins_ref
  59.3 5.8 %grams.1 = bf16[16,2,48,384]{3,2,1,0:T(8,128)(2,1)S(1)} custom-call(s32[64,32]{1,0:T(8,128)S(1)} %shift-right-arithmetic_add_fusion.slots_ref, bf16[8,128]{1,0:T(8,128)(2,1)S(1)} %slice_bitcast_fusion.1.own_w_ref, bf16[8,128]{1,0:T(8,128)(2,1)S(1)} %slice_bitcast_fusion.sib_w_ref, bf16[512,24,256]{2,1,0:T(8,128)(2,1)S(1)} %unpack.15.bins_ref), custom_call_target="tpu_custom_call" | custom-call | flops 12000000000 | bytes 8000000 | tf_op jit(solution)/shard_map/grams/pallas_call | solution.py:192
  65.1 20.9 %all_to_all.10 = bf16[16,2,48,384]{3,2,1,0:T(8,128)(2,1)S(1)} all-to-all(bf16[16,2,48,384]{3,2,1,0:T(8,128)(2,1)S(1)} %grams.1), channel_id=1, replica_groups=mesh['x'=4,'yh'=2,'z'=8,'yl'=2,'core'=2] {'x','yh','yl'}, dimensions={0} | all-to-all | bytes 2359296 | tf_op jit(solution)/shard_map/all_to_all | solution.py:250
  87.0 8.2 %all_gather.3 = f32[8,1,16,1152]{3,2,1,0:T(8,128)S(1)} all-gather(f32[2,1,16,1152]{3,2,1,0:T(8,128)S(1)} %bitcast.22), channel_id=1, replica_groups=mesh['x'=4,'yh'=2,'z'=8,'yl'=2,'core'=2] {'yl','core'}, dimensions={0}, use_global_device_ids=true | all-gather | bytes 737280 | tf_op jit(solution)/shard_map/all_gather | solution.py:254
  95.3 0.9 broadcast_select_fusion
  (37 shorter events, 2.7 us)
Async XLA Ops:
  0.0 1.0 copy-start
  1.0 0.7 copy-start.1
  1.6 0.7 copy-start.2
  3.7 15.0 %all-to-all-start = ((bf16[8,152,128]{2,1,0:T(8,128)(2,1)}), bf16[8,152,128]{2,1,0:T(8,128)(2,1)S(1)}, u32[]{:S(2)}, u32[]{:S(2)}) async-start(bf16[8,152,128]{2,1,0:T(8,128)(2,1)} %split.1), calls=%async_computation | async-start | bytes 622592 | tf_op jit(solution)/shard_map/all_to_all | solution.py:215
  18.7 11.1 %collective-permute-start.1 = (bf16[8,144,128]{2,1,0:T(8,128)(2,1)S(1)}, bf16[8,144,128]{2,1,0:T(8,128)(2,1)S(1)}, u32[]{:S(2)}, u32[]{:S(2)}) collective-permute-start(bf16[8,144,128]{2,1,0:T(8,128)(2,1)S(1)} %slice.33.own_ref), channel_id=1, source_target_pairs={{0,4},{1,29},{4,8},{5,1},{8,12},{9,5},{12,16},{13,9},{16,20},{17,1... | collective-permute-start | bytes 884744 | tf_op jit(solution)/shard_map/ppermute | solution.py:165
  24.4 6.4 %collective-permute-start.5 = (bf16[8,144,128]{2,1,0:T(8,128)(2,1)S(1)}, bf16[8,144,128]{2,1,0:T(8,128)(2,1)S(1)}, u32[]{:S(2)}, u32[]{:S(2)}) collective-permute-start(bf16[8,144,128]{2,1,0:T(8,128)(2,1)S(1)} %slice.33.own_ref), channel_id=1, source_target_pairs={{0,29},{1,4},{4,1},{5,8},{8,5},{9,12},{12,9},{13,16},{16,13},{17,2... | collective-permute-start | bytes 884744 | tf_op jit(solution)/shard_map/ppermute | solution.py:165
  24.8 12.8 %collective-permute-start = (bf16[8,152,128]{2,1,0:T(8,128)(2,1)S(1)}, bf16[8,152,128]{2,1,0:T(8,128)(2,1)S(1)}, u32[]{:S(2)}, u32[]{:S(2)}) collective-permute-start(bf16[8,152,128]{2,1,0:T(8,128)(2,1)S(1)} %all-to-all-done), channel_id=1, source_target_pairs={{0,1},{1,0},{2,3},{3,2},{4,5},{5,4},{6,7},{7,6},{8,9},{9,8},{10,11... | collective-permute-start | bytes 933896 | tf_op jit(solution)/shard_map/ppermute | solution.py:153
  30.8 14.0 %collective-permute-start.10 = (bf16[8,144,128]{2,1,0:T(8,128)(2,1)S(1)}, bf16[8,144,128]{2,1,0:T(8,128)(2,1)S(1)}, u32[]{:S(2)}, u32[]{:S(2)}) collective-permute-start(bf16[8,144,128]{2,1,0:T(8,128)(2,1)S(1)} %collective-permute-done.5.sib_ref), channel_id=1, source_target_pairs={{0,1},{1,0},{2,3},{3,2},{4,5},{5,4},{6,7},{7,6},{8,9},{9,8},{10,11... | collective-permute-start | bytes 884744 | tf_op jit(solution)/shard_map/ppermute | solution.py:153
  33.7 6.2 %collective-permute-start.2 = (bf16[8,144,128]{2,1,0:T(8,128)(2,1)S(1)}, bf16[8,144,128]{2,1,0:T(8,128)(2,1)S(1)}, u32[]{:S(2)}, u32[]{:S(2)}) collective-permute-start(bf16[8,144,128]{2,1,0:T(8,128)(2,1)S(1)} %collective-permute-done.1.own_ref), channel_id=1, source_target_pairs={{0,4},{1,29},{4,8},{5,1},{8,12},{9,5},{12,16},{13,9},{16,20},{17,1... | collective-permute-start | bytes 884744 | tf_op jit(solution)/shard_map/ppermute | solution.py:165
  36.3 7.3 %collective-permute-start.6 = (bf16[8,144,128]{2,1,0:T(8,128)(2,1)S(1)}, bf16[8,144,128]{2,1,0:T(8,128)(2,1)S(1)}, u32[]{:S(2)}, u32[]{:S(2)}) collective-permute-start(bf16[8,144,128]{2,1,0:T(8,128)(2,1)S(1)} %collective-permute-done.5.sib_ref), channel_id=1, source_target_pairs={{0,4},{1,29},{4,8},{5,1},{8,12},{9,5},{12,16},{13,9},{16,20},{17,1... | collective-permute-start | bytes 884744 | tf_op jit(solution)/shard_map/ppermute | solution.py:165
  37.5 9.8 %collective-permute-start.11 = (bf16[8,144,128]{2,1,0:T(8,128)(2,1)S(1)}, bf16[8,144,128]{2,1,0:T(8,128)(2,1)S(1)}, u32[]{:S(2)}, u32[]{:S(2)}) collective-permute-start(bf16[8,144,128]{2,1,0:T(8,128)(2,1)S(1)} %collective-permute-done.1.own_ref), channel_id=1, source_target_pairs={{0,1},{1,0},{2,3},{3,2},{4,5},{5,4},{6,7},{7,6},{8,9},{9,8},{10,11... | collective-permute-start | bytes 884744 | tf_op jit(solution)/shard_map/ppermute | solution.py:153
  40.0 7.8 %collective-permute-start.3 = (bf16[8,144,128]{2,1,0:T(8,128)(2,1)S(1)}, bf16[8,144,128]{2,1,0:T(8,128)(2,1)S(1)}, u32[]{:S(2)}, u32[]{:S(2)}) collective-permute-start(bf16[8,144,128]{2,1,0:T(8,128)(2,1)S(1)} %collective-permute-done.2.own_ref), channel_id=1, source_target_pairs={{0,4},{1,29},{4,8},{5,1},{8,12},{9,5},{12,16},{13,9},{16,20},{17,1... | collective-permute-start | bytes 884744 | tf_op jit(solution)/shard_map/ppermute | solution.py:165
  43.6 9.7 %collective-permute-start.8 = (bf16[8,144,128]{2,1,0:T(8,128)(2,1)S(1)}, bf16[8,144,128]{2,1,0:T(8,128)(2,1)S(1)}, u32[]{:S(2)}, u32[]{:S(2)}) collective-permute-start(bf16[8,144,128]{2,1,0:T(8,128)(2,1)S(1)} %collective-permute-done.6.sib_ref), channel_id=1, source_target_pairs={{0,1},{1,0},{2,3},{3,2},{4,5},{5,4},{6,7},{7,6},{8,9},{9,8},{10,11... | collective-permute-start | bytes 884744 | tf_op jit(solution)/shard_map/ppermute | solution.py:153
  44.8 8.5 %collective-permute-start.9 = (bf16[8,144,128]{2,1,0:T(8,128)(2,1)S(1)}, bf16[8,144,128]{2,1,0:T(8,128)(2,1)S(1)}, u32[]{:S(2)}, u32[]{:S(2)}) collective-permute-start(bf16[8,144,128]{2,1,0:T(8,128)(2,1)S(1)} %collective-permute-done.2.own_ref), channel_id=1, source_target_pairs={{0,1},{1,0},{2,3},{3,2},{4,5},{5,4},{6,7},{7,6},{8,9},{9,8},{10,11... | collective-permute-start | bytes 884744 | tf_op jit(solution)/shard_map/ppermute | solution.py:153
  44.8 5.9 %collective-permute-start.7 = (bf16[8,144,128]{2,1,0:T(8,128)(2,1)S(1)}, bf16[8,144,128]{2,1,0:T(8,128)(2,1)S(1)}, u32[]{:S(2)}, u32[]{:S(2)}) collective-permute-start(bf16[8,144,128]{2,1,0:T(8,128)(2,1)S(1)} %collective-permute-done.6.sib_ref), channel_id=1, source_target_pairs={{0,4},{1,29},{4,8},{5,1},{8,12},{9,5},{12,16},{13,9},{16,20},{17,1... | collective-permute-start | bytes 884744 | tf_op jit(solution)/shard_map/ppermute | solution.py:165
  47.8 6.5 %collective-permute-start.4 = (bf16[8,144,128]{2,1,0:T(8,128)(2,1)S(1)}, bf16[8,144,128]{2,1,0:T(8,128)(2,1)S(1)}, u32[]{:S(2)}, u32[]{:S(2)}) collective-permute-start(bf16[8,144,128]{2,1,0:T(8,128)(2,1)S(1)} %collective-permute-done.3.own_ref), channel_id=1, source_target_pairs={{0,4},{1,29},{4,8},{5,1},{8,12},{9,5},{12,16},{13,9},{16,20},{17,1... | collective-permute-start | bytes 884744 | tf_op jit(solution)/shard_map/ppermute | solution.py:165
  50.7 6.8 %collective-permute-start.13 = (bf16[8,144,128]{2,1,0:T(8,128)(2,1)S(1)}, bf16[8,144,128]{2,1,0:T(8,128)(2,1)S(1)}, u32[]{:S(2)}, u32[]{:S(2)}) collective-permute-start(bf16[8,144,128]{2,1,0:T(8,128)(2,1)S(1)} %collective-permute-done.7.sib_ref), channel_id=1, source_target_pairs={{0,1},{1,0},{2,3},{3,2},{4,5},{5,4},{6,7},{7,6},{8,9},{9,8},{10,11... | collective-permute-start | bytes 884744 | tf_op jit(solution)/shard_map/ppermute | solution.py:153
  53.3 4.3 %collective-permute-start.14 = (bf16[8,144,128]{2,1,0:T(8,128)(2,1)S(1)}, bf16[8,144,128]{2,1,0:T(8,128)(2,1)S(1)}, u32[]{:S(2)}, u32[]{:S(2)}) collective-permute-start(bf16[8,144,128]{2,1,0:T(8,128)(2,1)S(1)} %collective-permute-done.3.own_ref), channel_id=1, source_target_pairs={{0,1},{1,0},{2,3},{3,2},{4,5},{5,4},{6,7},{7,6},{8,9},{9,8},{10,11... | collective-permute-start | bytes 884744 | tf_op jit(solution)/shard_map/ppermute | solution.py:153
  54.3 4.4 %collective-permute-start.12 = (bf16[8,144,128]{2,1,0:T(8,128)(2,1)S(1)}, bf16[8,144,128]{2,1,0:T(8,128)(2,1)S(1)}, u32[]{:S(2)}, u32[]{:S(2)}) collective-permute-start(bf16[8,144,128]{2,1,0:T(8,128)(2,1)S(1)} %collective-permute-done.4.own_ref), channel_id=1, source_target_pairs={{0,1},{1,0},{2,3},{3,2},{4,5},{5,4},{6,7},{7,6},{8,9},{9,8},{10,11... | collective-permute-start | bytes 884744 | tf_op jit(solution)/shard_map/ppermute | solution.py:153
  65.1 30.1 %copy-start.3 = (s32[8,1]{0,1:T(1,128)S(1)}, s32[8,1]{0,1:T(1,128)}, u32[]{:S(2)}) copy-start(s32[8,1]{0,1:T(1,128)} %param.7) | copy-start | bytes 100

commit v16 on v14

--- a/solution.py
+++ b/solution.py
@@ -100,7 +100,8 @@
                 l_real, l_imag = second[:, :LANES], second[:, LANES:]
                 real = (k_real * l_real - k_imag * l_imag).astype(BF16)
                 imag = k_real * l_imag + k_imag * l_real
-                plus, minus = imag.astype(BF16), (-imag).astype(BF16)
+                plus = imag.astype(BF16)
+                minus = -plus
                 w_ref[48 * t : 48 * t + 24, :LANES] = real
                 w_ref[48 * t : 48 * t + 24, LANES:] = plus
                 w_ref[48 * t + 24 : 48 * t + 48, :LANES] = minus

time: 95.1 us -> 95.3 us (level)
  no operation moved by 1% of the time
where the time goes in v16:
time: 95.3 us; the launch traced here: 95.1 us
  starting transfers between devices  35.1 us (37%)
  blocking collectives  29.1 us (31%)
  waiting for transfers between devices  15.9 us (17%)
  Pallas kernels  12.4 us (13%)
  other arithmetic  1.5 us (2%)
    all_to_all x1, blocking collectives, body(): parts = lax.all_to_all(partial, ('x', 'yh', 'yl'), 0, 0)  20.8 us
    ppermute x7, starting transfers between devices, ring(): return lax.ppermute(array, ('z', 'core'), pairs)  16.9 us
    ppermute x8, starting transfers between devices, step(): lax.ppermute(array, axes, [(i, (i + by) % size) for i in range(size)])  10.8 us
    all_gather x1, blocking collectives, body(): gathered = lax.all_gather(rows, ('yl', 'core'), tiled=True)  8.27 us
    ppermute x7, waiting for transfers between devices, ring(): return lax.ppermute(array, ('z', 'core'), pairs)  7.81 us
    all_to_all x1, starting transfers between devices, body(): received = lax.all_to_all(pieces, ('x', 'yh'), 0, 0)  7.48 us
    all_to_all x1, waiting for transfers between devices, body(): received = lax.all_to_all(pieces, ('x', 'yh'), 0, 0)  7.4 us
    pallas_call x1, Pallas kernels, grams(): pl.pallas_call(grams_kernel, out_shape=jax.ShapeDtypeStruct((16, 2, 48, 3...  6.02 us
  transfers between devices with their start and end apart: 16, of which 6 were waited for; matrix products, arithmetic and copies ran while one was open for 0% of the time, Pallas kernels for 4%

profile of v16, /device:TPU:1, one launch (start us, length us, event | category | flops | bytes accessed | tf_op | source)
XLA Modules:
  0.0 95.1 jit_solution(12374942933613837576)
XLA Ops:
  0.0 2.4 %split.1 = bf16[8,152,128]{2,1,0:T(8,128)(2,1)} custom-call(bf16[48,24,128]{2,1,0:T(8,128)(2,1)} %bitcast.20, s32[8,16]{1,0:T(8,128)} %bitcast.21, f32[1,128]{1,0:T(1,128)} %bitcast.22), custom_call_target="tpu_custom_call" | custom-call | tf_op jit(solution)/shard_map/split/pallas_call | solution.py:208
  2.4 7.5 %all-to-all-start = ((bf16[8,152,128]{2,1,0:T(8,128)(2,1)}), bf16[8,152,128]{2,1,0:T(8,128)(2,1)S(1)}, u32[]{:S(2)}, u32[]{:S(2)}) async-start(bf16[8,152,128]{2,1,0:T(8,128)(2,1)} %split.1), calls=%async_computation | async-start | bytes 622592 | tf_op jit(solution)/shard_map/all_to_all | solution.py:216
  10.0 7.4 %all-to-all-done = bf16[8,152,128]{2,1,0:T(8,128)(2,1)S(1)} async-done(((bf16[8,152,128]{2,1,0:T(8,128)(2,1)}), bf16[8,152,128]{2,1,0:T(8,128)(2,1)S(1)}, u32[]{:S(2)}, u32[]{:S(2)}) %all-to-all-start) | async-done | bytes 311328 | tf_op jit(solution)/shard_map/all_to_all | solution.py:216
  17.4 5.7 %collective-permute-start.1 = (bf16[8,144,128]{2,1,0:T(8,128)(2,1)S(1)}, bf16[8,144,128]{2,1,0:T(8,128)(2,1)S(1)}, u32[]{:S(2)}, u32[]{:S(2)}) collective-permute-start(bf16[8,144,128]{2,1,0:T(8,128)(2,1)S(1)} %slice.33.own_ref), channel_id=1, source_target_pairs={{0,4},{1,29},{4,8},{5,1},{8,12},{9,5},{12,16},{13,9},{16,20},{17,1... | collective-permute-start | bytes 884744 | tf_op jit(solution)/shard_map/ppermute | solution.py:166
  23.0 0.4 collective-permute-start.5
  23.5 0.8 collective-permute-start
  24.4 4.2 %collective-permute-done.1.own_ref = bf16[8,144,128]{2,1,0:T(8,128)(2,1)S(1)} collective-permute-done((bf16[8,144,128]{2,1,0:T(8,128)(2,1)S(1)}, bf16[8,144,128]{2,1,0:T(8,128)(2,1)S(1)}, u32[]{:S(2)}, u32[]{:S(2)}) %collective-permute-start.1) | collective-permute-done | bytes 294944 | tf_op jit(solution)/shard_map/ppermute | solution.py:166
  28.5 1.0 %collective-permute-done.5.sib_ref = bf16[8,144,128]{2,1,0:T(8,128)(2,1)S(1)} collective-permute-done((bf16[8,144,128]{2,1,0:T(8,128)(2,1)S(1)}, bf16[8,144,128]{2,1,0:T(8,128)(2,1)S(1)}, u32[]{:S(2)}, u32[]{:S(2)}) %collective-permute-start.5) | collective-permute-done | bytes 294944 | tf_op jit(solution)/shard_map/ppermute | solution.py:166
  29.5 2.9 %collective-permute-start.10 = (bf16[8,144,128]{2,1,0:T(8,128)(2,1)S(1)}, bf16[8,144,128]{2,1,0:T(8,128)(2,1)S(1)}, u32[]{:S(2)}, u32[]{:S(2)}) collective-permute-start(bf16[8,144,128]{2,1,0:T(8,128)(2,1)S(1)} %collective-permute-done.5.sib_ref), channel_id=1, source_target_pairs={{0,1},{1,0},{2,3},{3,2},{4,5},{5,4},{6,7},{7,6},{8,9},{9,8},{10,11... | collective-permute-start | bytes 884744 | tf_op jit(solution)/shard_map/ppermute | solution.py:154
  32.4 2.5 %collective-permute-start.2 = (bf16[8,144,128]{2,1,0:T(8,128)(2,1)S(1)}, bf16[8,144,128]{2,1,0:T(8,128)(2,1)S(1)}, u32[]{:S(2)}, u32[]{:S(2)}) collective-permute-start(bf16[8,144,128]{2,1,0:T(8,128)(2,1)S(1)} %collective-permute-done.1.own_ref), channel_id=1, source_target_pairs={{0,4},{1,29},{4,8},{5,1},{8,12},{9,5},{12,16},{13,9},{16,20},{17,1... | collective-permute-start | bytes 884744 | tf_op jit(solution)/shard_map/ppermute | solution.py:166
  35.0 1.2 %collective-permute-start.6 = (bf16[8,144,128]{2,1,0:T(8,128)(2,1)S(1)}, bf16[8,144,128]{2,1,0:T(8,128)(2,1)S(1)}, u32[]{:S(2)}, u32[]{:S(2)}) collective-permute-start(bf16[8,144,128]{2,1,0:T(8,128)(2,1)S(1)} %collective-permute-done.5.sib_ref), channel_id=1, source_target_pairs={{0,4},{1,29},{4,8},{5,1},{8,12},{9,5},{12,16},{13,9},{16,20},{17,1... | collective-permute-start | bytes 884744 | tf_op jit(solution)/shard_map/ppermute | solution.py:166
  36.3 2.3 %collective-permute-done.2.own_ref = bf16[8,144,128]{2,1,0:T(8,128)(2,1)S(1)} collective-permute-done((bf16[8,144,128]{2,1,0:T(8,128)(2,1)S(1)}, bf16[8,144,128]{2,1,0:T(8,128)(2,1)S(1)}, u32[]{:S(2)}, u32[]{:S(2)}) %collective-permute-start.2) | collective-permute-done | bytes 294944 | tf_op jit(solution)/shard_map/ppermute | solution.py:166
  38.6 3.1 %collective-permute-start.3 = (bf16[8,144,128]{2,1,0:T(8,128)(2,1)S(1)}, bf16[8,144,128]{2,1,0:T(8,128)(2,1)S(1)}, u32[]{:S(2)}, u32[]{:S(2)}) collective-permute-start(bf16[8,144,128]{2,1,0:T(8,128)(2,1)S(1)} %collective-permute-done.2.own_ref), channel_id=1, source_target_pairs={{0,4},{1,29},{4,8},{5,1},{8,12},{9,5},{12,16},{13,9},{16,20},{17,1... | collective-permute-start | bytes 884744 | tf_op jit(solution)/shard_map/ppermute | solution.py:166
  41.7 0.5 unpack.8.refs_0_
  42.3 1.2 %collective-permute-start.8 = (bf16[8,144,128]{2,1,0:T(8,128)(2,1)S(1)}, bf16[8,144,128]{2,1,0:T(8,128)(2,1)S(1)}, u32[]{:S(2)}, u32[]{:S(2)}) collective-permute-start(bf16[8,144,128]{2,1,0:T(8,128)(2,1)S(1)} %collective-permute-done.6.sib_ref), channel_id=1, source_target_pairs={{0,1},{1,0},{2,3},{3,2},{4,5},{5,4},{6,7},{7,6},{8,9},{9,8},{10,11... | collective-permute-start | bytes 884744 | tf_op jit(solution)/shard_map/ppermute | solution.py:154
  43.5 1.9 %collective-permute-start.7 = (bf16[8,144,128]{2,1,0:T(8,128)(2,1)S(1)}, bf16[8,144,128]{2,1,0:T(8,128)(2,1)S(1)}, u32[]{:S(2)}, u32[]{:S(2)}) collective-permute-start(bf16[8,144,128]{2,1,0:T(8,128)(2,1)S(1)} %collective-permute-done.6.sib_ref), channel_id=1, source_target_pairs={{0,4},{1,29},{4,8},{5,1},{8,12},{9,5},{12,16},{13,9},{16,20},{17,1... | collective-permute-start | bytes 884744 | tf_op jit(solution)/shard_map/ppermute | solution.py:166
  45.4 0.5 unpack.9.refs_0_
  45.9 0.5 unpack.10.refs_0_
  46.5 2.1 %collective-permute-start.4 = (bf16[8,144,128]{2,1,0:T(8,128)(2,1)S(1)}, bf16[8,144,128]{2,1,0:T(8,128)(2,1)S(1)}, u32[]{:S(2)}, u32[]{:S(2)}) collective-permute-start(bf16[8,144,128]{2,1,0:T(8,128)(2,1)S(1)} %collective-permute-done.3.own_ref), channel_id=1, source_target_pairs={{0,4},{1,29},{4,8},{5,1},{8,12},{9,5},{12,16},{13,9},{16,20},{17,1... | collective-permute-start | bytes 884744 | tf_op jit(solution)/shard_map/ppermute | solution.py:166
  48.5 0.5 unpack.11.refs_0_
  49.4 2.6 %collective-permute-start.13 = (bf16[8,144,128]{2,1,0:T(8,128)(2,1)S(1)}, bf16[8,144,128]{2,1,0:T(8,128)(2,1)S(1)}, u32[]{:S(2)}, u32[]{:S(2)}) collective-permute-start(bf16[8,144,128]{2,1,0:T(8,128)(2,1)S(1)} %collective-permute-done.7.sib_ref), channel_id=1, source_target_pairs={{0,1},{1,0},{2,3},{3,2},{4,5},{5,4},{6,7},{7,6},{8,9},{9,8},{10,11... | collective-permute-start | bytes 884744 | tf_op jit(solution)/shard_map/ppermute | solution.py:154
  52.0 0.5 unpack.12.refs_0_
  52.5 0.5 unpack.13.refs_0_
  53.0 3.2 %collective-permute-start.12 = (bf16[8,144,128]{2,1,0:T(8,128)(2,1)S(1)}, bf16[8,144,128]{2,1,0:T(8,128)(2,1)S(1)}, u32[]{:S(2)}, u32[]{:S(2)}) collective-permute-start(bf16[8,144,128]{2,1,0:T(8,128)(2,1)S(1)} %collective-permute-done.4.own_ref), channel_id=1, source_target_pairs={{0,1},{1,0},{2,3},{3,2},{4,5},{5,4},{6,7},{7,6},{8,9},{9,8},{10,11... | collective-permute-start | bytes 884744 | tf_op jit(solution)/shard_map/ppermute | solution.py:154
  56.2 0.5 unpack.14.refs_0_
  56.7 0.7 collective-permute-done.12.sib_ref
  57.4 0.5 unpack.15.bins_ref
  57.9 6.0 %grams.1 = bf16[16,2,48,384]{3,2,1,0:T(8,128)(2,1)S(1)} custom-call(s32[64,32]{1,0:T(8,128)S(1)} %shift-right-arithmetic_add_fusion.slots_ref, bf16[8,128]{1,0:T(8,128)(2,1)S(1)} %slice_bitcast_fusion.1.own_w_ref, bf16[8,128]{1,0:T(8,128)(2,1)S(1)} %slice_bitcast_fusion.sib_w_ref, bf16[512,24,256]{2,1,0:T(8,128)(2,1)S(1)} %unpack.15.bins_ref), custom_call_target="tpu_custom_call" | custom-call | flops 12000000000 | bytes 8000000 | tf_op jit(solution)/shard_map/grams/pallas_call | solution.py:193
  64.0 20.8 %all_to_all.10 = bf16[16,2,48,384]{3,2,1,0:T(8,128)(2,1)S(1)} all-to-all(bf16[16,2,48,384]{3,2,1,0:T(8,128)(2,1)S(1)} %grams.1), channel_id=1, replica_groups=mesh['x'=4,'yh'=2,'z'=8,'yl'=2,'core'=2] {'x','yh','yl'}, dimensions={0} | all-to-all | bytes 2359296 | tf_op jit(solution)/shard_map/all_to_all | solution.py:251
  85.5 0.4 reshape.68
  85.8 8.3 %all_gather.3 = f32[8,1,16,1152]{3,2,1,0:T(8,128)S(1)} all-gather(f32[2,1,16,1152]{3,2,1,0:T(8,128)S(1)} %bitcast.19), channel_id=1, replica_groups=mesh['x'=4,'yh'=2,'z'=8,'yl'=2,'core'=2] {'yl','core'}, dimensions={0}, use_global_device_ids=true | all-gather | bytes 737280 | tf_op jit(solution)/shard_map/all_gather | solution.py:255
  94.2 0.9 broadcast_select_fusion
  (31 shorter events, 1.5 us)
Async XLA Ops:
  2.4 15.0 %all-to-all-start = ((bf16[8,152,128]{2,1,0:T(8,128)(2,1)}), bf16[8,152,128]{2,1,0:T(8,128)(2,1)S(1)}, u32[]{:S(2)}, u32[]{:S(2)}) async-start(bf16[8,152,128]{2,1,0:T(8,128)(2,1)} %split.1), calls=%async_computation | async-start | bytes 622592 | tf_op jit(solution)/shard_map/all_to_all | solution.py:216
  17.4 11.1 %collective-permute-start.1 = (bf16[8,144,128]{2,1,0:T(8,128)(2,1)S(1)}, bf16[8,144,128]{2,1,0:T(8,128)(2,1)S(1)}, u32[]{:S(2)}, u32[]{:S(2)}) collective-permute-start(bf16[8,144,128]{2,1,0:T(8,128)(2,1)S(1)} %slice.33.own_ref), channel_id=1, source_target_pairs={{0,4},{1,29},{4,8},{5,1},{8,12},{9,5},{12,16},{13,9},{16,20},{17,1... | collective-permute-start | bytes 884744 | tf_op jit(solution)/shard_map/ppermute | solution.py:166
  23.0 6.4 %collective-permute-start.5 = (bf16[8,144,128]{2,1,0:T(8,128)(2,1)S(1)}, bf16[8,144,128]{2,1,0:T(8,128)(2,1)S(1)}, u32[]{:S(2)}, u32[]{:S(2)}) collective-permute-start(bf16[8,144,128]{2,1,0:T(8,128)(2,1)S(1)} %slice.33.own_ref), channel_id=1, source_target_pairs={{0,29},{1,4},{4,1},{5,8},{8,5},{9,12},{12,9},{13,16},{16,13},{17,2... | collective-permute-start | bytes 884744 | tf_op jit(solution)/shard_map/ppermute | solution.py:166
  23.5 12.8 %collective-permute-start = (bf16[8,152,128]{2,1,0:T(8,128)(2,1)S(1)}, bf16[8,152,128]{2,1,0:T(8,128)(2,1)S(1)}, u32[]{:S(2)}, u32[]{:S(2)}) collective-permute-start(bf16[8,152,128]{2,1,0:T(8,128)(2,1)S(1)} %all-to-all-done), channel_id=1, source_target_pairs={{0,1},{1,0},{2,3},{3,2},{4,5},{5,4},{6,7},{7,6},{8,9},{9,8},{10,11... | collective-permute-start | bytes 933896 | tf_op jit(solution)/shard_map/ppermute | solution.py:154
  29.5 14.0 %collective-permute-start.10 = (bf16[8,144,128]{2,1,0:T(8,128)(2,1)S(1)}, bf16[8,144,128]{2,1,0:T(8,128)(2,1)S(1)}, u32[]{:S(2)}, u32[]{:S(2)}) collective-permute-start(bf16[8,144,128]{2,1,0:T(8,128)(2,1)S(1)} %collective-permute-done.5.sib_ref), channel_id=1, source_target_pairs={{0,1},{1,0},{2,3},{3,2},{4,5},{5,4},{6,7},{7,6},{8,9},{9,8},{10,11... | collective-permute-start | bytes 884744 | tf_op jit(solution)/shard_map/ppermute | solution.py:154
  32.4 6.2 %collective-permute-start.2 = (bf16[8,144,128]{2,1,0:T(8,128)(2,1)S(1)}, bf16[8,144,128]{2,1,0:T(8,128)(2,1)S(1)}, u32[]{:S(2)}, u32[]{:S(2)}) collective-permute-start(bf16[8,144,128]{2,1,0:T(8,128)(2,1)S(1)} %collective-permute-done.1.own_ref), channel_id=1, source_target_pairs={{0,4},{1,29},{4,8},{5,1},{8,12},{9,5},{12,16},{13,9},{16,20},{17,1... | collective-permute-start | bytes 884744 | tf_op jit(solution)/shard_map/ppermute | solution.py:166
  35.0 7.3 %collective-permute-start.6 = (bf16[8,144,128]{2,1,0:T(8,128)(2,1)S(1)}, bf16[8,144,128]{2,1,0:T(8,128)(2,1)S(1)}, u32[]{:S(2)}, u32[]{:S(2)}) collective-permute-start(bf16[8,144,128]{2,1,0:T(8,128)(2,1)S(1)} %collective-permute-done.5.sib_ref), channel_id=1, source_target_pairs={{0,4},{1,29},{4,8},{5,1},{8,12},{9,5},{12,16},{13,9},{16,20},{17,1... | collective-permute-start | bytes 884744 | tf_op jit(solution)/shard_map/ppermute | solution.py:166
  36.2 9.8 %collective-permute-start.11 = (bf16[8,144,128]{2,1,0:T(8,128)(2,1)S(1)}, bf16[8,144,128]{2,1,0:T(8,128)(2,1)S(1)}, u32[]{:S(2)}, u32[]{:S(2)}) collective-permute-start(bf16[8,144,128]{2,1,0:T(8,128)(2,1)S(1)} %collective-permute-done.1.own_ref), channel_id=1, source_target_pairs={{0,1},{1,0},{2,3},{3,2},{4,5},{5,4},{6,7},{7,6},{8,9},{9,8},{10,11... | collective-permute-start | bytes 884744 | tf_op jit(solution)/shard_map/ppermute | solution.py:154
  38.6 7.8 %collective-permute-start.3 = (bf16[8,144,128]{2,1,0:T(8,128)(2,1)S(1)}, bf16[8,144,128]{2,1,0:T(8,128)(2,1)S(1)}, u32[]{:S(2)}, u32[]{:S(2)}) collective-permute-start(bf16[8,144,128]{2,1,0:T(8,128)(2,1)S(1)} %collective-permute-done.2.own_ref), channel_id=1, source_target_pairs={{0,4},{1,29},{4,8},{5,1},{8,12},{9,5},{12,16},{13,9},{16,20},{17,1... | collective-permute-start | bytes 884744 | tf_op jit(solution)/shard_map/ppermute | solution.py:166
  42.3 9.7 %collective-permute-start.8 = (bf16[8,144,128]{2,1,0:T(8,128)(2,1)S(1)}, bf16[8,144,128]{2,1,0:T(8,128)(2,1)S(1)}, u32[]{:S(2)}, u32[]{:S(2)}) collective-permute-start(bf16[8,144,128]{2,1,0:T(8,128)(2,1)S(1)} %collective-permute-done.6.sib_ref), channel_id=1, source_target_pairs={{0,1},{1,0},{2,3},{3,2},{4,5},{5,4},{6,7},{7,6},{8,9},{9,8},{10,11... | collective-permute-start | bytes 884744 | tf_op jit(solution)/shard_map/ppermute | solution.py:154
  43.5 8.5 %collective-permute-start.9 = (bf16[8,144,128]{2,1,0:T(8,128)(2,1)S(1)}, bf16[8,144,128]{2,1,0:T(8,128)(2,1)S(1)}, u32[]{:S(2)}, u32[]{:S(2)}) collective-permute-start(bf16[8,144,128]{2,1,0:T(8,128)(2,1)S(1)} %collective-permute-done.2.own_ref), channel_id=1, source_target_pairs={{0,1},{1,0},{2,3},{3,2},{4,5},{5,4},{6,7},{7,6},{8,9},{9,8},{10,11... | collective-permute-start | bytes 884744 | tf_op jit(solution)/shard_map/ppermute | solution.py:154
  43.5 5.9 %collective-permute-start.7 = (bf16[8,144,128]{2,1,0:T(8,128)(2,1)S(1)}, bf16[8,144,128]{2,1,0:T(8,128)(2,1)S(1)}, u32[]{:S(2)}, u32[]{:S(2)}) collective-permute-start(bf16[8,144,128]{2,1,0:T(8,128)(2,1)S(1)} %collective-permute-done.6.sib_ref), channel_id=1, source_target_pairs={{0,4},{1,29},{4,8},{5,1},{8,12},{9,5},{12,16},{13,9},{16,20},{17,1... | collective-permute-start | bytes 884744 | tf_op jit(solution)/shard_map/ppermute | solution.py:166
  46.5 6.5 %collective-permute-start.4 = (bf16[8,144,128]{2,1,0:T(8,128)(2,1)S(1)}, bf16[8,144,128]{2,1,0:T(8,128)(2,1)S(1)}, u32[]{:S(2)}, u32[]{:S(2)}) collective-permute-start(bf16[8,144,128]{2,1,0:T(8,128)(2,1)S(1)} %collective-permute-done.3.own_ref), channel_id=1, source_target_pairs={{0,4},{1,29},{4,8},{5,1},{8,12},{9,5},{12,16},{13,9},{16,20},{17,1... | collective-permute-start | bytes 884744 | tf_op jit(solution)/shard_map/ppermute | solution.py:166
  49.4 6.8 %collective-permute-start.13 = (bf16[8,144,128]{2,1,0:T(8,128)(2,1)S(1)}, bf16[8,144,128]{2,1,0:T(8,128)(2,1)S(1)}, u32[]{:S(2)}, u32[]{:S(2)}) collective-permute-start(bf16[8,144,128]{2,1,0:T(8,128)(2,1)S(1)} %collective-permute-done.7.sib_ref), channel_id=1, source_target_pairs={{0,1},{1,0},{2,3},{3,2},{4,5},{5,4},{6,7},{7,6},{8,9},{9,8},{10,11... | collective-permute-start | bytes 884744 | tf_op jit(solution)/shard_map/ppermute | solution.py:154
  52.0 4.3 %collective-permute-start.14 = (bf16[8,144,128]{2,1,0:T(8,128)(2,1)S(1)}, bf16[8,144,128]{2,1,0:T(8,128)(2,1)S(1)}, u32[]{:S(2)}, u32[]{:S(2)}) collective-permute-start(bf16[8,144,128]{2,1,0:T(8,128)(2,1)S(1)} %collective-permute-done.3.own_ref), channel_id=1, source_target_pairs={{0,1},{1,0},{2,3},{3,2},{4,5},{5,4},{6,7},{7,6},{8,9},{9,8},{10,11... | collective-permute-start | bytes 884744 | tf_op jit(solution)/shard_map/ppermute | solution.py:154
  53.0 4.4 %collective-permute-start.12 = (bf16[8,144,128]{2,1,0:T(8,128)(2,1)S(1)}, bf16[8,144,128]{2,1,0:T(8,128)(2,1)S(1)}, u32[]{:S(2)}, u32[]{:S(2)}) collective-permute-start(bf16[8,144,128]{2,1,0:T(8,128)(2,1)S(1)} %collective-permute-done.4.own_ref), channel_id=1, source_target_pairs={{0,1},{1,0},{2,3},{3,2},{4,5},{5,4},{6,7},{7,6},{8,9},{9,8},{10,11... | collective-permute-start | bytes 884744 | tf_op jit(solution)/shard_map/ppermute | solution.py:154
  64.0 30.1 %copy-start = (s32[8,1]{0,1:T(1,128)S(1)}, s32[8,1]{0,1:T(1,128)}, u32[]{:S(2)}) copy-start(s32[8,1]{0,1:T(1,128)} %param.7) | copy-start | bytes 100
